TPU v7x, 512 devices: a whole 4x8x8 slice. The times are simulated.
512 devices in a mesh: mesh: 32 (over y, z_lo), panel: 16 (over z_hi, x, core).
Axes of the slice: x: 4, y: 8, z: 8 (z_hi: 2, z_lo: 4; z = z_hi * 4 + z_lo), core: 2. Of those that a mesh axis runs over, the one named last changes fastest.
Arguments:
- basis_vectors: bfloat16 [256, 1024, 192], P('mesh', 'panel'), may hold values from -0.75 to 0.75
- stiffness_blocks: bfloat16 [1792, 192, 192], P('mesh'), may hold values from -0.21875 to 0.21875
- block_rows: int32 [1792], P('mesh'), may hold values from 0 to 7
- block_columns: int32 [1792], P('mesh'), may hold values from 0 to 23
- density: float32 [1792], P('mesh'), may hold values from 0.1 to 1
- block_counts: int32 [32], P('mesh'), may hold values from 14 to 56, as said below
- send_list: int32 [512], P('mesh'), may hold values from 0 to 7
Outputs:
- reduced: float32 [1024, 1024], P('panel', 'mesh')
Inputs may be any that keep to these rules, and one draw needn't show every extreme that they name: `block_counts`: in every draw some partition holds exactly 56 and another exactly 14.
All inputs are finite; a program needn't handle non-finite values.
Results may differ from a plain program's by a relative error of at most 0.0029.
Values may be sent and summed in bfloat16 or wider, within the bound.
No kernel may reach another device: no remote copies, remote signals or barrier semaphores. Data moves between devices by JAX's collectives and lax.ppermute only.
A program may use at most 64 MiB of HBM per device.

v0:
```python
import jax
import jax.numpy as jnp
from jax import lax
from jax.sharding import PartitionSpec as P

GMAX = 4


neighbour_offsets = (1, -1, 2, -2)


def passed_along(block, axis, distance):
    devices = range(lax.axis_size(axis))
    route = [((i - distance) % len(devices), i) for i in devices]
    return lax.ppermute(block, axis, route)


def group_term(source_pool, blocks_here, rows_here, columns, scale, clusters):
    sources = source_pool[columns]
    product = jnp.einsum("bpj,bij->bpi", sources, blocks_here, preferred_element_type=jnp.float32)
    selector = (rows_here[None, :] == jnp.arange(clusters, dtype=jnp.int32)[:, None]).astype(
        jnp.float32
    ) * scale[None, :]
    return jnp.dot(selector, product.reshape(product.shape[0], -1), precision=lax.Precision.HIGHEST)


def local(
    basis_vectors, stiffness_blocks, block_rows, block_columns, density, block_counts, send_list
):
    clusters, panel_width, cluster_dofs = basis_vectors.shape
    capacity = stiffness_blocks.shape[0]
    arriving = []
    for neighbour, offset in enumerate(neighbour_offsets):
        listed = send_list[neighbour * GMAX : (neighbour + 1) * GMAX]
        picked = basis_vectors[listed]
        arriving.append(passed_along(picked, "mesh", offset))
    source_pool = jnp.concatenate([basis_vectors] + arriving, axis=0)
    active = jnp.arange(capacity, dtype=jnp.int32) < block_counts[0]
    scale = jnp.where(active, 0.001 + density**3, jnp.float32(0.0))
    summed = group_term(source_pool, stiffness_blocks, block_rows, block_columns, scale, clusters)
    products = summed.reshape(clusters, panel_width, cluster_dofs).astype(jnp.bfloat16)
    gathered = lax.all_gather(products, "panel", axis=1, tiled=True)
    partial_tile = jnp.einsum(
        "npc,nqc->pq", basis_vectors, gathered, preferred_element_type=jnp.float32
    )
    return lax.psum_scatter(partial_tile, "mesh", scatter_dimension=1, tiled=True)


def solution(mesh):
    placed = (
        P("mesh", "panel", None),
        P("mesh", None, None),
        P("mesh"),
        P("mesh"),
        P("mesh"),
        P("mesh"),
        P("mesh"),
    )
    return jax.shard_map(
        local, mesh=mesh, in_specs=placed, out_specs=P("panel", "mesh"), check_vma=False
    )
```

profile of v0, /device:TPU:6, one launch (start us, length us, event | category | flops | bytes accessed | tf_op | source)
XLA Modules:
  0.0 313.6 jit_solution(4097579712472747053)
XLA Ops:
  6.5 0.9 compare_select_fusion.1
  7.4 1.5 gather_fusion
  8.9 4.3 %collective-permute-start = (bf16[4,64,192]{2,1,0:T(8,128)(2,1)S(1)}, bf16[4,64,192]{2,1,0:T(8,128)(2,1)S(1)}, u32[]{:S(2)}, u32[]{:S(2)}) collective-permute-start(bf16[4,64,192]{2,1,0:T(8,128)(2,1)S(1)} %gather_fusion), channel_id=1, source_target_pairs={{496,0},{0,16},{16,32},{32,48},{48,64},{64,80},{80,96},{96,112},{1... | collective-permute-start | bytes 294920 | tf_op jit(solution)/shard_map/ppermute | solution.py:15
  13.2 1.5 gather_fusion.1
  14.8 8.4 %collective-permute-start.1 = (bf16[4,64,192]{2,1,0:T(8,128)(2,1)S(1)}, bf16[4,64,192]{2,1,0:T(8,128)(2,1)S(1)}, u32[]{:S(2)}, u32[]{:S(2)}) collective-permute-start(bf16[4,64,192]{2,1,0:T(8,128)(2,1)S(1)} %gather_fusion.1), channel_id=1, source_target_pairs={{16,0},{32,16},{48,32},{64,48},{80,64},{96,80},{112,96},{128,112},... | collective-permute-start | bytes 294920 | tf_op jit(solution)/shard_map/ppermute | solution.py:15
  23.2 1.5 gather_fusion.2
  24.7 1.9 collective-permute-start.2
  26.7 1.5 gather_fusion.3
  28.2 6.9 %collective-permute-start.3 = (bf16[4,64,192]{2,1,0:T(8,128)(2,1)S(1)}, bf16[4,64,192]{2,1,0:T(8,128)(2,1)S(1)}, u32[]{:S(2)}, u32[]{:S(2)}) collective-permute-start(bf16[4,64,192]{2,1,0:T(8,128)(2,1)S(1)} %gather_fusion.3), channel_id=1, source_target_pairs={{32,0},{48,16},{64,32},{80,48},{96,64},{112,80},{128,96},{144,112}... | collective-permute-start | bytes 294920 | tf_op jit(solution)/shard_map/ppermute | solution.py:15
  35.1 1.0 constant_dynamic-update-slice_fusion.4
  36.1 0.7 compare_select_fusion
  37.4 0.7 compare_select_fusion.5
  38.2 1.9 collective-permute-done.3
  40.1 0.7 gather_fusion.4
  40.8 6.2 %fusion.9 = f32[56,64,192]{2,1,0:T(8,128)} fusion(bf16[56,64,192]{2,1,0:T(8,128)(2,1)S(1)} %gather_fusion.4, bf16[56,192,192]{2,1,0:T(8,128)(2,1)} %param.8), kind=kOutput, calls=%fused_computation.34 | convolution fusion | flops 264241152 | bytes 8257536 | tf_op jit(solution)/shard_map/bpj,bij->bpi/dot_general | solution.py:20
  47.0 3.3 %reshape.7 = f32[56,12288]{1,0:T(8,128)S(1)} reshape(f32[56,64,192]{2,1,0:T(8,128)} %fusion.9) | data formatting | bytes 5505024 | tf_op jit(solution)/shard_map/reshape | solution.py:24
  50.4 3.5 %dot_general.17 = f32[64,192,56]{1,0,2:T(8,128)} reshape(f32[12288,56]{0,1:T(8,128)S(1)} %bitcast.18) | data formatting | bytes 5505024 | tf_op jit(solution)/shard_map/dot_general | solution.py:24
  53.8 5.9 %fusion = bf16[8,64,192]{2,0,1:T(8,128)(2,1)S(1)} fusion(f32[64,192,56]{1,0,2:T(8,128)} %dot_general.17, f32[56]{0:T(128)S(1)} %compare_select_fusion.5, s32[56]{0:T(128)S(1)} %copy-done.1), kind=kOutput, calls=%fused_computation.5 | convolution fusion | flops 66061184 | bytes 2949568 | tf_op jit(solution)/shard_map/dot_general | solution.py:24
  59.7 0.8 copy.17
  60.5 0.0 reduce-scatter.4.cloned.1.call-start
  60.5 84.6 %all-gather.2.cloned.1.call-done = bf16[8,1024,192]{2,1,0:T(8,128)(2,1)} async-done(((bf16[8,64,192]{2,1,0:T(8,128)(2,1)}), bf16[8,1024,192]{2,1,0:T(8,128)(2,1)}) %all-gather.2.cloned.1.call-update) | async-done | bytes 3145744 | tf_op jit(solution)/shard_map/all_gather | solution.py:42
  145.1 3.6 %convolution_bitcast_fusion = f32[64,1024]{1,0:T(8,128)S(1)} fusion(bf16[8,1024,192]{2,1,0:T(8,128)(2,1)} %all-gather.2.cloned.1.call-done, bf16[8,64,192]{2,1,0:T(8,128)(2,1)S(1)} %copy-done), kind=kOutput, calls=%fused_computation.7 | convolution fusion | flops 201326592 | bytes 3604480 | tf_op jit(solution)/shard_map/npc,nqc->pq/dot_general | solution.py:43
  148.7 1.0 copy.12
  149.7 157.1 %reduce-scatter.4.cloned.1.call-done = f32[32,64]{1,0:T(8,128)} async-done(((f32[1024,64]{1,0:T(8,128)}), f32[32,64]{1,0:T(8,128)}) %reduce-scatter.4.cloned.1.call-update) | async-done | bytes 8208
  (19 shorter events, 0.1 us)
Async XLA Ops:
  6.5 138.6 %all-gather.2.cloned.1.call-start = ((), (), s32[]{:S(2)}) async-start(), calls=%async_computation.1 | async-start | bytes 4456448 | tf_op jit(solution)/shard_map/all_gather | solution.py:42
  8.9 29.1 %collective-permute-start = (bf16[4,64,192]{2,1,0:T(8,128)(2,1)S(1)}, bf16[4,64,192]{2,1,0:T(8,128)(2,1)S(1)}, u32[]{:S(2)}, u32[]{:S(2)}) collective-permute-start(bf16[4,64,192]{2,1,0:T(8,128)(2,1)S(1)} %gather_fusion), channel_id=1, source_target_pairs={{496,0},{0,16},{16,32},{32,48},{48,64},{64,80},{80,96},{96,112},{1... | collective-permute-start | bytes 294920 | tf_op jit(solution)/shard_map/ppermute | solution.py:15
  14.8 23.4 %collective-permute-start.1 = (bf16[4,64,192]{2,1,0:T(8,128)(2,1)S(1)}, bf16[4,64,192]{2,1,0:T(8,128)(2,1)S(1)}, u32[]{:S(2)}, u32[]{:S(2)}) collective-permute-start(bf16[4,64,192]{2,1,0:T(8,128)(2,1)S(1)} %gather_fusion.1), channel_id=1, source_target_pairs={{16,0},{32,16},{48,32},{64,48},{80,64},{96,80},{112,96},{128,112},... | collective-permute-start | bytes 294920 | tf_op jit(solution)/shard_map/ppermute | solution.py:15
  24.7 13.4 %collective-permute-start.2 = (bf16[4,64,192]{2,1,0:T(8,128)(2,1)S(1)}, bf16[4,64,192]{2,1,0:T(8,128)(2,1)S(1)}, u32[]{:S(2)}, u32[]{:S(2)}) collective-permute-start(bf16[4,64,192]{2,1,0:T(8,128)(2,1)S(1)} %gather_fusion.2), channel_id=1, source_target_pairs={{480,0},{496,16},{0,32},{16,48},{32,64},{48,80},{64,96},{80,112},{... | collective-permute-start | bytes 294920 | tf_op jit(solution)/shard_map/ppermute | solution.py:15
  28.2 11.9 %collective-permute-start.3 = (bf16[4,64,192]{2,1,0:T(8,128)(2,1)S(1)}, bf16[4,64,192]{2,1,0:T(8,128)(2,1)S(1)}, u32[]{:S(2)}, u32[]{:S(2)}) collective-permute-start(bf16[4,64,192]{2,1,0:T(8,128)(2,1)S(1)} %gather_fusion.3), channel_id=1, source_target_pairs={{32,0},{48,16},{64,32},{80,48},{96,64},{112,80},{128,96},{144,112}... | collective-permute-start | bytes 294920 | tf_op jit(solution)/shard_map/ppermute | solution.py:15
  50.3 3.5 %copy-start.1 = (s32[56]{0:T(128)S(1)}, s32[56]{0:T(128)}, u32[]{:S(2)}) copy-start(s32[56]{0:T(128)} %param.9) | copy-start | bytes 676
  53.8 91.3 %copy-start = (bf16[8,64,192]{2,1,0:T(8,128)(2,1)S(1)}, bf16[8,64,192]{2,1,0:T(8,128)(2,1)}, u32[]{:S(2)}) copy-start(bf16[8,64,192]{2,1,0:T(8,128)(2,1)} %param.7) | copy-start | bytes 589828
  60.5 246.3 %reduce-scatter.4.cloned.1.call-start = ((), (), s32[]{:S(2)}) async-start(), calls=%async_computation.2 | async-start | bytes 540672
Sparse Core Ops, SparseCore 0:
  60.6 84.4 all-gather.1
  149.8 156.9 reduce-scatter.3
where the time goes:
time: 314 us
  waiting for transfers between devices  244 us (78%)
  starting transfers between devices  21.6 us (7%)
  local copies, waits for them, and re-layouts  16.3 us (5%)
  matrix products  15.7 us (5%)
  between operations  14.2 us (5%)
    unnamed x3, waiting for transfers between devices  157 us
    all_gather x1, waiting for transfers between devices, local(): gathered = lax.all_gather(products, 'panel', axis=1, tiled=True)  84.6 us
    ppermute x4, starting transfers between devices, passed_along(): return lax.ppermute(block, axis, route)  21.6 us
  transfers between devices with their start and end apart: 6, of which 3 were waited for; matrix products, arithmetic and copies ran while one was open for 2% of the time, Pallas kernels for 0%

commit v1 on v0

v1 whole, which is shorter than its diff:
```python
import functools

import jax
import jax.numpy as jnp
from jax import lax
from jax.experimental import pallas as pl
from jax.experimental.pallas import tpu as pltpu
from jax.sharding import Mesh
from jax.sharding import PartitionSpec as P

GMAX = 4
NEIGH = 4
DOFS = 192
OWN = 8
WIDTH = 64
CAP = 56
CHUNK = 8
PACKED = OWN * DOFS

neighbour_offsets = (1, -1, 2, -2)
VMEM = pl.BlockSpec(memory_space=pltpu.VMEM)
SMEM = pl.BlockSpec(memory_space=pltpu.SMEM)


def pack_pair(first, second, out_ref, at):
    dtype = out_ref.dtype
    out_ref[:, at : at + 128] = first[:, :128].astype(dtype)
    out_ref[:, at + 128 : at + 256] = second[:, :128].astype(dtype)
    rest = jnp.concatenate([first[:, 128:], second[:, 128:]], axis=1)
    out_ref[:, at + 256 : at + 384] = rest.astype(dtype)


def select_kernel(send_ref, basis_ref, packed_ref, *ghost_refs):
    for neighbour, ghost_ref in enumerate(ghost_refs):
        for pair in range(GMAX // 2):
            at = neighbour * GMAX + 2 * pair
            pack_pair(
                basis_ref[send_ref[at]], basis_ref[send_ref[at + 1]], ghost_ref, 384 * pair
            )
    for pair in range(OWN // 2):
        pack_pair(basis_ref[2 * pair], basis_ref[2 * pair + 1], packed_ref, 384 * pair)


def block_kernel(
    rows_ref, columns_ref, density_ref, count_ref, basis_ref, *rest
):
    ghost_refs = rest[:NEIGH]
    blocks_hbm, out_ref, blocks, pool, total, arrived = rest[NEIGH:]
    copies = []
    for chunk in range(CAP // CHUNK):
        part = pl.ds(chunk * CHUNK, CHUNK)
        copies.append(
            pltpu.make_async_copy(blocks_hbm.at[part], blocks.at[part], arrived.at[chunk])
        )
        copies[-1].start()
    pool[:OWN] = basis_ref[...]
    for neighbour, ghost_ref in enumerate(ghost_refs):
        for pair in range(GMAX // 2):
            at, slot = 384 * pair, OWN + neighbour * GMAX + 2 * pair
            pool[slot, :, :128] = ghost_ref[:, at : at + 128]
            pool[slot + 1, :, :128] = ghost_ref[:, at + 128 : at + 256]
            pool[slot, :, 128:] = ghost_ref[:, at + 256 : at + 320]
            pool[slot + 1, :, 128:] = ghost_ref[:, at + 320 : at + 384]
    total[...] = jnp.zeros_like(total)
    count = count_ref[0]
    for chunk in range(CAP // CHUNK):
        copies[chunk].wait()
        for block in range(chunk * CHUNK, (chunk + 1) * CHUNK):
            density = density_ref[block]
            scale = jnp.where(block < count, 0.001 + density * density * density, 0.0)
            product = lax.dot_general(
                pool[columns_ref[block]],
                blocks[block],
                (((1,), (1,)), ((), ())),
                preferred_element_type=jnp.float32,
            )
            row = rows_ref[block]
            total[row] = total[row] + scale * product
    for pair in range(OWN // 2):
        pack_pair(total[2 * pair], total[2 * pair + 1], out_ref, 384 * pair)


def tile_kernel(half_ref, rows_ref, own_ref, other_ref, out_ref):
    half = half_ref[0]
    low_lanes = lax.broadcasted_iota(jnp.int32, (16, 128), 1) < WIDTH
    for index, ref in ((half, own_ref), (1 - half, other_ref)):
        tile = lax.dot_general(
            ref[...], rows_ref[...], (((1,), (1,)), ((), ())), preferred_element_type=jnp.float32
        )
        for h in range(2):
            for x in range(4):
                low = tile[32 * h : 32 * h + 16, 128 * x : 128 * x + 128]
                high = tile[32 * h + 16 : 32 * h + 32, 128 * x : 128 * x + 128]
                low_turned = pltpu.roll(low, WIDTH, 1)
                high_turned = pltpu.roll(high, WIDTH, 1)
                at = 16 * index + 4 * x + h
                out_ref[at] = jnp.where(low_lanes, low, high_turned).astype(out_ref.dtype)
                out_ref[at + 2] = jnp.where(low_lanes, low_turned, high).astype(out_ref.dtype)


def sum_kernel(parts_ref, out_ref):
    total = jnp.sum(parts_ref[...].astype(jnp.float32), axis=0)
    out_ref[:16] = total[:, :WIDTH]
    out_ref[16:] = total[:, WIDTH:]


def local(
    basis_vectors, stiffness_blocks, block_rows, block_columns, density, block_counts, send_list
):
    mesh_axes, whole = ("y", "z_lo"), ("y", "z_lo", "z_hi", "x", "core")
    parts = lax.axis_size(mesh_axes)
    shape = jax.ShapeDtypeStruct
    packed, *picked = pl.pallas_call(
        select_kernel,
        out_shape=[shape((WIDTH, PACKED), jnp.bfloat16)]
        + [shape((WIDTH, GMAX * DOFS), jnp.bfloat16)] * NEIGH,
        in_specs=[SMEM, VMEM],
        out_specs=[VMEM] * (1 + NEIGH),
        name="select",
    )(send_list, basis_vectors)
    basis_rows = lax.all_gather(packed, ("x", "core"), axis=0, tiled=True)
    arriving = []
    for block, offset in zip(picked, neighbour_offsets):
        route = [((i - offset) % parts, i) for i in range(parts)]
        arriving.append(lax.ppermute(block, mesh_axes, route))
    products = pl.pallas_call(
        block_kernel,
        out_shape=shape((WIDTH, PACKED), jnp.bfloat16),
        in_specs=[SMEM] * 4 + [VMEM] * (1 + NEIGH) + [pl.BlockSpec(memory_space=pl.ANY)],
        out_specs=VMEM,
        scratch_shapes=[
            pltpu.VMEM((CAP, DOFS, DOFS), jnp.bfloat16),
            pltpu.VMEM((OWN + NEIGH * GMAX, WIDTH, DOFS), jnp.bfloat16),
            pltpu.VMEM((OWN, WIDTH, DOFS), jnp.float32),
            pltpu.SemaphoreType.DMA((CAP // CHUNK,)),
        ],
        compiler_params=pltpu.CompilerParams(vmem_limit_bytes=32 << 20),
        name="blocks",
    )(block_rows, block_columns, density, block_counts, basis_vectors, *arriving, stiffness_blocks)
    other = lax.ppermute(products, "z_hi", [(0, 1), (1, 0)])
    half = lax.axis_index("z_hi").astype(jnp.int32).reshape(1)
    chunks = pl.pallas_call(
        tile_kernel,
        out_shape=shape((parts, 16, 128), jnp.float32),
        in_specs=[SMEM] + [VMEM] * 3,
        out_specs=VMEM,
        compiler_params=pltpu.CompilerParams(vmem_limit_bytes=32 << 20),
        name="tile",
    )(half, basis_rows, products, other)
    shares = lax.all_to_all(chunks, mesh_axes, 0, 0, tiled=True)
    block = pl.pallas_call(
        sum_kernel,
        out_shape=shape((32, WIDTH), jnp.float32),
        in_specs=[VMEM],
        out_specs=VMEM,
        name="sum",
    )(shares)
    route = []
    for zh2 in range(2):
        for h in range(2):
            for zh in range(2):
                for a in range(8):
                    for b in range(8):
                        source = (zh2 * 16 + b * 2 + h) * 16 + zh * 8 + a
                        target = (zh2 * 16 + a * 2 + h) * 16 + zh * 8 + b
                        route.append((source, target))
    return lax.ppermute(block, whole, route).T


def solution(mesh):
    fine = Mesh(mesh.devices.reshape(8, 4, 2, 4, 2), ("y", "z_lo", "z_hi", "x", "core"))
    over_mesh, over_panel = ("y", "z_lo"), ("z_hi", "x", "core")
    placed = (
        P(over_mesh, over_panel, None),
        P(over_mesh, None, None),
        P(over_mesh),
        P(over_mesh),
        P(over_mesh),
        P(over_mesh),
        P(over_mesh),
    )
    return jax.shard_map(
        local, mesh=fine, in_specs=placed, out_specs=P(over_panel, over_mesh), check_vma=False
    )
```

time: 314 us -> 102 us (0.32)
  waiting for transfers between devices: 244 us -> 17.8 us
  blocking collectives: 0 us -> 20.4 us
  matrix products: 15.7 us -> 0 us
  starting transfers between devices: 21.6 us -> 33.2 us
  local copies, waits for them, and re-layouts: 16.3 us -> 7.51 us
  Pallas kernels: 0 us -> 8.58 us
    unnamed x3 -> x1, waiting for transfers between devices: 157 us -> 0.02 us
    all_gather x1, waiting for transfers between devices: 84.6 us -> 0.01 us  [local(): basis_rows = lax.all_gather(packed, ('x', 'core'), axis=0, tiled=True)]
    all_to_all x0 -> x1, blocking collectives: none -> 20.4 us  [local(): shares = lax.all_to_all(chunks, mesh_axes, 0, 0, tiled=True)]
    ppermute x4 -> x6, waiting for transfers between devices: 1.93 us -> 17.8 us  [the longest x1 7.98 us: local(): other = lax.ppermute(products, 'z_hi', [(0, 1), (1, 0)])]
    dot_general x3 -> x0, matrix products: 15.7 us -> none  [the longest x1 6.24 us: group_term(): jnp.einsum('bpj,bij->bpi', sources, blocks_here, preferred_element_type=j...]
    ppermute x4 -> x6, starting transfers between devices: 21.6 us -> 33.2 us  [the longest x4 21.6 us: local(): arriving.append(lax.ppermute(block, mesh_axes, route))]
    pallas_call x0 -> x4, Pallas kernels: none -> 8.58 us  [the longest x1 3.93 us: local(): pl.pallas_call(block_kernel, out_shape=shape((WIDTH, PACKED), jnp.bfloat1...]
    gather x5 -> x0, local copies, waits for them, and re-layouts: 6.7 us -> none  [the longest x4 6.03 us: local(): picked = basis_vectors[listed]]
  transfers between devices with their start and end apart: 6 -> 7, of which waited for: 3 -> 4; matrix products, arithmetic and copies ran while one was open for 2% -> 0% of each run, Pallas kernels for 0% -> 4%
where the time goes in v1:
time: 102 us
  starting transfers between devices  33.2 us (33%)
  blocking collectives  20.4 us (20%)
  waiting for transfers between devices  17.8 us (17%)
  between operations  14.1 us (14%)
  Pallas kernels  8.58 us (8%)
  local copies, waits for them, and re-layouts  7.51 us (7%)
    ppermute x4, starting transfers between devices, local(): arriving.append(lax.ppermute(block, mesh_axes, route))  21.6 us
    all_to_all x1, blocking collectives, local(): shares = lax.all_to_all(chunks, mesh_axes, 0, 0, tiled=True)  20.4 us
    ppermute x1, starting transfers between devices, local(): other = lax.ppermute(products, 'z_hi', [(0, 1), (1, 0)])  8.22 us
    ppermute x1, waiting for transfers between devices, local(): other = lax.ppermute(products, 'z_hi', [(0, 1), (1, 0)])  7.98 us
    unnamed x13, local copies, waits for them, and re-layouts  7.51 us
    ppermute x1, waiting for transfers between devices, local(): return lax.ppermute(block, whole, route).T  6.31 us
    pallas_call x1, Pallas kernels, local(): pl.pallas_call(block_kernel, out_shape=shape((WIDTH, PACKED), jnp.bfloat1...  3.93 us
    ppermute x4, waiting for transfers between devices, local(): arriving.append(lax.ppermute(block, mesh_axes, route))  3.46 us
  transfers between devices with their start and end apart: 7, of which 4 were waited for; matrix products, arithmetic and copies ran while one was open for 0% of the time, Pallas kernels for 4%

profile of v1, /device:TPU:6, one launch (start us, length us, event | category | flops | bytes accessed | tf_op | source)
XLA Modules:
  0.0 101.6 jit_solution(17174100196352872151)
XLA Ops:
  6.5 1.8 %select.1 = (bf16[64,1536]{1,0:T(8,128)(2,1)}, bf16[64,768]{1,0:T(8,128)(2,1)}, bf16[64,768]{1,0:T(8,128)(2,1)}, bf16[64,768]{1,0:T(8,128)(2,1)}, bf16[64,768]{1,0:T(8,128)(2,1)}) custom-call(s32[16]{0:T(128)} %send_ref.1, bf16[8,64,192]{2,1,0:T(8,128)(2,1)} %basis_ref.3), custom_call_target="tpu_custom_call" | custom-call | tf_op jit(solution)/shard_map/select/pallas_call | solution.py:113
  8.4 0.0 all-gather.2.cloned.1.call-update
  8.4 4.3 %collective-permute-start = (bf16[64,768]{1,0:T(8,128)(2,1)}, bf16[64,768]{1,0:T(8,128)(2,1)S(1)}, u32[]{:S(2)}, u32[]{:S(2)}) collective-permute-start(bf16[64,768]{1,0:T(8,128)(2,1)} %get-tuple-element.11), channel_id=1, source_target_pairs={{496,0},{0,16},{16,32},{32,48},{48,64},{64,80},{80,96},{96,112},{1... | collective-permute-start | bytes 294920 | tf_op jit(solution)/shard_map/ppermute | solution.py:125
  12.7 8.4 %collective-permute-start.1 = (bf16[64,768]{1,0:T(8,128)(2,1)}, bf16[64,768]{1,0:T(8,128)(2,1)S(1)}, u32[]{:S(2)}, u32[]{:S(2)}) collective-permute-start(bf16[64,768]{1,0:T(8,128)(2,1)} %get-tuple-element.12), channel_id=1, source_target_pairs={{16,0},{32,16},{48,32},{64,48},{80,64},{96,80},{112,96},{128,112},... | collective-permute-start | bytes 294920 | tf_op jit(solution)/shard_map/ppermute | solution.py:125
  21.1 1.9 %collective-permute-start.2 = (bf16[64,768]{1,0:T(8,128)(2,1)}, bf16[64,768]{1,0:T(8,128)(2,1)S(1)}, u32[]{:S(2)}, u32[]{:S(2)}) collective-permute-start(bf16[64,768]{1,0:T(8,128)(2,1)} %get-tuple-element.13), channel_id=1, source_target_pairs={{480,0},{496,16},{0,32},{16,48},{32,64},{48,80},{64,96},{80,112},{... | collective-permute-start | bytes 294920 | tf_op jit(solution)/shard_map/ppermute | solution.py:125
  23.1 6.9 %collective-permute-start.3 = (bf16[64,768]{1,0:T(8,128)(2,1)}, bf16[64,768]{1,0:T(8,128)(2,1)S(1)}, u32[]{:S(2)}, u32[]{:S(2)}) collective-permute-start(bf16[64,768]{1,0:T(8,128)(2,1)} %get-tuple-element.14), channel_id=1, source_target_pairs={{32,0},{48,16},{64,32},{80,48},{96,64},{112,80},{128,96},{144,112}... | collective-permute-start | bytes 294920 | tf_op jit(solution)/shard_map/ppermute | solution.py:125
  30.7 0.0 collective-permute-done.rest_0_
  30.7 1.4 %collective-permute-done.2.rest_2_ = bf16[64,768]{1,0:T(8,128)(2,1)S(1)} collective-permute-done((bf16[64,768]{1,0:T(8,128)(2,1)}, bf16[64,768]{1,0:T(8,128)(2,1)S(1)}, u32[]{:S(2)}, u32[]{:S(2)}) %collective-permute-start.2) | collective-permute-done | bytes 98336 | tf_op jit(solution)/shard_map/ppermute | solution.py:125
  32.1 2.0 %collective-permute-done.3.rest_3_ = bf16[64,768]{1,0:T(8,128)(2,1)S(1)} collective-permute-done((bf16[64,768]{1,0:T(8,128)(2,1)}, bf16[64,768]{1,0:T(8,128)(2,1)S(1)}, u32[]{:S(2)}, u32[]{:S(2)}) %collective-permute-start.3) | collective-permute-done | bytes 98336 | tf_op jit(solution)/shard_map/ppermute | solution.py:125
  34.1 2.6 %copy-done = bf16[56,192,192]{2,1,0:T(8,128)(2,1)S(1)} copy-done((bf16[56,192,192]{2,1,0:T(8,128)(2,1)S(1)}, bf16[56,192,192]{2,1,0:T(8,128)(2,1)}, u32[]{:S(2)}) %copy-start) | copy-done | bytes 4128792
  36.7 0.9 copy-done.2
  37.7 0.7 copy-done.3
  38.3 0.7 copy-done.4
  39.0 0.7 copy-done.5
  39.6 3.9 %blocks.1.own_ref = bf16[64,1536]{1,0:T(8,128)(2,1)S(1)} custom-call(s32[56]{0:T(128)S(1)} %copy-done.3, s32[56]{0:T(128)S(1)} %copy-done.4, f32[56]{0:T(128)S(1)} %copy-done.5, s32[1]{0:T(128)S(6)} %copy.9.count_ref, bf16[8,64,192]{2,1,0:T(8,128)(2,1)S(1)} %copy-done.2, bf16[64,768]{1,0:T(8,128)(2,1)S(1)} %collective-permute-done.rest_0_, ...), custom_call_target="tpu_custom_call" | custom-call | tf_op jit(solution)/shard_map/blocks/pallas_call | solution.py:126
  43.6 8.2 %collective-permute-start.4 = (bf16[64,1536]{1,0:T(8,128)(2,1)S(1)}, bf16[64,1536]{1,0:T(8,128)(2,1)S(1)}, u32[]{:S(2)}, u32[]{:S(2)}) collective-permute-start(bf16[64,1536]{1,0:T(8,128)(2,1)S(1)} %blocks.1.own_ref), channel_id=1, source_target_pairs={{0,8},{8,0},{1,9},{9,1},{2,10},{10,2},{3,11},{11,3},{4,12},{12,4},... | collective-permute-start | bytes 589832 | tf_op jit(solution)/shard_map/ppermute | solution.py:140
  51.8 8.0 %collective-permute-done.4.other_ref = bf16[64,1536]{1,0:T(8,128)(2,1)S(1)} collective-permute-done((bf16[64,1536]{1,0:T(8,128)(2,1)S(1)}, bf16[64,1536]{1,0:T(8,128)(2,1)S(1)}, u32[]{:S(2)}, u32[]{:S(2)}) %collective-permute-start.4) | collective-permute-done | bytes 196640 | tf_op jit(solution)/shard_map/ppermute | solution.py:140
  59.8 1.4 %copy-done.1 = bf16[512,1536]{1,0:T(8,128)(2,1)S(1)} copy-done((bf16[512,1536]{1,0:T(8,128)(2,1)S(1)}, bf16[512,1536]{1,0:T(8,128)(2,1)}, u32[]{:S(2)}) %copy-start.1) | copy-done | bytes 1572888
  61.2 1.1 %tile.1 = f32[32,16,128]{2,1,0:T(8,128)S(1)} custom-call(s32[1]{0:T(128)} %bitcast.half_ref, bf16[512,1536]{1,0:T(8,128)(2,1)S(1)} %copy-done.1, bf16[64,1536]{1,0:T(8,128)(2,1)S(1)} %blocks.1.own_ref, bf16[64,1536]{1,0:T(8,128)(2,1)S(1)} %collective-permute-done.4.other_ref), custom_call_target="tpu_custom_call" | custom-call | tf_op jit(solution)/shard_map/tile/pallas_call | solution.py:142
  62.4 20.4 %all_to_all.5.parts_ref = f32[32,16,128]{2,1,0:T(8,128)} all-to-all(f32[32,16,128]{2,1,0:T(8,128)S(1)} %tile.1), channel_id=1, replica_groups=mesh['y'=8,'z_lo'=4,'z_hi'=2,'x'=4,'core'=2] {'y','z_lo'}, dimensions={0} | all-to-all | bytes 524288 | tf_op jit(solution)/shard_map/all_to_all | solution.py:150
  82.7 1.7 %sum.1 = f32[32,64]{1,0:T(8,128)} custom-call(f32[32,16,128]{2,1,0:T(8,128)} %all_to_all.5.parts_ref), custom_call_target="tpu_custom_call" | custom-call | tf_op jit(solution)/shard_map/sum/pallas_call | solution.py:151
  84.4 3.4 %collective-permute-start.5 = (f32[32,64]{1,0:T(8,128)}, f32[32,64]{1,0:T(8,128)S(1)}, u32[]{:S(2)}, u32[]{:S(2)}) collective-permute-start(f32[32,64]{1,0:T(8,128)} %sum.1), channel_id=1, source_target_pairs={{0,0},{32,1},{64,2},{96,3},{128,4},{160,5},{192,6},{224,7},{1,32},... | collective-permute-start | bytes 24584 | tf_op jit(solution)/shard_map/ppermute | solution.py:167
  87.8 6.3 %collective-permute-done.5 = f32[32,64]{1,0:T(8,128)S(1)} collective-permute-done((f32[32,64]{1,0:T(8,128)}, f32[32,64]{1,0:T(8,128)S(1)}, u32[]{:S(2)}, u32[]{:S(2)}) %collective-permute-start.5) | collective-permute-done | bytes 8224 | tf_op jit(solution)/shard_map/ppermute | solution.py:167
  94.1 0.6 copy.10
  (9 shorter events, 0.0 us)
Async XLA Ops:
  6.5 53.3 %all-gather.2.cloned.1.call-start = ((), (), s32[]{:S(2)}) async-start(), calls=%async_computation.1 | async-start | bytes 1769472 | tf_op jit(solution)/shard_map/all_gather | solution.py:121
  8.4 22.3 %collective-permute-start = (bf16[64,768]{1,0:T(8,128)(2,1)}, bf16[64,768]{1,0:T(8,128)(2,1)S(1)}, u32[]{:S(2)}, u32[]{:S(2)}) collective-permute-start(bf16[64,768]{1,0:T(8,128)(2,1)} %get-tuple-element.11), channel_id=1, source_target_pairs={{496,0},{0,16},{16,32},{32,48},{48,64},{64,80},{80,96},{96,112},{1... | collective-permute-start | bytes 294920 | tf_op jit(solution)/shard_map/ppermute | solution.py:125
  12.7 18.0 %collective-permute-start.1 = (bf16[64,768]{1,0:T(8,128)(2,1)}, bf16[64,768]{1,0:T(8,128)(2,1)S(1)}, u32[]{:S(2)}, u32[]{:S(2)}) collective-permute-start(bf16[64,768]{1,0:T(8,128)(2,1)} %get-tuple-element.12), channel_id=1, source_target_pairs={{16,0},{32,16},{48,32},{64,48},{80,64},{96,80},{112,96},{128,112},... | collective-permute-start | bytes 294920 | tf_op jit(solution)/shard_map/ppermute | solution.py:125
  21.1 11.0 %collective-permute-start.2 = (bf16[64,768]{1,0:T(8,128)(2,1)}, bf16[64,768]{1,0:T(8,128)(2,1)S(1)}, u32[]{:S(2)}, u32[]{:S(2)}) collective-permute-start(bf16[64,768]{1,0:T(8,128)(2,1)} %get-tuple-element.13), channel_id=1, source_target_pairs={{480,0},{496,16},{0,32},{16,48},{32,64},{48,80},{64,96},{80,112},{... | collective-permute-start | bytes 294920 | tf_op jit(solution)/shard_map/ppermute | solution.py:125
  23.1 11.1 %collective-permute-start.3 = (bf16[64,768]{1,0:T(8,128)(2,1)}, bf16[64,768]{1,0:T(8,128)(2,1)S(1)}, u32[]{:S(2)}, u32[]{:S(2)}) collective-permute-start(bf16[64,768]{1,0:T(8,128)(2,1)} %get-tuple-element.14), channel_id=1, source_target_pairs={{32,0},{48,16},{64,32},{80,48},{96,64},{112,80},{128,96},{144,112}... | collective-permute-start | bytes 294920 | tf_op jit(solution)/shard_map/ppermute | solution.py:125
  34.1 2.6 %copy-start = (bf16[56,192,192]{2,1,0:T(8,128)(2,1)S(1)}, bf16[56,192,192]{2,1,0:T(8,128)(2,1)}, u32[]{:S(2)}) copy-start(bf16[56,192,192]{2,1,0:T(8,128)(2,1)} %rest_4_.1) | copy-start | bytes 12386308
  36.7 0.9 copy-start.2
  37.7 0.7 copy-start.3
  38.3 0.7 copy-start.4
  39.0 0.7 copy-start.5
  43.6 16.2 %collective-permute-start.4 = (bf16[64,1536]{1,0:T(8,128)(2,1)S(1)}, bf16[64,1536]{1,0:T(8,128)(2,1)S(1)}, u32[]{:S(2)}, u32[]{:S(2)}) collective-permute-start(bf16[64,1536]{1,0:T(8,128)(2,1)S(1)} %blocks.1.own_ref), channel_id=1, source_target_pairs={{0,8},{8,0},{1,9},{9,1},{2,10},{10,2},{3,11},{11,3},{4,12},{12,4},... | collective-permute-start | bytes 589832 | tf_op jit(solution)/shard_map/ppermute | solution.py:140
  59.8 1.4 %copy-start.1 = (bf16[512,1536]{1,0:T(8,128)(2,1)S(1)}, bf16[512,1536]{1,0:T(8,128)(2,1)}, u32[]{:S(2)}) copy-start(bf16[512,1536]{1,0:T(8,128)(2,1)} %all-gather.2.cloned.1.call-done.rows_ref) | copy-start | bytes 4718596
  84.4 9.7 %collective-permute-start.5 = (f32[32,64]{1,0:T(8,128)}, f32[32,64]{1,0:T(8,128)S(1)}, u32[]{:S(2)}, u32[]{:S(2)}) collective-permute-start(f32[32,64]{1,0:T(8,128)} %sum.1), channel_id=1, source_target_pairs={{0,0},{32,1},{64,2},{96,3},{128,4},{160,5},{192,6},{224,7},{1,32},... | collective-permute-start | bytes 24584 | tf_op jit(solution)/shard_map/ppermute | solution.py:167
Sparse Core Ops, SparseCore 0:
  9.5 32.8 all-gather.1

commit v2 on v1

--- a/solution.py
+++ b/solution.py
@@ -18,8 +18,10 @@
 PACKED = OWN * DOFS
 
 neighbour_offsets = (1, -1, 2, -2)
+x_offsets = (1, -1, 2)
 VMEM = pl.BlockSpec(memory_space=pltpu.VMEM)
 SMEM = pl.BlockSpec(memory_space=pltpu.SMEM)
+HBM = pl.BlockSpec(memory_space=pltpu.HBM)
 
 
 def pack_pair(first, second, out_ref, at):
@@ -42,10 +44,22 @@
 
 
 def block_kernel(
-    rows_ref, columns_ref, density_ref, count_ref, basis_ref, *rest
+    rows_hbm, columns_hbm, density_hbm, count_hbm, basis_hbm, blocks_hbm, *rest
 ):
     ghost_refs = rest[:NEIGH]
-    blocks_hbm, out_ref, blocks, pool, total, arrived = rest[NEIGH:]
+    out_ref, rows_ref, columns_ref, density_ref, count_ref, blocks, pool, total, arrived, lists = rest[NEIGH:]
+    small = [
+        pltpu.make_async_copy(source, target, lists.at[index])
+        for index, (source, target) in enumerate((
+            (rows_hbm, rows_ref),
+            (columns_hbm, columns_ref),
+            (density_hbm, density_ref),
+            (count_hbm, count_ref),
+            (basis_hbm, pool.at[pl.ds(0, OWN)]),
+        ))
+    ]
+    for copy in small:
+        copy.start()
     copies = []
     for chunk in range(CAP // CHUNK):
         part = pl.ds(chunk * CHUNK, CHUNK)
@@ -53,7 +67,6 @@
             pltpu.make_async_copy(blocks_hbm.at[part], blocks.at[part], arrived.at[chunk])
         )
         copies[-1].start()
-    pool[:OWN] = basis_ref[...]
     for neighbour, ghost_ref in enumerate(ghost_refs):
         for pair in range(GMAX // 2):
             at, slot = 384 * pair, OWN + neighbour * GMAX + 2 * pair
@@ -62,6 +75,8 @@
             pool[slot, :, 128:] = ghost_ref[:, at + 256 : at + 320]
             pool[slot + 1, :, 128:] = ghost_ref[:, at + 320 : at + 384]
     total[...] = jnp.zeros_like(total)
+    for copy in small:
+        copy.wait()
     count = count_ref[0]
     for chunk in range(CAP // CHUNK):
         copies[chunk].wait()
@@ -80,22 +95,23 @@
         pack_pair(total[2 * pair], total[2 * pair + 1], out_ref, 384 * pair)
 
 
-def tile_kernel(half_ref, rows_ref, own_ref, other_ref, out_ref):
-    half = half_ref[0]
-    low_lanes = lax.broadcasted_iota(jnp.int32, (16, 128), 1) < WIDTH
+def tile_kernel(place_ref, *rest):
+    *row_refs, own_ref, other_ref, out_ref = rest
+    half, x, core = place_ref[0], place_ref[1], place_ref[2]
+    low_lanes = lax.broadcasted_iota(jnp.int32, (16, 2 * WIDTH), 1) < WIDTH
     for index, ref in ((half, own_ref), (1 - half, other_ref)):
-        tile = lax.dot_general(
-            ref[...], rows_ref[...], (((1,), (1,)), ((), ())), preferred_element_type=jnp.float32
-        )
-        for h in range(2):
-            for x in range(4):
-                low = tile[32 * h : 32 * h + 16, 128 * x : 128 * x + 128]
-                high = tile[32 * h + 16 : 32 * h + 32, 128 * x : 128 * x + 128]
+        for slot, offset in enumerate((0,) + x_offsets):
+            rows = jnp.concatenate([row_refs[0][slot], row_refs[1][slot]], axis=0)
+            tile = lax.dot_general(
+                ref[...], rows, (((1,), (1,)), ((), ())), preferred_element_type=jnp.float32
+            )
+            for h in range(2):
+                low, high = tile[32 * h : 32 * h + 16], tile[32 * h + 16 : 32 * h + 32]
                 low_turned = pltpu.roll(low, WIDTH, 1)
                 high_turned = pltpu.roll(high, WIDTH, 1)
-                at = 16 * index + 4 * x + h
-                out_ref[at] = jnp.where(low_lanes, low, high_turned).astype(out_ref.dtype)
-                out_ref[at + 2] = jnp.where(low_lanes, low_turned, high).astype(out_ref.dtype)
+                at = 16 * index + 4 * ((x - offset + 4) % 4) + h
+                out_ref[at + 2 * core] = jnp.where(low_lanes, low, high_turned)
+                out_ref[at + 2 - 2 * core] = jnp.where(low_lanes, low_turned, high)
 
 
 def sum_kernel(parts_ref, out_ref):
@@ -118,35 +134,45 @@
         out_specs=[VMEM] * (1 + NEIGH),
         name="select",
     )(send_list, basis_vectors)
-    basis_rows = lax.all_gather(packed, ("x", "core"), axis=0, tiled=True)
-    arriving = []
+    arriving, gathered = [], [packed]
     for block, offset in zip(picked, neighbour_offsets):
         route = [((i - offset) % parts, i) for i in range(parts)]
         arriving.append(lax.ppermute(block, mesh_axes, route))
+        if len(gathered) <= len(x_offsets):
+            x_offset = x_offsets[len(gathered) - 1]
+            route = [((i - x_offset) % 4, i) for i in range(4)]
+            gathered.append(lax.ppermute(packed, "x", route))
+    core_rows = jnp.stack(gathered)
+    other_rows = lax.ppermute(core_rows, "core", [(0, 1), (1, 0)])
     products = pl.pallas_call(
         block_kernel,
         out_shape=shape((WIDTH, PACKED), jnp.bfloat16),
-        in_specs=[SMEM] * 4 + [VMEM] * (1 + NEIGH) + [pl.BlockSpec(memory_space=pl.ANY)],
+        in_specs=[HBM] * 6 + [VMEM] * NEIGH,
         out_specs=VMEM,
         scratch_shapes=[
+            pltpu.SMEM((CAP,), jnp.int32),
+            pltpu.SMEM((CAP,), jnp.int32),
+            pltpu.SMEM((CAP,), jnp.float32),
+            pltpu.SMEM((1,), jnp.int32),
             pltpu.VMEM((CAP, DOFS, DOFS), jnp.bfloat16),
             pltpu.VMEM((OWN + NEIGH * GMAX, WIDTH, DOFS), jnp.bfloat16),
             pltpu.VMEM((OWN, WIDTH, DOFS), jnp.float32),
             pltpu.SemaphoreType.DMA((CAP // CHUNK,)),
+            pltpu.SemaphoreType.DMA((5,)),
         ],
-        compiler_params=pltpu.CompilerParams(vmem_limit_bytes=32 << 20),
+        compiler_params=pltpu.CompilerParams(vmem_limit_bytes=64 << 20),
         name="blocks",
-    )(block_rows, block_columns, density, block_counts, basis_vectors, *arriving, stiffness_blocks)
+    )(block_rows, block_columns, density, block_counts, basis_vectors, stiffness_blocks, *arriving)
     other = lax.ppermute(products, "z_hi", [(0, 1), (1, 0)])
-    half = lax.axis_index("z_hi").astype(jnp.int32).reshape(1)
+    place = jnp.stack([lax.axis_index(name) for name in ("z_hi", "x", "core")]).astype(jnp.int32)
     chunks = pl.pallas_call(
         tile_kernel,
         out_shape=shape((parts, 16, 128), jnp.float32),
-        in_specs=[SMEM] + [VMEM] * 3,
+        in_specs=[SMEM] + [VMEM] * 4,
         out_specs=VMEM,
-        compiler_params=pltpu.CompilerParams(vmem_limit_bytes=32 << 20),
+        compiler_params=pltpu.CompilerParams(vmem_limit_bytes=64 << 20),
         name="tile",
-    )(half, basis_rows, products, other)
+    )(place, core_rows, other_rows, products, other)
     shares = lax.all_to_all(chunks, mesh_axes, 0, 0, tiled=True)
     block = pl.pallas_call(
         sum_kernel,

time: 102 us -> 106 us (1.039)
  starting transfers between devices: 33.2 us -> 47.2 us
  between operations: 14.1 us -> 0.77 us
  local copies, waits for them, and re-layouts: 7.51 us -> 0.61 us
  Pallas kernels: 8.58 us -> 12.8 us
  waiting for transfers between devices: 17.8 us -> 20.4 us
  other arithmetic: 0 us -> 2.46 us
    ppermute x0 -> x4, starting transfers between devices: none -> 14.3 us  [the longest x3 12.4 us: local(): gathered.append(lax.ppermute(packed, 'x', route))]
    unnamed x13 -> x1, local copies, waits for them, and re-layouts: 7.51 us -> 0.61 us
    ppermute x0 -> x4, waiting for transfers between devices: none -> 5.84 us  [the longest x3 5.84 us: local(): gathered.append(lax.ppermute(packed, 'x', route))]
    ppermute x4, starting transfers between devices: 21.6 us -> 18.6 us  [local(): arriving.append(lax.ppermute(block, mesh_axes, route))]
    ppermute x1, waiting for transfers between devices: 6.31 us -> 3.75 us  [local(): return lax.ppermute(block, whole, route).T]
    ppermute x1, starting transfers between devices: 3.42 us -> 5.98 us  [local(): return lax.ppermute(block, whole, route).T]
    another operation x0 -> x2, other arithmetic: none -> 2.46 us  [the longest x1 1.9 us: local(): core_rows = jnp.stack(gathered)]
    pallas_call x1, Pallas kernels: 1.15 us -> 3.44 us  [local(): pl.pallas_call(tile_kernel, out_shape=shape((parts, 16, 128), jnp.float32...]
  transfers between devices with their start and end apart: 7 -> 10, of which waited for: 4 -> 6; matrix products, arithmetic and copies ran while one was open for 0% -> 1% of each run, Pallas kernels for 4% -> 6%
where the time goes in v2:
time: 106 us; the launch traced here: 105 us
  starting transfers between devices  47.2 us (45%)
  blocking collectives  20.6 us (19%)
  waiting for transfers between devices  20.4 us (19%)
  Pallas kernels  12.8 us (12%)
  other arithmetic  2.46 us (2%)
    all_to_all x1, blocking collectives, local(): shares = lax.all_to_all(chunks, mesh_axes, 0, 0, tiled=True)  20.6 us
    ppermute x4, starting transfers between devices, local(): arriving.append(lax.ppermute(block, mesh_axes, route))  18.6 us
    ppermute x3, starting transfers between devices, local(): gathered.append(lax.ppermute(packed, 'x', route))  12.4 us
    ppermute x1, starting transfers between devices, local(): other = lax.ppermute(products, 'z_hi', [(0, 1), (1, 0)])  8.22 us
    ppermute x1, waiting for transfers between devices, local(): other = lax.ppermute(products, 'z_hi', [(0, 1), (1, 0)])  7.81 us
    ppermute x1, starting transfers between devices, local(): return lax.ppermute(block, whole, route).T  5.98 us
    pallas_call x1, Pallas kernels, local(): pl.pallas_call(block_kernel, out_shape=shape((WIDTH, PACKED), jnp.bfloat1...  5.84 us
    ppermute x3, waiting for transfers between devices, local(): gathered.append(lax.ppermute(packed, 'x', route))  5.84 us
  transfers between devices with their start and end apart: 10, of which 6 were waited for; matrix products, arithmetic and copies ran while one was open for 1% of the time, Pallas kernels for 6%

profile of v2, /device:TPU:6, one launch (start us, length us, event | category | flops | bytes accessed | tf_op | source)
XLA Modules:
  0.0 104.8 jit_solution(17945178456837571793)
XLA Ops:
  0.0 1.9 %select.1 = (bf16[64,1536]{1,0:T(8,128)(2,1)}, bf16[64,768]{1,0:T(8,128)(2,1)}, bf16[64,768]{1,0:T(8,128)(2,1)}, bf16[64,768]{1,0:T(8,128)(2,1)}, bf16[64,768]{1,0:T(8,128)(2,1)}) custom-call(s32[16]{0:T(128)} %send_ref.1, bf16[8,64,192]{2,1,0:T(8,128)(2,1)} %basis_hbm.1), custom_call_target="tpu_custom_call" | custom-call | tf_op jit(solution)/shard_map/select/pallas_call | solution.py:129
  1.9 3.3 %collective-permute-start.2 = (bf16[64,1536]{1,0:T(8,128)(2,1)}, bf16[64,1536]{1,0:T(8,128)(2,1)S(1)}, u32[]{:S(2)}, u32[]{:S(2)}) collective-permute-start(bf16[64,1536]{1,0:T(8,128)(2,1)} %get-tuple-element.10), channel_id=1, source_target_pairs={{4,0},{6,2},{0,4},{2,6},{5,1},{7,3},{1,5},{3,7},{12,8},{14,10},{8,... | collective-permute-start | bytes 589832 | tf_op jit(solution)/shard_map/ppermute | solution.py:144
  5.2 7.2 %collective-permute-start.1 = (bf16[64,1536]{1,0:T(8,128)(2,1)}, bf16[64,1536]{1,0:T(8,128)(2,1)S(1)}, u32[]{:S(2)}, u32[]{:S(2)}) collective-permute-start(bf16[64,1536]{1,0:T(8,128)(2,1)} %get-tuple-element.10), channel_id=1, source_target_pairs={{2,0},{4,2},{6,4},{0,6},{3,1},{5,3},{7,5},{1,7},{10,8},{12,10},{14... | collective-permute-start | bytes 589832 | tf_op jit(solution)/shard_map/ppermute | solution.py:144
  12.4 1.9 %collective-permute-start = (bf16[64,1536]{1,0:T(8,128)(2,1)}, bf16[64,1536]{1,0:T(8,128)(2,1)S(1)}, u32[]{:S(2)}, u32[]{:S(2)}) collective-permute-start(bf16[64,1536]{1,0:T(8,128)(2,1)} %get-tuple-element.10), channel_id=1, source_target_pairs={{6,0},{0,2},{2,4},{4,6},{7,1},{1,3},{3,5},{5,7},{14,8},{8,10},{10,... | collective-permute-start | bytes 589832 | tf_op jit(solution)/shard_map/ppermute | solution.py:144
  14.3 2.0 %collective-permute-done.1 = bf16[64,1536]{1,0:T(8,128)(2,1)S(1)} collective-permute-done((bf16[64,1536]{1,0:T(8,128)(2,1)}, bf16[64,1536]{1,0:T(8,128)(2,1)S(1)}, u32[]{:S(2)}, u32[]{:S(2)}) %collective-permute-start.1) | collective-permute-done | bytes 196640 | tf_op jit(solution)/shard_map/ppermute | solution.py:144
  16.3 3.9 %collective-permute-done = bf16[64,1536]{1,0:T(8,128)(2,1)S(1)} collective-permute-done((bf16[64,1536]{1,0:T(8,128)(2,1)}, bf16[64,1536]{1,0:T(8,128)(2,1)S(1)}, u32[]{:S(2)}, u32[]{:S(2)}) %collective-permute-start) | collective-permute-done | bytes 196640 | tf_op jit(solution)/shard_map/ppermute | solution.py:144
  20.2 1.9 %pad_maximum_fusion.rest_0_ = bf16[4,64,1536]{2,1,0:T(8,128)(2,1)} fusion(bf16[1,64,1536]{2,1,0:T(8,128)(2,1)S(1)} %bitcast.9, bf16[1,64,1536]{2,1,0:T(8,128)(2,1)S(1)} %bitcast.10, bf16[1,64,1536]{2,1,0:T(8,128)(2,1)S(1)} %bitcast.11, bf16[1,64,1536]{2,1,0:T(8,128)(2,1)} %bitcast.8), kind=kLoop, calls=%fused_computation | loop fusion | flops 1179648 | bytes 1572864 | tf_op jit(solution)/shard_map/stack | solution.py:145
  22.1 1.9 %collective-permute-start.3 = (bf16[4,64,1536]{2,1,0:T(8,128)(2,1)}, bf16[4,64,1536]{2,1,0:T(8,128)(2,1)}, u32[]{:S(2)}, u32[]{:S(2)}) collective-permute-start(bf16[4,64,1536]{2,1,0:T(8,128)(2,1)} %pad_maximum_fusion.rest_0_), channel_id=1, source_target_pairs={{0,1},{1,0},{2,3},{3,2},{4,5},{5,4},{6,7},{7,6},{8,9},{9,8},{10,11... | collective-permute-start | bytes 2359304 | tf_op jit(solution)/shard_map/ppermute | solution.py:146
  24.0 1.9 %collective-permute-start.4 = (bf16[64,768]{1,0:T(8,128)(2,1)}, bf16[64,768]{1,0:T(8,128)(2,1)}, u32[]{:S(2)}, u32[]{:S(2)}) collective-permute-start(bf16[64,768]{1,0:T(8,128)(2,1)} %get-tuple-element.11), channel_id=1, source_target_pairs={{496,0},{0,16},{16,32},{32,48},{48,64},{64,80},{80,96},{96,112},{1... | collective-permute-start | bytes 294920 | tf_op jit(solution)/shard_map/ppermute | solution.py:140
  25.9 7.8 %collective-permute-start.5 = (bf16[64,768]{1,0:T(8,128)(2,1)}, bf16[64,768]{1,0:T(8,128)(2,1)}, u32[]{:S(2)}, u32[]{:S(2)}) collective-permute-start(bf16[64,768]{1,0:T(8,128)(2,1)} %get-tuple-element.12), channel_id=1, source_target_pairs={{16,0},{32,16},{48,32},{64,48},{80,64},{96,80},{112,96},{128,112},... | collective-permute-start | bytes 294920 | tf_op jit(solution)/shard_map/ppermute | solution.py:140
  33.8 1.9 %collective-permute-start.6 = (bf16[64,768]{1,0:T(8,128)(2,1)}, bf16[64,768]{1,0:T(8,128)(2,1)}, u32[]{:S(2)}, u32[]{:S(2)}) collective-permute-start(bf16[64,768]{1,0:T(8,128)(2,1)} %get-tuple-element.13), channel_id=1, source_target_pairs={{480,0},{496,16},{0,32},{16,48},{32,64},{48,80},{64,96},{80,112},{... | collective-permute-start | bytes 294920 | tf_op jit(solution)/shard_map/ppermute | solution.py:140
  35.7 6.9 %collective-permute-start.7 = (bf16[64,768]{1,0:T(8,128)(2,1)}, bf16[64,768]{1,0:T(8,128)(2,1)}, u32[]{:S(2)}, u32[]{:S(2)}) collective-permute-start(bf16[64,768]{1,0:T(8,128)(2,1)} %get-tuple-element.14), channel_id=1, source_target_pairs={{32,0},{48,16},{64,32},{80,48},{96,64},{112,80},{128,96},{144,112}... | collective-permute-start | bytes 294920 | tf_op jit(solution)/shard_map/ppermute | solution.py:140
  43.3 1.0 collective-permute-done.6.rest_2_
  44.3 2.0 %collective-permute-done.7.rest_3_ = bf16[64,768]{1,0:T(8,128)(2,1)} collective-permute-done((bf16[64,768]{1,0:T(8,128)(2,1)}, bf16[64,768]{1,0:T(8,128)(2,1)}, u32[]{:S(2)}, u32[]{:S(2)}) %collective-permute-start.7) | collective-permute-done | bytes 98336 | tf_op jit(solution)/shard_map/ppermute | solution.py:140
  46.3 5.8 %blocks.1.rest_2_ = bf16[64,1536]{1,0:T(8,128)(2,1)} custom-call(s32[56]{0:T(128)} %rows_hbm.1, s32[56]{0:T(128)} %columns_hbm.1, f32[56]{0:T(128)} %density_hbm.1, s32[1]{0:T(128)S(6)} %copy.9.count_hbm, bf16[8,64,192]{2,1,0:T(8,128)(2,1)} %basis_hbm.1, bf16[56,192,192]{2,1,0:T(8,128)(2,1)} %blocks_hbm.1, bf16[64,768]{1,0:T(8,128)(2,1)} %collective-permute-done.4.rest_0_, ...), custom_call_target="tpu_custom_call" | custom-call | tf_op jit(solution)/shard_map/blocks/pallas_call | solution.py:147
  52.2 8.2 %collective-permute-start.8 = (bf16[64,1536]{1,0:T(8,128)(2,1)}, bf16[64,1536]{1,0:T(8,128)(2,1)}, u32[]{:S(2)}, u32[]{:S(2)}) collective-permute-start(bf16[64,1536]{1,0:T(8,128)(2,1)} %blocks.1.rest_2_), channel_id=1, source_target_pairs={{0,8},{8,0},{1,9},{9,1},{2,10},{10,2},{3,11},{11,3},{4,12},{12,4},... | collective-permute-start | bytes 589832 | tf_op jit(solution)/shard_map/ppermute | solution.py:166
  60.4 0.6 pad_add_fusion.place_ref
  61.0 7.8 %collective-permute-done.8.rest_3_ = bf16[64,1536]{1,0:T(8,128)(2,1)} collective-permute-done((bf16[64,1536]{1,0:T(8,128)(2,1)}, bf16[64,1536]{1,0:T(8,128)(2,1)}, u32[]{:S(2)}, u32[]{:S(2)}) %collective-permute-start.8) | collective-permute-done | bytes 196640 | tf_op jit(solution)/shard_map/ppermute | solution.py:166
  68.8 3.4 %tile.1 = f32[32,16,128]{2,1,0:T(8,128)} custom-call(s32[3]{0:T(128)} %pad_add_fusion.place_ref, bf16[4,64,1536]{2,1,0:T(8,128)(2,1)} %pad_maximum_fusion.rest_0_, bf16[4,64,1536]{2,1,0:T(8,128)(2,1)} %collective-permute-done.3.rest_1_, bf16[64,1536]{1,0:T(8,128)(2,1)} %blocks.1.rest_2_, bf16[64,1536]{1,0:T(8,128)(2,1)} %collective-permute-done.8.rest_3_), custom_call_target="tpu_custom_call" | custom-call | tf_op jit(solution)/shard_map/tile/pallas_call | solution.py:168
  72.2 20.6 %all_to_all.5.parts_ref = f32[32,16,128]{2,1,0:T(8,128)} all-to-all(f32[32,16,128]{2,1,0:T(8,128)} %tile.1), channel_id=1, replica_groups=mesh['y'=8,'z_lo'=4,'z_hi'=2,'x'=4,'core'=2] {'y','z_lo'}, dimensions={0} | all-to-all | bytes 524288 | tf_op jit(solution)/shard_map/all_to_all | solution.py:176
  92.8 1.7 %sum.1 = f32[32,64]{1,0:T(8,128)} custom-call(f32[32,16,128]{2,1,0:T(8,128)} %all_to_all.5.parts_ref), custom_call_target="tpu_custom_call" | custom-call | tf_op jit(solution)/shard_map/sum/pallas_call | solution.py:177
  94.5 6.0 %collective-permute-start.9 = (f32[32,64]{1,0:T(8,128)}, f32[32,64]{1,0:T(8,128)S(1)}, u32[]{:S(2)}, u32[]{:S(2)}) collective-permute-start(f32[32,64]{1,0:T(8,128)} %sum.1), channel_id=1, source_target_pairs={{0,0},{32,1},{64,2},{96,3},{128,4},{160,5},{192,6},{224,7},{1,32},... | collective-permute-start | bytes 24584 | tf_op jit(solution)/shard_map/ppermute | solution.py:193
  100.5 3.7 %collective-permute-done.9 = f32[32,64]{1,0:T(8,128)S(1)} collective-permute-done((f32[32,64]{1,0:T(8,128)}, f32[32,64]{1,0:T(8,128)S(1)}, u32[]{:S(2)}, u32[]{:S(2)}) %collective-permute-start.9) | collective-permute-done | bytes 8224 | tf_op jit(solution)/shard_map/ppermute | solution.py:193
  104.2 0.6 copy.10
  (4 shorter events, 0.0 us)
Async XLA Ops:
  1.9 12.5 %collective-permute-start.2 = (bf16[64,1536]{1,0:T(8,128)(2,1)}, bf16[64,1536]{1,0:T(8,128)(2,1)S(1)}, u32[]{:S(2)}, u32[]{:S(2)}) collective-permute-start(bf16[64,1536]{1,0:T(8,128)(2,1)} %get-tuple-element.10), channel_id=1, source_target_pairs={{4,0},{6,2},{0,4},{2,6},{5,1},{7,3},{1,5},{3,7},{12,8},{14,10},{8,... | collective-permute-start | bytes 589832 | tf_op jit(solution)/shard_map/ppermute | solution.py:144
  5.2 11.1 %collective-permute-start.1 = (bf16[64,1536]{1,0:T(8,128)(2,1)}, bf16[64,1536]{1,0:T(8,128)(2,1)S(1)}, u32[]{:S(2)}, u32[]{:S(2)}) collective-permute-start(bf16[64,1536]{1,0:T(8,128)(2,1)} %get-tuple-element.10), channel_id=1, source_target_pairs={{2,0},{4,2},{6,4},{0,6},{3,1},{5,3},{7,5},{1,7},{10,8},{12,10},{14... | collective-permute-start | bytes 589832 | tf_op jit(solution)/shard_map/ppermute | solution.py:144
  12.4 7.8 %collective-permute-start = (bf16[64,1536]{1,0:T(8,128)(2,1)}, bf16[64,1536]{1,0:T(8,128)(2,1)S(1)}, u32[]{:S(2)}, u32[]{:S(2)}) collective-permute-start(bf16[64,1536]{1,0:T(8,128)(2,1)} %get-tuple-element.10), channel_id=1, source_target_pairs={{6,0},{0,2},{2,4},{4,6},{7,1},{1,3},{3,5},{5,7},{14,8},{8,10},{10,... | collective-permute-start | bytes 589832 | tf_op jit(solution)/shard_map/ppermute | solution.py:144
  22.1 46.7 %collective-permute-start.3 = (bf16[4,64,1536]{2,1,0:T(8,128)(2,1)}, bf16[4,64,1536]{2,1,0:T(8,128)(2,1)}, u32[]{:S(2)}, u32[]{:S(2)}) collective-permute-start(bf16[4,64,1536]{2,1,0:T(8,128)(2,1)} %pad_maximum_fusion.rest_0_), channel_id=1, source_target_pairs={{0,1},{1,0},{2,3},{3,2},{4,5},{5,4},{6,7},{7,6},{8,9},{9,8},{10,11... | collective-permute-start | bytes 2359304 | tf_op jit(solution)/shard_map/ppermute | solution.py:146
  24.0 19.3 %collective-permute-start.4 = (bf16[64,768]{1,0:T(8,128)(2,1)}, bf16[64,768]{1,0:T(8,128)(2,1)}, u32[]{:S(2)}, u32[]{:S(2)}) collective-permute-start(bf16[64,768]{1,0:T(8,128)(2,1)} %get-tuple-element.11), channel_id=1, source_target_pairs={{496,0},{0,16},{16,32},{32,48},{48,64},{64,80},{80,96},{96,112},{1... | collective-permute-start | bytes 294920 | tf_op jit(solution)/shard_map/ppermute | solution.py:140
  25.9 17.4 %collective-permute-start.5 = (bf16[64,768]{1,0:T(8,128)(2,1)}, bf16[64,768]{1,0:T(8,128)(2,1)}, u32[]{:S(2)}, u32[]{:S(2)}) collective-permute-start(bf16[64,768]{1,0:T(8,128)(2,1)} %get-tuple-element.12), channel_id=1, source_target_pairs={{16,0},{32,16},{48,32},{64,48},{80,64},{96,80},{112,96},{128,112},... | collective-permute-start | bytes 294920 | tf_op jit(solution)/shard_map/ppermute | solution.py:140
  33.8 10.6 %collective-permute-start.6 = (bf16[64,768]{1,0:T(8,128)(2,1)}, bf16[64,768]{1,0:T(8,128)(2,1)}, u32[]{:S(2)}, u32[]{:S(2)}) collective-permute-start(bf16[64,768]{1,0:T(8,128)(2,1)} %get-tuple-element.13), channel_id=1, source_target_pairs={{480,0},{496,16},{0,32},{16,48},{32,64},{48,80},{64,96},{80,112},{... | collective-permute-start | bytes 294920 | tf_op jit(solution)/shard_map/ppermute | solution.py:140
  35.7 10.6 %collective-permute-start.7 = (bf16[64,768]{1,0:T(8,128)(2,1)}, bf16[64,768]{1,0:T(8,128)(2,1)}, u32[]{:S(2)}, u32[]{:S(2)}) collective-permute-start(bf16[64,768]{1,0:T(8,128)(2,1)} %get-tuple-element.14), channel_id=1, source_target_pairs={{32,0},{48,16},{64,32},{80,48},{96,64},{112,80},{128,96},{144,112}... | collective-permute-start | bytes 294920 | tf_op jit(solution)/shard_map/ppermute | solution.py:140
  52.2 16.6 %collective-permute-start.8 = (bf16[64,1536]{1,0:T(8,128)(2,1)}, bf16[64,1536]{1,0:T(8,128)(2,1)}, u32[]{:S(2)}, u32[]{:S(2)}) collective-permute-start(bf16[64,1536]{1,0:T(8,128)(2,1)} %blocks.1.rest_2_), channel_id=1, source_target_pairs={{0,8},{8,0},{1,9},{9,1},{2,10},{10,2},{3,11},{11,3},{4,12},{12,4},... | collective-permute-start | bytes 589832 | tf_op jit(solution)/shard_map/ppermute | solution.py:166
  94.5 9.7 %collective-permute-start.9 = (f32[32,64]{1,0:T(8,128)}, f32[32,64]{1,0:T(8,128)S(1)}, u32[]{:S(2)}, u32[]{:S(2)}) collective-permute-start(f32[32,64]{1,0:T(8,128)} %sum.1), channel_id=1, source_target_pairs={{0,0},{32,1},{64,2},{96,3},{128,4},{160,5},{192,6},{224,7},{1,32},... | collective-permute-start | bytes 24584 | tf_op jit(solution)/shard_map/ppermute | solution.py:193

commit v3 on v2

--- a/solution.py
+++ b/solution.py
@@ -101,9 +101,11 @@
     low_lanes = lax.broadcasted_iota(jnp.int32, (16, 2 * WIDTH), 1) < WIDTH
     for index, ref in ((half, own_ref), (1 - half, other_ref)):
         for slot, offset in enumerate((0,) + x_offsets):
-            rows = jnp.concatenate([row_refs[0][slot], row_refs[1][slot]], axis=0)
             tile = lax.dot_general(
-                ref[...], rows, (((1,), (1,)), ((), ())), preferred_element_type=jnp.float32
+                ref[...],
+                row_refs[slot][...],
+                (((1,), (1,)), ((), ())),
+                preferred_element_type=jnp.float32,
             )
             for h in range(2):
                 low, high = tile[32 * h : 32 * h + 16], tile[32 * h + 16 : 32 * h + 32]
@@ -134,16 +136,15 @@
         out_specs=[VMEM] * (1 + NEIGH),
         name="select",
     )(send_list, basis_vectors)
-    arriving, gathered = [], [packed]
+    other_packed = lax.ppermute(packed, "core", [(0, 1), (1, 0)])
+    arriving = []
     for block, offset in zip(picked, neighbour_offsets):
         route = [((i - offset) % parts, i) for i in range(parts)]
         arriving.append(lax.ppermute(block, mesh_axes, route))
-        if len(gathered) <= len(x_offsets):
-            x_offset = x_offsets[len(gathered) - 1]
-            route = [((i - x_offset) % 4, i) for i in range(4)]
-            gathered.append(lax.ppermute(packed, "x", route))
-    core_rows = jnp.stack(gathered)
-    other_rows = lax.ppermute(core_rows, "core", [(0, 1), (1, 0)])
+    pair = jnp.concatenate([packed, other_packed])
+    basis_rows = [pair]
+    for offset in x_offsets:
+        basis_rows.append(lax.ppermute(pair, "x", [((i - offset) % 4, i) for i in range(4)]))
     products = pl.pallas_call(
         block_kernel,
         out_shape=shape((WIDTH, PACKED), jnp.bfloat16),
@@ -168,11 +169,11 @@
     chunks = pl.pallas_call(
         tile_kernel,
         out_shape=shape((parts, 16, 128), jnp.float32),
-        in_specs=[SMEM] + [VMEM] * 4,
+        in_specs=[SMEM] + [VMEM] * 6,
         out_specs=VMEM,
         compiler_params=pltpu.CompilerParams(vmem_limit_bytes=64 << 20),
         name="tile",
-    )(place, core_rows, other_rows, products, other)
+    )(place, *basis_rows, products, other)
     shares = lax.all_to_all(chunks, mesh_axes, 0, 0, tiled=True)
     block = pl.pallas_call(
         sum_kernel,

time: 106 us -> 101 us (0.953)
  waiting for transfers between devices: 20.4 us -> 17.7 us
  local copies, waits for them, and re-layouts: 0.61 us -> 2.91 us
  other arithmetic: 2.46 us -> 0.56 us
  starting transfers between devices: 47.2 us -> 45.5 us
    ppermute x4, waiting for transfers between devices: 5.84 us -> 0.01 us  [the longest x3 0.01 us: local(): lax.ppermute(pair, 'x', [((i - offset) % 4, i) for i in range(4)])]
    ppermute x4, starting transfers between devices: 18.6 us -> 21.6 us  [local(): arriving.append(lax.ppermute(block, mesh_axes, route))]
    ppermute x1, waiting for transfers between devices: 3.75 us -> 6.28 us  [local(): return lax.ppermute(block, whole, route).T]
    ppermute x1, starting transfers between devices: 5.98 us -> 3.45 us  [local(): return lax.ppermute(block, whole, route).T]
    ppermute x4, starting transfers between devices: 14.3 us -> 12.3 us  [the longest x3 10.4 us: local(): lax.ppermute(pair, 'x', [((i - offset) % 4, i) for i in range(4)])]
    another operation x1 -> x0, other arithmetic: 1.9 us -> none  [local(): core_rows = jnp.stack(gathered)]
    unnamed x1 -> x2, local copies, waits for them, and re-layouts: 0.61 us -> 2.22 us
  transfers between devices with their start and end apart: 10 -> 10, of which waited for: 6 -> 4; matrix products, arithmetic and copies ran while one was open for 1% -> 3% of each run, Pallas kernels for 6% -> 6%
where the time goes in v3:
time: 101 us
  starting transfers between devices  45.5 us (45%)
  blocking collectives  20.4 us (20%)
  waiting for transfers between devices  17.7 us (18%)
  Pallas kernels  12.8 us (13%)
  local copies, waits for them, and re-layouts  2.91 us (3%)
    ppermute x4, starting transfers between devices, local(): arriving.append(lax.ppermute(block, mesh_axes, route))  21.6 us
    all_to_all x1, blocking collectives, local(): shares = lax.all_to_all(chunks, mesh_axes, 0, 0, tiled=True)  20.4 us
    ppermute x3, starting transfers between devices, local(): lax.ppermute(pair, 'x', [((i - offset) % 4, i) for i in range(4)])  10.4 us
    ppermute x1, starting transfers between devices, local(): other = lax.ppermute(products, 'z_hi', [(0, 1), (1, 0)])  8.22 us
    ppermute x1, waiting for transfers between devices, local(): other = lax.ppermute(products, 'z_hi', [(0, 1), (1, 0)])  7.78 us
    ppermute x1, waiting for transfers between devices, local(): return lax.ppermute(block, whole, route).T  6.28 us
    pallas_call x1, Pallas kernels, local(): pl.pallas_call(block_kernel, out_shape=shape((WIDTH, PACKED), jnp.bfloat1...  5.84 us
    ppermute x4, waiting for transfers between devices, local(): arriving.append(lax.ppermute(block, mesh_axes, route))  3.65 us
  transfers between devices with their start and end apart: 10, of which 4 were waited for; matrix products, arithmetic and copies ran while one was open for 3% of the time, Pallas kernels for 6%

profile of v3, /device:TPU:6, one launch (start us, length us, event | category | flops | bytes accessed | tf_op | source)
XLA Modules:
  0.0 100.7 jit_solution(6549382024573058760)
XLA Ops:
  0.0 1.9 %select.1 = (bf16[64,1536]{1,0:T(8,128)(2,1)}, bf16[64,768]{1,0:T(8,128)(2,1)}, bf16[64,768]{1,0:T(8,128)(2,1)}, bf16[64,768]{1,0:T(8,128)(2,1)}, bf16[64,768]{1,0:T(8,128)(2,1)}) custom-call(s32[16]{0:T(128)} %send_ref.1, bf16[8,64,192]{2,1,0:T(8,128)(2,1)} %basis_hbm.1), custom_call_target="tpu_custom_call" | custom-call | tf_op jit(solution)/shard_map/select/pallas_call | solution.py:131
  1.9 4.3 %collective-permute-start.4 = (bf16[64,768]{1,0:T(8,128)(2,1)}, bf16[64,768]{1,0:T(8,128)(2,1)}, u32[]{:S(2)}, u32[]{:S(2)}) collective-permute-start(bf16[64,768]{1,0:T(8,128)(2,1)} %get-tuple-element.11), channel_id=1, source_target_pairs={{496,0},{0,16},{16,32},{32,48},{48,64},{64,80},{80,96},{96,112},{1... | collective-permute-start | bytes 294920 | tf_op jit(solution)/shard_map/ppermute | solution.py:143
  6.1 8.4 %collective-permute-start.5 = (bf16[64,768]{1,0:T(8,128)(2,1)}, bf16[64,768]{1,0:T(8,128)(2,1)}, u32[]{:S(2)}, u32[]{:S(2)}) collective-permute-start(bf16[64,768]{1,0:T(8,128)(2,1)} %get-tuple-element.12), channel_id=1, source_target_pairs={{16,0},{32,16},{48,32},{64,48},{80,64},{96,80},{112,96},{128,112},... | collective-permute-start | bytes 294920 | tf_op jit(solution)/shard_map/ppermute | solution.py:143
  14.6 1.9 %collective-permute-start = (bf16[64,1536]{1,0:T(8,128)(2,1)}, bf16[64,1536]{1,0:T(8,128)(2,1)S(1)}, u32[]{:S(2)}, u32[]{:S(2)}) collective-permute-start(bf16[64,1536]{1,0:T(8,128)(2,1)} %get-tuple-element.10), channel_id=1, source_target_pairs={{0,1},{1,0},{2,3},{3,2},{4,5},{5,4},{6,7},{7,6},{8,9},{9,8},{10,11... | collective-permute-start | bytes 589832 | tf_op jit(solution)/shard_map/ppermute | solution.py:139
  16.5 1.6 %constant_dynamic-update-slice_fusion.1 = bf16[128,1536]{1,0:T(8,128)(2,1)} fusion(bf16[64,1536]{1,0:T(8,128)(2,1)} %get-tuple-element.10), kind=kLoop, calls=%fused_computation.1 | loop fusion | bytes 393216
  18.1 0.0 collective-permute-done
  18.1 0.7 constant_dynamic-update-slice_fusion.rest_0_
  18.8 3.3 %collective-permute-start.3 = (bf16[128,1536]{1,0:T(8,128)(2,1)}, bf16[128,1536]{1,0:T(8,128)(2,1)}, u32[]{:S(2)}, u32[]{:S(2)}) collective-permute-start(bf16[128,1536]{1,0:T(8,128)(2,1)} %constant_dynamic-update-slice_fusion.rest_0_), channel_id=1, source_target_pairs={{4,0},{6,2},{0,4},{2,6},{5,1},{7,3},{1,5},{3,7},{12,8},{14,10},{8,... | collective-permute-start | bytes 1179656 | tf_op jit(solution)/shard_map/ppermute | solution.py:147
  22.1 4.2 %collective-permute-start.2 = (bf16[128,1536]{1,0:T(8,128)(2,1)}, bf16[128,1536]{1,0:T(8,128)(2,1)}, u32[]{:S(2)}, u32[]{:S(2)}) collective-permute-start(bf16[128,1536]{1,0:T(8,128)(2,1)} %constant_dynamic-update-slice_fusion.rest_0_), channel_id=1, source_target_pairs={{2,0},{4,2},{6,4},{0,6},{3,1},{5,3},{7,5},{1,7},{10,8},{12,10},{14... | collective-permute-start | bytes 1179656 | tf_op jit(solution)/shard_map/ppermute | solution.py:147
  26.4 2.8 %collective-permute-start.1 = (bf16[128,1536]{1,0:T(8,128)(2,1)}, bf16[128,1536]{1,0:T(8,128)(2,1)}, u32[]{:S(2)}, u32[]{:S(2)}) collective-permute-start(bf16[128,1536]{1,0:T(8,128)(2,1)} %constant_dynamic-update-slice_fusion.rest_0_), channel_id=1, source_target_pairs={{6,0},{0,2},{2,4},{4,6},{7,1},{1,3},{3,5},{5,7},{14,8},{8,10},{10,... | collective-permute-start | bytes 1179656 | tf_op jit(solution)/shard_map/ppermute | solution.py:147
  29.2 1.9 %collective-permute-start.6 = (bf16[64,768]{1,0:T(8,128)(2,1)}, bf16[64,768]{1,0:T(8,128)(2,1)}, u32[]{:S(2)}, u32[]{:S(2)}) collective-permute-start(bf16[64,768]{1,0:T(8,128)(2,1)} %get-tuple-element.13), channel_id=1, source_target_pairs={{480,0},{496,16},{0,32},{16,48},{32,64},{48,80},{64,96},{80,112},{... | collective-permute-start | bytes 294920 | tf_op jit(solution)/shard_map/ppermute | solution.py:143
  31.2 6.9 %collective-permute-start.7 = (bf16[64,768]{1,0:T(8,128)(2,1)}, bf16[64,768]{1,0:T(8,128)(2,1)}, u32[]{:S(2)}, u32[]{:S(2)}) collective-permute-start(bf16[64,768]{1,0:T(8,128)(2,1)} %get-tuple-element.14), channel_id=1, source_target_pairs={{32,0},{48,16},{64,32},{80,48},{96,64},{112,80},{128,96},{144,112}... | collective-permute-start | bytes 294920 | tf_op jit(solution)/shard_map/ppermute | solution.py:143
  38.7 1.6 %collective-permute-done.6.rest_2_ = bf16[64,768]{1,0:T(8,128)(2,1)} collective-permute-done((bf16[64,768]{1,0:T(8,128)(2,1)}, bf16[64,768]{1,0:T(8,128)(2,1)}, u32[]{:S(2)}, u32[]{:S(2)}) %collective-permute-start.6) | collective-permute-done | bytes 98336 | tf_op jit(solution)/shard_map/ppermute | solution.py:143
  40.4 2.0 %collective-permute-done.7.rest_3_ = bf16[64,768]{1,0:T(8,128)(2,1)} collective-permute-done((bf16[64,768]{1,0:T(8,128)(2,1)}, bf16[64,768]{1,0:T(8,128)(2,1)}, u32[]{:S(2)}, u32[]{:S(2)}) %collective-permute-start.7) | collective-permute-done | bytes 98336 | tf_op jit(solution)/shard_map/ppermute | solution.py:143
  42.4 5.8 %blocks.1.rest_4_ = bf16[64,1536]{1,0:T(8,128)(2,1)} custom-call(s32[56]{0:T(128)} %rows_hbm.1, s32[56]{0:T(128)} %columns_hbm.1, f32[56]{0:T(128)} %density_hbm.1, s32[1]{0:T(128)S(6)} %copy.10.count_hbm, bf16[8,64,192]{2,1,0:T(8,128)(2,1)} %basis_hbm.1, bf16[56,192,192]{2,1,0:T(8,128)(2,1)} %blocks_hbm.1, bf16[64,768]{1,0:T(8,128)(2,1)} %collective-permute-done.4.rest_0_, ...), custom_call_target="tpu_custom_call" | custom-call | tf_op jit(solution)/shard_map/blocks/pallas_call | solution.py:148
  48.2 8.2 %collective-permute-start.8 = (bf16[64,1536]{1,0:T(8,128)(2,1)}, bf16[64,1536]{1,0:T(8,128)(2,1)}, u32[]{:S(2)}, u32[]{:S(2)}) collective-permute-start(bf16[64,1536]{1,0:T(8,128)(2,1)} %blocks.1.rest_4_), channel_id=1, source_target_pairs={{0,8},{8,0},{1,9},{9,1},{2,10},{10,2},{3,11},{11,3},{4,12},{12,4},... | collective-permute-start | bytes 589832 | tf_op jit(solution)/shard_map/ppermute | solution.py:167
  56.5 0.6 pad_add_fusion.place_ref
  57.0 7.8 %collective-permute-done.8.rest_5_ = bf16[64,1536]{1,0:T(8,128)(2,1)} collective-permute-done((bf16[64,1536]{1,0:T(8,128)(2,1)}, bf16[64,1536]{1,0:T(8,128)(2,1)}, u32[]{:S(2)}, u32[]{:S(2)}) %collective-permute-start.8) | collective-permute-done | bytes 196640 | tf_op jit(solution)/shard_map/ppermute | solution.py:167
  64.8 3.4 %tile.1 = f32[32,16,128]{2,1,0:T(8,128)} custom-call(s32[3]{0:T(128)} %pad_add_fusion.place_ref, bf16[128,1536]{1,0:T(8,128)(2,1)} %constant_dynamic-update-slice_fusion.rest_0_, bf16[128,1536]{1,0:T(8,128)(2,1)} %collective-permute-done.1.rest_1_, bf16[128,1536]{1,0:T(8,128)(2,1)} %collective-permute-done.2.rest_2_, ...), custom_call_target="tpu_custom_call" | custom-call | tf_op jit(solution)/shard_map/tile/pallas_call | solution.py:169
  68.3 20.4 %all_to_all.5.parts_ref = f32[32,16,128]{2,1,0:T(8,128)} all-to-all(f32[32,16,128]{2,1,0:T(8,128)} %tile.1), channel_id=1, replica_groups=mesh['y'=8,'z_lo'=4,'z_hi'=2,'x'=4,'core'=2] {'y','z_lo'}, dimensions={0} | all-to-all | bytes 524288 | tf_op jit(solution)/shard_map/all_to_all | solution.py:177
  88.7 1.7 %sum.1 = f32[32,64]{1,0:T(8,128)} custom-call(f32[32,16,128]{2,1,0:T(8,128)} %all_to_all.5.parts_ref), custom_call_target="tpu_custom_call" | custom-call | tf_op jit(solution)/shard_map/sum/pallas_call | solution.py:178
  90.3 3.4 %collective-permute-start.9 = (f32[32,64]{1,0:T(8,128)}, f32[32,64]{1,0:T(8,128)S(1)}, u32[]{:S(2)}, u32[]{:S(2)}) collective-permute-start(f32[32,64]{1,0:T(8,128)} %sum.1), channel_id=1, source_target_pairs={{0,0},{32,1},{64,2},{96,3},{128,4},{160,5},{192,6},{224,7},{1,32},... | collective-permute-start | bytes 24584 | tf_op jit(solution)/shard_map/ppermute | solution.py:194
  93.8 6.3 %collective-permute-done.9 = f32[32,64]{1,0:T(8,128)S(1)} collective-permute-done((f32[32,64]{1,0:T(8,128)}, f32[32,64]{1,0:T(8,128)S(1)}, u32[]{:S(2)}, u32[]{:S(2)}) %collective-permute-start.9) | collective-permute-done | bytes 8224 | tf_op jit(solution)/shard_map/ppermute | solution.py:194
  100.1 0.6 copy.11
  (5 shorter events, 0.0 us)
Async XLA Ops:
  1.9 27.3 %collective-permute-start.4 = (bf16[64,768]{1,0:T(8,128)(2,1)}, bf16[64,768]{1,0:T(8,128)(2,1)}, u32[]{:S(2)}, u32[]{:S(2)}) collective-permute-start(bf16[64,768]{1,0:T(8,128)(2,1)} %get-tuple-element.11), channel_id=1, source_target_pairs={{496,0},{0,16},{16,32},{32,48},{48,64},{64,80},{80,96},{96,112},{1... | collective-permute-start | bytes 294920 | tf_op jit(solution)/shard_map/ppermute | solution.py:143
  6.1 25.0 %collective-permute-start.5 = (bf16[64,768]{1,0:T(8,128)(2,1)}, bf16[64,768]{1,0:T(8,128)(2,1)}, u32[]{:S(2)}, u32[]{:S(2)}) collective-permute-start(bf16[64,768]{1,0:T(8,128)(2,1)} %get-tuple-element.12), channel_id=1, source_target_pairs={{16,0},{32,16},{48,32},{64,48},{80,64},{96,80},{112,96},{128,112},... | collective-permute-start | bytes 294920 | tf_op jit(solution)/shard_map/ppermute | solution.py:143
  14.6 3.5 %collective-permute-start = (bf16[64,1536]{1,0:T(8,128)(2,1)}, bf16[64,1536]{1,0:T(8,128)(2,1)S(1)}, u32[]{:S(2)}, u32[]{:S(2)}) collective-permute-start(bf16[64,1536]{1,0:T(8,128)(2,1)} %get-tuple-element.10), channel_id=1, source_target_pairs={{0,1},{1,0},{2,3},{3,2},{4,5},{5,4},{6,7},{7,6},{8,9},{9,8},{10,11... | collective-permute-start | bytes 589832 | tf_op jit(solution)/shard_map/ppermute | solution.py:139
  18.8 46.0 %collective-permute-start.3 = (bf16[128,1536]{1,0:T(8,128)(2,1)}, bf16[128,1536]{1,0:T(8,128)(2,1)}, u32[]{:S(2)}, u32[]{:S(2)}) collective-permute-start(bf16[128,1536]{1,0:T(8,128)(2,1)} %constant_dynamic-update-slice_fusion.rest_0_), channel_id=1, source_target_pairs={{4,0},{6,2},{0,4},{2,6},{5,1},{7,3},{1,5},{3,7},{12,8},{14,10},{8,... | collective-permute-start | bytes 1179656 | tf_op jit(solution)/shard_map/ppermute | solution.py:147
  22.1 42.7 %collective-permute-start.2 = (bf16[128,1536]{1,0:T(8,128)(2,1)}, bf16[128,1536]{1,0:T(8,128)(2,1)}, u32[]{:S(2)}, u32[]{:S(2)}) collective-permute-start(bf16[128,1536]{1,0:T(8,128)(2,1)} %constant_dynamic-update-slice_fusion.rest_0_), channel_id=1, source_target_pairs={{2,0},{4,2},{6,4},{0,6},{3,1},{5,3},{7,5},{1,7},{10,8},{12,10},{14... | collective-permute-start | bytes 1179656 | tf_op jit(solution)/shard_map/ppermute | solution.py:147
  26.4 38.4 %collective-permute-start.1 = (bf16[128,1536]{1,0:T(8,128)(2,1)}, bf16[128,1536]{1,0:T(8,128)(2,1)}, u32[]{:S(2)}, u32[]{:S(2)}) collective-permute-start(bf16[128,1536]{1,0:T(8,128)(2,1)} %constant_dynamic-update-slice_fusion.rest_0_), channel_id=1, source_target_pairs={{6,0},{0,2},{2,4},{4,6},{7,1},{1,3},{3,5},{5,7},{14,8},{8,10},{10,... | collective-permute-start | bytes 1179656 | tf_op jit(solution)/shard_map/ppermute | solution.py:147
  29.2 11.2 %collective-permute-start.6 = (bf16[64,768]{1,0:T(8,128)(2,1)}, bf16[64,768]{1,0:T(8,128)(2,1)}, u32[]{:S(2)}, u32[]{:S(2)}) collective-permute-start(bf16[64,768]{1,0:T(8,128)(2,1)} %get-tuple-element.13), channel_id=1, source_target_pairs={{480,0},{496,16},{0,32},{16,48},{32,64},{48,80},{64,96},{80,112},{... | collective-permute-start | bytes 294920 | tf_op jit(solution)/shard_map/ppermute | solution.py:143
  31.2 11.2 %collective-permute-start.7 = (bf16[64,768]{1,0:T(8,128)(2,1)}, bf16[64,768]{1,0:T(8,128)(2,1)}, u32[]{:S(2)}, u32[]{:S(2)}) collective-permute-start(bf16[64,768]{1,0:T(8,128)(2,1)} %get-tuple-element.14), channel_id=1, source_target_pairs={{32,0},{48,16},{64,32},{80,48},{96,64},{112,80},{128,96},{144,112}... | collective-permute-start | bytes 294920 | tf_op jit(solution)/shard_map/ppermute | solution.py:143
  48.2 16.6 %collective-permute-start.8 = (bf16[64,1536]{1,0:T(8,128)(2,1)}, bf16[64,1536]{1,0:T(8,128)(2,1)}, u32[]{:S(2)}, u32[]{:S(2)}) collective-permute-start(bf16[64,1536]{1,0:T(8,128)(2,1)} %blocks.1.rest_4_), channel_id=1, source_target_pairs={{0,8},{8,0},{1,9},{9,1},{2,10},{10,2},{3,11},{11,3},{4,12},{12,4},... | collective-permute-start | bytes 589832 | tf_op jit(solution)/shard_map/ppermute | solution.py:167
  90.3 9.7 %collective-permute-start.9 = (f32[32,64]{1,0:T(8,128)}, f32[32,64]{1,0:T(8,128)S(1)}, u32[]{:S(2)}, u32[]{:S(2)}) collective-permute-start(f32[32,64]{1,0:T(8,128)} %sum.1), channel_id=1, source_target_pairs={{0,0},{32,1},{64,2},{96,3},{128,4},{160,5},{192,6},{224,7},{1,32},... | collective-permute-start | bytes 24584 | tf_op jit(solution)/shard_map/ppermute | solution.py:194

commit v4 on v3

--- a/solution.py
+++ b/solution.py
@@ -99,7 +99,7 @@
     *row_refs, own_ref, other_ref, out_ref = rest
     half, x, core = place_ref[0], place_ref[1], place_ref[2]
     low_lanes = lax.broadcasted_iota(jnp.int32, (16, 2 * WIDTH), 1) < WIDTH
-    for index, ref in ((half, own_ref), (1 - half, other_ref)):
+    for column, ref in ((core, own_ref), (1 - core, other_ref)):
         for slot, offset in enumerate((0,) + x_offsets):
             tile = lax.dot_general(
                 ref[...],
@@ -111,9 +111,9 @@
                 low, high = tile[32 * h : 32 * h + 16], tile[32 * h + 16 : 32 * h + 32]
                 low_turned = pltpu.roll(low, WIDTH, 1)
                 high_turned = pltpu.roll(high, WIDTH, 1)
-                at = 16 * index + 4 * ((x - offset + 4) % 4) + h
-                out_ref[at + 2 * core] = jnp.where(low_lanes, low, high_turned)
-                out_ref[at + 2 - 2 * core] = jnp.where(low_lanes, low_turned, high)
+                at = 4 * ((x - offset + 4) % 4) + 2 * column + h
+                out_ref[16 * half + at] = jnp.where(low_lanes, low, high_turned)
+                out_ref[16 - 16 * half + at] = jnp.where(low_lanes, low_turned, high)
 
 
 def sum_kernel(parts_ref, out_ref):
@@ -136,12 +136,13 @@
         out_specs=[VMEM] * (1 + NEIGH),
         name="select",
     )(send_list, basis_vectors)
-    other_packed = lax.ppermute(packed, "core", [(0, 1), (1, 0)])
+    other_packed = lax.ppermute(packed, "z_hi", [(0, 1), (1, 0)])
     arriving = []
     for block, offset in zip(picked, neighbour_offsets):
         route = [((i - offset) % parts, i) for i in range(parts)]
         arriving.append(lax.ppermute(block, mesh_axes, route))
     pair = jnp.concatenate([packed, other_packed])
+    pair, _ = lax.optimization_barrier((pair, arriving[0]))
     basis_rows = [pair]
     for offset in x_offsets:
         basis_rows.append(lax.ppermute(pair, "x", [((i - offset) % 4, i) for i in range(4)]))
@@ -164,7 +165,7 @@
         compiler_params=pltpu.CompilerParams(vmem_limit_bytes=64 << 20),
         name="blocks",
     )(block_rows, block_columns, density, block_counts, basis_vectors, stiffness_blocks, *arriving)
-    other = lax.ppermute(products, "z_hi", [(0, 1), (1, 0)])
+    other = lax.ppermute(products, "core", [(0, 1), (1, 0)])
     place = jnp.stack([lax.axis_index(name) for name in ("z_hi", "x", "core")]).astype(jnp.int32)
     chunks = pl.pallas_call(
         tile_kernel,
@@ -183,14 +184,13 @@
         name="sum",
     )(shares)
     route = []
-    for zh2 in range(2):
-        for h in range(2):
-            for zh in range(2):
-                for a in range(8):
-                    for b in range(8):
-                        source = (zh2 * 16 + b * 2 + h) * 16 + zh * 8 + a
-                        target = (zh2 * 16 + a * 2 + h) * 16 + zh * 8 + b
-                        route.append((source, target))
+    for a in range(8):
+        for b in range(8):
+            for rest in range(4):
+                for core in range(2):
+                    source = (a * 4 + rest) * 16 + b * 2 + core
+                    target = (b * 4 + rest) * 16 + a * 2 + core
+                    route.append((source, target))
     return lax.ppermute(block, whole, route).T
 
 

time: 101 us -> 103 us (1.020)
  the two profiles are of different devices: /device:TPU:6 before, /device:TPU:48 now
where the time goes in v4:
time: 103 us; the launch traced here: 102 us
  starting transfers between devices  50.6 us (49%)
  blocking collectives  19.8 us (19%)
  waiting for transfers between devices  15 us (15%)
  Pallas kernels  12.8 us (12%)
  other arithmetic  2.26 us (2%)
    all_to_all x1, blocking collectives, local(): shares = lax.all_to_all(chunks, mesh_axes, 0, 0, tiled=True)  19.8 us
    ppermute x4, starting transfers between devices, local(): arriving.append(lax.ppermute(block, mesh_axes, route))  16.2 us
    ppermute x1, starting transfers between devices, local(): other_packed = lax.ppermute(packed, 'z_hi', [(0, 1), (1, 0)])  10.9 us
    ppermute x1, starting transfers between devices, local(): return lax.ppermute(block, whole, route).T  10.8 us
    ppermute x3, starting transfers between devices, local(): lax.ppermute(pair, 'x', [((i - offset) % 4, i) for i in range(4)])  10.8 us
    ppermute x4, waiting for transfers between devices, local(): arriving.append(lax.ppermute(block, mesh_axes, route))  6.22 us
    pallas_call x1, Pallas kernels, local(): pl.pallas_call(block_kernel, out_shape=shape((WIDTH, PACKED), jnp.bfloat1...  5.83 us
    ppermute x1, waiting for transfers between devices, local(): return lax.ppermute(block, whole, route).T  4.51 us
  transfers between devices with their start and end apart: 10, of which 5 were waited for; matrix products, arithmetic and copies ran while one was open for 2% of the time, Pallas kernels for 6%

profile of v4, /device:TPU:48, one launch (start us, length us, event | category | flops | bytes accessed | tf_op | source)
XLA Modules:
  0.0 101.9 jit_solution(14107168594555937224)
XLA Ops:
  0.0 1.9 %select.1 = (bf16[64,1536]{1,0:T(8,128)(2,1)}, bf16[64,768]{1,0:T(8,128)(2,1)}, bf16[64,768]{1,0:T(8,128)(2,1)}, bf16[64,768]{1,0:T(8,128)(2,1)}, bf16[64,768]{1,0:T(8,128)(2,1)}) custom-call(s32[16]{0:T(128)} %send_ref.1, bf16[8,64,192]{2,1,0:T(8,128)(2,1)} %basis_hbm.1), custom_call_target="tpu_custom_call" | custom-call | tf_op jit(solution)/shard_map/select/pallas_call | solution.py:131
  1.9 10.9 %collective-permute-start = (bf16[64,1536]{1,0:T(8,128)(2,1)}, bf16[64,1536]{1,0:T(8,128)(2,1)S(1)}, u32[]{:S(2)}, u32[]{:S(2)}) collective-permute-start(bf16[64,1536]{1,0:T(8,128)(2,1)} %get-tuple-element.11), channel_id=1, source_target_pairs={{0,8},{8,0},{1,9},{9,1},{2,10},{10,2},{3,11},{11,3},{4,12},{12,4},... | collective-permute-start | bytes 589832 | tf_op jit(solution)/shard_map/ppermute | solution.py:139
  12.8 3.4 %collective-permute-start.1 = (bf16[64,768]{1,0:T(8,128)(2,1)}, bf16[64,768]{1,0:T(8,128)(2,1)}, u32[]{:S(2)}, u32[]{:S(2)}) collective-permute-start(bf16[64,768]{1,0:T(8,128)(2,1)} %get-tuple-element.12), channel_id=1, source_target_pairs={{496,0},{0,16},{16,32},{32,48},{48,64},{64,80},{80,96},{96,112},{1... | collective-permute-start | bytes 294920 | tf_op jit(solution)/shard_map/ppermute | solution.py:143
  16.2 5.2 %collective-permute-start.5 = (bf16[64,768]{1,0:T(8,128)(2,1)}, bf16[64,768]{1,0:T(8,128)(2,1)}, u32[]{:S(2)}, u32[]{:S(2)}) collective-permute-start(bf16[64,768]{1,0:T(8,128)(2,1)} %get-tuple-element.14), channel_id=1, source_target_pairs={{16,0},{32,16},{48,32},{64,48},{80,64},{96,80},{112,96},{128,112},... | collective-permute-start | bytes 294920 | tf_op jit(solution)/shard_map/ppermute | solution.py:143
  21.3 3.1 %collective-permute-done = bf16[64,1536]{1,0:T(8,128)(2,1)S(1)} collective-permute-done((bf16[64,1536]{1,0:T(8,128)(2,1)}, bf16[64,1536]{1,0:T(8,128)(2,1)S(1)}, u32[]{:S(2)}, u32[]{:S(2)}) %collective-permute-start) | collective-permute-done | bytes 196640 | tf_op jit(solution)/shard_map/ppermute | solution.py:139
  24.5 1.7 %pad_maximum_fusion.rest_0_ = bf16[128,1536]{1,0:T(8,128)(2,1)} fusion(bf16[64,1536]{1,0:T(8,128)(2,1)S(1)} %collective-permute-done, bf16[64,1536]{1,0:T(8,128)(2,1)} %get-tuple-element.11), kind=kLoop, calls=%fused_computation | loop fusion | flops 786432 | bytes 786432 | tf_op jit(solution)/shard_map/concatenate | solution.py:144
  26.2 0.0 collective-permute-done.1.rest_0_
  26.2 4.9 %collective-permute-start.4 = (bf16[128,1536]{1,0:T(8,128)(2,1)}, bf16[128,1536]{1,0:T(8,128)(2,1)}, u32[]{:S(2)}, u32[]{:S(2)}) collective-permute-start(bf16[128,1536]{1,0:T(8,128)(2,1)} %pad_maximum_fusion.rest_0_), channel_id=1, source_target_pairs={{4,0},{6,2},{0,4},{2,6},{5,1},{7,3},{1,5},{3,7},{12,8},{14,10},{8,... | collective-permute-start | bytes 1179656 | tf_op jit(solution)/shard_map/ppermute | solution.py:148
  31.1 3.0 %collective-permute-start.3 = (bf16[128,1536]{1,0:T(8,128)(2,1)}, bf16[128,1536]{1,0:T(8,128)(2,1)}, u32[]{:S(2)}, u32[]{:S(2)}) collective-permute-start(bf16[128,1536]{1,0:T(8,128)(2,1)} %pad_maximum_fusion.rest_0_), channel_id=1, source_target_pairs={{2,0},{4,2},{6,4},{0,6},{3,1},{5,3},{7,5},{1,7},{10,8},{12,10},{14... | collective-permute-start | bytes 1179656 | tf_op jit(solution)/shard_map/ppermute | solution.py:148
  34.1 2.8 %collective-permute-start.2 = (bf16[128,1536]{1,0:T(8,128)(2,1)}, bf16[128,1536]{1,0:T(8,128)(2,1)}, u32[]{:S(2)}, u32[]{:S(2)}) collective-permute-start(bf16[128,1536]{1,0:T(8,128)(2,1)} %pad_maximum_fusion.rest_0_), channel_id=1, source_target_pairs={{6,0},{0,2},{2,4},{4,6},{7,1},{1,3},{3,5},{5,7},{14,8},{8,10},{10,... | collective-permute-start | bytes 1179656 | tf_op jit(solution)/shard_map/ppermute | solution.py:148
  36.9 4.8 %collective-permute-start.6 = (bf16[64,768]{1,0:T(8,128)(2,1)}, bf16[64,768]{1,0:T(8,128)(2,1)}, u32[]{:S(2)}, u32[]{:S(2)}) collective-permute-start(bf16[64,768]{1,0:T(8,128)(2,1)} %get-tuple-element.15), channel_id=1, source_target_pairs={{480,0},{496,16},{0,32},{16,48},{32,64},{48,80},{64,96},{80,112},{... | collective-permute-start | bytes 294920 | tf_op jit(solution)/shard_map/ppermute | solution.py:143
  41.7 2.9 %collective-permute-start.7 = (bf16[64,768]{1,0:T(8,128)(2,1)}, bf16[64,768]{1,0:T(8,128)(2,1)}, u32[]{:S(2)}, u32[]{:S(2)}) collective-permute-start(bf16[64,768]{1,0:T(8,128)(2,1)} %get-tuple-element.16), channel_id=1, source_target_pairs={{32,0},{48,16},{64,32},{80,48},{96,64},{112,80},{128,96},{144,112}... | collective-permute-start | bytes 294920 | tf_op jit(solution)/shard_map/ppermute | solution.py:143
  45.3 1.0 collective-permute-done.6.rest_2_
  46.2 5.2 %collective-permute-done.7.rest_3_ = bf16[64,768]{1,0:T(8,128)(2,1)} collective-permute-done((bf16[64,768]{1,0:T(8,128)(2,1)}, bf16[64,768]{1,0:T(8,128)(2,1)}, u32[]{:S(2)}, u32[]{:S(2)}) %collective-permute-start.7) | collective-permute-done | bytes 98336 | tf_op jit(solution)/shard_map/ppermute | solution.py:143
  51.5 5.8 %blocks.1.rest_4_ = bf16[64,1536]{1,0:T(8,128)(2,1)} custom-call(s32[56]{0:T(128)} %rows_hbm.1, s32[56]{0:T(128)} %columns_hbm.1, f32[56]{0:T(128)} %density_hbm.1, s32[1]{0:T(128)S(6)} %copy.9.count_hbm, bf16[8,64,192]{2,1,0:T(8,128)(2,1)} %basis_hbm.1, bf16[56,192,192]{2,1,0:T(8,128)(2,1)} %blocks_hbm.1, bf16[64,768]{1,0:T(8,128)(2,1)} %collective-permute-done.1.rest_0_, ...), custom_call_target="tpu_custom_call" | custom-call | tf_op jit(solution)/shard_map/blocks/pallas_call | solution.py:149
  57.3 1.9 %collective-permute-start.8 = (bf16[64,1536]{1,0:T(8,128)(2,1)}, bf16[64,1536]{1,0:T(8,128)(2,1)}, u32[]{:S(2)}, u32[]{:S(2)}) collective-permute-start(bf16[64,1536]{1,0:T(8,128)(2,1)} %blocks.1.rest_4_), channel_id=1, source_target_pairs={{0,1},{1,0},{2,3},{3,2},{4,5},{5,4},{6,7},{7,6},{8,9},{9,8},{10,11... | collective-permute-start | bytes 589832 | tf_op jit(solution)/shard_map/ppermute | solution.py:168
  59.3 0.6 pad_add_fusion.place_ref
  59.8 1.2 %collective-permute-done.8.rest_5_ = bf16[64,1536]{1,0:T(8,128)(2,1)} collective-permute-done((bf16[64,1536]{1,0:T(8,128)(2,1)}, bf16[64,1536]{1,0:T(8,128)(2,1)}, u32[]{:S(2)}, u32[]{:S(2)}) %collective-permute-start.8) | collective-permute-done | bytes 196640 | tf_op jit(solution)/shard_map/ppermute | solution.py:168
  61.0 3.5 %tile.1 = f32[32,16,128]{2,1,0:T(8,128)} custom-call(s32[3]{0:T(128)} %pad_add_fusion.place_ref, bf16[128,1536]{1,0:T(8,128)(2,1)} %pad_maximum_fusion.rest_0_, bf16[128,1536]{1,0:T(8,128)(2,1)} %collective-permute-done.2.rest_1_, bf16[128,1536]{1,0:T(8,128)(2,1)} %collective-permute-done.3.rest_2_, bf16[128,1536]{1,0:T(8,128)(2,1)} %collective-permute-done.4.rest_3_, ...), custom_call_target="tpu_custom_call" | custom-call | tf_op jit(solution)/shard_map/tile/pallas_call | solution.py:170
  64.5 19.8 %all_to_all.5.parts_ref = f32[32,16,128]{2,1,0:T(8,128)} all-to-all(f32[32,16,128]{2,1,0:T(8,128)} %tile.1), channel_id=1, replica_groups=mesh['y'=8,'z_lo'=4,'z_hi'=2,'x'=4,'core'=2] {'y','z_lo'}, dimensions={0} | all-to-all | bytes 524288 | tf_op jit(solution)/shard_map/all_to_all | solution.py:178
  84.3 1.7 %sum.1 = f32[32,64]{1,0:T(8,128)} custom-call(f32[32,16,128]{2,1,0:T(8,128)} %all_to_all.5.parts_ref), custom_call_target="tpu_custom_call" | custom-call | tf_op jit(solution)/shard_map/sum/pallas_call | solution.py:179
  86.0 10.8 %collective-permute-start.9 = (f32[32,64]{1,0:T(8,128)}, f32[32,64]{1,0:T(8,128)S(1)}, u32[]{:S(2)}, u32[]{:S(2)}) collective-permute-start(f32[32,64]{1,0:T(8,128)} %sum.1), channel_id=1, source_target_pairs={{0,0},{1,1},{16,16},{17,17},{32,32},{33,33},{48,48},{49,49},{2,64}... | collective-permute-start | bytes 24584 | tf_op jit(solution)/shard_map/ppermute | solution.py:194
  96.8 4.5 %collective-permute-done.9 = f32[32,64]{1,0:T(8,128)S(1)} collective-permute-done((f32[32,64]{1,0:T(8,128)}, f32[32,64]{1,0:T(8,128)S(1)}, u32[]{:S(2)}, u32[]{:S(2)}) %collective-permute-start.9) | collective-permute-done | bytes 8224 | tf_op jit(solution)/shard_map/ppermute | solution.py:194
  101.3 0.6 copy.10
  (4 shorter events, 0.0 us)
Async XLA Ops:
  1.9 22.6 %collective-permute-start = (bf16[64,1536]{1,0:T(8,128)(2,1)}, bf16[64,1536]{1,0:T(8,128)(2,1)S(1)}, u32[]{:S(2)}, u32[]{:S(2)}) collective-permute-start(bf16[64,1536]{1,0:T(8,128)(2,1)} %get-tuple-element.11), channel_id=1, source_target_pairs={{0,8},{8,0},{1,9},{9,1},{2,10},{10,2},{3,11},{11,3},{4,12},{12,4},... | collective-permute-start | bytes 589832 | tf_op jit(solution)/shard_map/ppermute | solution.py:139
  12.8 13.4 %collective-permute-start.1 = (bf16[64,768]{1,0:T(8,128)(2,1)}, bf16[64,768]{1,0:T(8,128)(2,1)}, u32[]{:S(2)}, u32[]{:S(2)}) collective-permute-start(bf16[64,768]{1,0:T(8,128)(2,1)} %get-tuple-element.12), channel_id=1, source_target_pairs={{496,0},{0,16},{16,32},{32,48},{48,64},{64,80},{80,96},{96,112},{1... | collective-permute-start | bytes 294920 | tf_op jit(solution)/shard_map/ppermute | solution.py:143
  16.2 25.6 %collective-permute-start.5 = (bf16[64,768]{1,0:T(8,128)(2,1)}, bf16[64,768]{1,0:T(8,128)(2,1)}, u32[]{:S(2)}, u32[]{:S(2)}) collective-permute-start(bf16[64,768]{1,0:T(8,128)(2,1)} %get-tuple-element.14), channel_id=1, source_target_pairs={{16,0},{32,16},{48,32},{64,48},{80,64},{96,80},{112,96},{128,112},... | collective-permute-start | bytes 294920 | tf_op jit(solution)/shard_map/ppermute | solution.py:143
  26.2 34.8 %collective-permute-start.4 = (bf16[128,1536]{1,0:T(8,128)(2,1)}, bf16[128,1536]{1,0:T(8,128)(2,1)}, u32[]{:S(2)}, u32[]{:S(2)}) collective-permute-start(bf16[128,1536]{1,0:T(8,128)(2,1)} %pad_maximum_fusion.rest_0_), channel_id=1, source_target_pairs={{4,0},{6,2},{0,4},{2,6},{5,1},{7,3},{1,5},{3,7},{12,8},{14,10},{8,... | collective-permute-start | bytes 1179656 | tf_op jit(solution)/shard_map/ppermute | solution.py:148
  31.1 29.9 %collective-permute-start.3 = (bf16[128,1536]{1,0:T(8,128)(2,1)}, bf16[128,1536]{1,0:T(8,128)(2,1)}, u32[]{:S(2)}, u32[]{:S(2)}) collective-permute-start(bf16[128,1536]{1,0:T(8,128)(2,1)} %pad_maximum_fusion.rest_0_), channel_id=1, source_target_pairs={{2,0},{4,2},{6,4},{0,6},{3,1},{5,3},{7,5},{1,7},{10,8},{12,10},{14... | collective-permute-start | bytes 1179656 | tf_op jit(solution)/shard_map/ppermute | solution.py:148
  34.1 26.9 %collective-permute-start.2 = (bf16[128,1536]{1,0:T(8,128)(2,1)}, bf16[128,1536]{1,0:T(8,128)(2,1)}, u32[]{:S(2)}, u32[]{:S(2)}) collective-permute-start(bf16[128,1536]{1,0:T(8,128)(2,1)} %pad_maximum_fusion.rest_0_), channel_id=1, source_target_pairs={{6,0},{0,2},{2,4},{4,6},{7,1},{1,3},{3,5},{5,7},{14,8},{8,10},{10,... | collective-permute-start | bytes 1179656 | tf_op jit(solution)/shard_map/ppermute | solution.py:148
  36.9 9.3 %collective-permute-start.6 = (bf16[64,768]{1,0:T(8,128)(2,1)}, bf16[64,768]{1,0:T(8,128)(2,1)}, u32[]{:S(2)}, u32[]{:S(2)}) collective-permute-start(bf16[64,768]{1,0:T(8,128)(2,1)} %get-tuple-element.15), channel_id=1, source_target_pairs={{480,0},{496,16},{0,32},{16,48},{32,64},{48,80},{64,96},{80,112},{... | collective-permute-start | bytes 294920 | tf_op jit(solution)/shard_map/ppermute | solution.py:143
  41.7 9.7 %collective-permute-start.7 = (bf16[64,768]{1,0:T(8,128)(2,1)}, bf16[64,768]{1,0:T(8,128)(2,1)}, u32[]{:S(2)}, u32[]{:S(2)}) collective-permute-start(bf16[64,768]{1,0:T(8,128)(2,1)} %get-tuple-element.16), channel_id=1, source_target_pairs={{32,0},{48,16},{64,32},{80,48},{96,64},{112,80},{128,96},{144,112}... | collective-permute-start | bytes 294920 | tf_op jit(solution)/shard_map/ppermute | solution.py:143
  57.3 3.7 %collective-permute-start.8 = (bf16[64,1536]{1,0:T(8,128)(2,1)}, bf16[64,1536]{1,0:T(8,128)(2,1)}, u32[]{:S(2)}, u32[]{:S(2)}) collective-permute-start(bf16[64,1536]{1,0:T(8,128)(2,1)} %blocks.1.rest_4_), channel_id=1, source_target_pairs={{0,1},{1,0},{2,3},{3,2},{4,5},{5,4},{6,7},{7,6},{8,9},{9,8},{10,11... | collective-permute-start | bytes 589832 | tf_op jit(solution)/shard_map/ppermute | solution.py:168
  86.0 15.3 %collective-permute-start.9 = (f32[32,64]{1,0:T(8,128)}, f32[32,64]{1,0:T(8,128)S(1)}, u32[]{:S(2)}, u32[]{:S(2)}) collective-permute-start(f32[32,64]{1,0:T(8,128)} %sum.1), channel_id=1, source_target_pairs={{0,0},{1,1},{16,16},{17,17},{32,32},{33,33},{48,48},{49,49},{2,64}... | collective-permute-start | bytes 24584 | tf_op jit(solution)/shard_map/ppermute | solution.py:194

commit v5 on v4

--- a/solution.py
+++ b/solution.py
@@ -96,24 +96,24 @@
 
 
 def tile_kernel(place_ref, *rest):
-    *row_refs, own_ref, other_ref, out_ref = rest
+    row_refs, product_refs, out_ref = rest[:4], rest[4:8], rest[8]
     half, x, core = place_ref[0], place_ref[1], place_ref[2]
     low_lanes = lax.broadcasted_iota(jnp.int32, (16, 2 * WIDTH), 1) < WIDTH
-    for column, ref in ((core, own_ref), (1 - core, other_ref)):
-        for slot, offset in enumerate((0,) + x_offsets):
+    row_places = [(x - offset + 4) % 4 for offset in (0,) + x_offsets]
+    column_places = [(half, core), (1 - half, core), (half, 1 - core), (1 - half, 1 - core)]
+    for slot in (0, 2):
+        rows = jnp.concatenate([row_refs[slot][...], row_refs[slot + 1][...]], axis=0)
+        for (z_place, core_place), ref in zip(column_places, product_refs):
             tile = lax.dot_general(
-                ref[...],
-                row_refs[slot][...],
-                (((1,), (1,)), ((), ())),
-                preferred_element_type=jnp.float32,
+                ref[...], rows, (((1,), (1,)), ((), ())), preferred_element_type=jnp.float32
             )
             for h in range(2):
                 low, high = tile[32 * h : 32 * h + 16], tile[32 * h + 16 : 32 * h + 32]
                 low_turned = pltpu.roll(low, WIDTH, 1)
                 high_turned = pltpu.roll(high, WIDTH, 1)
-                at = 4 * ((x - offset + 4) % 4) + 2 * column + h
-                out_ref[16 * half + at] = jnp.where(low_lanes, low, high_turned)
-                out_ref[16 - 16 * half + at] = jnp.where(low_lanes, low_turned, high)
+                at = 16 * z_place + 2 * core_place + h
+                out_ref[at + 4 * row_places[slot]] = jnp.where(low_lanes, low, high_turned)
+                out_ref[at + 4 * row_places[slot + 1]] = jnp.where(low_lanes, low_turned, high)
 
 
 def sum_kernel(parts_ref, out_ref):
@@ -136,16 +136,10 @@
         out_specs=[VMEM] * (1 + NEIGH),
         name="select",
     )(send_list, basis_vectors)
-    other_packed = lax.ppermute(packed, "z_hi", [(0, 1), (1, 0)])
     arriving = []
     for block, offset in zip(picked, neighbour_offsets):
         route = [((i - offset) % parts, i) for i in range(parts)]
         arriving.append(lax.ppermute(block, mesh_axes, route))
-    pair = jnp.concatenate([packed, other_packed])
-    pair, _ = lax.optimization_barrier((pair, arriving[0]))
-    basis_rows = [pair]
-    for offset in x_offsets:
-        basis_rows.append(lax.ppermute(pair, "x", [((i - offset) % 4, i) for i in range(4)]))
     products = pl.pallas_call(
         block_kernel,
         out_shape=shape((WIDTH, PACKED), jnp.bfloat16),
@@ -165,16 +159,23 @@
         compiler_params=pltpu.CompilerParams(vmem_limit_bytes=64 << 20),
         name="blocks",
     )(block_rows, block_columns, density, block_counts, basis_vectors, stiffness_blocks, *arriving)
-    other = lax.ppermute(products, "core", [(0, 1), (1, 0)])
+    swap = [(0, 1), (1, 0)]
+    over_z = lax.ppermute(products, "z_hi", swap)
+    over_core = lax.ppermute(products, "core", swap)
+    over_both = lax.ppermute(over_z, "core", swap)
+    packed, _ = lax.optimization_barrier((packed, products))
+    basis_rows = [packed]
+    for offset in x_offsets:
+        basis_rows.append(lax.ppermute(packed, "x", [((i - offset) % 4, i) for i in range(4)]))
     place = jnp.stack([lax.axis_index(name) for name in ("z_hi", "x", "core")]).astype(jnp.int32)
     chunks = pl.pallas_call(
         tile_kernel,
         out_shape=shape((parts, 16, 128), jnp.float32),
-        in_specs=[SMEM] + [VMEM] * 6,
+        in_specs=[SMEM] + [VMEM] * 8,
         out_specs=VMEM,
-        compiler_params=pltpu.CompilerParams(vmem_limit_bytes=64 << 20),
+        compiler_params=pltpu.CompilerParams(vmem_limit_bytes=8 << 20),
         name="tile",
-    )(place, *basis_rows, products, other)
+    )(place, *basis_rows, products, over_z, over_core, over_both)
     shares = lax.all_to_all(chunks, mesh_axes, 0, 0, tiled=True)
     block = pl.pallas_call(
         sum_kernel,
@@ -184,13 +185,15 @@
         name="sum",
     )(shares)
     route = []
-    for a in range(8):
-        for b in range(8):
-            for rest in range(4):
-                for core in range(2):
-                    source = (a * 4 + rest) * 16 + b * 2 + core
-                    target = (b * 4 + rest) * 16 + a * 2 + core
+    for a in range(4):
+        for b in range(4):
+            for place2 in range(8):
+                for panel in range(4):
+                    z2, rest, z, c = place2 // 4, place2 % 4, panel // 2, panel % 2
+                    source = (z2 * 16 + a * 4 + rest) * 16 + z * 8 + b * 2 + c
+                    target = (z2 * 16 + b * 4 + rest) * 16 + z * 8 + a * 2 + c
                     route.append((source, target))
+
     return lax.ppermute(block, whole, route).T
 
 

time: 103 us -> 96.1 us (0.933)
  the two profiles are of different devices: /device:TPU:48 before, /device:TPU:6 now
where the time goes in v5:
time: 96.1 us; the launch traced here: 95.5 us
  starting transfers between devices  47.8 us (50%)
  blocking collectives  22.3 us (23%)
  Pallas kernels  11.2 us (12%)
  waiting for transfers between devices  10.9 us (11%)
  local copies, waits for them, and re-layouts  2.46 us (3%)
    all_to_all x1, blocking collectives, local(): shares = lax.all_to_all(chunks, mesh_axes, 0, 0, tiled=True)  22.3 us
    ppermute x4, starting transfers between devices, local(): arriving.append(lax.ppermute(block, mesh_axes, route))  21.6 us
    ppermute x3, starting transfers between devices, local(): lax.ppermute(packed, 'x', [((i - offset) % 4, i) for i in range(4)])  10.4 us
    ppermute x1, starting transfers between devices, local(): over_z = lax.ppermute(products, 'z_hi', swap)  8.22 us
    ppermute x1, waiting for transfers between devices, local(): return lax.ppermute(block, whole, route).T  6.37 us
    pallas_call x1, Pallas kernels, local(): pl.pallas_call(block_kernel, out_shape=shape((WIDTH, PACKED), jnp.bfloat1...  5.85 us
    ppermute x4, waiting for transfers between devices, local(): arriving.append(lax.ppermute(block, mesh_axes, route))  3.56 us
    ppermute x1, starting transfers between devices, local(): return lax.ppermute(block, whole, route).T  3.36 us
  transfers between devices with their start and end apart: 11, of which 4 were waited for; matrix products, arithmetic and copies ran while one was open for 0% of the time, Pallas kernels for 0%

profile of v5, /device:TPU:6, one launch (start us, length us, event | category | flops | bytes accessed | tf_op | source)
XLA Modules:
  0.0 95.5 jit_solution(16381876772500329425)
XLA Ops:
  0.0 1.9 %select.1 = (bf16[64,1536]{1,0:T(8,128)(2,1)}, bf16[64,768]{1,0:T(8,128)(2,1)}, bf16[64,768]{1,0:T(8,128)(2,1)}, bf16[64,768]{1,0:T(8,128)(2,1)}, bf16[64,768]{1,0:T(8,128)(2,1)}) custom-call(s32[16]{0:T(128)} %send_ref.1, bf16[8,64,192]{2,1,0:T(8,128)(2,1)} %basis_hbm.1), custom_call_target="tpu_custom_call" | custom-call | tf_op jit(solution)/shard_map/select/pallas_call | solution.py:131
  1.9 4.3 %collective-permute-start = (bf16[64,768]{1,0:T(8,128)(2,1)}, bf16[64,768]{1,0:T(8,128)(2,1)}, u32[]{:S(2)}, u32[]{:S(2)}) collective-permute-start(bf16[64,768]{1,0:T(8,128)(2,1)} %get-tuple-element.12), channel_id=1, source_target_pairs={{496,0},{0,16},{16,32},{32,48},{48,64},{64,80},{80,96},{96,112},{1... | collective-permute-start | bytes 294920 | tf_op jit(solution)/shard_map/ppermute | solution.py:142
  6.1 8.4 %collective-permute-start.1 = (bf16[64,768]{1,0:T(8,128)(2,1)}, bf16[64,768]{1,0:T(8,128)(2,1)}, u32[]{:S(2)}, u32[]{:S(2)}) collective-permute-start(bf16[64,768]{1,0:T(8,128)(2,1)} %get-tuple-element.13), channel_id=1, source_target_pairs={{16,0},{32,16},{48,32},{64,48},{80,64},{96,80},{112,96},{128,112},... | collective-permute-start | bytes 294920 | tf_op jit(solution)/shard_map/ppermute | solution.py:142
  14.6 1.9 %collective-permute-start.2 = (bf16[64,768]{1,0:T(8,128)(2,1)}, bf16[64,768]{1,0:T(8,128)(2,1)}, u32[]{:S(2)}, u32[]{:S(2)}) collective-permute-start(bf16[64,768]{1,0:T(8,128)(2,1)} %get-tuple-element.14), channel_id=1, source_target_pairs={{480,0},{496,16},{0,32},{16,48},{32,64},{48,80},{64,96},{80,112},{... | collective-permute-start | bytes 294920 | tf_op jit(solution)/shard_map/ppermute | solution.py:142
  16.5 6.9 %collective-permute-start.3 = (bf16[64,768]{1,0:T(8,128)(2,1)}, bf16[64,768]{1,0:T(8,128)(2,1)}, u32[]{:S(2)}, u32[]{:S(2)}) collective-permute-start(bf16[64,768]{1,0:T(8,128)(2,1)} %get-tuple-element.15), channel_id=1, source_target_pairs={{32,0},{48,16},{64,32},{80,48},{96,64},{112,80},{128,96},{144,112}... | collective-permute-start | bytes 294920 | tf_op jit(solution)/shard_map/ppermute | solution.py:142
  24.1 1.6 %collective-permute-done.2.rest_2_ = bf16[64,768]{1,0:T(8,128)(2,1)} collective-permute-done((bf16[64,768]{1,0:T(8,128)(2,1)}, bf16[64,768]{1,0:T(8,128)(2,1)}, u32[]{:S(2)}, u32[]{:S(2)}) %collective-permute-start.2) | collective-permute-done | bytes 98336 | tf_op jit(solution)/shard_map/ppermute | solution.py:142
  25.7 2.0 %collective-permute-done.3.rest_3_ = bf16[64,768]{1,0:T(8,128)(2,1)} collective-permute-done((bf16[64,768]{1,0:T(8,128)(2,1)}, bf16[64,768]{1,0:T(8,128)(2,1)}, u32[]{:S(2)}, u32[]{:S(2)}) %collective-permute-start.3) | collective-permute-done | bytes 98336 | tf_op jit(solution)/shard_map/ppermute | solution.py:142
  27.7 5.8 %blocks.1.rest_4_ = bf16[64,1536]{1,0:T(8,128)(2,1)} custom-call(s32[56]{0:T(128)} %rows_hbm.1, s32[56]{0:T(128)} %columns_hbm.1, f32[56]{0:T(128)} %density_hbm.1, s32[1]{0:T(128)S(6)} %copy.9.count_hbm, bf16[8,64,192]{2,1,0:T(8,128)(2,1)} %basis_hbm.1, bf16[56,192,192]{2,1,0:T(8,128)(2,1)} %blocks_hbm.1, bf16[64,768]{1,0:T(8,128)(2,1)} %collective-permute-done.rest_0_, ...), custom_call_target="tpu_custom_call" | custom-call | tf_op jit(solution)/shard_map/blocks/pallas_call | solution.py:143
  33.5 8.2 %collective-permute-start.7 = (bf16[64,1536]{1,0:T(8,128)(2,1)}, bf16[64,1536]{1,0:T(8,128)(2,1)S(1)}, u32[]{:S(2)}, u32[]{:S(2)}) collective-permute-start(bf16[64,1536]{1,0:T(8,128)(2,1)} %blocks.1.rest_4_), channel_id=1, source_target_pairs={{0,8},{8,0},{1,9},{9,1},{2,10},{10,2},{3,11},{11,3},{4,12},{12,4},... | collective-permute-start | bytes 589832 | tf_op jit(solution)/shard_map/ppermute | solution.py:163
  41.8 3.3 %collective-permute-start.6 = (bf16[64,1536]{1,0:T(8,128)(2,1)}, bf16[64,1536]{1,0:T(8,128)(2,1)S(1)}, u32[]{:S(2)}, u32[]{:S(2)}) collective-permute-start(bf16[64,1536]{1,0:T(8,128)(2,1)} %get-tuple-element.16.rest_0_), channel_id=1, source_target_pairs={{4,0},{6,2},{0,4},{2,6},{5,1},{7,3},{1,5},{3,7},{12,8},{14,10},{8,... | collective-permute-start | bytes 589832 | tf_op jit(solution)/shard_map/ppermute | solution.py:169
  45.1 1.9 %collective-permute-start.5 = (bf16[64,1536]{1,0:T(8,128)(2,1)}, bf16[64,1536]{1,0:T(8,128)(2,1)S(1)}, u32[]{:S(2)}, u32[]{:S(2)}) collective-permute-start(bf16[64,1536]{1,0:T(8,128)(2,1)} %get-tuple-element.16.rest_0_), channel_id=1, source_target_pairs={{2,0},{4,2},{6,4},{0,6},{3,1},{5,3},{7,5},{1,7},{10,8},{12,10},{14... | collective-permute-start | bytes 589832 | tf_op jit(solution)/shard_map/ppermute | solution.py:169
  47.0 5.1 %collective-permute-start.4 = (bf16[64,1536]{1,0:T(8,128)(2,1)}, bf16[64,1536]{1,0:T(8,128)(2,1)S(1)}, u32[]{:S(2)}, u32[]{:S(2)}) collective-permute-start(bf16[64,1536]{1,0:T(8,128)(2,1)} %get-tuple-element.16.rest_0_), channel_id=1, source_target_pairs={{6,0},{0,2},{2,4},{4,6},{7,1},{1,3},{3,5},{5,7},{14,8},{8,10},{10,... | collective-permute-start | bytes 589832 | tf_op jit(solution)/shard_map/ppermute | solution.py:169
  52.2 1.9 %collective-permute-start.8 = (bf16[64,1536]{1,0:T(8,128)(2,1)}, bf16[64,1536]{1,0:T(8,128)(2,1)S(1)}, u32[]{:S(2)}, u32[]{:S(2)}) collective-permute-start(bf16[64,1536]{1,0:T(8,128)(2,1)} %blocks.1.rest_4_), channel_id=1, source_target_pairs={{0,1},{1,0},{2,3},{3,2},{4,5},{5,4},{6,7},{7,6},{8,9},{9,8},{10,11... | collective-permute-start | bytes 589832 | tf_op jit(solution)/shard_map/ppermute | solution.py:164
  54.1 2.4 %collective-permute-start.9 = (bf16[64,1536]{1,0:T(8,128)(2,1)S(1)}, bf16[64,1536]{1,0:T(8,128)(2,1)S(1)}, u32[]{:S(2)}, u32[]{:S(2)}) collective-permute-start(bf16[64,1536]{1,0:T(8,128)(2,1)S(1)} %collective-permute-done.7.rest_5_), channel_id=1, source_target_pairs={{0,1},{1,0},{2,3},{3,2},{4,5},{5,4},{6,7},{7,6},{8,9},{9,8},{10,11... | collective-permute-start | bytes 589832 | tf_op jit(solution)/shard_map/ppermute | solution.py:165
  56.5 0.1 pad_add_fusion.place_ref
  56.6 0.9 collective-permute-done.9.rest_7_
  57.6 0.9 copy-done
  58.5 0.9 copy-done.1
  59.4 1.8 %tile.1 = f32[32,16,128]{2,1,0:T(8,128)S(1)} custom-call(s32[3]{0:T(128)S(1)} %pad_add_fusion.place_ref, bf16[64,1536]{1,0:T(8,128)(2,1)S(1)} %copy-done.1, bf16[64,1536]{1,0:T(8,128)(2,1)S(1)} %collective-permute-done.4.rest_1_, bf16[64,1536]{1,0:T(8,128)(2,1)S(1)} %collective-permute-done.5.rest_2_, bf16[64,1536]{1,0:T(8,128)(2,1)S(1)} %collective-permute-done.6.rest_3_, ...), custom_call_target="tpu_custom_call" | custom-call | tf_op jit(solution)/shard_map/tile/pallas_call | solution.py:171
  61.2 22.3 %all_to_all.5.parts_ref = f32[32,16,128]{2,1,0:T(8,128)} all-to-all(f32[32,16,128]{2,1,0:T(8,128)S(1)} %tile.1), channel_id=1, replica_groups=mesh['y'=8,'z_lo'=4,'z_hi'=2,'x'=4,'core'=2] {'y','z_lo'}, dimensions={0} | all-to-all | bytes 524288 | tf_op jit(solution)/shard_map/all_to_all | solution.py:179
  83.5 1.7 %sum.1 = f32[32,64]{1,0:T(8,128)} custom-call(f32[32,16,128]{2,1,0:T(8,128)} %all_to_all.5.parts_ref), custom_call_target="tpu_custom_call" | custom-call | tf_op jit(solution)/shard_map/sum/pallas_call | solution.py:180
  85.1 3.4 %collective-permute-start.10 = (f32[32,64]{1,0:T(8,128)}, f32[32,64]{1,0:T(8,128)S(1)}, u32[]{:S(2)}, u32[]{:S(2)}) collective-permute-start(f32[32,64]{1,0:T(8,128)} %sum.1), channel_id=1, source_target_pairs={{0,0},{1,1},{8,8},{9,9},{16,16},{17,17},{24,24},{25,25},{32,32},{3... | collective-permute-start | bytes 24584 | tf_op jit(solution)/shard_map/ppermute | solution.py:197
  88.5 6.4 %collective-permute-done.10 = f32[32,64]{1,0:T(8,128)S(1)} collective-permute-done((f32[32,64]{1,0:T(8,128)}, f32[32,64]{1,0:T(8,128)S(1)}, u32[]{:S(2)}, u32[]{:S(2)}) %collective-permute-start.10) | collective-permute-done | bytes 8224 | tf_op jit(solution)/shard_map/ppermute | solution.py:197
  94.9 0.6 copy.10
  (9 shorter events, 0.0 us)
Async XLA Ops:
  1.9 22.2 %collective-permute-start = (bf16[64,768]{1,0:T(8,128)(2,1)}, bf16[64,768]{1,0:T(8,128)(2,1)}, u32[]{:S(2)}, u32[]{:S(2)}) collective-permute-start(bf16[64,768]{1,0:T(8,128)(2,1)} %get-tuple-element.12), channel_id=1, source_target_pairs={{496,0},{0,16},{16,32},{32,48},{48,64},{64,80},{80,96},{96,112},{1... | collective-permute-start | bytes 294920 | tf_op jit(solution)/shard_map/ppermute | solution.py:142
  6.1 18.0 %collective-permute-start.1 = (bf16[64,768]{1,0:T(8,128)(2,1)}, bf16[64,768]{1,0:T(8,128)(2,1)}, u32[]{:S(2)}, u32[]{:S(2)}) collective-permute-start(bf16[64,768]{1,0:T(8,128)(2,1)} %get-tuple-element.13), channel_id=1, source_target_pairs={{16,0},{32,16},{48,32},{64,48},{80,64},{96,80},{112,96},{128,112},... | collective-permute-start | bytes 294920 | tf_op jit(solution)/shard_map/ppermute | solution.py:142
  14.6 11.1 %collective-permute-start.2 = (bf16[64,768]{1,0:T(8,128)(2,1)}, bf16[64,768]{1,0:T(8,128)(2,1)}, u32[]{:S(2)}, u32[]{:S(2)}) collective-permute-start(bf16[64,768]{1,0:T(8,128)(2,1)} %get-tuple-element.14), channel_id=1, source_target_pairs={{480,0},{496,16},{0,32},{16,48},{32,64},{48,80},{64,96},{80,112},{... | collective-permute-start | bytes 294920 | tf_op jit(solution)/shard_map/ppermute | solution.py:142
  16.5 11.2 %collective-permute-start.3 = (bf16[64,768]{1,0:T(8,128)(2,1)}, bf16[64,768]{1,0:T(8,128)(2,1)}, u32[]{:S(2)}, u32[]{:S(2)}) collective-permute-start(bf16[64,768]{1,0:T(8,128)(2,1)} %get-tuple-element.15), channel_id=1, source_target_pairs={{32,0},{48,16},{64,32},{80,48},{96,64},{112,80},{128,96},{144,112}... | collective-permute-start | bytes 294920 | tf_op jit(solution)/shard_map/ppermute | solution.py:142
  33.5 20.5 %collective-permute-start.7 = (bf16[64,1536]{1,0:T(8,128)(2,1)}, bf16[64,1536]{1,0:T(8,128)(2,1)S(1)}, u32[]{:S(2)}, u32[]{:S(2)}) collective-permute-start(bf16[64,1536]{1,0:T(8,128)(2,1)} %blocks.1.rest_4_), channel_id=1, source_target_pairs={{0,8},{8,0},{1,9},{9,1},{2,10},{10,2},{3,11},{11,3},{4,12},{12,4},... | collective-permute-start | bytes 589832 | tf_op jit(solution)/shard_map/ppermute | solution.py:163
  41.8 14.8 %collective-permute-start.6 = (bf16[64,1536]{1,0:T(8,128)(2,1)}, bf16[64,1536]{1,0:T(8,128)(2,1)S(1)}, u32[]{:S(2)}, u32[]{:S(2)}) collective-permute-start(bf16[64,1536]{1,0:T(8,128)(2,1)} %get-tuple-element.16.rest_0_), channel_id=1, source_target_pairs={{4,0},{6,2},{0,4},{2,6},{5,1},{7,3},{1,5},{3,7},{12,8},{14,10},{8,... | collective-permute-start | bytes 589832 | tf_op jit(solution)/shard_map/ppermute | solution.py:169
  45.1 11.5 %collective-permute-start.5 = (bf16[64,1536]{1,0:T(8,128)(2,1)}, bf16[64,1536]{1,0:T(8,128)(2,1)S(1)}, u32[]{:S(2)}, u32[]{:S(2)}) collective-permute-start(bf16[64,1536]{1,0:T(8,128)(2,1)} %get-tuple-element.16.rest_0_), channel_id=1, source_target_pairs={{2,0},{4,2},{6,4},{0,6},{3,1},{5,3},{7,5},{1,7},{10,8},{12,10},{14... | collective-permute-start | bytes 589832 | tf_op jit(solution)/shard_map/ppermute | solution.py:169
  47.0 9.6 %collective-permute-start.4 = (bf16[64,1536]{1,0:T(8,128)(2,1)}, bf16[64,1536]{1,0:T(8,128)(2,1)S(1)}, u32[]{:S(2)}, u32[]{:S(2)}) collective-permute-start(bf16[64,1536]{1,0:T(8,128)(2,1)} %get-tuple-element.16.rest_0_), channel_id=1, source_target_pairs={{6,0},{0,2},{2,4},{4,6},{7,1},{1,3},{3,5},{5,7},{14,8},{8,10},{10,... | collective-permute-start | bytes 589832 | tf_op jit(solution)/shard_map/ppermute | solution.py:169
  52.2 4.5 %collective-permute-start.8 = (bf16[64,1536]{1,0:T(8,128)(2,1)}, bf16[64,1536]{1,0:T(8,128)(2,1)S(1)}, u32[]{:S(2)}, u32[]{:S(2)}) collective-permute-start(bf16[64,1536]{1,0:T(8,128)(2,1)} %blocks.1.rest_4_), channel_id=1, source_target_pairs={{0,1},{1,0},{2,3},{3,2},{4,5},{5,4},{6,7},{7,6},{8,9},{9,8},{10,11... | collective-permute-start | bytes 589832 | tf_op jit(solution)/shard_map/ppermute | solution.py:164
  54.1 3.5 %collective-permute-start.9 = (bf16[64,1536]{1,0:T(8,128)(2,1)S(1)}, bf16[64,1536]{1,0:T(8,128)(2,1)S(1)}, u32[]{:S(2)}, u32[]{:S(2)}) collective-permute-start(bf16[64,1536]{1,0:T(8,128)(2,1)S(1)} %collective-permute-done.7.rest_5_), channel_id=1, source_target_pairs={{0,1},{1,0},{2,3},{3,2},{4,5},{5,4},{6,7},{7,6},{8,9},{9,8},{10,11... | collective-permute-start | bytes 589832 | tf_op jit(solution)/shard_map/ppermute | solution.py:165
  57.6 0.9 copy-start
  58.5 0.9 copy-start.1
  85.1 9.7 %collective-permute-start.10 = (f32[32,64]{1,0:T(8,128)}, f32[32,64]{1,0:T(8,128)S(1)}, u32[]{:S(2)}, u32[]{:S(2)}) collective-permute-start(f32[32,64]{1,0:T(8,128)} %sum.1), channel_id=1, source_target_pairs={{0,0},{1,1},{8,8},{9,9},{16,16},{17,17},{24,24},{25,25},{32,32},{3... | collective-permute-start | bytes 24584 | tf_op jit(solution)/shard_map/ppermute | solution.py:197

commit v6 on v5

--- a/solution.py
+++ b/solution.py
@@ -1,7 +1,6 @@
-import functools
-
 import jax
 import jax.numpy as jnp
+import numpy as np
 from jax import lax
 from jax.experimental import pallas as pl
 from jax.experimental.pallas import tpu as pltpu
@@ -14,11 +13,11 @@
 OWN = 8
 WIDTH = 64
 CAP = 56
-CHUNK = 8
+CHUNK = 4
 PACKED = OWN * DOFS
 
 neighbour_offsets = (1, -1, 2, -2)
-x_offsets = (1, -1, 2)
+ROW_STEP, COLUMN_STEP = 1, 3
 VMEM = pl.BlockSpec(memory_space=pltpu.VMEM)
 SMEM = pl.BlockSpec(memory_space=pltpu.SMEM)
 HBM = pl.BlockSpec(memory_space=pltpu.HBM)
@@ -44,10 +43,11 @@
 
 
 def block_kernel(
-    rows_hbm, columns_hbm, density_hbm, count_hbm, basis_hbm, blocks_hbm, *rest
+    rows_hbm, columns_hbm, density_hbm, count_hbm, basis_hbm, blocks_hbm, own_hbm, other_hbm, *rest
 ):
     ghost_refs = rest[:NEIGH]
-    out_ref, rows_ref, columns_ref, density_ref, count_ref, blocks, pool, total, arrived, lists = rest[NEIGH:]
+    out_ref, pair_hbm, rows_ref, columns_ref, density_ref, count_ref, *rest = rest[NEIGH:]
+    blocks, pool, total, arrived, lists, joined = rest
     small = [
         pltpu.make_async_copy(source, target, lists.at[index])
         for index, (source, target) in enumerate((
@@ -67,6 +67,12 @@
             pltpu.make_async_copy(blocks_hbm.at[part], blocks.at[part], arrived.at[chunk])
         )
         copies[-1].start()
+    joins = [
+        pltpu.make_async_copy(source, pair_hbm.at[pl.ds(index * WIDTH, WIDTH)], joined.at[index])
+        for index, source in enumerate((own_hbm, other_hbm))
+    ]
+    for copy in joins:
+        copy.start()
     for neighbour, ghost_ref in enumerate(ghost_refs):
         for pair in range(GMAX // 2):
             at, slot = 384 * pair, OWN + neighbour * GMAX + 2 * pair
@@ -93,27 +99,43 @@
             total[row] = total[row] + scale * product
     for pair in range(OWN // 2):
         pack_pair(total[2 * pair], total[2 * pair + 1], out_ref, 384 * pair)
-
-
-def tile_kernel(place_ref, *rest):
-    row_refs, product_refs, out_ref = rest[:4], rest[4:8], rest[8]
+    for copy in joins:
+        copy.wait()
+
+
+def put_tile(place_ref, products_ref, rows_ref, out_ref, z_step, column_step, row_step):
     half, x, core = place_ref[0], place_ref[1], place_ref[2]
     low_lanes = lax.broadcasted_iota(jnp.int32, (16, 2 * WIDTH), 1) < WIDTH
-    row_places = [(x - offset + 4) % 4 for offset in (0,) + x_offsets]
-    column_places = [(half, core), (1 - half, core), (half, 1 - core), (1 - half, 1 - core)]
-    for slot in (0, 2):
-        rows = jnp.concatenate([row_refs[slot][...], row_refs[slot + 1][...]], axis=0)
-        for (z_place, core_place), ref in zip(column_places, product_refs):
-            tile = lax.dot_general(
-                ref[...], rows, (((1,), (1,)), ((), ())), preferred_element_type=jnp.float32
-            )
-            for h in range(2):
-                low, high = tile[32 * h : 32 * h + 16], tile[32 * h + 16 : 32 * h + 32]
-                low_turned = pltpu.roll(low, WIDTH, 1)
-                high_turned = pltpu.roll(high, WIDTH, 1)
-                at = 16 * z_place + 2 * core_place + h
-                out_ref[at + 4 * row_places[slot]] = jnp.where(low_lanes, low, high_turned)
-                out_ref[at + 4 * row_places[slot + 1]] = jnp.where(low_lanes, low_turned, high)
+    tile = lax.dot_general(
+        products_ref[...],
+        rows_ref[...],
+        (((1,), (1,)), ((), ())),
+        preferred_element_type=jnp.float32,
+    )
+    for h in range(2):
+        low, high = tile[32 * h : 32 * h + 16], tile[32 * h + 16 : 32 * h + 32]
+        low_turned = pltpu.roll(low, WIDTH, 1)
+        high_turned = pltpu.roll(high, WIDTH, 1)
+        at = 16 * (half ^ z_step) + 4 * (x ^ (row_step ^ column_step)) + h
+        out_ref[at + 2 * core] = jnp.where(low_lanes, low, high_turned)
+        out_ref[at + 2 - 2 * core] = jnp.where(low_lanes, low_turned, high)
+
+
+def own_tile_kernel(place_ref, pair_ref, products_ref, out_ref, pair_out_ref, products_out_ref):
+    pair_out_ref[...] = pair_ref[...]
+    products_out_ref[...] = products_ref[...]
+    put_tile(place_ref, products_ref, pair_ref, out_ref, 0, 0, 0)
+
+
+def tile_kernel(place_ref, pair_ref, other_pair_ref, *rest):
+    *product_refs, begun_ref, out_ref = rest
+    steps = ((0, 0), (1, 0), (0, COLUMN_STEP), (1, COLUMN_STEP))
+    for (z_step, column_step), products_ref in zip(steps, product_refs):
+        for row_step, rows_ref in ((0, pair_ref), (ROW_STEP, other_pair_ref)):
+            if z_step or column_step or row_step:
+                put_tile(
+                    place_ref, products_ref, rows_ref, out_ref, z_step, column_step, row_step
+                )
 
 
 def sum_kernel(parts_ref, out_ref):
@@ -140,11 +162,16 @@
     for block, offset in zip(picked, neighbour_offsets):
         route = [((i - offset) % parts, i) for i in range(parts)]
         arriving.append(lax.ppermute(block, mesh_axes, route))
-    products = pl.pallas_call(
+    swap = [(0, 1), (1, 0)]
+    other_packed = lax.ppermute(packed, "core", swap)
+    products, pair = pl.pallas_call(
         block_kernel,
-        out_shape=shape((WIDTH, PACKED), jnp.bfloat16),
-        in_specs=[HBM] * 6 + [VMEM] * NEIGH,
-        out_specs=VMEM,
+        out_shape=[
+            shape((WIDTH, PACKED), jnp.bfloat16),
+            shape((2 * WIDTH, PACKED), jnp.bfloat16),
+        ],
+        in_specs=[HBM] * 8 + [VMEM] * NEIGH,
+        out_specs=[VMEM, HBM],
         scratch_shapes=[
             pltpu.SMEM((CAP,), jnp.int32),
             pltpu.SMEM((CAP,), jnp.int32),
@@ -155,45 +182,65 @@
             pltpu.VMEM((OWN, WIDTH, DOFS), jnp.float32),
             pltpu.SemaphoreType.DMA((CAP // CHUNK,)),
             pltpu.SemaphoreType.DMA((5,)),
+            pltpu.SemaphoreType.DMA((2,)),
         ],
         compiler_params=pltpu.CompilerParams(vmem_limit_bytes=64 << 20),
         name="blocks",
-    )(block_rows, block_columns, density, block_counts, basis_vectors, stiffness_blocks, *arriving)
-    swap = [(0, 1), (1, 0)]
+    )(
+        block_rows,
+        block_columns,
+        density,
+        block_counts,
+        basis_vectors,
+        stiffness_blocks,
+        packed,
+        other_packed,
+        *arriving,
+    )
     over_z = lax.ppermute(products, "z_hi", swap)
-    over_core = lax.ppermute(products, "core", swap)
-    over_both = lax.ppermute(over_z, "core", swap)
-    packed, _ = lax.optimization_barrier((packed, products))
-    basis_rows = [packed]
-    for offset in x_offsets:
-        basis_rows.append(lax.ppermute(packed, "x", [((i - offset) % 4, i) for i in range(4)]))
+    over_x = lax.ppermute(products, "x", [(i, i ^ COLUMN_STEP) for i in range(4)])
+    over_both = lax.ppermute(over_z, "x", [(i, i ^ COLUMN_STEP) for i in range(4)])
+    other_pair = lax.ppermute(pair, "x", [(i, i ^ ROW_STEP) for i in range(4)])
     place = jnp.stack([lax.axis_index(name) for name in ("z_hi", "x", "core")]).astype(jnp.int32)
+    chunks_shape = shape((parts, 16, 128), jnp.float32)
+    begun, pair, products = pl.pallas_call(
+        own_tile_kernel,
+        out_shape=[
+            chunks_shape,
+            shape(pair.shape, pair.dtype),
+            shape(products.shape, products.dtype),
+        ],
+        in_specs=[SMEM] + [VMEM] * 2,
+        out_specs=[VMEM] * 3,
+        compiler_params=pltpu.CompilerParams(vmem_limit_bytes=16 << 20),
+        cost_estimate=pl.CostEstimate(flops=2 << 23, bytes_accessed=1 << 20, transcendentals=0),
+        name="own_tile",
+    )(place, pair, products)
     chunks = pl.pallas_call(
         tile_kernel,
-        out_shape=shape((parts, 16, 128), jnp.float32),
-        in_specs=[SMEM] + [VMEM] * 8,
+        out_shape=chunks_shape,
+        in_specs=[SMEM] + [VMEM] * 7,
         out_specs=VMEM,
-        compiler_params=pltpu.CompilerParams(vmem_limit_bytes=8 << 20),
+        input_output_aliases={7: 0},
+        compiler_params=pltpu.CompilerParams(vmem_limit_bytes=16 << 20),
         name="tile",
-    )(place, *basis_rows, products, over_z, over_core, over_both)
+    )(place, pair, other_pair, products, over_z, over_x, over_both, begun)
     shares = lax.all_to_all(chunks, mesh_axes, 0, 0, tiled=True)
     block = pl.pallas_call(
         sum_kernel,
         out_shape=shape((32, WIDTH), jnp.float32),
         in_specs=[VMEM],
         out_specs=VMEM,
+        compiler_params=pltpu.CompilerParams(vmem_limit_bytes=8 << 20),
         name="sum",
     )(shares)
     route = []
-    for a in range(4):
-        for b in range(4):
-            for place2 in range(8):
-                for panel in range(4):
-                    z2, rest, z, c = place2 // 4, place2 % 4, panel // 2, panel % 2
-                    source = (z2 * 16 + a * 4 + rest) * 16 + z * 8 + b * 2 + c
-                    target = (z2 * 16 + b * 4 + rest) * 16 + z * 8 + a * 2 + c
-                    route.append((source, target))
-
+    for place in range(512):
+        z2, x, u, v, c2, h, z, c = np.unravel_index(place, (2, 4, 2, 2, 2, 2, 2, 2))
+        u, v = u * ROW_STEP, v * COLUMN_STEP
+        source = (z2 * 16 + (x ^ u ^ v) * 4 + c2 * 2 + h) * 16 + z * 8 + x * 2 + c
+        target = (z2 * 16 + (x ^ v) * 4 + c * 2 + h) * 16 + z * 8 + (x ^ u) * 2 + c2
+        route.append((int(source), int(target)))
     return lax.ppermute(block, whole, route).T
 
 

time: 96.1 us -> 101 us (1.051)
  the two profiles are of different devices: /device:TPU:6 before, /device:TPU:8 now
where the time goes in v6:
time: 101 us
  starting transfers between devices  42.9 us (42%)
  blocking collectives  21 us (21%)
  Pallas kernels  19.4 us (19%)
  waiting for transfers between devices  14.1 us (14%)
  local copies, waits for them, and re-layouts  2.53 us (3%)
    all_to_all x1, blocking collectives, local(): shares = lax.all_to_all(chunks, mesh_axes, 0, 0, tiled=True)  21 us
    ppermute x4, starting transfers between devices, local(): arriving.append(lax.ppermute(block, mesh_axes, route))  17.3 us
    pallas_call x1, Pallas kernels, local(): pl.pallas_call(block_kernel, out_shape=[shape((WIDTH, PACKED), jnp.bfloat...  14.9 us
    ppermute x1, starting transfers between devices, local(): over_z = lax.ppermute(products, 'z_hi', swap)  9.28 us
    ppermute x4, waiting for transfers between devices, local(): arriving.append(lax.ppermute(block, mesh_axes, route))  5.33 us
    ppermute x1, starting transfers between devices, local(): lax.ppermute(products, 'x', [(i, i ^ COLUMN_STEP) for i in range(4)])  4 us
    ppermute x1, starting transfers between devices, local(): lax.ppermute(over_z, 'x', [(i, i ^ COLUMN_STEP) for i in range(4)])  3.99 us
    ppermute x1, waiting for transfers between devices, local(): return lax.ppermute(block, whole, route).T  3.53 us
  transfers between devices with their start and end apart: 10, of which 5 were waited for; matrix products, arithmetic and copies ran while one was open for 0% of the time, Pallas kernels for 1%

profile of v6, /device:TPU:8, one launch (start us, length us, event | category | flops | bytes accessed | tf_op | source)
XLA Modules:
  0.0 100.8 jit_solution(10469155725156764064)
XLA Ops:
  0.0 1.9 %select.1 = (bf16[64,1536]{1,0:T(8,128)(2,1)}, bf16[64,768]{1,0:T(8,128)(2,1)}, bf16[64,768]{1,0:T(8,128)(2,1)}, bf16[64,768]{1,0:T(8,128)(2,1)}, bf16[64,768]{1,0:T(8,128)(2,1)}) custom-call(s32[16]{0:T(128)} %send_ref.1, bf16[8,64,192]{2,1,0:T(8,128)(2,1)} %basis_hbm.1), custom_call_target="tpu_custom_call" | custom-call | tf_op jit(solution)/shard_map/select/pallas_call | solution.py:153
  1.9 1.9 %collective-permute-start = (bf16[64,1536]{1,0:T(8,128)(2,1)}, bf16[64,1536]{1,0:T(8,128)(2,1)}, u32[]{:S(2)}, u32[]{:S(2)}) collective-permute-start(bf16[64,1536]{1,0:T(8,128)(2,1)} %get-tuple-element.15.own_hbm), channel_id=1, source_target_pairs={{0,1},{1,0},{2,3},{3,2},{4,5},{5,4},{6,7},{7,6},{8,9},{9,8},{10,11... | collective-permute-start | bytes 589832 | tf_op jit(solution)/shard_map/ppermute | solution.py:166
  3.8 4.3 %collective-permute-start.1 = (bf16[64,768]{1,0:T(8,128)(2,1)}, bf16[64,768]{1,0:T(8,128)(2,1)}, u32[]{:S(2)}, u32[]{:S(2)}) collective-permute-start(bf16[64,768]{1,0:T(8,128)(2,1)} %get-tuple-element.16), channel_id=1, source_target_pairs={{496,0},{0,16},{16,32},{32,48},{48,64},{64,80},{80,96},{96,112},{1... | collective-permute-start | bytes 294920 | tf_op jit(solution)/shard_map/ppermute | solution.py:164
  8.1 5.4 %collective-permute-start.2 = (bf16[64,768]{1,0:T(8,128)(2,1)}, bf16[64,768]{1,0:T(8,128)(2,1)}, u32[]{:S(2)}, u32[]{:S(2)}) collective-permute-start(bf16[64,768]{1,0:T(8,128)(2,1)} %get-tuple-element.17), channel_id=1, source_target_pairs={{16,0},{32,16},{48,32},{64,48},{80,64},{96,80},{112,96},{128,112},... | collective-permute-start | bytes 294920 | tf_op jit(solution)/shard_map/ppermute | solution.py:164
  13.5 2.6 %collective-permute-start.3 = (bf16[64,768]{1,0:T(8,128)(2,1)}, bf16[64,768]{1,0:T(8,128)(2,1)}, u32[]{:S(2)}, u32[]{:S(2)}) collective-permute-start(bf16[64,768]{1,0:T(8,128)(2,1)} %get-tuple-element.18), channel_id=1, source_target_pairs={{480,0},{496,16},{0,32},{16,48},{32,64},{48,80},{64,96},{80,112},{... | collective-permute-start | bytes 294920 | tf_op jit(solution)/shard_map/ppermute | solution.py:164
  16.1 5.1 %collective-permute-start.4 = (bf16[64,768]{1,0:T(8,128)(2,1)}, bf16[64,768]{1,0:T(8,128)(2,1)}, u32[]{:S(2)}, u32[]{:S(2)}) collective-permute-start(bf16[64,768]{1,0:T(8,128)(2,1)} %get-tuple-element.19), channel_id=1, source_target_pairs={{32,0},{48,16},{64,32},{80,48},{96,64},{112,80},{128,96},{144,112}... | collective-permute-start | bytes 294920 | tf_op jit(solution)/shard_map/ppermute | solution.py:164
  21.8 1.2 %collective-permute-done.3.rest_2_ = bf16[64,768]{1,0:T(8,128)(2,1)} collective-permute-done((bf16[64,768]{1,0:T(8,128)(2,1)}, bf16[64,768]{1,0:T(8,128)(2,1)}, u32[]{:S(2)}, u32[]{:S(2)}) %collective-permute-start.3) | collective-permute-done | bytes 98336 | tf_op jit(solution)/shard_map/ppermute | solution.py:164
  23.0 4.2 %collective-permute-done.4.rest_3_ = bf16[64,768]{1,0:T(8,128)(2,1)} collective-permute-done((bf16[64,768]{1,0:T(8,128)(2,1)}, bf16[64,768]{1,0:T(8,128)(2,1)}, u32[]{:S(2)}, u32[]{:S(2)}) %collective-permute-start.4) | collective-permute-done | bytes 98336 | tf_op jit(solution)/shard_map/ppermute | solution.py:164
  27.2 14.9 %blocks.1 = (bf16[64,1536]{1,0:T(8,128)(2,1)}, bf16[128,1536]{1,0:T(8,128)(2,1)}) custom-call(s32[56]{0:T(128)} %rows_hbm.1, s32[56]{0:T(128)} %columns_hbm.1, f32[56]{0:T(128)} %density_hbm.1, s32[1]{0:T(128)S(6)} %copy.11.count_hbm, bf16[8,64,192]{2,1,0:T(8,128)(2,1)} %basis_hbm.1, bf16[56,192,192]{2,1,0:T(8,128)(2,1)} %blocks_hbm.1, ...), custom_call_target="tpu_custom_call" | custom-call | tf_op jit(solution)/shard_map/blocks/pallas_call | solution.py:167
  42.1 3.4 %collective-permute-start.5 = (bf16[128,1536]{1,0:T(8,128)(2,1)}, bf16[128,1536]{1,0:T(8,128)(2,1)S(1)}, u32[]{:S(2)}, u32[]{:S(2)}) collective-permute-start(bf16[128,1536]{1,0:T(8,128)(2,1)} %get-tuple-element.20.pair_ref), channel_id=1, source_target_pairs={{0,2},{2,0},{4,6},{6,4},{1,3},{3,1},{5,7},{7,5},{8,10},{10,8},{12,... | collective-permute-start | bytes 1179656 | tf_op jit(solution)/shard_map/ppermute | solution.py:203
  45.5 9.3 %collective-permute-start.6 = (bf16[64,1536]{1,0:T(8,128)(2,1)}, bf16[64,1536]{1,0:T(8,128)(2,1)S(1)}, u32[]{:S(2)}, u32[]{:S(2)}) collective-permute-start(bf16[64,1536]{1,0:T(8,128)(2,1)} %get-tuple-element.21.products_ref), channel_id=1, source_target_pairs={{0,8},{8,0},{1,9},{9,1},{2,10},{10,2},{3,11},{11,3},{4,12},{12,4},... | collective-permute-start | bytes 589832 | tf_op jit(solution)/shard_map/ppermute | solution.py:200
  54.8 4.0 %collective-permute-start.7 = (bf16[64,1536]{1,0:T(8,128)(2,1)}, bf16[64,1536]{1,0:T(8,128)(2,1)S(1)}, u32[]{:S(2)}, u32[]{:S(2)}) collective-permute-start(bf16[64,1536]{1,0:T(8,128)(2,1)} %get-tuple-element.21.products_ref), channel_id=1, source_target_pairs={{0,6},{2,4},{4,2},{6,0},{1,7},{3,5},{5,3},{7,1},{8,14},{10,12},{12... | collective-permute-start | bytes 589832 | tf_op jit(solution)/shard_map/ppermute | solution.py:201
  58.8 3.2 %collective-permute-done.6.rest_1_ = bf16[64,1536]{1,0:T(8,128)(2,1)S(1)} collective-permute-done((bf16[64,1536]{1,0:T(8,128)(2,1)}, bf16[64,1536]{1,0:T(8,128)(2,1)S(1)}, u32[]{:S(2)}, u32[]{:S(2)}) %collective-permute-start.6) | collective-permute-done | bytes 196640 | tf_op jit(solution)/shard_map/ppermute | solution.py:200
  62.0 4.0 %collective-permute-start.8 = (bf16[64,1536]{1,0:T(8,128)(2,1)S(1)}, bf16[64,1536]{1,0:T(8,128)(2,1)S(1)}, u32[]{:S(2)}, u32[]{:S(2)}) collective-permute-start(bf16[64,1536]{1,0:T(8,128)(2,1)S(1)} %collective-permute-done.6.rest_1_), channel_id=1, source_target_pairs={{0,6},{2,4},{4,2},{6,0},{1,7},{3,5},{5,3},{7,1},{8,14},{10,12},{12... | collective-permute-start | bytes 589832 | tf_op jit(solution)/shard_map/ppermute | solution.py:202
  66.1 1.0 copy-done
  67.1 0.9 copy-done.1
  68.0 0.9 own_tile.1
  68.9 2.0 %collective-permute-done.8.rest_3_ = bf16[64,1536]{1,0:T(8,128)(2,1)S(1)} collective-permute-done((bf16[64,1536]{1,0:T(8,128)(2,1)S(1)}, bf16[64,1536]{1,0:T(8,128)(2,1)S(1)}, u32[]{:S(2)}, u32[]{:S(2)}) %collective-permute-start.8) | collective-permute-done | bytes 196640 | tf_op jit(solution)/shard_map/ppermute | solution.py:202
  71.0 1.7 %tile.1 = f32[32,16,128]{2,1,0:T(8,128)S(1)} custom-call(s32[3]{0:T(128)S(1)} %pad_add_fusion.place_ref, bf16[128,1536]{1,0:T(8,128)(2,1)S(1)} %get-tuple-element.22.pair_ref, bf16[128,1536]{1,0:T(8,128)(2,1)S(1)} %collective-permute-done.5.other_pair_ref, bf16[64,1536]{1,0:T(8,128)(2,1)S(1)} %get-tuple-element.23.rest_0_, ...), custom_call_target="tpu_custom_call", output_to_operand_aliasing={{}: (7, {})} | custom-call | tf_op jit(solution)/shard_map/tile/pallas_call | solution.py:219
  72.6 21.0 %all_to_all.5.parts_ref = f32[32,16,128]{2,1,0:T(8,128)S(1)} all-to-all(f32[32,16,128]{2,1,0:T(8,128)S(1)} %tile.1), channel_id=1, replica_groups=mesh['y'=8,'z_lo'=4,'z_hi'=2,'x'=4,'core'=2] {'y','z_lo'}, dimensions={0} | all-to-all | bytes 524288 | tf_op jit(solution)/shard_map/all_to_all | solution.py:228
  93.6 0.1 sum.1
  93.7 3.0 %collective-permute-start.9 = (f32[32,64]{1,0:T(8,128)S(1)}, f32[32,64]{1,0:T(8,128)S(1)}, u32[]{:S(2)}, u32[]{:S(2)}) collective-permute-start(f32[32,64]{1,0:T(8,128)S(1)} %sum.1), channel_id=1, source_target_pairs={{0,0},{1,32},{8,8},{9,40},{16,16},{17,48},{24,24},{25,56},{32,1},{... | collective-permute-start | bytes 24584 | tf_op jit(solution)/shard_map/ppermute | solution.py:244
  96.7 3.5 %collective-permute-done.9 = f32[32,64]{1,0:T(8,128)S(1)} collective-permute-done((f32[32,64]{1,0:T(8,128)S(1)}, f32[32,64]{1,0:T(8,128)S(1)}, u32[]{:S(2)}, u32[]{:S(2)}) %collective-permute-start.9) | collective-permute-done | bytes 8224 | tf_op jit(solution)/shard_map/ppermute | solution.py:244
  100.2 0.6 copy.12
  (8 shorter events, 0.1 us)
Async XLA Ops:
  1.9 25.3 %collective-permute-start = (bf16[64,1536]{1,0:T(8,128)(2,1)}, bf16[64,1536]{1,0:T(8,128)(2,1)}, u32[]{:S(2)}, u32[]{:S(2)}) collective-permute-start(bf16[64,1536]{1,0:T(8,128)(2,1)} %get-tuple-element.15.own_hbm), channel_id=1, source_target_pairs={{0,1},{1,0},{2,3},{3,2},{4,5},{5,4},{6,7},{7,6},{8,9},{9,8},{10,11... | collective-permute-start | bytes 589832 | tf_op jit(solution)/shard_map/ppermute | solution.py:166
  3.8 18.0 %collective-permute-start.1 = (bf16[64,768]{1,0:T(8,128)(2,1)}, bf16[64,768]{1,0:T(8,128)(2,1)}, u32[]{:S(2)}, u32[]{:S(2)}) collective-permute-start(bf16[64,768]{1,0:T(8,128)(2,1)} %get-tuple-element.16), channel_id=1, source_target_pairs={{496,0},{0,16},{16,32},{32,48},{48,64},{64,80},{80,96},{96,112},{1... | collective-permute-start | bytes 294920 | tf_op jit(solution)/shard_map/ppermute | solution.py:164
  8.1 13.8 %collective-permute-start.2 = (bf16[64,768]{1,0:T(8,128)(2,1)}, bf16[64,768]{1,0:T(8,128)(2,1)}, u32[]{:S(2)}, u32[]{:S(2)}) collective-permute-start(bf16[64,768]{1,0:T(8,128)(2,1)} %get-tuple-element.17), channel_id=1, source_target_pairs={{16,0},{32,16},{48,32},{64,48},{80,64},{96,80},{112,96},{128,112},... | collective-permute-start | bytes 294920 | tf_op jit(solution)/shard_map/ppermute | solution.py:164
  13.5 9.5 %collective-permute-start.3 = (bf16[64,768]{1,0:T(8,128)(2,1)}, bf16[64,768]{1,0:T(8,128)(2,1)}, u32[]{:S(2)}, u32[]{:S(2)}) collective-permute-start(bf16[64,768]{1,0:T(8,128)(2,1)} %get-tuple-element.18), channel_id=1, source_target_pairs={{480,0},{496,16},{0,32},{16,48},{32,64},{48,80},{64,96},{80,112},{... | collective-permute-start | bytes 294920 | tf_op jit(solution)/shard_map/ppermute | solution.py:164
  16.1 11.1 %collective-permute-start.4 = (bf16[64,768]{1,0:T(8,128)(2,1)}, bf16[64,768]{1,0:T(8,128)(2,1)}, u32[]{:S(2)}, u32[]{:S(2)}) collective-permute-start(bf16[64,768]{1,0:T(8,128)(2,1)} %get-tuple-element.19), channel_id=1, source_target_pairs={{32,0},{48,16},{64,32},{80,48},{96,64},{112,80},{128,96},{144,112}... | collective-permute-start | bytes 294920 | tf_op jit(solution)/shard_map/ppermute | solution.py:164
  42.1 26.8 %collective-permute-start.5 = (bf16[128,1536]{1,0:T(8,128)(2,1)}, bf16[128,1536]{1,0:T(8,128)(2,1)S(1)}, u32[]{:S(2)}, u32[]{:S(2)}) collective-permute-start(bf16[128,1536]{1,0:T(8,128)(2,1)} %get-tuple-element.20.pair_ref), channel_id=1, source_target_pairs={{0,2},{2,0},{4,6},{6,4},{1,3},{3,1},{5,7},{7,5},{8,10},{10,8},{12,... | collective-permute-start | bytes 1179656 | tf_op jit(solution)/shard_map/ppermute | solution.py:203
  45.5 16.5 %collective-permute-start.6 = (bf16[64,1536]{1,0:T(8,128)(2,1)}, bf16[64,1536]{1,0:T(8,128)(2,1)S(1)}, u32[]{:S(2)}, u32[]{:S(2)}) collective-permute-start(bf16[64,1536]{1,0:T(8,128)(2,1)} %get-tuple-element.21.products_ref), channel_id=1, source_target_pairs={{0,8},{8,0},{1,9},{9,1},{2,10},{10,2},{3,11},{11,3},{4,12},{12,4},... | collective-permute-start | bytes 589832 | tf_op jit(solution)/shard_map/ppermute | solution.py:200
  54.8 14.1 %collective-permute-start.7 = (bf16[64,1536]{1,0:T(8,128)(2,1)}, bf16[64,1536]{1,0:T(8,128)(2,1)S(1)}, u32[]{:S(2)}, u32[]{:S(2)}) collective-permute-start(bf16[64,1536]{1,0:T(8,128)(2,1)} %get-tuple-element.21.products_ref), channel_id=1, source_target_pairs={{0,6},{2,4},{4,2},{6,0},{1,7},{3,5},{5,3},{7,1},{8,14},{10,12},{12... | collective-permute-start | bytes 589832 | tf_op jit(solution)/shard_map/ppermute | solution.py:201
  62.0 8.9 %collective-permute-start.8 = (bf16[64,1536]{1,0:T(8,128)(2,1)S(1)}, bf16[64,1536]{1,0:T(8,128)(2,1)S(1)}, u32[]{:S(2)}, u32[]{:S(2)}) collective-permute-start(bf16[64,1536]{1,0:T(8,128)(2,1)S(1)} %collective-permute-done.6.rest_1_), channel_id=1, source_target_pairs={{0,6},{2,4},{4,2},{6,0},{1,7},{3,5},{5,3},{7,1},{8,14},{10,12},{12... | collective-permute-start | bytes 589832 | tf_op jit(solution)/shard_map/ppermute | solution.py:202
  66.1 1.0 copy-start
  67.1 0.9 copy-start.1
  93.7 6.5 %collective-permute-start.9 = (f32[32,64]{1,0:T(8,128)S(1)}, f32[32,64]{1,0:T(8,128)S(1)}, u32[]{:S(2)}, u32[]{:S(2)}) collective-permute-start(f32[32,64]{1,0:T(8,128)S(1)} %sum.1), channel_id=1, source_target_pairs={{0,0},{1,32},{8,8},{9,40},{16,16},{17,48},{24,24},{25,56},{32,1},{... | collective-permute-start | bytes 24584 | tf_op jit(solution)/shard_map/ppermute | solution.py:244

commit v7 on v6

--- a/solution.py
+++ b/solution.py
@@ -17,7 +17,7 @@
 PACKED = OWN * DOFS
 
 neighbour_offsets = (1, -1, 2, -2)
-ROW_STEP, COLUMN_STEP = 1, 3
+NEAR, FAR = 1, 3
 VMEM = pl.BlockSpec(memory_space=pltpu.VMEM)
 SMEM = pl.BlockSpec(memory_space=pltpu.SMEM)
 HBM = pl.BlockSpec(memory_space=pltpu.HBM)
@@ -46,7 +46,7 @@
     rows_hbm, columns_hbm, density_hbm, count_hbm, basis_hbm, blocks_hbm, own_hbm, other_hbm, *rest
 ):
     ghost_refs = rest[:NEIGH]
-    out_ref, pair_hbm, rows_ref, columns_ref, density_ref, count_ref, *rest = rest[NEIGH:]
+    out_ref, pair_ref, rows_ref, columns_ref, density_ref, count_ref, *rest = rest[NEIGH:]
     blocks, pool, total, arrived, lists, joined = rest
     small = [
         pltpu.make_async_copy(source, target, lists.at[index])
@@ -68,7 +68,7 @@
         )
         copies[-1].start()
     joins = [
-        pltpu.make_async_copy(source, pair_hbm.at[pl.ds(index * WIDTH, WIDTH)], joined.at[index])
+        pltpu.make_async_copy(source, pair_ref.at[pl.ds(index * WIDTH, WIDTH)], joined.at[index])
         for index, source in enumerate((own_hbm, other_hbm))
     ]
     for copy in joins:
@@ -103,8 +103,8 @@
         copy.wait()
 
 
-def put_tile(place_ref, products_ref, rows_ref, out_ref, z_step, column_step, row_step):
-    half, x, core = place_ref[0], place_ref[1], place_ref[2]
+def put_tile(place_ref, products_ref, rows_ref, out_ref, z_step, core_step, row_step):
+    half, x, core = place_ref[0] ^ z_step, place_ref[1] ^ row_step, place_ref[2] ^ core_step
     low_lanes = lax.broadcasted_iota(jnp.int32, (16, 2 * WIDTH), 1) < WIDTH
     tile = lax.dot_general(
         products_ref[...],
@@ -116,9 +116,9 @@
         low, high = tile[32 * h : 32 * h + 16], tile[32 * h + 16 : 32 * h + 32]
         low_turned = pltpu.roll(low, WIDTH, 1)
         high_turned = pltpu.roll(high, WIDTH, 1)
-        at = 16 * (half ^ z_step) + 4 * (x ^ (row_step ^ column_step)) + h
-        out_ref[at + 2 * core] = jnp.where(low_lanes, low, high_turned)
-        out_ref[at + 2 - 2 * core] = jnp.where(low_lanes, low_turned, high)
+        at = 16 * half + 2 * core + h
+        out_ref[at + 4 * x] = jnp.where(low_lanes, low, high_turned)
+        out_ref[at + 4 * (x ^ NEAR)] = jnp.where(low_lanes, low_turned, high)
 
 
 def own_tile_kernel(place_ref, pair_ref, products_ref, out_ref, pair_out_ref, products_out_ref):
@@ -129,12 +129,11 @@
 
 def tile_kernel(place_ref, pair_ref, other_pair_ref, *rest):
     *product_refs, begun_ref, out_ref = rest
-    steps = ((0, 0), (1, 0), (0, COLUMN_STEP), (1, COLUMN_STEP))
-    for (z_step, column_step), products_ref in zip(steps, product_refs):
-        for row_step, rows_ref in ((0, pair_ref), (ROW_STEP, other_pair_ref)):
-            if z_step or column_step or row_step:
+    for (z_step, core_step), products_ref in zip(((0, 0), (0, 1), (1, 0), (1, 1)), product_refs):
+        for row_step, rows_ref in ((0, pair_ref), (FAR, other_pair_ref)):
+            if z_step or core_step or row_step:
                 put_tile(
-                    place_ref, products_ref, rows_ref, out_ref, z_step, column_step, row_step
+                    place_ref, products_ref, rows_ref, out_ref, z_step, core_step, row_step
                 )
 
 
@@ -163,7 +162,7 @@
         route = [((i - offset) % parts, i) for i in range(parts)]
         arriving.append(lax.ppermute(block, mesh_axes, route))
     swap = [(0, 1), (1, 0)]
-    other_packed = lax.ppermute(packed, "core", swap)
+    other_packed = lax.ppermute(packed, "x", [(i, i ^ NEAR) for i in range(4)])
     products, pair = pl.pallas_call(
         block_kernel,
         out_shape=[
@@ -171,7 +170,7 @@
             shape((2 * WIDTH, PACKED), jnp.bfloat16),
         ],
         in_specs=[HBM] * 8 + [VMEM] * NEIGH,
-        out_specs=[VMEM, HBM],
+        out_specs=[VMEM] * 2,
         scratch_shapes=[
             pltpu.SMEM((CAP,), jnp.int32),
             pltpu.SMEM((CAP,), jnp.int32),
@@ -198,9 +197,8 @@
         *arriving,
     )
     over_z = lax.ppermute(products, "z_hi", swap)
-    over_x = lax.ppermute(products, "x", [(i, i ^ COLUMN_STEP) for i in range(4)])
-    over_both = lax.ppermute(over_z, "x", [(i, i ^ COLUMN_STEP) for i in range(4)])
-    other_pair = lax.ppermute(pair, "x", [(i, i ^ ROW_STEP) for i in range(4)])
+    over_core = lax.ppermute(products, "core", swap)
+    other_pair = lax.ppermute(pair, "x", [(i, i ^ FAR) for i in range(4)])
     place = jnp.stack([lax.axis_index(name) for name in ("z_hi", "x", "core")]).astype(jnp.int32)
     chunks_shape = shape((parts, 16, 128), jnp.float32)
     begun, pair, products = pl.pallas_call(
@@ -216,6 +214,8 @@
         cost_estimate=pl.CostEstimate(flops=2 << 23, bytes_accessed=1 << 20, transcendentals=0),
         name="own_tile",
     )(place, pair, products)
+    behind, begun = lax.optimization_barrier((over_z, begun))
+    over_both = lax.ppermute(behind, "core", swap)
     chunks = pl.pallas_call(
         tile_kernel,
         out_shape=chunks_shape,
@@ -224,7 +224,7 @@
         input_output_aliases={7: 0},
         compiler_params=pltpu.CompilerParams(vmem_limit_bytes=16 << 20),
         name="tile",
-    )(place, pair, other_pair, products, over_z, over_x, over_both, begun)
+    )(place, pair, other_pair, products, over_core, over_z, over_both, begun)
     shares = lax.all_to_all(chunks, mesh_axes, 0, 0, tiled=True)
     block = pl.pallas_call(
         sum_kernel,
@@ -236,11 +236,10 @@
     )(shares)
     route = []
     for place in range(512):
-        z2, x, u, v, c2, h, z, c = np.unravel_index(place, (2, 4, 2, 2, 2, 2, 2, 2))
-        u, v = u * ROW_STEP, v * COLUMN_STEP
-        source = (z2 * 16 + (x ^ u ^ v) * 4 + c2 * 2 + h) * 16 + z * 8 + x * 2 + c
-        target = (z2 * 16 + (x ^ v) * 4 + c * 2 + h) * 16 + z * 8 + (x ^ u) * 2 + c2
-        route.append((int(source), int(target)))
+        z2, a, c2, h, z, b, c = (int(i) for i in np.unravel_index(place, (2, 4, 2, 2, 2, 4, 2)))
+        source = (z2 * 16 + a * 4 + c2 * 2 + h) * 16 + z * 8 + b * 2 + c
+        target = (z2 * 16 + b * 4 + c2 * 2 + h) * 16 + z * 8 + a * 2 + c
+        route.append((source, target))
     return lax.ppermute(block, whole, route).T
 
 

time: 101 us -> 91.9 us (0.910)
  the two profiles are of different devices: /device:TPU:8 before, /device:TPU:6 now
where the time goes in v7:
time: 91.9 us; the launch traced here: 91.3 us
  starting transfers between devices  43.7 us (48%)
  blocking collectives  20.1 us (22%)
  waiting for transfers between devices  12.8 us (14%)
  Pallas kernels  11.4 us (12%)
  local copies, waits for them, and re-layouts  2.52 us (3%)
    ppermute x4, starting transfers between devices, local(): arriving.append(lax.ppermute(block, mesh_axes, route))  21.6 us
    all_to_all x1, blocking collectives, local(): shares = lax.all_to_all(chunks, mesh_axes, 0, 0, tiled=True)  20.1 us
    ppermute x1, starting transfers between devices, local(): over_z = lax.ppermute(products, 'z_hi', swap)  8.22 us
    pallas_call x1, Pallas kernels, local(): pl.pallas_call(block_kernel, out_shape=[shape((WIDTH, PACKED), jnp.bfloat...  6.88 us
    ppermute x1, waiting for transfers between devices, local(): return lax.ppermute(block, whole, route).T  5.35 us
    ppermute x1, starting transfers between devices, local(): return lax.ppermute(block, whole, route).T  4.17 us
    ppermute x1, waiting for transfers between devices, local(): other_pair = lax.ppermute(pair, 'x', [(i, i ^ FAR) for i in range(4)])  3.78 us
    ppermute x4, waiting for transfers between devices, local(): arriving.append(lax.ppermute(block, mesh_axes, route))  3.28 us
  transfers between devices with their start and end apart: 10, of which 5 were waited for; matrix products, arithmetic and copies ran while one was open for 0% of the time, Pallas kernels for 1%

profile of v7, /device:TPU:6, one launch (start us, length us, event | category | flops | bytes accessed | tf_op | source)
XLA Modules:
  0.0 91.3 jit_solution(2288871236847814853)
XLA Ops:
  0.0 1.9 %select.1 = (bf16[64,1536]{1,0:T(8,128)(2,1)}, bf16[64,768]{1,0:T(8,128)(2,1)}, bf16[64,768]{1,0:T(8,128)(2,1)}, bf16[64,768]{1,0:T(8,128)(2,1)}, bf16[64,768]{1,0:T(8,128)(2,1)}) custom-call(s32[16]{0:T(128)} %send_ref.1, bf16[8,64,192]{2,1,0:T(8,128)(2,1)} %basis_hbm.1), custom_call_target="tpu_custom_call" | custom-call | tf_op jit(solution)/shard_map/select/pallas_call | solution.py:152
  1.9 2.7 %collective-permute-start = (bf16[64,1536]{1,0:T(8,128)(2,1)}, bf16[64,1536]{1,0:T(8,128)(2,1)}, u32[]{:S(2)}, u32[]{:S(2)}) collective-permute-start(bf16[64,1536]{1,0:T(8,128)(2,1)} %get-tuple-element.17.own_hbm), channel_id=1, source_target_pairs={{0,2},{2,0},{4,6},{6,4},{1,3},{3,1},{5,7},{7,5},{8,10},{10,8},{12,... | collective-permute-start | bytes 589832 | tf_op jit(solution)/shard_map/ppermute | solution.py:165
  4.6 4.3 %collective-permute-start.1 = (bf16[64,768]{1,0:T(8,128)(2,1)}, bf16[64,768]{1,0:T(8,128)(2,1)}, u32[]{:S(2)}, u32[]{:S(2)}) collective-permute-start(bf16[64,768]{1,0:T(8,128)(2,1)} %get-tuple-element.18), channel_id=1, source_target_pairs={{496,0},{0,16},{16,32},{32,48},{48,64},{64,80},{80,96},{96,112},{1... | collective-permute-start | bytes 294920 | tf_op jit(solution)/shard_map/ppermute | solution.py:163
  8.9 8.4 %collective-permute-start.2 = (bf16[64,768]{1,0:T(8,128)(2,1)}, bf16[64,768]{1,0:T(8,128)(2,1)}, u32[]{:S(2)}, u32[]{:S(2)}) collective-permute-start(bf16[64,768]{1,0:T(8,128)(2,1)} %get-tuple-element.19), channel_id=1, source_target_pairs={{16,0},{32,16},{48,32},{64,48},{80,64},{96,80},{112,96},{128,112},... | collective-permute-start | bytes 294920 | tf_op jit(solution)/shard_map/ppermute | solution.py:163
  17.3 1.9 %collective-permute-start.3 = (bf16[64,768]{1,0:T(8,128)(2,1)}, bf16[64,768]{1,0:T(8,128)(2,1)}, u32[]{:S(2)}, u32[]{:S(2)}) collective-permute-start(bf16[64,768]{1,0:T(8,128)(2,1)} %get-tuple-element.20), channel_id=1, source_target_pairs={{480,0},{496,16},{0,32},{16,48},{32,64},{48,80},{64,96},{80,112},{... | collective-permute-start | bytes 294920 | tf_op jit(solution)/shard_map/ppermute | solution.py:163
  19.3 6.9 %collective-permute-start.4 = (bf16[64,768]{1,0:T(8,128)(2,1)}, bf16[64,768]{1,0:T(8,128)(2,1)}, u32[]{:S(2)}, u32[]{:S(2)}) collective-permute-start(bf16[64,768]{1,0:T(8,128)(2,1)} %get-tuple-element.21), channel_id=1, source_target_pairs={{32,0},{48,16},{64,32},{80,48},{96,64},{112,80},{128,96},{144,112}... | collective-permute-start | bytes 294920 | tf_op jit(solution)/shard_map/ppermute | solution.py:163
  26.9 1.3 %collective-permute-done.3.rest_2_ = bf16[64,768]{1,0:T(8,128)(2,1)} collective-permute-done((bf16[64,768]{1,0:T(8,128)(2,1)}, bf16[64,768]{1,0:T(8,128)(2,1)}, u32[]{:S(2)}, u32[]{:S(2)}) %collective-permute-start.3) | collective-permute-done | bytes 98336 | tf_op jit(solution)/shard_map/ppermute | solution.py:163
  28.2 2.0 %collective-permute-done.4.rest_3_ = bf16[64,768]{1,0:T(8,128)(2,1)} collective-permute-done((bf16[64,768]{1,0:T(8,128)(2,1)}, bf16[64,768]{1,0:T(8,128)(2,1)}, u32[]{:S(2)}, u32[]{:S(2)}) %collective-permute-start.4) | collective-permute-done | bytes 98336 | tf_op jit(solution)/shard_map/ppermute | solution.py:163
  30.2 6.9 %blocks.1 = (bf16[64,1536]{1,0:T(8,128)(2,1)}, bf16[128,1536]{1,0:T(8,128)(2,1)}) custom-call(s32[56]{0:T(128)} %rows_hbm.1, s32[56]{0:T(128)} %columns_hbm.1, f32[56]{0:T(128)} %density_hbm.1, s32[1]{0:T(128)S(6)} %copy.11.count_hbm, bf16[8,64,192]{2,1,0:T(8,128)(2,1)} %basis_hbm.1, bf16[56,192,192]{2,1,0:T(8,128)(2,1)} %blocks_hbm.1, ...), custom_call_target="tpu_custom_call" | custom-call | tf_op jit(solution)/shard_map/blocks/pallas_call | solution.py:166
  37.1 8.2 %collective-permute-start.7 = (bf16[64,1536]{1,0:T(8,128)(2,1)}, bf16[64,1536]{1,0:T(8,128)(2,1)S(1)}, u32[]{:S(2)}, u32[]{:S(2)}) collective-permute-start(bf16[64,1536]{1,0:T(8,128)(2,1)} %get-tuple-element.23.products_ref), channel_id=1, source_target_pairs={{0,8},{8,0},{1,9},{9,1},{2,10},{10,2},{3,11},{11,3},{4,12},{12,4},... | collective-permute-start | bytes 589832 | tf_op jit(solution)/shard_map/ppermute | solution.py:199
  45.3 3.0 %collective-permute-start.5 = (bf16[128,1536]{1,0:T(8,128)(2,1)}, bf16[128,1536]{1,0:T(8,128)(2,1)S(1)}, u32[]{:S(2)}, u32[]{:S(2)}) collective-permute-start(bf16[128,1536]{1,0:T(8,128)(2,1)} %get-tuple-element.22.pair_ref), channel_id=1, source_target_pairs={{0,6},{2,4},{4,2},{6,0},{1,7},{3,5},{5,3},{7,1},{8,14},{10,12},{12... | collective-permute-start | bytes 1179656 | tf_op jit(solution)/shard_map/ppermute | solution.py:201
  48.4 1.9 %collective-permute-start.6 = (bf16[64,1536]{1,0:T(8,128)(2,1)}, bf16[64,1536]{1,0:T(8,128)(2,1)S(1)}, u32[]{:S(2)}, u32[]{:S(2)}) collective-permute-start(bf16[64,1536]{1,0:T(8,128)(2,1)} %get-tuple-element.23.products_ref), channel_id=1, source_target_pairs={{0,1},{1,0},{2,3},{3,2},{4,5},{5,4},{6,7},{7,6},{8,9},{9,8},{10,11... | collective-permute-start | bytes 589832 | tf_op jit(solution)/shard_map/ppermute | solution.py:200
  50.4 1.0 %copy-done = bf16[128,1536]{1,0:T(8,128)(2,1)S(1)} copy-done((bf16[128,1536]{1,0:T(8,128)(2,1)S(1)}, bf16[128,1536]{1,0:T(8,128)(2,1)}, u32[]{:S(2)}) %copy-start) | copy-done | bytes 393240
  51.3 0.9 %copy-done.1 = bf16[64,1536]{1,0:T(8,128)(2,1)S(1)} copy-done((bf16[64,1536]{1,0:T(8,128)(2,1)S(1)}, bf16[64,1536]{1,0:T(8,128)(2,1)}, u32[]{:S(2)}) %copy-start.1) | copy-done | bytes 196632
  52.3 0.9 own_tile.1
  53.1 0.4 collective-permute-done.7.rest_2_
  53.5 2.0 %collective-permute-start.8 = (bf16[64,1536]{1,0:T(8,128)(2,1)S(1)}, bf16[64,1536]{1,0:T(8,128)(2,1)S(1)}, u32[]{:S(2)}, u32[]{:S(2)}) collective-permute-start(bf16[64,1536]{1,0:T(8,128)(2,1)S(1)} %collective-permute-done.7.rest_2_), channel_id=1, source_target_pairs={{0,1},{1,0},{2,3},{3,2},{4,5},{5,4},{6,7},{7,6},{8,9},{9,8},{10,11... | collective-permute-start | bytes 589832 | tf_op jit(solution)/shard_map/ppermute | solution.py:218
  55.6 3.8 %collective-permute-done.5.other_pair_ref = bf16[128,1536]{1,0:T(8,128)(2,1)S(1)} collective-permute-done((bf16[128,1536]{1,0:T(8,128)(2,1)}, bf16[128,1536]{1,0:T(8,128)(2,1)S(1)}, u32[]{:S(2)}, u32[]{:S(2)}) %collective-permute-start.5) | collective-permute-done | bytes 393248 | tf_op jit(solution)/shard_map/ppermute | solution.py:201
  59.4 1.6 %tile.1 = f32[32,16,128]{2,1,0:T(8,128)S(1)} custom-call(s32[3]{0:T(128)S(1)} %pad_add_fusion.place_ref, bf16[128,1536]{1,0:T(8,128)(2,1)S(1)} %get-tuple-element.24.pair_ref, bf16[128,1536]{1,0:T(8,128)(2,1)S(1)} %collective-permute-done.5.other_pair_ref, bf16[64,1536]{1,0:T(8,128)(2,1)S(1)} %get-tuple-element.25.rest_0_, ...), custom_call_target="tpu_custom_call", output_to_operand_aliasing={{}: (7, {})} | custom-call | tf_op jit(solution)/shard_map/tile/pallas_call | solution.py:219
  61.0 20.1 %all_to_all.5.parts_ref = f32[32,16,128]{2,1,0:T(8,128)S(1)} all-to-all(f32[32,16,128]{2,1,0:T(8,128)S(1)} %tile.1), channel_id=1, replica_groups=mesh['y'=8,'z_lo'=4,'z_hi'=2,'x'=4,'core'=2] {'y','z_lo'}, dimensions={0} | all-to-all | bytes 524288 | tf_op jit(solution)/shard_map/all_to_all | solution.py:228
  81.1 0.1 sum.1
  81.2 4.2 %collective-permute-start.9 = (f32[32,64]{1,0:T(8,128)S(1)}, f32[32,64]{1,0:T(8,128)S(1)}, u32[]{:S(2)}, u32[]{:S(2)}) collective-permute-start(f32[32,64]{1,0:T(8,128)S(1)} %sum.1), channel_id=1, source_target_pairs={{0,0},{1,1},{2,64},{3,65},{4,128},{5,129},{6,192},{7,193},{8,8},{9... | collective-permute-start | bytes 24584 | tf_op jit(solution)/shard_map/ppermute | solution.py:243
  85.4 5.3 %collective-permute-done.9 = f32[32,64]{1,0:T(8,128)S(1)} collective-permute-done((f32[32,64]{1,0:T(8,128)S(1)}, f32[32,64]{1,0:T(8,128)S(1)}, u32[]{:S(2)}, u32[]{:S(2)}) %collective-permute-start.9) | collective-permute-done | bytes 8224 | tf_op jit(solution)/shard_map/ppermute | solution.py:243
  90.7 0.6 copy.12
  (8 shorter events, 0.1 us)
Async XLA Ops:
  1.9 28.3 %collective-permute-start = (bf16[64,1536]{1,0:T(8,128)(2,1)}, bf16[64,1536]{1,0:T(8,128)(2,1)}, u32[]{:S(2)}, u32[]{:S(2)}) collective-permute-start(bf16[64,1536]{1,0:T(8,128)(2,1)} %get-tuple-element.17.own_hbm), channel_id=1, source_target_pairs={{0,2},{2,0},{4,6},{6,4},{1,3},{3,1},{5,7},{7,5},{8,10},{10,8},{12,... | collective-permute-start | bytes 589832 | tf_op jit(solution)/shard_map/ppermute | solution.py:165
  4.6 22.3 %collective-permute-start.1 = (bf16[64,768]{1,0:T(8,128)(2,1)}, bf16[64,768]{1,0:T(8,128)(2,1)}, u32[]{:S(2)}, u32[]{:S(2)}) collective-permute-start(bf16[64,768]{1,0:T(8,128)(2,1)} %get-tuple-element.18), channel_id=1, source_target_pairs={{496,0},{0,16},{16,32},{32,48},{48,64},{64,80},{80,96},{96,112},{1... | collective-permute-start | bytes 294920 | tf_op jit(solution)/shard_map/ppermute | solution.py:163
  8.9 18.0 %collective-permute-start.2 = (bf16[64,768]{1,0:T(8,128)(2,1)}, bf16[64,768]{1,0:T(8,128)(2,1)}, u32[]{:S(2)}, u32[]{:S(2)}) collective-permute-start(bf16[64,768]{1,0:T(8,128)(2,1)} %get-tuple-element.19), channel_id=1, source_target_pairs={{16,0},{32,16},{48,32},{64,48},{80,64},{96,80},{112,96},{128,112},... | collective-permute-start | bytes 294920 | tf_op jit(solution)/shard_map/ppermute | solution.py:163
  17.3 10.8 %collective-permute-start.3 = (bf16[64,768]{1,0:T(8,128)(2,1)}, bf16[64,768]{1,0:T(8,128)(2,1)}, u32[]{:S(2)}, u32[]{:S(2)}) collective-permute-start(bf16[64,768]{1,0:T(8,128)(2,1)} %get-tuple-element.20), channel_id=1, source_target_pairs={{480,0},{496,16},{0,32},{16,48},{32,64},{48,80},{64,96},{80,112},{... | collective-permute-start | bytes 294920 | tf_op jit(solution)/shard_map/ppermute | solution.py:163
  19.3 10.9 %collective-permute-start.4 = (bf16[64,768]{1,0:T(8,128)(2,1)}, bf16[64,768]{1,0:T(8,128)(2,1)}, u32[]{:S(2)}, u32[]{:S(2)}) collective-permute-start(bf16[64,768]{1,0:T(8,128)(2,1)} %get-tuple-element.21), channel_id=1, source_target_pairs={{32,0},{48,16},{64,32},{80,48},{96,64},{112,80},{128,96},{144,112}... | collective-permute-start | bytes 294920 | tf_op jit(solution)/shard_map/ppermute | solution.py:163
  37.1 16.5 %collective-permute-start.7 = (bf16[64,1536]{1,0:T(8,128)(2,1)}, bf16[64,1536]{1,0:T(8,128)(2,1)S(1)}, u32[]{:S(2)}, u32[]{:S(2)}) collective-permute-start(bf16[64,1536]{1,0:T(8,128)(2,1)} %get-tuple-element.23.products_ref), channel_id=1, source_target_pairs={{0,8},{8,0},{1,9},{9,1},{2,10},{10,2},{3,11},{11,3},{4,12},{12,4},... | collective-permute-start | bytes 589832 | tf_op jit(solution)/shard_map/ppermute | solution.py:199
  45.3 14.1 %collective-permute-start.5 = (bf16[128,1536]{1,0:T(8,128)(2,1)}, bf16[128,1536]{1,0:T(8,128)(2,1)S(1)}, u32[]{:S(2)}, u32[]{:S(2)}) collective-permute-start(bf16[128,1536]{1,0:T(8,128)(2,1)} %get-tuple-element.22.pair_ref), channel_id=1, source_target_pairs={{0,6},{2,4},{4,2},{6,0},{1,7},{3,5},{5,3},{7,1},{8,14},{10,12},{12... | collective-permute-start | bytes 1179656 | tf_op jit(solution)/shard_map/ppermute | solution.py:201
  48.4 7.1 %collective-permute-start.6 = (bf16[64,1536]{1,0:T(8,128)(2,1)}, bf16[64,1536]{1,0:T(8,128)(2,1)S(1)}, u32[]{:S(2)}, u32[]{:S(2)}) collective-permute-start(bf16[64,1536]{1,0:T(8,128)(2,1)} %get-tuple-element.23.products_ref), channel_id=1, source_target_pairs={{0,1},{1,0},{2,3},{3,2},{4,5},{5,4},{6,7},{7,6},{8,9},{9,8},{10,11... | collective-permute-start | bytes 589832 | tf_op jit(solution)/shard_map/ppermute | solution.py:200
  50.3 1.0 %copy-start = (bf16[128,1536]{1,0:T(8,128)(2,1)S(1)}, bf16[128,1536]{1,0:T(8,128)(2,1)}, u32[]{:S(2)}) copy-start(bf16[128,1536]{1,0:T(8,128)(2,1)} %get-tuple-element.22.pair_ref) | copy-start | bytes 1179652
  51.3 0.9 %copy-start.1 = (bf16[64,1536]{1,0:T(8,128)(2,1)S(1)}, bf16[64,1536]{1,0:T(8,128)(2,1)}, u32[]{:S(2)}) copy-start(bf16[64,1536]{1,0:T(8,128)(2,1)} %get-tuple-element.23.products_ref) | copy-start | bytes 589828
  53.5 5.8 %collective-permute-start.8 = (bf16[64,1536]{1,0:T(8,128)(2,1)S(1)}, bf16[64,1536]{1,0:T(8,128)(2,1)S(1)}, u32[]{:S(2)}, u32[]{:S(2)}) collective-permute-start(bf16[64,1536]{1,0:T(8,128)(2,1)S(1)} %collective-permute-done.7.rest_2_), channel_id=1, source_target_pairs={{0,1},{1,0},{2,3},{3,2},{4,5},{5,4},{6,7},{7,6},{8,9},{9,8},{10,11... | collective-permute-start | bytes 589832 | tf_op jit(solution)/shard_map/ppermute | solution.py:218
  81.2 9.5 %collective-permute-start.9 = (f32[32,64]{1,0:T(8,128)S(1)}, f32[32,64]{1,0:T(8,128)S(1)}, u32[]{:S(2)}, u32[]{:S(2)}) collective-permute-start(f32[32,64]{1,0:T(8,128)S(1)} %sum.1), channel_id=1, source_target_pairs={{0,0},{1,1},{2,64},{3,65},{4,128},{5,129},{6,192},{7,193},{8,8},{9... | collective-permute-start | bytes 24584 | tf_op jit(solution)/shard_map/ppermute | solution.py:243

commit v8 on v7

--- a/solution.py
+++ b/solution.py
@@ -117,8 +117,8 @@
         low_turned = pltpu.roll(low, WIDTH, 1)
         high_turned = pltpu.roll(high, WIDTH, 1)
         at = 16 * half + 2 * core + h
-        out_ref[at + 4 * x] = jnp.where(low_lanes, low, high_turned)
-        out_ref[at + 4 * (x ^ NEAR)] = jnp.where(low_lanes, low_turned, high)
+        out_ref[at + 4 * x] = jnp.where(low_lanes, low, high_turned).astype(out_ref.dtype)
+        out_ref[at + 4 * (x ^ NEAR)] = jnp.where(low_lanes, low_turned, high).astype(out_ref.dtype)
 
 
 def own_tile_kernel(place_ref, pair_ref, products_ref, out_ref, pair_out_ref, products_out_ref):
@@ -200,7 +200,7 @@
     over_core = lax.ppermute(products, "core", swap)
     other_pair = lax.ppermute(pair, "x", [(i, i ^ FAR) for i in range(4)])
     place = jnp.stack([lax.axis_index(name) for name in ("z_hi", "x", "core")]).astype(jnp.int32)
-    chunks_shape = shape((parts, 16, 128), jnp.float32)
+    chunks_shape = shape((parts, 16, 128), jnp.bfloat16)
     begun, pair, products = pl.pallas_call(
         own_tile_kernel,
         out_shape=[

time: 91.9 us -> 90.3 us (0.983)
  blocking collectives: 20.1 us -> 18.5 us
    all_to_all x1, blocking collectives: 20.1 us -> 18.5 us  [local(): shares = lax.all_to_all(chunks, mesh_axes, 0, 0, tiled=True)]
    ppermute x1, waiting for transfers between devices: 5.35 us -> 6.27 us  [local(): return lax.ppermute(block, whole, route).T]
    ppermute x1, starting transfers between devices: 4.17 us -> 3.25 us  [local(): return lax.ppermute(block, whole, route).T]
where the time goes in v8:
time: 90.3 us; the launch traced here: 89.8 us
  starting transfers between devices  42.8 us (47%)
  blocking collectives  18.5 us (20%)
  waiting for transfers between devices  13.7 us (15%)
  Pallas kernels  11.4 us (13%)
  local copies, waits for them, and re-layouts  2.52 us (3%)
    ppermute x4, starting transfers between devices, local(): arriving.append(lax.ppermute(block, mesh_axes, route))  21.6 us
    all_to_all x1, blocking collectives, local(): shares = lax.all_to_all(chunks, mesh_axes, 0, 0, tiled=True)  18.5 us
    ppermute x1, starting transfers between devices, local(): over_z = lax.ppermute(products, 'z_hi', swap)  8.22 us
    pallas_call x1, Pallas kernels, local(): pl.pallas_call(block_kernel, out_shape=[shape((WIDTH, PACKED), jnp.bfloat...  6.88 us
    ppermute x1, waiting for transfers between devices, local(): return lax.ppermute(block, whole, route).T  6.27 us
    ppermute x1, waiting for transfers between devices, local(): other_pair = lax.ppermute(pair, 'x', [(i, i ^ FAR) for i in range(4)])  3.77 us
    ppermute x4, waiting for transfers between devices, local(): arriving.append(lax.ppermute(block, mesh_axes, route))  3.28 us
    ppermute x1, starting transfers between devices, local(): return lax.ppermute(block, whole, route).T  3.25 us
  transfers between devices with their start and end apart: 10, of which 5 were waited for; matrix products, arithmetic and copies ran while one was open for 0% of the time, Pallas kernels for 1%

profile of v8, /device:TPU:6, one launch (start us, length us, event | category | flops | bytes accessed | tf_op | source)
XLA Modules:
  0.0 89.8 jit_solution(2086449716549588187)
XLA Ops:
  0.0 1.9 %select.1 = (bf16[64,1536]{1,0:T(8,128)(2,1)}, bf16[64,768]{1,0:T(8,128)(2,1)}, bf16[64,768]{1,0:T(8,128)(2,1)}, bf16[64,768]{1,0:T(8,128)(2,1)}, bf16[64,768]{1,0:T(8,128)(2,1)}) custom-call(s32[16]{0:T(128)} %send_ref.1, bf16[8,64,192]{2,1,0:T(8,128)(2,1)} %basis_hbm.1), custom_call_target="tpu_custom_call" | custom-call | tf_op jit(solution)/shard_map/select/pallas_call | solution.py:152
  1.9 2.7 %collective-permute-start = (bf16[64,1536]{1,0:T(8,128)(2,1)}, bf16[64,1536]{1,0:T(8,128)(2,1)}, u32[]{:S(2)}, u32[]{:S(2)}) collective-permute-start(bf16[64,1536]{1,0:T(8,128)(2,1)} %get-tuple-element.17.own_hbm), channel_id=1, source_target_pairs={{0,2},{2,0},{4,6},{6,4},{1,3},{3,1},{5,7},{7,5},{8,10},{10,8},{12,... | collective-permute-start | bytes 589832 | tf_op jit(solution)/shard_map/ppermute | solution.py:165
  4.6 4.3 %collective-permute-start.1 = (bf16[64,768]{1,0:T(8,128)(2,1)}, bf16[64,768]{1,0:T(8,128)(2,1)}, u32[]{:S(2)}, u32[]{:S(2)}) collective-permute-start(bf16[64,768]{1,0:T(8,128)(2,1)} %get-tuple-element.18), channel_id=1, source_target_pairs={{496,0},{0,16},{16,32},{32,48},{48,64},{64,80},{80,96},{96,112},{1... | collective-permute-start | bytes 294920 | tf_op jit(solution)/shard_map/ppermute | solution.py:163
  8.9 8.4 %collective-permute-start.2 = (bf16[64,768]{1,0:T(8,128)(2,1)}, bf16[64,768]{1,0:T(8,128)(2,1)}, u32[]{:S(2)}, u32[]{:S(2)}) collective-permute-start(bf16[64,768]{1,0:T(8,128)(2,1)} %get-tuple-element.19), channel_id=1, source_target_pairs={{16,0},{32,16},{48,32},{64,48},{80,64},{96,80},{112,96},{128,112},... | collective-permute-start | bytes 294920 | tf_op jit(solution)/shard_map/ppermute | solution.py:163
  17.3 1.9 %collective-permute-start.3 = (bf16[64,768]{1,0:T(8,128)(2,1)}, bf16[64,768]{1,0:T(8,128)(2,1)}, u32[]{:S(2)}, u32[]{:S(2)}) collective-permute-start(bf16[64,768]{1,0:T(8,128)(2,1)} %get-tuple-element.20), channel_id=1, source_target_pairs={{480,0},{496,16},{0,32},{16,48},{32,64},{48,80},{64,96},{80,112},{... | collective-permute-start | bytes 294920 | tf_op jit(solution)/shard_map/ppermute | solution.py:163
  19.3 6.9 %collective-permute-start.4 = (bf16[64,768]{1,0:T(8,128)(2,1)}, bf16[64,768]{1,0:T(8,128)(2,1)}, u32[]{:S(2)}, u32[]{:S(2)}) collective-permute-start(bf16[64,768]{1,0:T(8,128)(2,1)} %get-tuple-element.21), channel_id=1, source_target_pairs={{32,0},{48,16},{64,32},{80,48},{96,64},{112,80},{128,96},{144,112}... | collective-permute-start | bytes 294920 | tf_op jit(solution)/shard_map/ppermute | solution.py:163
  26.9 1.3 %collective-permute-done.3.rest_2_ = bf16[64,768]{1,0:T(8,128)(2,1)} collective-permute-done((bf16[64,768]{1,0:T(8,128)(2,1)}, bf16[64,768]{1,0:T(8,128)(2,1)}, u32[]{:S(2)}, u32[]{:S(2)}) %collective-permute-start.3) | collective-permute-done | bytes 98336 | tf_op jit(solution)/shard_map/ppermute | solution.py:163
  28.2 2.0 %collective-permute-done.4.rest_3_ = bf16[64,768]{1,0:T(8,128)(2,1)} collective-permute-done((bf16[64,768]{1,0:T(8,128)(2,1)}, bf16[64,768]{1,0:T(8,128)(2,1)}, u32[]{:S(2)}, u32[]{:S(2)}) %collective-permute-start.4) | collective-permute-done | bytes 98336 | tf_op jit(solution)/shard_map/ppermute | solution.py:163
  30.2 6.9 %blocks.1 = (bf16[64,1536]{1,0:T(8,128)(2,1)}, bf16[128,1536]{1,0:T(8,128)(2,1)}) custom-call(s32[56]{0:T(128)} %rows_hbm.1, s32[56]{0:T(128)} %columns_hbm.1, f32[56]{0:T(128)} %density_hbm.1, s32[1]{0:T(128)S(6)} %copy.11.count_hbm, bf16[8,64,192]{2,1,0:T(8,128)(2,1)} %basis_hbm.1, bf16[56,192,192]{2,1,0:T(8,128)(2,1)} %blocks_hbm.1, ...), custom_call_target="tpu_custom_call" | custom-call | tf_op jit(solution)/shard_map/blocks/pallas_call | solution.py:166
  37.1 8.2 %collective-permute-start.7 = (bf16[64,1536]{1,0:T(8,128)(2,1)}, bf16[64,1536]{1,0:T(8,128)(2,1)S(1)}, u32[]{:S(2)}, u32[]{:S(2)}) collective-permute-start(bf16[64,1536]{1,0:T(8,128)(2,1)} %get-tuple-element.23.products_ref), channel_id=1, source_target_pairs={{0,8},{8,0},{1,9},{9,1},{2,10},{10,2},{3,11},{11,3},{4,12},{12,4},... | collective-permute-start | bytes 589832 | tf_op jit(solution)/shard_map/ppermute | solution.py:199
  45.3 3.0 %collective-permute-start.5 = (bf16[128,1536]{1,0:T(8,128)(2,1)}, bf16[128,1536]{1,0:T(8,128)(2,1)S(1)}, u32[]{:S(2)}, u32[]{:S(2)}) collective-permute-start(bf16[128,1536]{1,0:T(8,128)(2,1)} %get-tuple-element.22.pair_ref), channel_id=1, source_target_pairs={{0,6},{2,4},{4,2},{6,0},{1,7},{3,5},{5,3},{7,1},{8,14},{10,12},{12... | collective-permute-start | bytes 1179656 | tf_op jit(solution)/shard_map/ppermute | solution.py:201
  48.4 1.9 %collective-permute-start.6 = (bf16[64,1536]{1,0:T(8,128)(2,1)}, bf16[64,1536]{1,0:T(8,128)(2,1)S(1)}, u32[]{:S(2)}, u32[]{:S(2)}) collective-permute-start(bf16[64,1536]{1,0:T(8,128)(2,1)} %get-tuple-element.23.products_ref), channel_id=1, source_target_pairs={{0,1},{1,0},{2,3},{3,2},{4,5},{5,4},{6,7},{7,6},{8,9},{9,8},{10,11... | collective-permute-start | bytes 589832 | tf_op jit(solution)/shard_map/ppermute | solution.py:200
  50.4 1.0 %copy-done = bf16[128,1536]{1,0:T(8,128)(2,1)S(1)} copy-done((bf16[128,1536]{1,0:T(8,128)(2,1)S(1)}, bf16[128,1536]{1,0:T(8,128)(2,1)}, u32[]{:S(2)}) %copy-start) | copy-done | bytes 393240
  51.3 0.9 %copy-done.1 = bf16[64,1536]{1,0:T(8,128)(2,1)S(1)} copy-done((bf16[64,1536]{1,0:T(8,128)(2,1)S(1)}, bf16[64,1536]{1,0:T(8,128)(2,1)}, u32[]{:S(2)}) %copy-start.1) | copy-done | bytes 196632
  52.3 0.9 own_tile.1
  53.1 0.4 collective-permute-done.7.rest_2_
  53.5 2.0 %collective-permute-start.8 = (bf16[64,1536]{1,0:T(8,128)(2,1)S(1)}, bf16[64,1536]{1,0:T(8,128)(2,1)S(1)}, u32[]{:S(2)}, u32[]{:S(2)}) collective-permute-start(bf16[64,1536]{1,0:T(8,128)(2,1)S(1)} %collective-permute-done.7.rest_2_), channel_id=1, source_target_pairs={{0,1},{1,0},{2,3},{3,2},{4,5},{5,4},{6,7},{7,6},{8,9},{9,8},{10,11... | collective-permute-start | bytes 589832 | tf_op jit(solution)/shard_map/ppermute | solution.py:218
  55.6 3.8 %collective-permute-done.5.other_pair_ref = bf16[128,1536]{1,0:T(8,128)(2,1)S(1)} collective-permute-done((bf16[128,1536]{1,0:T(8,128)(2,1)}, bf16[128,1536]{1,0:T(8,128)(2,1)S(1)}, u32[]{:S(2)}, u32[]{:S(2)}) %collective-permute-start.5) | collective-permute-done | bytes 393248 | tf_op jit(solution)/shard_map/ppermute | solution.py:201
  59.4 1.7 %tile.1 = bf16[32,16,128]{2,1,0:T(8,128)(2,1)S(1)} custom-call(s32[3]{0:T(128)S(1)} %pad_add_fusion.place_ref, bf16[128,1536]{1,0:T(8,128)(2,1)S(1)} %get-tuple-element.24.pair_ref, bf16[128,1536]{1,0:T(8,128)(2,1)S(1)} %collective-permute-done.5.other_pair_ref, bf16[64,1536]{1,0:T(8,128)(2,1)S(1)} %get-tuple-element.25.rest_0_, ...), custom_call_target="tpu_custom_call", output_to_operand_aliasing={{}: (7, {})} | custom-call | tf_op jit(solution)/shard_map/tile/pallas_call | solution.py:219
  61.0 18.5 %all_to_all.5.parts_ref = bf16[32,16,128]{2,1,0:T(8,128)(2,1)S(1)} all-to-all(bf16[32,16,128]{2,1,0:T(8,128)(2,1)S(1)} %tile.1), channel_id=1, replica_groups=mesh['y'=8,'z_lo'=4,'z_hi'=2,'x'=4,'core'=2] {'y','z_lo'}, dimensions={0} | all-to-all | bytes 262144 | tf_op jit(solution)/shard_map/all_to_all | solution.py:228
  79.5 0.1 sum.1
  79.6 3.3 %collective-permute-start.9 = (f32[32,64]{1,0:T(8,128)S(1)}, f32[32,64]{1,0:T(8,128)S(1)}, u32[]{:S(2)}, u32[]{:S(2)}) collective-permute-start(f32[32,64]{1,0:T(8,128)S(1)} %sum.1), channel_id=1, source_target_pairs={{0,0},{1,1},{2,64},{3,65},{4,128},{5,129},{6,192},{7,193},{8,8},{9... | collective-permute-start | bytes 24584 | tf_op jit(solution)/shard_map/ppermute | solution.py:243
  82.9 6.3 %collective-permute-done.9 = f32[32,64]{1,0:T(8,128)S(1)} collective-permute-done((f32[32,64]{1,0:T(8,128)S(1)}, f32[32,64]{1,0:T(8,128)S(1)}, u32[]{:S(2)}, u32[]{:S(2)}) %collective-permute-start.9) | collective-permute-done | bytes 8224 | tf_op jit(solution)/shard_map/ppermute | solution.py:243
  89.2 0.6 copy.12
  (8 shorter events, 0.1 us)
Async XLA Ops:
  1.9 28.3 %collective-permute-start = (bf16[64,1536]{1,0:T(8,128)(2,1)}, bf16[64,1536]{1,0:T(8,128)(2,1)}, u32[]{:S(2)}, u32[]{:S(2)}) collective-permute-start(bf16[64,1536]{1,0:T(8,128)(2,1)} %get-tuple-element.17.own_hbm), channel_id=1, source_target_pairs={{0,2},{2,0},{4,6},{6,4},{1,3},{3,1},{5,7},{7,5},{8,10},{10,8},{12,... | collective-permute-start | bytes 589832 | tf_op jit(solution)/shard_map/ppermute | solution.py:165
  4.6 22.3 %collective-permute-start.1 = (bf16[64,768]{1,0:T(8,128)(2,1)}, bf16[64,768]{1,0:T(8,128)(2,1)}, u32[]{:S(2)}, u32[]{:S(2)}) collective-permute-start(bf16[64,768]{1,0:T(8,128)(2,1)} %get-tuple-element.18), channel_id=1, source_target_pairs={{496,0},{0,16},{16,32},{32,48},{48,64},{64,80},{80,96},{96,112},{1... | collective-permute-start | bytes 294920 | tf_op jit(solution)/shard_map/ppermute | solution.py:163
  8.9 18.0 %collective-permute-start.2 = (bf16[64,768]{1,0:T(8,128)(2,1)}, bf16[64,768]{1,0:T(8,128)(2,1)}, u32[]{:S(2)}, u32[]{:S(2)}) collective-permute-start(bf16[64,768]{1,0:T(8,128)(2,1)} %get-tuple-element.19), channel_id=1, source_target_pairs={{16,0},{32,16},{48,32},{64,48},{80,64},{96,80},{112,96},{128,112},... | collective-permute-start | bytes 294920 | tf_op jit(solution)/shard_map/ppermute | solution.py:163
  17.3 10.8 %collective-permute-start.3 = (bf16[64,768]{1,0:T(8,128)(2,1)}, bf16[64,768]{1,0:T(8,128)(2,1)}, u32[]{:S(2)}, u32[]{:S(2)}) collective-permute-start(bf16[64,768]{1,0:T(8,128)(2,1)} %get-tuple-element.20), channel_id=1, source_target_pairs={{480,0},{496,16},{0,32},{16,48},{32,64},{48,80},{64,96},{80,112},{... | collective-permute-start | bytes 294920 | tf_op jit(solution)/shard_map/ppermute | solution.py:163
  19.3 10.9 %collective-permute-start.4 = (bf16[64,768]{1,0:T(8,128)(2,1)}, bf16[64,768]{1,0:T(8,128)(2,1)}, u32[]{:S(2)}, u32[]{:S(2)}) collective-permute-start(bf16[64,768]{1,0:T(8,128)(2,1)} %get-tuple-element.21), channel_id=1, source_target_pairs={{32,0},{48,16},{64,32},{80,48},{96,64},{112,80},{128,96},{144,112}... | collective-permute-start | bytes 294920 | tf_op jit(solution)/shard_map/ppermute | solution.py:163
  37.1 16.5 %collective-permute-start.7 = (bf16[64,1536]{1,0:T(8,128)(2,1)}, bf16[64,1536]{1,0:T(8,128)(2,1)S(1)}, u32[]{:S(2)}, u32[]{:S(2)}) collective-permute-start(bf16[64,1536]{1,0:T(8,128)(2,1)} %get-tuple-element.23.products_ref), channel_id=1, source_target_pairs={{0,8},{8,0},{1,9},{9,1},{2,10},{10,2},{3,11},{11,3},{4,12},{12,4},... | collective-permute-start | bytes 589832 | tf_op jit(solution)/shard_map/ppermute | solution.py:199
  45.3 14.1 %collective-permute-start.5 = (bf16[128,1536]{1,0:T(8,128)(2,1)}, bf16[128,1536]{1,0:T(8,128)(2,1)S(1)}, u32[]{:S(2)}, u32[]{:S(2)}) collective-permute-start(bf16[128,1536]{1,0:T(8,128)(2,1)} %get-tuple-element.22.pair_ref), channel_id=1, source_target_pairs={{0,6},{2,4},{4,2},{6,0},{1,7},{3,5},{5,3},{7,1},{8,14},{10,12},{12... | collective-permute-start | bytes 1179656 | tf_op jit(solution)/shard_map/ppermute | solution.py:201
  48.4 7.2 %collective-permute-start.6 = (bf16[64,1536]{1,0:T(8,128)(2,1)}, bf16[64,1536]{1,0:T(8,128)(2,1)S(1)}, u32[]{:S(2)}, u32[]{:S(2)}) collective-permute-start(bf16[64,1536]{1,0:T(8,128)(2,1)} %get-tuple-element.23.products_ref), channel_id=1, source_target_pairs={{0,1},{1,0},{2,3},{3,2},{4,5},{5,4},{6,7},{7,6},{8,9},{9,8},{10,11... | collective-permute-start | bytes 589832 | tf_op jit(solution)/shard_map/ppermute | solution.py:200
  50.3 1.0 %copy-start = (bf16[128,1536]{1,0:T(8,128)(2,1)S(1)}, bf16[128,1536]{1,0:T(8,128)(2,1)}, u32[]{:S(2)}) copy-start(bf16[128,1536]{1,0:T(8,128)(2,1)} %get-tuple-element.22.pair_ref) | copy-start | bytes 1179652
  51.3 0.9 %copy-start.1 = (bf16[64,1536]{1,0:T(8,128)(2,1)S(1)}, bf16[64,1536]{1,0:T(8,128)(2,1)}, u32[]{:S(2)}) copy-start(bf16[64,1536]{1,0:T(8,128)(2,1)} %get-tuple-element.23.products_ref) | copy-start | bytes 589828
  53.5 5.8 %collective-permute-start.8 = (bf16[64,1536]{1,0:T(8,128)(2,1)S(1)}, bf16[64,1536]{1,0:T(8,128)(2,1)S(1)}, u32[]{:S(2)}, u32[]{:S(2)}) collective-permute-start(bf16[64,1536]{1,0:T(8,128)(2,1)S(1)} %collective-permute-done.7.rest_2_), channel_id=1, source_target_pairs={{0,1},{1,0},{2,3},{3,2},{4,5},{5,4},{6,7},{7,6},{8,9},{9,8},{10,11... | collective-permute-start | bytes 589832 | tf_op jit(solution)/shard_map/ppermute | solution.py:218
  79.6 9.5 %collective-permute-start.9 = (f32[32,64]{1,0:T(8,128)S(1)}, f32[32,64]{1,0:T(8,128)S(1)}, u32[]{:S(2)}, u32[]{:S(2)}) collective-permute-start(f32[32,64]{1,0:T(8,128)S(1)} %sum.1), channel_id=1, source_target_pairs={{0,0},{1,1},{2,64},{3,65},{4,128},{5,129},{6,192},{7,193},{8,8},{9... | collective-permute-start | bytes 24584 | tf_op jit(solution)/shard_map/ppermute | solution.py:243

commit v9 on v8

--- a/solution.py
+++ b/solution.py
@@ -1,6 +1,5 @@
 import jax
 import jax.numpy as jnp
-import numpy as np
 from jax import lax
 from jax.experimental import pallas as pl
 from jax.experimental.pallas import tpu as pltpu
@@ -17,7 +16,7 @@
 PACKED = OWN * DOFS
 
 neighbour_offsets = (1, -1, 2, -2)
-NEAR, FAR = 1, 3
+NEAR, FAR = 1, 2
 VMEM = pl.BlockSpec(memory_space=pltpu.VMEM)
 SMEM = pl.BlockSpec(memory_space=pltpu.SMEM)
 HBM = pl.BlockSpec(memory_space=pltpu.HBM)
@@ -43,11 +42,11 @@
 
 
 def block_kernel(
-    rows_hbm, columns_hbm, density_hbm, count_hbm, basis_hbm, blocks_hbm, own_hbm, other_hbm, *rest
+    rows_hbm, columns_hbm, density_hbm, count_hbm, basis_hbm, blocks_hbm, *rest
 ):
     ghost_refs = rest[:NEIGH]
-    out_ref, pair_ref, rows_ref, columns_ref, density_ref, count_ref, *rest = rest[NEIGH:]
-    blocks, pool, total, arrived, lists, joined = rest
+    out_ref, rows_ref, columns_ref, density_ref, count_ref, *rest = rest[NEIGH:]
+    blocks, pool, total, arrived, lists = rest
     small = [
         pltpu.make_async_copy(source, target, lists.at[index])
         for index, (source, target) in enumerate((
@@ -67,12 +66,6 @@
             pltpu.make_async_copy(blocks_hbm.at[part], blocks.at[part], arrived.at[chunk])
         )
         copies[-1].start()
-    joins = [
-        pltpu.make_async_copy(source, pair_ref.at[pl.ds(index * WIDTH, WIDTH)], joined.at[index])
-        for index, source in enumerate((own_hbm, other_hbm))
-    ]
-    for copy in joins:
-        copy.start()
     for neighbour, ghost_ref in enumerate(ghost_refs):
         for pair in range(GMAX // 2):
             at, slot = 384 * pair, OWN + neighbour * GMAX + 2 * pair
@@ -99,8 +92,6 @@
             total[row] = total[row] + scale * product
     for pair in range(OWN // 2):
         pack_pair(total[2 * pair], total[2 * pair + 1], out_ref, 384 * pair)
-    for copy in joins:
-        copy.wait()
 
 
 def put_tile(place_ref, products_ref, rows_ref, out_ref, z_step, core_step, row_step):
@@ -121,20 +112,16 @@
         out_ref[at + 4 * (x ^ NEAR)] = jnp.where(low_lanes, low_turned, high).astype(out_ref.dtype)
 
 
-def own_tile_kernel(place_ref, pair_ref, products_ref, out_ref, pair_out_ref, products_out_ref):
-    pair_out_ref[...] = pair_ref[...]
-    products_out_ref[...] = products_ref[...]
-    put_tile(place_ref, products_ref, pair_ref, out_ref, 0, 0, 0)
+def join_kernel(own_ref, other_ref, pair_ref):
+    pair_ref[:WIDTH] = own_ref[...]
+    pair_ref[WIDTH:] = other_ref[...]
 
 
 def tile_kernel(place_ref, pair_ref, other_pair_ref, *rest):
-    *product_refs, begun_ref, out_ref = rest
+    *product_refs, out_ref = rest
     for (z_step, core_step), products_ref in zip(((0, 0), (0, 1), (1, 0), (1, 1)), product_refs):
         for row_step, rows_ref in ((0, pair_ref), (FAR, other_pair_ref)):
-            if z_step or core_step or row_step:
-                put_tile(
-                    place_ref, products_ref, rows_ref, out_ref, z_step, core_step, row_step
-                )
+            put_tile(place_ref, products_ref, rows_ref, out_ref, z_step, core_step, row_step)
 
 
 def sum_kernel(parts_ref, out_ref):
@@ -146,7 +133,7 @@
 def local(
     basis_vectors, stiffness_blocks, block_rows, block_columns, density, block_counts, send_list
 ):
-    mesh_axes, whole = ("y", "z_lo"), ("y", "z_lo", "z_hi", "x", "core")
+    mesh_axes = ("y_high", "y_low", "z_low")
     parts = lax.axis_size(mesh_axes)
     shape = jax.ShapeDtypeStruct
     packed, *picked = pl.pallas_call(
@@ -163,14 +150,19 @@
         arriving.append(lax.ppermute(block, mesh_axes, route))
     swap = [(0, 1), (1, 0)]
     other_packed = lax.ppermute(packed, "x", [(i, i ^ NEAR) for i in range(4)])
-    products, pair = pl.pallas_call(
+    pair = pl.pallas_call(
+        join_kernel,
+        out_shape=shape((2 * WIDTH, PACKED), jnp.bfloat16),
+        in_specs=[VMEM] * 2,
+        out_specs=VMEM,
+        name="join",
+    )(packed, other_packed)
+    block_rows, pair = lax.optimization_barrier((block_rows, pair))
+    products = pl.pallas_call(
         block_kernel,
-        out_shape=[
-            shape((WIDTH, PACKED), jnp.bfloat16),
-            shape((2 * WIDTH, PACKED), jnp.bfloat16),
-        ],
-        in_specs=[HBM] * 8 + [VMEM] * NEIGH,
-        out_specs=[VMEM] * 2,
+        out_shape=shape((WIDTH, PACKED), jnp.bfloat16),
+        in_specs=[HBM] * 6 + [VMEM] * NEIGH,
+        out_specs=VMEM,
         scratch_shapes=[
             pltpu.SMEM((CAP,), jnp.int32),
             pltpu.SMEM((CAP,), jnp.int32),
@@ -181,7 +173,6 @@
             pltpu.VMEM((OWN, WIDTH, DOFS), jnp.float32),
             pltpu.SemaphoreType.DMA((CAP // CHUNK,)),
             pltpu.SemaphoreType.DMA((5,)),
-            pltpu.SemaphoreType.DMA((2,)),
         ],
         compiler_params=pltpu.CompilerParams(vmem_limit_bytes=64 << 20),
         name="blocks",
@@ -192,40 +183,34 @@
         block_counts,
         basis_vectors,
         stiffness_blocks,
-        packed,
-        other_packed,
         *arriving,
     )
-    over_z = lax.ppermute(products, "z_hi", swap)
-    over_core = lax.ppermute(products, "core", swap)
-    other_pair = lax.ppermute(pair, "x", [(i, i ^ FAR) for i in range(4)])
-    place = jnp.stack([lax.axis_index(name) for name in ("z_hi", "x", "core")]).astype(jnp.int32)
-    chunks_shape = shape((parts, 16, 128), jnp.bfloat16)
-    begun, pair, products = pl.pallas_call(
-        own_tile_kernel,
-        out_shape=[
-            chunks_shape,
-            shape(pair.shape, pair.dtype),
-            shape(products.shape, products.dtype),
-        ],
-        in_specs=[SMEM] + [VMEM] * 2,
-        out_specs=[VMEM] * 3,
-        compiler_params=pltpu.CompilerParams(vmem_limit_bytes=16 << 20),
-        cost_estimate=pl.CostEstimate(flops=2 << 23, bytes_accessed=1 << 20, transcendentals=0),
-        name="own_tile",
-    )(place, pair, products)
-    behind, begun = lax.optimization_barrier((over_z, begun))
-    over_both = lax.ppermute(behind, "core", swap)
+    across = ("y_low", "z_high", "x")
+    swap_low = [(4 * b + a, 4 * a + b) for a in range(4) for b in range(4)]
+    both = [(8 * b + 4 * z + a, 8 * a + 4 * (1 - z) + b) for a in range(4) for b in range(4) for z in range(2)]
+    over_z = lax.ppermute(products, across, both)
+    over_x = lax.ppermute(products, ("y_low", "x"), swap_low)
+    over_x_core = lax.ppermute(over_x, "core", swap)
+    over_z_core = lax.ppermute(over_z, "core", swap)
+    pair, _ = lax.optimization_barrier((pair, products))
+    pairs = [
+        lax.ppermute(
+            pair,
+            ("y_low", "x"),
+            [(4 * b + a, 4 * (a ^ step) + b) for a in range(4) for b in range(4)],
+        )
+        for step in (0, FAR)
+    ]
+    place = jnp.stack([lax.axis_index(name) for name in ("z_high", "y_low", "core")])
     chunks = pl.pallas_call(
         tile_kernel,
-        out_shape=chunks_shape,
-        in_specs=[SMEM] + [VMEM] * 7,
-        out_specs=VMEM,
-        input_output_aliases={7: 0},
+        out_shape=shape((parts, 16, 128), jnp.bfloat16),
+        in_specs=[SMEM] + [VMEM] * 6,
+        out_specs=VMEM,
         compiler_params=pltpu.CompilerParams(vmem_limit_bytes=16 << 20),
         name="tile",
-    )(place, pair, other_pair, products, over_core, over_z, over_both, begun)
-    shares = lax.all_to_all(chunks, mesh_axes, 0, 0, tiled=True)
+    )(place.astype(jnp.int32), *pairs, over_x, over_x_core, over_z, over_z_core)
+    shares = lax.all_to_all(chunks, ("y_high", "x", "z_low"), 0, 0, tiled=True)
     block = pl.pallas_call(
         sum_kernel,
         out_shape=shape((32, WIDTH), jnp.float32),
@@ -234,18 +219,13 @@
         compiler_params=pltpu.CompilerParams(vmem_limit_bytes=8 << 20),
         name="sum",
     )(shares)
-    route = []
-    for place in range(512):
-        z2, a, c2, h, z, b, c = (int(i) for i in np.unravel_index(place, (2, 4, 2, 2, 2, 4, 2)))
-        source = (z2 * 16 + a * 4 + c2 * 2 + h) * 16 + z * 8 + b * 2 + c
-        target = (z2 * 16 + b * 4 + c2 * 2 + h) * 16 + z * 8 + a * 2 + c
-        route.append((source, target))
-    return lax.ppermute(block, whole, route).T
+    return block.T
 
 
 def solution(mesh):
-    fine = Mesh(mesh.devices.reshape(8, 4, 2, 4, 2), ("y", "z_lo", "z_hi", "x", "core"))
-    over_mesh, over_panel = ("y", "z_lo"), ("z_hi", "x", "core")
+    names = ("y_high", "y_low", "z_low", "z_high", "x", "core")
+    fine = Mesh(mesh.devices.reshape(2, 4, 4, 2, 4, 2), names)
+    over_mesh, over_panel = names[:3], names[3:]
     placed = (
         P(over_mesh, over_panel, None),
         P(over_mesh, None, None),

time: 90.3 us -> 133 us (1.47); the launches traced: 89.8 us -> 131 us
  waiting for transfers between devices: 13.7 us -> 31.2 us
  blocking collectives: 18.5 us -> 35 us
  starting transfers between devices: 42.8 us -> 50.4 us
  local copies, waits for them, and re-layouts: 2.52 us -> 0.66 us
  Pallas kernels: 11.4 us -> 12.9 us
    ppermute x5 -> x6, waiting for transfers between devices: 10.4 us -> 30.4 us  [the longest x1 17.1 us: local(): over_x = lax.ppermute(products, ('y_low', 'x'), swap_low)]
    all_to_all x1, blocking collectives: 18.5 us -> 35 us  [local(): shares = lax.all_to_all(chunks, ('y_high', 'x', 'z_low'), 0, 0, tiled=True)]
    ppermute x5 -> x6, starting transfers between devices: 18.5 us -> 26.1 us  [the longest x1 10.6 us: local(): over_z = lax.ppermute(products, across, both)]
    ppermute x4, waiting for transfers between devices: 3.28 us -> 0.83 us  [local(): arriving.append(lax.ppermute(block, mesh_axes, route))]
    unnamed x5 -> x2, local copies, waits for them, and re-layouts: 2.52 us -> 0.66 us
  transfers between devices with their start and end apart: 10 -> 11, of which waited for: 5 -> 4; matrix products, arithmetic and copies ran while one was open for 0% -> 0% of each run, Pallas kernels for 1% -> 1%
where the time goes in v9:
time: 133 us; the launch traced here: 131 us
  starting transfers between devices  50.4 us (38%)
  blocking collectives  35 us (26%)
  waiting for transfers between devices  31.2 us (23%)
  Pallas kernels  12.9 us (10%)
    all_to_all x1, blocking collectives, local(): shares = lax.all_to_all(chunks, ('y_high', 'x', 'z_low'), 0, 0, tiled=True)  35 us
    ppermute x4, starting transfers between devices, local(): arriving.append(lax.ppermute(block, mesh_axes, route))  21.6 us
    ppermute x1, waiting for transfers between devices, local(): over_x = lax.ppermute(products, ('y_low', 'x'), swap_low)  17.1 us
    ppermute x1, starting transfers between devices, local(): over_z = lax.ppermute(products, across, both)  10.6 us
    ppermute x2, waiting for transfers between devices, local(): lax.ppermute(pair, ('y_low', 'x'), [(4 * b + a, 4 * (a ^ step) + b) for a...  10.1 us
    ppermute x2, starting transfers between devices, local(): lax.ppermute(pair, ('y_low', 'x'), [(4 * b + a, 4 * (a ^ step) + b) for a...  6.79 us
    pallas_call x1, Pallas kernels, local(): pl.pallas_call(block_kernel, out_shape=shape((WIDTH, PACKED), jnp.bfloat1...  6.7 us
    ppermute x1, starting transfers between devices, local(): over_x = lax.ppermute(products, ('y_low', 'x'), swap_low)  4.87 us
  transfers between devices with their start and end apart: 11, of which 4 were waited for; matrix products, arithmetic and copies ran while one was open for 0% of the time, Pallas kernels for 1%

profile of v9, /device:TPU:6, one launch (start us, length us, event | category | flops | bytes accessed | tf_op | source)
XLA Modules:
  0.0 131.0 jit_solution(8242726646572571073)
XLA Ops:
  0.0 1.9 %select.1 = (bf16[64,1536]{1,0:T(8,128)(2,1)}, bf16[64,768]{1,0:T(8,128)(2,1)}, bf16[64,768]{1,0:T(8,128)(2,1)}, bf16[64,768]{1,0:T(8,128)(2,1)}, bf16[64,768]{1,0:T(8,128)(2,1)}) custom-call(s32[16]{0:T(128)} %send_ref.1, bf16[8,64,192]{2,1,0:T(8,128)(2,1)} %basis_hbm.1), custom_call_target="tpu_custom_call" | custom-call | tf_op jit(solution)/shard_map/select/pallas_call | solution.py:139
  1.9 2.7 %collective-permute-start = (bf16[64,1536]{1,0:T(8,128)(2,1)}, bf16[64,1536]{1,0:T(8,128)(2,1)S(1)}, u32[]{:S(2)}, u32[]{:S(2)}) collective-permute-start(bf16[64,1536]{1,0:T(8,128)(2,1)} %get-tuple-element.13.own_ref), channel_id=1, source_target_pairs={{0,2},{2,0},{4,6},{6,4},{1,3},{3,1},{5,7},{7,5},{8,10},{10,8},{12,... | collective-permute-start | bytes 589832 | tf_op jit(solution)/shard_map/ppermute | solution.py:152
  4.6 4.3 %collective-permute-start.1 = (bf16[64,768]{1,0:T(8,128)(2,1)}, bf16[64,768]{1,0:T(8,128)(2,1)}, u32[]{:S(2)}, u32[]{:S(2)}) collective-permute-start(bf16[64,768]{1,0:T(8,128)(2,1)} %get-tuple-element.16), channel_id=1, source_target_pairs={{496,0},{0,16},{16,32},{32,48},{48,64},{64,80},{80,96},{96,112},{1... | collective-permute-start | bytes 294920 | tf_op jit(solution)/shard_map/ppermute | solution.py:150
  8.9 8.4 %collective-permute-start.2 = (bf16[64,768]{1,0:T(8,128)(2,1)}, bf16[64,768]{1,0:T(8,128)(2,1)}, u32[]{:S(2)}, u32[]{:S(2)}) collective-permute-start(bf16[64,768]{1,0:T(8,128)(2,1)} %get-tuple-element.17), channel_id=1, source_target_pairs={{16,0},{32,16},{48,32},{64,48},{80,64},{96,80},{112,96},{128,112},... | collective-permute-start | bytes 294920 | tf_op jit(solution)/shard_map/ppermute | solution.py:150
  17.4 1.9 %collective-permute-start.3 = (bf16[64,768]{1,0:T(8,128)(2,1)}, bf16[64,768]{1,0:T(8,128)(2,1)}, u32[]{:S(2)}, u32[]{:S(2)}) collective-permute-start(bf16[64,768]{1,0:T(8,128)(2,1)} %get-tuple-element.18), channel_id=1, source_target_pairs={{480,0},{496,16},{0,32},{16,48},{32,64},{48,80},{64,96},{80,112},{... | collective-permute-start | bytes 294920 | tf_op jit(solution)/shard_map/ppermute | solution.py:150
  19.3 6.9 %collective-permute-start.4 = (bf16[64,768]{1,0:T(8,128)(2,1)}, bf16[64,768]{1,0:T(8,128)(2,1)}, u32[]{:S(2)}, u32[]{:S(2)}) collective-permute-start(bf16[64,768]{1,0:T(8,128)(2,1)} %get-tuple-element.19), channel_id=1, source_target_pairs={{32,0},{48,16},{64,32},{80,48},{96,64},{112,80},{128,96},{144,112}... | collective-permute-start | bytes 294920 | tf_op jit(solution)/shard_map/ppermute | solution.py:150
  26.9 0.7 copy-done
  27.6 1.8 %join.1 = bf16[128,1536]{1,0:T(8,128)(2,1)} custom-call(bf16[64,1536]{1,0:T(8,128)(2,1)} %get-tuple-element.13.own_ref, bf16[64,1536]{1,0:T(8,128)(2,1)} %copy-done), custom_call_target="tpu_custom_call" | custom-call | tf_op jit(solution)/shard_map/join/pallas_call | solution.py:153
  29.3 0.0 collective-permute-done.1.rest_0_
  29.4 0.8 collective-permute-done.4.rest_3_
  30.2 6.7 %blocks.1 = bf16[64,1536]{1,0:T(8,128)(2,1)} custom-call(s32[56]{0:T(128)} %rows_hbm, s32[56]{0:T(128)} %columns_hbm.1, f32[56]{0:T(128)} %density_hbm.1, s32[1]{0:T(128)S(6)} %copy.8.count_hbm, bf16[8,64,192]{2,1,0:T(8,128)(2,1)} %basis_hbm.1, bf16[56,192,192]{2,1,0:T(8,128)(2,1)} %blocks_hbm.1, bf16[64,768]{1,0:T(8,128)(2,1)} %collective-permute-done.1.rest_0_, ...), custom_call_target="tpu_custom_call" | custom-call | tf_op jit(solution)/shard_map/blocks/pallas_call | solution.py:161
  36.9 10.6 %collective-permute-start.9 = (bf16[64,1536]{1,0:T(8,128)(2,1)}, bf16[64,1536]{1,0:T(8,128)(2,1)S(1)}, u32[]{:S(2)}, u32[]{:S(2)}) collective-permute-start(bf16[64,1536]{1,0:T(8,128)(2,1)} %blocks.1), channel_id=1, source_target_pairs={{0,8},{8,0},{64,10},{72,2},{128,12},{136,4},{192,14},{200,6},{2,72... | collective-permute-start | bytes 589832 | tf_op jit(solution)/shard_map/ppermute | solution.py:191
  47.5 4.9 %collective-permute-start.5 = (bf16[128,1536]{1,0:T(8,128)(2,1)}, bf16[128,1536]{1,0:T(8,128)(2,1)S(1)}, u32[]{:S(2)}, u32[]{:S(2)}) collective-permute-start(bf16[128,1536]{1,0:T(8,128)(2,1)} %join.1), channel_id=1, source_target_pairs={{0,0},{64,2},{128,4},{192,6},{2,64},{66,66},{130,68},{194,70},{4,1... | collective-permute-start | bytes 1179656 | tf_op jit(solution)/shard_map/ppermute | solution.py:197
  52.4 1.9 %collective-permute-start.6 = (bf16[128,1536]{1,0:T(8,128)(2,1)}, bf16[128,1536]{1,0:T(8,128)(2,1)S(1)}, u32[]{:S(2)}, u32[]{:S(2)}) collective-permute-start(bf16[128,1536]{1,0:T(8,128)(2,1)} %join.1), channel_id=1, source_target_pairs={{0,128},{64,130},{128,132},{192,134},{2,192},{66,194},{130,196},{1... | collective-permute-start | bytes 1179656 | tf_op jit(solution)/shard_map/ppermute | solution.py:197
  54.3 4.9 %collective-permute-start.7 = (bf16[64,1536]{1,0:T(8,128)(2,1)}, bf16[64,1536]{1,0:T(8,128)(2,1)S(1)}, u32[]{:S(2)}, u32[]{:S(2)}) collective-permute-start(bf16[64,1536]{1,0:T(8,128)(2,1)} %blocks.1), channel_id=1, source_target_pairs={{0,0},{64,2},{128,4},{192,6},{2,64},{66,66},{130,68},{194,70},{4,1... | collective-permute-start | bytes 589832 | tf_op jit(solution)/shard_map/ppermute | solution.py:192
  59.2 3.1 %collective-permute-done.9.rest_2_ = bf16[64,1536]{1,0:T(8,128)(2,1)S(1)} collective-permute-done((bf16[64,1536]{1,0:T(8,128)(2,1)}, bf16[64,1536]{1,0:T(8,128)(2,1)S(1)}, u32[]{:S(2)}, u32[]{:S(2)}) %collective-permute-start.9) | collective-permute-done | bytes 196640 | tf_op jit(solution)/shard_map/ppermute | solution.py:191
  62.4 1.9 %collective-permute-start.10 = (bf16[64,1536]{1,0:T(8,128)(2,1)S(1)}, bf16[64,1536]{1,0:T(8,128)(2,1)S(1)}, u32[]{:S(2)}, u32[]{:S(2)}) collective-permute-start(bf16[64,1536]{1,0:T(8,128)(2,1)S(1)} %collective-permute-done.9.rest_2_), channel_id=1, source_target_pairs={{0,1},{1,0},{2,3},{3,2},{4,5},{5,4},{6,7},{7,6},{8,9},{9,8},{10,11... | collective-permute-start | bytes 589832 | tf_op jit(solution)/shard_map/ppermute | solution.py:194
  64.3 17.1 %collective-permute-done.7.rest_0_ = bf16[64,1536]{1,0:T(8,128)(2,1)S(1)} collective-permute-done((bf16[64,1536]{1,0:T(8,128)(2,1)}, bf16[64,1536]{1,0:T(8,128)(2,1)S(1)}, u32[]{:S(2)}, u32[]{:S(2)}) %collective-permute-start.7) | collective-permute-done | bytes 196640 | tf_op jit(solution)/shard_map/ppermute | solution.py:192
  81.3 1.9 %collective-permute-start.8 = (bf16[64,1536]{1,0:T(8,128)(2,1)S(1)}, bf16[64,1536]{1,0:T(8,128)(2,1)S(1)}, u32[]{:S(2)}, u32[]{:S(2)}) collective-permute-start(bf16[64,1536]{1,0:T(8,128)(2,1)S(1)} %collective-permute-done.7.rest_0_), channel_id=1, source_target_pairs={{0,1},{1,0},{2,3},{3,2},{4,5},{5,4},{6,7},{7,6},{8,9},{9,8},{10,11... | collective-permute-start | bytes 589832 | tf_op jit(solution)/shard_map/ppermute | solution.py:193
  83.3 0.1 pad_add_fusion.place_ref
  83.3 10.1 %collective-permute-done.6.other_pair_ref = bf16[128,1536]{1,0:T(8,128)(2,1)S(1)} collective-permute-done((bf16[128,1536]{1,0:T(8,128)(2,1)}, bf16[128,1536]{1,0:T(8,128)(2,1)S(1)}, u32[]{:S(2)}, u32[]{:S(2)}) %collective-permute-start.6) | collective-permute-done | bytes 393248 | tf_op jit(solution)/shard_map/ppermute | solution.py:197
  93.5 1.8 %tile.1 = bf16[32,16,128]{2,1,0:T(8,128)(2,1)S(1)} custom-call(s32[3]{0:T(128)S(1)} %pad_add_fusion.place_ref, bf16[128,1536]{1,0:T(8,128)(2,1)S(1)} %collective-permute-done.5.pair_ref, bf16[128,1536]{1,0:T(8,128)(2,1)S(1)} %collective-permute-done.6.other_pair_ref, bf16[64,1536]{1,0:T(8,128)(2,1)S(1)} %collective-permute-done.7.rest_0_, ...), custom_call_target="tpu_custom_call" | custom-call | tf_op jit(solution)/shard_map/tile/pallas_call | solution.py:205
  95.3 35.0 %all_to_all.5.parts_ref = bf16[32,16,128]{2,1,0:T(8,128)(2,1)S(1)} all-to-all(bf16[32,16,128]{2,1,0:T(8,128)(2,1)S(1)} %tile.1), channel_id=1, replica_groups=mesh['y_high'=2,'y_low'=4,'z_low'=4,'z_high'=2,'x'=4,'core'=2] {'y_high'..., dimensions={0} | all-to-all | bytes 262144 | tf_op jit(solution)/shard_map/all_to_all | solution.py:213
  130.3 0.7 sum.1
  (7 shorter events, 0.0 us)
Async XLA Ops:
  1.9 25.0 %collective-permute-start = (bf16[64,1536]{1,0:T(8,128)(2,1)}, bf16[64,1536]{1,0:T(8,128)(2,1)S(1)}, u32[]{:S(2)}, u32[]{:S(2)}) collective-permute-start(bf16[64,1536]{1,0:T(8,128)(2,1)} %get-tuple-element.13.own_ref), channel_id=1, source_target_pairs={{0,2},{2,0},{4,6},{6,4},{1,3},{3,1},{5,7},{7,5},{8,10},{10,8},{12,... | collective-permute-start | bytes 589832 | tf_op jit(solution)/shard_map/ppermute | solution.py:152
  4.6 24.7 %collective-permute-start.1 = (bf16[64,768]{1,0:T(8,128)(2,1)}, bf16[64,768]{1,0:T(8,128)(2,1)}, u32[]{:S(2)}, u32[]{:S(2)}) collective-permute-start(bf16[64,768]{1,0:T(8,128)(2,1)} %get-tuple-element.16), channel_id=1, source_target_pairs={{496,0},{0,16},{16,32},{32,48},{48,64},{64,80},{80,96},{96,112},{1... | collective-permute-start | bytes 294920 | tf_op jit(solution)/shard_map/ppermute | solution.py:150
  8.9 20.4 %collective-permute-start.2 = (bf16[64,768]{1,0:T(8,128)(2,1)}, bf16[64,768]{1,0:T(8,128)(2,1)}, u32[]{:S(2)}, u32[]{:S(2)}) collective-permute-start(bf16[64,768]{1,0:T(8,128)(2,1)} %get-tuple-element.17), channel_id=1, source_target_pairs={{16,0},{32,16},{48,32},{64,48},{80,64},{96,80},{112,96},{128,112},... | collective-permute-start | bytes 294920 | tf_op jit(solution)/shard_map/ppermute | solution.py:150
  17.4 12.0 %collective-permute-start.3 = (bf16[64,768]{1,0:T(8,128)(2,1)}, bf16[64,768]{1,0:T(8,128)(2,1)}, u32[]{:S(2)}, u32[]{:S(2)}) collective-permute-start(bf16[64,768]{1,0:T(8,128)(2,1)} %get-tuple-element.18), channel_id=1, source_target_pairs={{480,0},{496,16},{0,32},{16,48},{32,64},{48,80},{64,96},{80,112},{... | collective-permute-start | bytes 294920 | tf_op jit(solution)/shard_map/ppermute | solution.py:150
  19.3 10.9 %collective-permute-start.4 = (bf16[64,768]{1,0:T(8,128)(2,1)}, bf16[64,768]{1,0:T(8,128)(2,1)}, u32[]{:S(2)}, u32[]{:S(2)}) collective-permute-start(bf16[64,768]{1,0:T(8,128)(2,1)} %get-tuple-element.19), channel_id=1, source_target_pairs={{32,0},{48,16},{64,32},{80,48},{96,64},{112,80},{128,96},{144,112}... | collective-permute-start | bytes 294920 | tf_op jit(solution)/shard_map/ppermute | solution.py:150
  26.9 0.7 copy-start
  36.9 25.5 %collective-permute-start.9 = (bf16[64,1536]{1,0:T(8,128)(2,1)}, bf16[64,1536]{1,0:T(8,128)(2,1)S(1)}, u32[]{:S(2)}, u32[]{:S(2)}) collective-permute-start(bf16[64,1536]{1,0:T(8,128)(2,1)} %blocks.1), channel_id=1, source_target_pairs={{0,8},{8,0},{64,10},{72,2},{128,12},{136,4},{192,14},{200,6},{2,72... | collective-permute-start | bytes 589832 | tf_op jit(solution)/shard_map/ppermute | solution.py:191
  47.5 35.8 %collective-permute-start.5 = (bf16[128,1536]{1,0:T(8,128)(2,1)}, bf16[128,1536]{1,0:T(8,128)(2,1)S(1)}, u32[]{:S(2)}, u32[]{:S(2)}) collective-permute-start(bf16[128,1536]{1,0:T(8,128)(2,1)} %join.1), channel_id=1, source_target_pairs={{0,0},{64,2},{128,4},{192,6},{2,64},{66,66},{130,68},{194,70},{4,1... | collective-permute-start | bytes 1179656 | tf_op jit(solution)/shard_map/ppermute | solution.py:197
  52.4 41.1 %collective-permute-start.6 = (bf16[128,1536]{1,0:T(8,128)(2,1)}, bf16[128,1536]{1,0:T(8,128)(2,1)S(1)}, u32[]{:S(2)}, u32[]{:S(2)}) collective-permute-start(bf16[128,1536]{1,0:T(8,128)(2,1)} %join.1), channel_id=1, source_target_pairs={{0,128},{64,130},{128,132},{192,134},{2,192},{66,194},{130,196},{1... | collective-permute-start | bytes 1179656 | tf_op jit(solution)/shard_map/ppermute | solution.py:197
  54.3 27.0 %collective-permute-start.7 = (bf16[64,1536]{1,0:T(8,128)(2,1)}, bf16[64,1536]{1,0:T(8,128)(2,1)S(1)}, u32[]{:S(2)}, u32[]{:S(2)}) collective-permute-start(bf16[64,1536]{1,0:T(8,128)(2,1)} %blocks.1), channel_id=1, source_target_pairs={{0,0},{64,2},{128,4},{192,6},{2,64},{66,66},{130,68},{194,70},{4,1... | collective-permute-start | bytes 589832 | tf_op jit(solution)/shard_map/ppermute | solution.py:192
  62.4 31.1 %collective-permute-start.10 = (bf16[64,1536]{1,0:T(8,128)(2,1)S(1)}, bf16[64,1536]{1,0:T(8,128)(2,1)S(1)}, u32[]{:S(2)}, u32[]{:S(2)}) collective-permute-start(bf16[64,1536]{1,0:T(8,128)(2,1)S(1)} %collective-permute-done.9.rest_2_), channel_id=1, source_target_pairs={{0,1},{1,0},{2,3},{3,2},{4,5},{5,4},{6,7},{7,6},{8,9},{9,8},{10,11... | collective-permute-start | bytes 589832 | tf_op jit(solution)/shard_map/ppermute | solution.py:194
  81.3 12.2 %collective-permute-start.8 = (bf16[64,1536]{1,0:T(8,128)(2,1)S(1)}, bf16[64,1536]{1,0:T(8,128)(2,1)S(1)}, u32[]{:S(2)}, u32[]{:S(2)}) collective-permute-start(bf16[64,1536]{1,0:T(8,128)(2,1)S(1)} %collective-permute-done.7.rest_0_), channel_id=1, source_target_pairs={{0,1},{1,0},{2,3},{3,2},{4,5},{5,4},{6,7},{7,6},{8,9},{9,8},{10,11... | collective-permute-start | bytes 589832 | tf_op jit(solution)/shard_map/ppermute | solution.py:193

commit v10 on v8

--- a/solution.py
+++ b/solution.py
@@ -13,7 +13,6 @@
 OWN = 8
 WIDTH = 64
 CAP = 56
-CHUNK = 4
 PACKED = OWN * DOFS
 
 neighbour_offsets = (1, -1, 2, -2)
@@ -42,37 +41,19 @@
         pack_pair(basis_ref[2 * pair], basis_ref[2 * pair + 1], packed_ref, 384 * pair)
 
 
-def block_kernel(
-    rows_hbm, columns_hbm, density_hbm, count_hbm, basis_hbm, blocks_hbm, own_hbm, other_hbm, *rest
-):
-    ghost_refs = rest[:NEIGH]
-    out_ref, pair_ref, rows_ref, columns_ref, density_ref, count_ref, *rest = rest[NEIGH:]
-    blocks, pool, total, arrived, lists, joined = rest
-    small = [
-        pltpu.make_async_copy(source, target, lists.at[index])
-        for index, (source, target) in enumerate((
-            (rows_hbm, rows_ref),
-            (columns_hbm, columns_ref),
-            (density_hbm, density_ref),
-            (count_hbm, count_ref),
-            (basis_hbm, pool.at[pl.ds(0, OWN)]),
-        ))
-    ]
-    for copy in small:
-        copy.start()
-    copies = []
-    for chunk in range(CAP // CHUNK):
-        part = pl.ds(chunk * CHUNK, CHUNK)
-        copies.append(
-            pltpu.make_async_copy(blocks_hbm.at[part], blocks.at[part], arrived.at[chunk])
-        )
-        copies[-1].start()
-    joins = [
-        pltpu.make_async_copy(source, pair_ref.at[pl.ds(index * WIDTH, WIDTH)], joined.at[index])
-        for index, source in enumerate((own_hbm, other_hbm))
-    ]
-    for copy in joins:
-        copy.start()
+def stage_kernel(blocks_ref, basis_ref, blocks_out_ref, own_ref):
+    blocks_out_ref[...] = blocks_ref[...]
+    own_ref[...] = basis_ref[...]
+
+
+def join_kernel(own_ref, other_ref, pair_ref):
+    pair_ref[:WIDTH] = own_ref[...]
+    pair_ref[WIDTH:] = other_ref[...]
+
+
+def block_kernel(table_ref, own_ref, blocks_ref, *rest):
+    *ghost_refs, out_ref, pool, total = rest
+    pool[:OWN] = own_ref[...]
     for neighbour, ghost_ref in enumerate(ghost_refs):
         for pair in range(GMAX // 2):
             at, slot = 384 * pair, OWN + neighbour * GMAX + 2 * pair
@@ -81,26 +62,17 @@
             pool[slot, :, 128:] = ghost_ref[:, at + 256 : at + 320]
             pool[slot + 1, :, 128:] = ghost_ref[:, at + 320 : at + 384]
     total[...] = jnp.zeros_like(total)
-    for copy in small:
-        copy.wait()
-    count = count_ref[0]
-    for chunk in range(CAP // CHUNK):
-        copies[chunk].wait()
-        for block in range(chunk * CHUNK, (chunk + 1) * CHUNK):
-            density = density_ref[block]
-            scale = jnp.where(block < count, 0.001 + density * density * density, 0.0)
-            product = lax.dot_general(
-                pool[columns_ref[block]],
-                blocks[block],
-                (((1,), (1,)), ((), ())),
-                preferred_element_type=jnp.float32,
-            )
-            row = rows_ref[block]
-            total[row] = total[row] + scale * product
+    for block in range(CAP):
+        row, column = table_ref[0, block].astype(jnp.int32), table_ref[1, block].astype(jnp.int32)
+        product = lax.dot_general(
+            pool[column],
+            blocks_ref[block],
+            (((1,), (1,)), ((), ())),
+            preferred_element_type=jnp.float32,
+        )
+        total[row] = total[row] + table_ref[2, block] * product
     for pair in range(OWN // 2):
         pack_pair(total[2 * pair], total[2 * pair + 1], out_ref, 384 * pair)
-    for copy in joins:
-        copy.wait()
 
 
 def put_tile(place_ref, products_ref, rows_ref, out_ref, z_step, core_step, row_step):
@@ -121,9 +93,7 @@
         out_ref[at + 4 * (x ^ NEAR)] = jnp.where(low_lanes, low_turned, high).astype(out_ref.dtype)
 
 
-def own_tile_kernel(place_ref, pair_ref, products_ref, out_ref, pair_out_ref, products_out_ref):
-    pair_out_ref[...] = pair_ref[...]
-    products_out_ref[...] = products_ref[...]
+def own_tile_kernel(place_ref, pair_ref, products_ref, out_ref):
     put_tile(place_ref, products_ref, pair_ref, out_ref, 0, 0, 0)
 
 
@@ -162,54 +132,55 @@
         route = [((i - offset) % parts, i) for i in range(parts)]
         arriving.append(lax.ppermute(block, mesh_axes, route))
     swap = [(0, 1), (1, 0)]
+    blocks, own = pl.pallas_call(
+        stage_kernel,
+        out_shape=[
+            shape(stiffness_blocks.shape, jnp.bfloat16),
+            shape(basis_vectors.shape, jnp.bfloat16),
+        ],
+        in_specs=[VMEM] * 2,
+        out_specs=[VMEM] * 2,
+        compiler_params=pltpu.CompilerParams(vmem_limit_bytes=24 << 20),
+        cost_estimate=pl.CostEstimate(flops=0, bytes_accessed=12 << 20, transcendentals=0),
+        name="stage",
+    )(stiffness_blocks, basis_vectors)
+    active = jnp.arange(CAP, dtype=jnp.int32) < block_counts[0]
+    scale = jnp.where(active, 0.001 + density * density * density, 0.0)
+    line = lax.broadcasted_iota(jnp.int32, (8, CAP), 0)
+    places = jnp.where(line == 0, block_rows[None], block_columns[None]).astype(jnp.float32)
+    table = jnp.where(line == 2, scale[None], places)
     other_packed = lax.ppermute(packed, "x", [(i, i ^ NEAR) for i in range(4)])
-    products, pair = pl.pallas_call(
+    products = pl.pallas_call(
         block_kernel,
-        out_shape=[
-            shape((WIDTH, PACKED), jnp.bfloat16),
-            shape((2 * WIDTH, PACKED), jnp.bfloat16),
-        ],
-        in_specs=[HBM] * 8 + [VMEM] * NEIGH,
-        out_specs=[VMEM] * 2,
+        out_shape=shape((WIDTH, PACKED), jnp.bfloat16),
+        in_specs=[SMEM] + [VMEM] * (2 + NEIGH),
+        out_specs=VMEM,
         scratch_shapes=[
-            pltpu.SMEM((CAP,), jnp.int32),
-            pltpu.SMEM((CAP,), jnp.int32),
-            pltpu.SMEM((CAP,), jnp.float32),
-            pltpu.SMEM((1,), jnp.int32),
-            pltpu.VMEM((CAP, DOFS, DOFS), jnp.bfloat16),
             pltpu.VMEM((OWN + NEIGH * GMAX, WIDTH, DOFS), jnp.bfloat16),
             pltpu.VMEM((OWN, WIDTH, DOFS), jnp.float32),
-            pltpu.SemaphoreType.DMA((CAP // CHUNK,)),
-            pltpu.SemaphoreType.DMA((5,)),
-            pltpu.SemaphoreType.DMA((2,)),
         ],
-        compiler_params=pltpu.CompilerParams(vmem_limit_bytes=64 << 20),
+        compiler_params=pltpu.CompilerParams(vmem_limit_bytes=24 << 20),
         name="blocks",
-    )(
-        block_rows,
-        block_columns,
-        density,
-        block_counts,
-        basis_vectors,
-        stiffness_blocks,
-        packed,
-        other_packed,
-        *arriving,
-    )
+    )(table, own, blocks, *arriving)
+    other_packed, _ = lax.optimization_barrier((other_packed, products))
+    pair = pl.pallas_call(
+        join_kernel,
+        out_shape=shape((2 * WIDTH, PACKED), jnp.bfloat16),
+        in_specs=[VMEM] * 2,
+        out_specs=VMEM,
+        compiler_params=pltpu.CompilerParams(vmem_limit_bytes=8 << 20),
+        name="join",
+    )(packed, other_packed)
     over_z = lax.ppermute(products, "z_hi", swap)
     over_core = lax.ppermute(products, "core", swap)
     other_pair = lax.ppermute(pair, "x", [(i, i ^ FAR) for i in range(4)])
     place = jnp.stack([lax.axis_index(name) for name in ("z_hi", "x", "core")]).astype(jnp.int32)
     chunks_shape = shape((parts, 16, 128), jnp.bfloat16)
-    begun, pair, products = pl.pallas_call(
+    begun = pl.pallas_call(
         own_tile_kernel,
-        out_shape=[
-            chunks_shape,
-            shape(pair.shape, pair.dtype),
-            shape(products.shape, products.dtype),
-        ],
+        out_shape=chunks_shape,
         in_specs=[SMEM] + [VMEM] * 2,
-        out_specs=[VMEM] * 3,
+        out_specs=VMEM,
         compiler_params=pltpu.CompilerParams(vmem_limit_bytes=16 << 20),
         cost_estimate=pl.CostEstimate(flops=2 << 23, bytes_accessed=1 << 20, transcendentals=0),
         name="own_tile",

time: 90.3 us -> 86.1 us (0.953)
  Pallas kernels: 11.4 us -> 7.54 us
  waiting for transfers between devices: 13.7 us -> 11 us
  local copies, waits for them, and re-layouts: 2.52 us -> 4.12 us
  other arithmetic: 0.08 us -> 1.49 us
    pallas_call x2 -> x4, Pallas kernels: 7.76 us -> 3.94 us  [the longest x1 2.69 us: local(): pl.pallas_call(block_kernel, out_shape=shape((WIDTH, PACKED), jnp.bfloat1...]
    ppermute x4, waiting for transfers between devices: 3.28 us -> 0.01 us  [local(): arriving.append(lax.ppermute(block, mesh_axes, route))]
    ppermute x1, waiting for transfers between devices: 3.77 us -> 1.31 us  [local(): other_pair = lax.ppermute(pair, 'x', [(i, i ^ FAR) for i in range(4)])]
    ppermute x1, waiting for transfers between devices: 0.38 us -> 2 us  [local(): over_z = lax.ppermute(products, 'z_hi', swap)]
    unnamed x5 -> x7, local copies, waits for them, and re-layouts: 2.52 us -> 4.12 us
    select_n x0 -> x2, other arithmetic: none -> 1.41 us  [the longest x1 0.74 us: local(): table = jnp.where(line == 2, scale[None], places)]
    ppermute x1, waiting for transfers between devices: 0.01 us -> 1.4 us  [local(): over_both = lax.ppermute(behind, 'core', swap)]
  transfers between devices with their start and end apart: 10 -> 10, of which waited for: 5 -> 4; matrix products, arithmetic and copies ran while one was open for 0% -> 2% of each run, Pallas kernels for 1% -> 5%
where the time goes in v10:
time: 86.1 us; the launch traced here: 85.6 us
  starting transfers between devices  42.6 us (49%)
  blocking collectives  17.9 us (21%)
  waiting for transfers between devices  11 us (13%)
  Pallas kernels  7.54 us (9%)
  local copies, waits for them, and re-layouts  4.12 us (5%)
  other arithmetic  1.49 us (2%)
    ppermute x4, starting transfers between devices, local(): arriving.append(lax.ppermute(block, mesh_axes, route))  21.6 us
    all_to_all x1, blocking collectives, local(): shares = lax.all_to_all(chunks, mesh_axes, 0, 0, tiled=True)  17.9 us
    ppermute x1, starting transfers between devices, local(): over_z = lax.ppermute(products, 'z_hi', swap)  8.22 us
    ppermute x1, waiting for transfers between devices, local(): return lax.ppermute(block, whole, route).T  6.28 us
    unnamed x7, local copies, waits for them, and re-layouts  4.12 us
    ppermute x1, starting transfers between devices, local(): return lax.ppermute(block, whole, route).T  3.24 us
    ppermute x1, starting transfers between devices, local(): other_pair = lax.ppermute(pair, 'x', [(i, i ^ FAR) for i in range(4)])  3.05 us
    ppermute x1, starting transfers between devices, local(): other_packed = lax.ppermute(packed, 'x', [(i, i ^ NEAR) for i in range(4)])  2.74 us
  transfers between devices with their start and end apart: 10, of which 4 were waited for; matrix products, arithmetic and copies ran while one was open for 2% of the time, Pallas kernels for 5%

profile of v10, /device:TPU:6, one launch (start us, length us, event | category | flops | bytes accessed | tf_op | source)
XLA Modules:
  0.0 85.6 jit_solution(12899302040179634629)
XLA Ops:
  0.0 1.9 %select.1 = (bf16[64,1536]{1,0:T(8,128)(2,1)}, bf16[64,768]{1,0:T(8,128)(2,1)}, bf16[64,768]{1,0:T(8,128)(2,1)}, bf16[64,768]{1,0:T(8,128)(2,1)}, bf16[64,768]{1,0:T(8,128)(2,1)}) custom-call(s32[16]{0:T(128)} %send_ref.1, bf16[8,64,192]{2,1,0:T(8,128)(2,1)} %basis_ref.3), custom_call_target="tpu_custom_call" | custom-call | tf_op jit(solution)/shard_map/select/pallas_call | solution.py:122
  1.9 4.3 %collective-permute-start.1 = (bf16[64,768]{1,0:T(8,128)(2,1)}, bf16[64,768]{1,0:T(8,128)(2,1)S(1)}, u32[]{:S(2)}, u32[]{:S(2)}) collective-permute-start(bf16[64,768]{1,0:T(8,128)(2,1)} %get-tuple-element.18), channel_id=1, source_target_pairs={{496,0},{0,16},{16,32},{32,48},{48,64},{64,80},{80,96},{96,112},{1... | collective-permute-start | bytes 294920 | tf_op jit(solution)/shard_map/ppermute | solution.py:133
  6.1 8.4 %collective-permute-start.2 = (bf16[64,768]{1,0:T(8,128)(2,1)}, bf16[64,768]{1,0:T(8,128)(2,1)S(1)}, u32[]{:S(2)}, u32[]{:S(2)}) collective-permute-start(bf16[64,768]{1,0:T(8,128)(2,1)} %get-tuple-element.19), channel_id=1, source_target_pairs={{16,0},{32,16},{48,32},{64,48},{80,64},{96,80},{112,96},{128,112},... | collective-permute-start | bytes 294920 | tf_op jit(solution)/shard_map/ppermute | solution.py:133
  14.6 1.9 %collective-permute-start.3 = (bf16[64,768]{1,0:T(8,128)(2,1)}, bf16[64,768]{1,0:T(8,128)(2,1)S(1)}, u32[]{:S(2)}, u32[]{:S(2)}) collective-permute-start(bf16[64,768]{1,0:T(8,128)(2,1)} %get-tuple-element.20), channel_id=1, source_target_pairs={{480,0},{496,16},{0,32},{16,48},{32,64},{48,80},{64,96},{80,112},{... | collective-permute-start | bytes 294920 | tf_op jit(solution)/shard_map/ppermute | solution.py:133
  16.5 6.9 %collective-permute-start.4 = (bf16[64,768]{1,0:T(8,128)(2,1)}, bf16[64,768]{1,0:T(8,128)(2,1)S(1)}, u32[]{:S(2)}, u32[]{:S(2)}) collective-permute-start(bf16[64,768]{1,0:T(8,128)(2,1)} %get-tuple-element.21), channel_id=1, source_target_pairs={{32,0},{48,16},{64,32},{80,48},{96,64},{112,80},{128,96},{144,112}... | collective-permute-start | bytes 294920 | tf_op jit(solution)/shard_map/ppermute | solution.py:133
  23.4 2.7 %collective-permute-start = (bf16[64,1536]{1,0:T(8,128)(2,1)}, bf16[64,1536]{1,0:T(8,128)(2,1)S(1)}, u32[]{:S(2)}, u32[]{:S(2)}) collective-permute-start(bf16[64,1536]{1,0:T(8,128)(2,1)} %get-tuple-element.15.own_ref), channel_id=1, source_target_pairs={{0,2},{2,0},{4,6},{6,4},{1,3},{3,1},{5,7},{7,5},{8,10},{10,8},{12,... | collective-permute-start | bytes 589832 | tf_op jit(solution)/shard_map/ppermute | solution.py:152
  26.8 0.7 compare_select_fusion
  27.5 0.7 convert_select_fusion.table_ref
  28.3 2.6 %copy-done = bf16[56,192,192]{2,1,0:T(8,128)(2,1)S(1)} copy-done((bf16[56,192,192]{2,1,0:T(8,128)(2,1)S(1)}, bf16[56,192,192]{2,1,0:T(8,128)(2,1)}, u32[]{:S(2)}) %copy-start) | copy-done | bytes 4128792
  30.8 0.9 %copy-done.1 = bf16[8,64,192]{2,1,0:T(8,128)(2,1)S(1)} copy-done((bf16[8,64,192]{2,1,0:T(8,128)(2,1)S(1)}, bf16[8,64,192]{2,1,0:T(8,128)(2,1)}, u32[]{:S(2)}) %copy-start.1) | copy-done | bytes 196632
  32.2 2.7 %blocks.1.products_ref.rest_0_ = bf16[64,1536]{1,0:T(8,128)(2,1)S(1)} custom-call(f32[8,56]{1,0:T(8,128)S(1)} %convert_select_fusion.table_ref, bf16[8,64,192]{2,1,0:T(8,128)(2,1)S(1)} %get-tuple-element.16.own_ref, bf16[56,192,192]{2,1,0:T(8,128)(2,1)S(1)} %get-tuple-element.17.blocks_ref, bf16[64,768]{1,0:T(8,128)(2,1)S(1)} %collective-permute-done.1.rest_0_, ...), custom_call_target="tpu_custom_call" | custom-call | tf_op jit(solution)/shard_map/blocks/pallas_call | solution.py:153
  34.9 8.2 %collective-permute-start.7 = (bf16[64,1536]{1,0:T(8,128)(2,1)S(1)}, bf16[64,1536]{1,0:T(8,128)(2,1)S(1)}, u32[]{:S(2)}, u32[]{:S(2)}) collective-permute-start(bf16[64,1536]{1,0:T(8,128)(2,1)S(1)} %blocks.1.products_ref.rest_0_), channel_id=1, source_target_pairs={{0,8},{8,0},{1,9},{9,1},{2,10},{10,2},{3,11},{11,3},{4,12},{12,4},... | collective-permute-start | bytes 589832 | tf_op jit(solution)/shard_map/ppermute | solution.py:174
  43.2 3.0 %collective-permute-start.5 = (bf16[128,1536]{1,0:T(8,128)(2,1)S(1)}, bf16[128,1536]{1,0:T(8,128)(2,1)S(1)}, u32[]{:S(2)}, u32[]{:S(2)}) collective-permute-start(bf16[128,1536]{1,0:T(8,128)(2,1)S(1)} %join.1.pair_ref), channel_id=1, source_target_pairs={{0,6},{2,4},{4,2},{6,0},{1,7},{3,5},{5,3},{7,1},{8,14},{10,12},{12... | collective-permute-start | bytes 1179656 | tf_op jit(solution)/shard_map/ppermute | solution.py:176
  46.3 1.9 %collective-permute-start.6 = (bf16[64,1536]{1,0:T(8,128)(2,1)S(1)}, bf16[64,1536]{1,0:T(8,128)(2,1)S(1)}, u32[]{:S(2)}, u32[]{:S(2)}) collective-permute-start(bf16[64,1536]{1,0:T(8,128)(2,1)S(1)} %blocks.1.products_ref.rest_0_), channel_id=1, source_target_pairs={{0,1},{1,0},{2,3},{3,2},{4,5},{5,4},{6,7},{7,6},{8,9},{9,8},{10,11... | collective-permute-start | bytes 589832 | tf_op jit(solution)/shard_map/ppermute | solution.py:175
  48.2 0.9 %own_tile.1.rest_4_ = bf16[32,16,128]{2,1,0:T(8,128)(2,1)S(1)} custom-call(s32[3]{0:T(128)S(1)} %pad_add_fusion.place_ref, bf16[128,1536]{1,0:T(8,128)(2,1)S(1)} %join.1.pair_ref, bf16[64,1536]{1,0:T(8,128)(2,1)S(1)} %blocks.1.products_ref.rest_0_), custom_call_target="tpu_custom_call" | custom-call | flops 16777216 | bytes 1048576 | tf_op jit(solution)/shard_map/own_tile/pallas_call | solution.py:179
  49.1 2.0 %collective-permute-done.7.rest_2_ = bf16[64,1536]{1,0:T(8,128)(2,1)S(1)} collective-permute-done((bf16[64,1536]{1,0:T(8,128)(2,1)S(1)}, bf16[64,1536]{1,0:T(8,128)(2,1)S(1)}, u32[]{:S(2)}, u32[]{:S(2)}) %collective-permute-start.7) | collective-permute-done | bytes 196640 | tf_op jit(solution)/shard_map/ppermute | solution.py:174
  51.1 1.9 %collective-permute-start.8 = (bf16[64,1536]{1,0:T(8,128)(2,1)S(1)}, bf16[64,1536]{1,0:T(8,128)(2,1)S(1)}, u32[]{:S(2)}, u32[]{:S(2)}) collective-permute-start(bf16[64,1536]{1,0:T(8,128)(2,1)S(1)} %collective-permute-done.7.rest_2_), channel_id=1, source_target_pairs={{0,1},{1,0},{2,3},{3,2},{4,5},{5,4},{6,7},{7,6},{8,9},{9,8},{10,11... | collective-permute-start | bytes 589832 | tf_op jit(solution)/shard_map/ppermute | solution.py:189
  53.0 1.4 %collective-permute-done.8.rest_3_ = bf16[64,1536]{1,0:T(8,128)(2,1)S(1)} collective-permute-done((bf16[64,1536]{1,0:T(8,128)(2,1)S(1)}, bf16[64,1536]{1,0:T(8,128)(2,1)S(1)}, u32[]{:S(2)}, u32[]{:S(2)}) %collective-permute-start.8) | collective-permute-done | bytes 196640 | tf_op jit(solution)/shard_map/ppermute | solution.py:189
  54.4 1.3 %collective-permute-done.5.other_pair_ref = bf16[128,1536]{1,0:T(8,128)(2,1)S(1)} collective-permute-done((bf16[128,1536]{1,0:T(8,128)(2,1)S(1)}, bf16[128,1536]{1,0:T(8,128)(2,1)S(1)}, u32[]{:S(2)}, u32[]{:S(2)}) %collective-permute-start.5) | collective-permute-done | bytes 393248 | tf_op jit(solution)/shard_map/ppermute | solution.py:176
  55.7 1.6 %tile.1 = bf16[32,16,128]{2,1,0:T(8,128)(2,1)S(1)} custom-call(s32[3]{0:T(128)S(1)} %pad_add_fusion.place_ref, bf16[128,1536]{1,0:T(8,128)(2,1)S(1)} %join.1.pair_ref, bf16[128,1536]{1,0:T(8,128)(2,1)S(1)} %collective-permute-done.5.other_pair_ref, bf16[64,1536]{1,0:T(8,128)(2,1)S(1)} %blocks.1.products_ref.rest_0_, ...), custom_call_target="tpu_custom_call", output_to_operand_aliasing={{}: (7, {})} | custom-call | tf_op jit(solution)/shard_map/tile/pallas_call | solution.py:190
  57.4 17.9 %all_to_all.5.parts_ref = bf16[32,16,128]{2,1,0:T(8,128)(2,1)S(1)} all-to-all(bf16[32,16,128]{2,1,0:T(8,128)(2,1)S(1)} %tile.1), channel_id=1, replica_groups=mesh['y'=8,'z_lo'=4,'z_hi'=2,'x'=4,'core'=2] {'y','z_lo'}, dimensions={0} | all-to-all | bytes 262144 | tf_op jit(solution)/shard_map/all_to_all | solution.py:199
  75.4 3.2 %collective-permute-start.9 = (f32[32,64]{1,0:T(8,128)S(1)}, f32[32,64]{1,0:T(8,128)S(1)}, u32[]{:S(2)}, u32[]{:S(2)}) collective-permute-start(f32[32,64]{1,0:T(8,128)S(1)} %sum.1), channel_id=1, source_target_pairs={{0,0},{1,1},{2,64},{3,65},{4,128},{5,129},{6,192},{7,193},{8,8},{9... | collective-permute-start | bytes 24584 | tf_op jit(solution)/shard_map/ppermute | solution.py:214
  78.7 6.3 %collective-permute-done.9 = f32[32,64]{1,0:T(8,128)S(1)} collective-permute-done((f32[32,64]{1,0:T(8,128)S(1)}, f32[32,64]{1,0:T(8,128)S(1)}, u32[]{:S(2)}, u32[]{:S(2)}) %collective-permute-start.9) | collective-permute-done | bytes 8224 | tf_op jit(solution)/shard_map/ppermute | solution.py:214
  85.0 0.6 copy.12
  (15 shorter events, 0.6 us)
Async XLA Ops:
  1.9 30.3 %collective-permute-start.1 = (bf16[64,768]{1,0:T(8,128)(2,1)}, bf16[64,768]{1,0:T(8,128)(2,1)S(1)}, u32[]{:S(2)}, u32[]{:S(2)}) collective-permute-start(bf16[64,768]{1,0:T(8,128)(2,1)} %get-tuple-element.18), channel_id=1, source_target_pairs={{496,0},{0,16},{16,32},{32,48},{48,64},{64,80},{80,96},{96,112},{1... | collective-permute-start | bytes 294920 | tf_op jit(solution)/shard_map/ppermute | solution.py:133
  6.1 26.0 %collective-permute-start.2 = (bf16[64,768]{1,0:T(8,128)(2,1)}, bf16[64,768]{1,0:T(8,128)(2,1)S(1)}, u32[]{:S(2)}, u32[]{:S(2)}) collective-permute-start(bf16[64,768]{1,0:T(8,128)(2,1)} %get-tuple-element.19), channel_id=1, source_target_pairs={{16,0},{32,16},{48,32},{64,48},{80,64},{96,80},{112,96},{128,112},... | collective-permute-start | bytes 294920 | tf_op jit(solution)/shard_map/ppermute | solution.py:133
  14.6 17.6 %collective-permute-start.3 = (bf16[64,768]{1,0:T(8,128)(2,1)}, bf16[64,768]{1,0:T(8,128)(2,1)S(1)}, u32[]{:S(2)}, u32[]{:S(2)}) collective-permute-start(bf16[64,768]{1,0:T(8,128)(2,1)} %get-tuple-element.20), channel_id=1, source_target_pairs={{480,0},{496,16},{0,32},{16,48},{32,64},{48,80},{64,96},{80,112},{... | collective-permute-start | bytes 294920 | tf_op jit(solution)/shard_map/ppermute | solution.py:133
  16.5 15.7 %collective-permute-start.4 = (bf16[64,768]{1,0:T(8,128)(2,1)}, bf16[64,768]{1,0:T(8,128)(2,1)S(1)}, u32[]{:S(2)}, u32[]{:S(2)}) collective-permute-start(bf16[64,768]{1,0:T(8,128)(2,1)} %get-tuple-element.21), channel_id=1, source_target_pairs={{32,0},{48,16},{64,32},{80,48},{96,64},{112,80},{128,96},{144,112}... | collective-permute-start | bytes 294920 | tf_op jit(solution)/shard_map/ppermute | solution.py:133
  23.4 19.7 %collective-permute-start = (bf16[64,1536]{1,0:T(8,128)(2,1)}, bf16[64,1536]{1,0:T(8,128)(2,1)S(1)}, u32[]{:S(2)}, u32[]{:S(2)}) collective-permute-start(bf16[64,1536]{1,0:T(8,128)(2,1)} %get-tuple-element.15.own_ref), channel_id=1, source_target_pairs={{0,2},{2,0},{4,6},{6,4},{1,3},{3,1},{5,7},{7,5},{8,10},{10,8},{12,... | collective-permute-start | bytes 589832 | tf_op jit(solution)/shard_map/ppermute | solution.py:152
  28.3 2.6 %copy-start = (bf16[56,192,192]{2,1,0:T(8,128)(2,1)S(1)}, bf16[56,192,192]{2,1,0:T(8,128)(2,1)}, u32[]{:S(2)}) copy-start(bf16[56,192,192]{2,1,0:T(8,128)(2,1)} %blocks_ref.1) | copy-start | bytes 12386308
  30.8 0.9 %copy-start.1 = (bf16[8,64,192]{2,1,0:T(8,128)(2,1)S(1)}, bf16[8,64,192]{2,1,0:T(8,128)(2,1)}, u32[]{:S(2)}) copy-start(bf16[8,64,192]{2,1,0:T(8,128)(2,1)} %basis_ref.3) | copy-start | bytes 589828
  31.8 11.4 %copy-start.2 = (bf16[64,1536]{1,0:T(8,128)(2,1)S(1)}, bf16[64,1536]{1,0:T(8,128)(2,1)}, u32[]{:S(2)}) copy-start(bf16[64,1536]{1,0:T(8,128)(2,1)} %get-tuple-element.15.own_ref) | copy-start | bytes 589828
  34.9 16.2 %collective-permute-start.7 = (bf16[64,1536]{1,0:T(8,128)(2,1)S(1)}, bf16[64,1536]{1,0:T(8,128)(2,1)S(1)}, u32[]{:S(2)}, u32[]{:S(2)}) collective-permute-start(bf16[64,1536]{1,0:T(8,128)(2,1)S(1)} %blocks.1.products_ref.rest_0_), channel_id=1, source_target_pairs={{0,8},{8,0},{1,9},{9,1},{2,10},{10,2},{3,11},{11,3},{4,12},{12,4},... | collective-permute-start | bytes 589832 | tf_op jit(solution)/shard_map/ppermute | solution.py:174
  43.2 12.6 %collective-permute-start.5 = (bf16[128,1536]{1,0:T(8,128)(2,1)S(1)}, bf16[128,1536]{1,0:T(8,128)(2,1)S(1)}, u32[]{:S(2)}, u32[]{:S(2)}) collective-permute-start(bf16[128,1536]{1,0:T(8,128)(2,1)S(1)} %join.1.pair_ref), channel_id=1, source_target_pairs={{0,6},{2,4},{4,2},{6,0},{1,7},{3,5},{5,3},{7,1},{8,14},{10,12},{12... | collective-permute-start | bytes 1179656 | tf_op jit(solution)/shard_map/ppermute | solution.py:176
  46.3 6.7 %collective-permute-start.6 = (bf16[64,1536]{1,0:T(8,128)(2,1)S(1)}, bf16[64,1536]{1,0:T(8,128)(2,1)S(1)}, u32[]{:S(2)}, u32[]{:S(2)}) collective-permute-start(bf16[64,1536]{1,0:T(8,128)(2,1)S(1)} %blocks.1.products_ref.rest_0_), channel_id=1, source_target_pairs={{0,1},{1,0},{2,3},{3,2},{4,5},{5,4},{6,7},{7,6},{8,9},{9,8},{10,11... | collective-permute-start | bytes 589832 | tf_op jit(solution)/shard_map/ppermute | solution.py:175
  51.1 3.3 %collective-permute-start.8 = (bf16[64,1536]{1,0:T(8,128)(2,1)S(1)}, bf16[64,1536]{1,0:T(8,128)(2,1)S(1)}, u32[]{:S(2)}, u32[]{:S(2)}) collective-permute-start(bf16[64,1536]{1,0:T(8,128)(2,1)S(1)} %collective-permute-done.7.rest_2_), channel_id=1, source_target_pairs={{0,1},{1,0},{2,3},{3,2},{4,5},{5,4},{6,7},{7,6},{8,9},{9,8},{10,11... | collective-permute-start | bytes 589832 | tf_op jit(solution)/shard_map/ppermute | solution.py:189
  75.4 9.5 %collective-permute-start.9 = (f32[32,64]{1,0:T(8,128)S(1)}, f32[32,64]{1,0:T(8,128)S(1)}, u32[]{:S(2)}, u32[]{:S(2)}) collective-permute-start(f32[32,64]{1,0:T(8,128)S(1)} %sum.1), channel_id=1, source_target_pairs={{0,0},{1,1},{2,64},{3,65},{4,128},{5,129},{6,192},{7,193},{8,8},{9... | collective-permute-start | bytes 24584 | tf_op jit(solution)/shard_map/ppermute | solution.py:214

commit v11 on v10

--- a/solution.py
+++ b/solution.py
@@ -41,9 +41,9 @@
         pack_pair(basis_ref[2 * pair], basis_ref[2 * pair + 1], packed_ref, 384 * pair)
 
 
-def stage_kernel(blocks_ref, basis_ref, blocks_out_ref, own_ref):
+def stage_kernel(blocks_ref, packed_ref, blocks_out_ref, packed_out_ref):
     blocks_out_ref[...] = blocks_ref[...]
-    own_ref[...] = basis_ref[...]
+    packed_out_ref[...] = packed_ref[...]
 
 
 def join_kernel(own_ref, other_ref, pair_ref):
@@ -53,15 +53,16 @@
 
 def block_kernel(table_ref, own_ref, blocks_ref, *rest):
     *ghost_refs, out_ref, pool, total = rest
-    pool[:OWN] = own_ref[...]
-    for neighbour, ghost_ref in enumerate(ghost_refs):
-        for pair in range(GMAX // 2):
-            at, slot = 384 * pair, OWN + neighbour * GMAX + 2 * pair
-            pool[slot, :, :128] = ghost_ref[:, at : at + 128]
-            pool[slot + 1, :, :128] = ghost_ref[:, at + 128 : at + 256]
-            pool[slot, :, 128:] = ghost_ref[:, at + 256 : at + 320]
-            pool[slot + 1, :, 128:] = ghost_ref[:, at + 320 : at + 384]
+    slot = 0
+    for slabs_ref in (own_ref, *ghost_refs):
+        for at in range(0, slabs_ref.shape[1], 384):
+            pool[slot, :, :128] = slabs_ref[:, at : at + 128]
+            pool[slot + 1, :, :128] = slabs_ref[:, at + 128 : at + 256]
+            pool[slot, :, 128:] = slabs_ref[:, at + 256 : at + 320]
+            pool[slot + 1, :, 128:] = slabs_ref[:, at + 320 : at + 384]
+            slot += 2
     total[...] = jnp.zeros_like(total)
+    count = table_ref[2, 0].astype(jnp.int32)
     for block in range(CAP):
         row, column = table_ref[0, block].astype(jnp.int32), table_ref[1, block].astype(jnp.int32)
         product = lax.dot_general(
@@ -70,41 +71,43 @@
             (((1,), (1,)), ((), ())),
             preferred_element_type=jnp.float32,
         )
-        total[row] = total[row] + table_ref[2, block] * product
+        density = table_ref[3, block]
+        scale = jnp.where(block < count, 0.001 + density * density * density, 0.0)
+        total[row] = total[row] + scale * product
     for pair in range(OWN // 2):
         pack_pair(total[2 * pair], total[2 * pair + 1], out_ref, 384 * pair)
 
 
-def put_tile(place_ref, products_ref, rows_ref, out_ref, z_step, core_step, row_step):
-    half, x, core = place_ref[0] ^ z_step, place_ref[1] ^ row_step, place_ref[2] ^ core_step
+def put_tile(place_ref, products, rows, out_ref, steps, row_step):
     low_lanes = lax.broadcasted_iota(jnp.int32, (16, 2 * WIDTH), 1) < WIDTH
     tile = lax.dot_general(
-        products_ref[...],
-        rows_ref[...],
-        (((1,), (1,)), ((), ())),
-        preferred_element_type=jnp.float32,
+        products, rows, (((1,), (1,)), ((), ())), preferred_element_type=jnp.float32
     )
-    for h in range(2):
-        low, high = tile[32 * h : 32 * h + 16], tile[32 * h + 16 : 32 * h + 32]
-        low_turned = pltpu.roll(low, WIDTH, 1)
-        high_turned = pltpu.roll(high, WIDTH, 1)
-        at = 16 * half + 2 * core + h
-        out_ref[at + 4 * x] = jnp.where(low_lanes, low, high_turned).astype(out_ref.dtype)
-        out_ref[at + 4 * (x ^ NEAR)] = jnp.where(low_lanes, low_turned, high).astype(out_ref.dtype)
+    x = place_ref[1] ^ row_step
+    for index, (z_step, core_step) in enumerate(steps):
+        half, core = place_ref[0] ^ z_step, place_ref[2] ^ core_step
+        for h in range(2):
+            at = WIDTH * index + 32 * h
+            low, high = tile[at : at + 16], tile[at + 16 : at + 32]
+            low_turned = pltpu.roll(low, WIDTH, 1)
+            high_turned = pltpu.roll(high, WIDTH, 1)
+            at = 16 * half + 2 * core + h
+            first = jnp.where(low_lanes, low, high_turned)
+            second = jnp.where(low_lanes, low_turned, high)
+            out_ref[at + 4 * x] = first.astype(out_ref.dtype)
+            out_ref[at + 4 * (x ^ NEAR)] = second.astype(out_ref.dtype)
 
 
 def own_tile_kernel(place_ref, pair_ref, products_ref, out_ref):
-    put_tile(place_ref, products_ref, pair_ref, out_ref, 0, 0, 0)
+    put_tile(place_ref, products_ref[...], pair_ref[...], out_ref, ((0, 0),), 0)
 
 
 def tile_kernel(place_ref, pair_ref, other_pair_ref, *rest):
     *product_refs, begun_ref, out_ref = rest
-    for (z_step, core_step), products_ref in zip(((0, 0), (0, 1), (1, 0), (1, 1)), product_refs):
-        for row_step, rows_ref in ((0, pair_ref), (FAR, other_pair_ref)):
-            if z_step or core_step or row_step:
-                put_tile(
-                    place_ref, products_ref, rows_ref, out_ref, z_step, core_step, row_step
-                )
+    steps = ((0, 0), (0, 1), (1, 0), (1, 1))
+    products = jnp.concatenate([ref[...] for ref in product_refs], axis=0)
+    put_tile(place_ref, products, other_pair_ref[...], out_ref, steps, FAR)
+    put_tile(place_ref, products[WIDTH:], pair_ref[...], out_ref, steps[1:], 0)
 
 
 def sum_kernel(parts_ref, out_ref):
@@ -136,19 +139,18 @@
         stage_kernel,
         out_shape=[
             shape(stiffness_blocks.shape, jnp.bfloat16),
-            shape(basis_vectors.shape, jnp.bfloat16),
+            shape((WIDTH, PACKED), jnp.bfloat16),
         ],
         in_specs=[VMEM] * 2,
         out_specs=[VMEM] * 2,
         compiler_params=pltpu.CompilerParams(vmem_limit_bytes=24 << 20),
         cost_estimate=pl.CostEstimate(flops=0, bytes_accessed=12 << 20, transcendentals=0),
         name="stage",
-    )(stiffness_blocks, basis_vectors)
-    active = jnp.arange(CAP, dtype=jnp.int32) < block_counts[0]
-    scale = jnp.where(active, 0.001 + density * density * density, 0.0)
+    )(stiffness_blocks, packed)
     line = lax.broadcasted_iota(jnp.int32, (8, CAP), 0)
-    places = jnp.where(line == 0, block_rows[None], block_columns[None]).astype(jnp.float32)
-    table = jnp.where(line == 2, scale[None], places)
+    listed = jnp.where(line == 0, block_rows[None], block_columns[None])
+    listed = jnp.where(line == 2, block_counts[0], listed).astype(jnp.float32)
+    table = jnp.where(line == 3, density[None], listed)
     other_packed = lax.ppermute(packed, "x", [(i, i ^ NEAR) for i in range(4)])
     products = pl.pallas_call(
         block_kernel,
@@ -170,7 +172,7 @@
         out_specs=VMEM,
         compiler_params=pltpu.CompilerParams(vmem_limit_bytes=8 << 20),
         name="join",
-    )(packed, other_packed)
+    )(own, other_packed)
     over_z = lax.ppermute(products, "z_hi", swap)
     over_core = lax.ppermute(products, "core", swap)
     other_pair = lax.ppermute(pair, "x", [(i, i ^ FAR) for i in range(4)])

time: 86.1 us -> 84.9 us (0.986)
    unnamed x7 -> x5, local copies, waits for them, and re-layouts: 4.12 us -> 4.09 us
  transfers between devices with their start and end apart: 10 -> 10, of which waited for: 4 -> 4; matrix products, arithmetic and copies ran while one was open for 2% -> 1% of each run, Pallas kernels for 5% -> 5%
where the time goes in v11:
time: 84.9 us; the launch traced here: 84.4 us
  starting transfers between devices  42.6 us (50%)
  blocking collectives  18 us (21%)
  waiting for transfers between devices  11 us (13%)
  Pallas kernels  7.06 us (8%)
  local copies, waits for them, and re-layouts  4.09 us (5%)
  other arithmetic  0.85 us (1%)
    ppermute x4, starting transfers between devices, local(): arriving.append(lax.ppermute(block, mesh_axes, route))  21.6 us
    all_to_all x1, blocking collectives, local(): shares = lax.all_to_all(chunks, mesh_axes, 0, 0, tiled=True)  18 us
    ppermute x1, starting transfers between devices, local(): over_z = lax.ppermute(products, 'z_hi', swap)  8.22 us
    ppermute x1, waiting for transfers between devices, local(): return lax.ppermute(block, whole, route).T  6.28 us
    unnamed x5, local copies, waits for them, and re-layouts  4.09 us
    ppermute x1, starting transfers between devices, local(): return lax.ppermute(block, whole, route).T  3.25 us
    ppermute x1, starting transfers between devices, local(): other_pair = lax.ppermute(pair, 'x', [(i, i ^ FAR) for i in range(4)])  3.05 us
    ppermute x1, starting transfers between devices, local(): other_packed = lax.ppermute(packed, 'x', [(i, i ^ NEAR) for i in range(4)])  2.74 us
  transfers between devices with their start and end apart: 10, of which 4 were waited for; matrix products, arithmetic and copies ran while one was open for 1% of the time, Pallas kernels for 5%

profile of v11, /device:TPU:6, one launch (start us, length us, event | category | flops | bytes accessed | tf_op | source)
XLA Modules:
  0.0 84.4 jit_solution(3172564912990428544)
XLA Ops:
  0.0 1.9 %select.1 = (bf16[64,1536]{1,0:T(8,128)(2,1)}, bf16[64,768]{1,0:T(8,128)(2,1)}, bf16[64,768]{1,0:T(8,128)(2,1)}, bf16[64,768]{1,0:T(8,128)(2,1)}, bf16[64,768]{1,0:T(8,128)(2,1)}) custom-call(s32[16]{0:T(128)} %send_ref.1, bf16[8,64,192]{2,1,0:T(8,128)(2,1)} %basis_ref.1), custom_call_target="tpu_custom_call" | custom-call | tf_op jit(solution)/shard_map/select/pallas_call | solution.py:125
  1.9 4.3 %collective-permute-start.1 = (bf16[64,768]{1,0:T(8,128)(2,1)}, bf16[64,768]{1,0:T(8,128)(2,1)S(1)}, u32[]{:S(2)}, u32[]{:S(2)}) collective-permute-start(bf16[64,768]{1,0:T(8,128)(2,1)} %get-tuple-element.18), channel_id=1, source_target_pairs={{496,0},{0,16},{16,32},{32,48},{48,64},{64,80},{80,96},{96,112},{1... | collective-permute-start | bytes 294920 | tf_op jit(solution)/shard_map/ppermute | solution.py:136
  6.1 8.4 %collective-permute-start.2 = (bf16[64,768]{1,0:T(8,128)(2,1)}, bf16[64,768]{1,0:T(8,128)(2,1)S(1)}, u32[]{:S(2)}, u32[]{:S(2)}) collective-permute-start(bf16[64,768]{1,0:T(8,128)(2,1)} %get-tuple-element.19), channel_id=1, source_target_pairs={{16,0},{32,16},{48,32},{64,48},{80,64},{96,80},{112,96},{128,112},... | collective-permute-start | bytes 294920 | tf_op jit(solution)/shard_map/ppermute | solution.py:136
  14.6 1.9 %collective-permute-start.3 = (bf16[64,768]{1,0:T(8,128)(2,1)}, bf16[64,768]{1,0:T(8,128)(2,1)S(1)}, u32[]{:S(2)}, u32[]{:S(2)}) collective-permute-start(bf16[64,768]{1,0:T(8,128)(2,1)} %get-tuple-element.20), channel_id=1, source_target_pairs={{480,0},{496,16},{0,32},{16,48},{32,64},{48,80},{64,96},{80,112},{... | collective-permute-start | bytes 294920 | tf_op jit(solution)/shard_map/ppermute | solution.py:136
  16.5 6.9 %collective-permute-start.4 = (bf16[64,768]{1,0:T(8,128)(2,1)}, bf16[64,768]{1,0:T(8,128)(2,1)S(1)}, u32[]{:S(2)}, u32[]{:S(2)}) collective-permute-start(bf16[64,768]{1,0:T(8,128)(2,1)} %get-tuple-element.21), channel_id=1, source_target_pairs={{32,0},{48,16},{64,32},{80,48},{96,64},{112,80},{128,96},{144,112}... | collective-permute-start | bytes 294920 | tf_op jit(solution)/shard_map/ppermute | solution.py:136
  23.4 2.7 %collective-permute-start = (bf16[64,1536]{1,0:T(8,128)(2,1)}, bf16[64,1536]{1,0:T(8,128)(2,1)S(1)}, u32[]{:S(2)}, u32[]{:S(2)}) collective-permute-start(bf16[64,1536]{1,0:T(8,128)(2,1)} %get-tuple-element.15.packed_ref), channel_id=1, source_target_pairs={{0,2},{2,0},{4,6},{6,4},{1,3},{3,1},{5,7},{7,5},{8,10},{10,8},{12,... | collective-permute-start | bytes 589832 | tf_op jit(solution)/shard_map/ppermute | solution.py:154
  26.9 0.8 convert_select_fusion.table_ref
  27.6 2.6 %copy-done = bf16[56,192,192]{2,1,0:T(8,128)(2,1)S(1)} copy-done((bf16[56,192,192]{2,1,0:T(8,128)(2,1)S(1)}, bf16[56,192,192]{2,1,0:T(8,128)(2,1)}, u32[]{:S(2)}) %copy-start) | copy-done | bytes 4128792
  30.2 0.9 %copy-done.1 = bf16[64,1536]{1,0:T(8,128)(2,1)S(1)} copy-done((bf16[64,1536]{1,0:T(8,128)(2,1)S(1)}, bf16[64,1536]{1,0:T(8,128)(2,1)}, u32[]{:S(2)}) %copy-start.1) | copy-done | bytes 196632
  31.1 0.4 stage.1
  31.5 2.7 %blocks.1.products_ref.rest_0_ = bf16[64,1536]{1,0:T(8,128)(2,1)S(1)} custom-call(f32[8,56]{1,0:T(8,128)S(1)} %convert_select_fusion.table_ref, bf16[64,1536]{1,0:T(8,128)(2,1)S(1)} %get-tuple-element.16.own_ref, bf16[56,192,192]{2,1,0:T(8,128)(2,1)S(1)} %get-tuple-element.17.blocks_ref, bf16[64,768]{1,0:T(8,128)(2,1)S(1)} %collective-permute-done.1.rest_0_, ...), custom_call_target="tpu_custom_call" | custom-call | tf_op jit(solution)/shard_map/blocks/pallas_call | solution.py:155
  34.3 8.2 %collective-permute-start.7 = (bf16[64,1536]{1,0:T(8,128)(2,1)S(1)}, bf16[64,1536]{1,0:T(8,128)(2,1)S(1)}, u32[]{:S(2)}, u32[]{:S(2)}) collective-permute-start(bf16[64,1536]{1,0:T(8,128)(2,1)S(1)} %blocks.1.products_ref.rest_0_), channel_id=1, source_target_pairs={{0,8},{8,0},{1,9},{9,1},{2,10},{10,2},{3,11},{11,3},{4,12},{12,4},... | collective-permute-start | bytes 589832 | tf_op jit(solution)/shard_map/ppermute | solution.py:176
  42.5 3.0 %collective-permute-start.5 = (bf16[128,1536]{1,0:T(8,128)(2,1)S(1)}, bf16[128,1536]{1,0:T(8,128)(2,1)S(1)}, u32[]{:S(2)}, u32[]{:S(2)}) collective-permute-start(bf16[128,1536]{1,0:T(8,128)(2,1)S(1)} %join.1.pair_ref), channel_id=1, source_target_pairs={{0,6},{2,4},{4,2},{6,0},{1,7},{3,5},{5,3},{7,1},{8,14},{10,12},{12... | collective-permute-start | bytes 1179656 | tf_op jit(solution)/shard_map/ppermute | solution.py:178
  45.7 1.9 %collective-permute-start.6 = (bf16[64,1536]{1,0:T(8,128)(2,1)S(1)}, bf16[64,1536]{1,0:T(8,128)(2,1)S(1)}, u32[]{:S(2)}, u32[]{:S(2)}) collective-permute-start(bf16[64,1536]{1,0:T(8,128)(2,1)S(1)} %blocks.1.products_ref.rest_0_), channel_id=1, source_target_pairs={{0,1},{1,0},{2,3},{3,2},{4,5},{5,4},{6,7},{7,6},{8,9},{9,8},{10,11... | collective-permute-start | bytes 589832 | tf_op jit(solution)/shard_map/ppermute | solution.py:177
  47.6 0.9 %own_tile.1.rest_4_ = bf16[32,16,128]{2,1,0:T(8,128)(2,1)S(1)} custom-call(s32[3]{0:T(128)S(1)} %pad_add_fusion.place_ref, bf16[128,1536]{1,0:T(8,128)(2,1)S(1)} %join.1.pair_ref, bf16[64,1536]{1,0:T(8,128)(2,1)S(1)} %blocks.1.products_ref.rest_0_), custom_call_target="tpu_custom_call" | custom-call | flops 16777216 | bytes 1048576 | tf_op jit(solution)/shard_map/own_tile/pallas_call | solution.py:181
  48.5 2.0 %collective-permute-done.7.rest_2_ = bf16[64,1536]{1,0:T(8,128)(2,1)S(1)} collective-permute-done((bf16[64,1536]{1,0:T(8,128)(2,1)S(1)}, bf16[64,1536]{1,0:T(8,128)(2,1)S(1)}, u32[]{:S(2)}, u32[]{:S(2)}) %collective-permute-start.7) | collective-permute-done | bytes 196640 | tf_op jit(solution)/shard_map/ppermute | solution.py:176
  50.5 1.9 %collective-permute-start.8 = (bf16[64,1536]{1,0:T(8,128)(2,1)S(1)}, bf16[64,1536]{1,0:T(8,128)(2,1)S(1)}, u32[]{:S(2)}, u32[]{:S(2)}) collective-permute-start(bf16[64,1536]{1,0:T(8,128)(2,1)S(1)} %collective-permute-done.7.rest_2_), channel_id=1, source_target_pairs={{0,1},{1,0},{2,3},{3,2},{4,5},{5,4},{6,7},{7,6},{8,9},{9,8},{10,11... | collective-permute-start | bytes 589832 | tf_op jit(solution)/shard_map/ppermute | solution.py:191
  52.4 1.4 %collective-permute-done.8.rest_3_ = bf16[64,1536]{1,0:T(8,128)(2,1)S(1)} collective-permute-done((bf16[64,1536]{1,0:T(8,128)(2,1)S(1)}, bf16[64,1536]{1,0:T(8,128)(2,1)S(1)}, u32[]{:S(2)}, u32[]{:S(2)}) %collective-permute-start.8) | collective-permute-done | bytes 196640 | tf_op jit(solution)/shard_map/ppermute | solution.py:191
  53.8 1.3 %collective-permute-done.5.other_pair_ref = bf16[128,1536]{1,0:T(8,128)(2,1)S(1)} collective-permute-done((bf16[128,1536]{1,0:T(8,128)(2,1)S(1)}, bf16[128,1536]{1,0:T(8,128)(2,1)S(1)}, u32[]{:S(2)}, u32[]{:S(2)}) %collective-permute-start.5) | collective-permute-done | bytes 393248 | tf_op jit(solution)/shard_map/ppermute | solution.py:178
  55.1 1.1 %tile.1 = bf16[32,16,128]{2,1,0:T(8,128)(2,1)S(1)} custom-call(s32[3]{0:T(128)S(1)} %pad_add_fusion.place_ref, bf16[128,1536]{1,0:T(8,128)(2,1)S(1)} %join.1.pair_ref, bf16[128,1536]{1,0:T(8,128)(2,1)S(1)} %collective-permute-done.5.other_pair_ref, bf16[64,1536]{1,0:T(8,128)(2,1)S(1)} %blocks.1.products_ref.rest_0_, ...), custom_call_target="tpu_custom_call", output_to_operand_aliasing={{}: (7, {})} | custom-call | tf_op jit(solution)/shard_map/tile/pallas_call | solution.py:192
  56.2 18.0 %all_to_all.5.parts_ref = bf16[32,16,128]{2,1,0:T(8,128)(2,1)S(1)} all-to-all(bf16[32,16,128]{2,1,0:T(8,128)(2,1)S(1)} %tile.1), channel_id=1, replica_groups=mesh['y'=8,'z_lo'=4,'z_hi'=2,'x'=4,'core'=2] {'y','z_lo'}, dimensions={0} | all-to-all | bytes 262144 | tf_op jit(solution)/shard_map/all_to_all | solution.py:201
  74.3 3.2 %collective-permute-start.9 = (f32[32,64]{1,0:T(8,128)S(1)}, f32[32,64]{1,0:T(8,128)S(1)}, u32[]{:S(2)}, u32[]{:S(2)}) collective-permute-start(f32[32,64]{1,0:T(8,128)S(1)} %sum.1), channel_id=1, source_target_pairs={{0,0},{1,1},{2,64},{3,65},{4,128},{5,129},{6,192},{7,193},{8,8},{9... | collective-permute-start | bytes 24584 | tf_op jit(solution)/shard_map/ppermute | solution.py:216
  77.6 6.3 %collective-permute-done.9 = f32[32,64]{1,0:T(8,128)S(1)} collective-permute-done((f32[32,64]{1,0:T(8,128)S(1)}, f32[32,64]{1,0:T(8,128)S(1)}, u32[]{:S(2)}, u32[]{:S(2)}) %collective-permute-start.9) | collective-permute-done | bytes 8224 | tf_op jit(solution)/shard_map/ppermute | solution.py:216
  83.8 0.6 copy.12
  (13 shorter events, 0.2 us)
Async XLA Ops:
  1.9 29.6 %collective-permute-start.1 = (bf16[64,768]{1,0:T(8,128)(2,1)}, bf16[64,768]{1,0:T(8,128)(2,1)S(1)}, u32[]{:S(2)}, u32[]{:S(2)}) collective-permute-start(bf16[64,768]{1,0:T(8,128)(2,1)} %get-tuple-element.18), channel_id=1, source_target_pairs={{496,0},{0,16},{16,32},{32,48},{48,64},{64,80},{80,96},{96,112},{1... | collective-permute-start | bytes 294920 | tf_op jit(solution)/shard_map/ppermute | solution.py:136
  6.1 25.4 %collective-permute-start.2 = (bf16[64,768]{1,0:T(8,128)(2,1)}, bf16[64,768]{1,0:T(8,128)(2,1)S(1)}, u32[]{:S(2)}, u32[]{:S(2)}) collective-permute-start(bf16[64,768]{1,0:T(8,128)(2,1)} %get-tuple-element.19), channel_id=1, source_target_pairs={{16,0},{32,16},{48,32},{64,48},{80,64},{96,80},{112,96},{128,112},... | collective-permute-start | bytes 294920 | tf_op jit(solution)/shard_map/ppermute | solution.py:136
  14.6 16.9 %collective-permute-start.3 = (bf16[64,768]{1,0:T(8,128)(2,1)}, bf16[64,768]{1,0:T(8,128)(2,1)S(1)}, u32[]{:S(2)}, u32[]{:S(2)}) collective-permute-start(bf16[64,768]{1,0:T(8,128)(2,1)} %get-tuple-element.20), channel_id=1, source_target_pairs={{480,0},{496,16},{0,32},{16,48},{32,64},{48,80},{64,96},{80,112},{... | collective-permute-start | bytes 294920 | tf_op jit(solution)/shard_map/ppermute | solution.py:136
  16.5 15.0 %collective-permute-start.4 = (bf16[64,768]{1,0:T(8,128)(2,1)}, bf16[64,768]{1,0:T(8,128)(2,1)S(1)}, u32[]{:S(2)}, u32[]{:S(2)}) collective-permute-start(bf16[64,768]{1,0:T(8,128)(2,1)} %get-tuple-element.21), channel_id=1, source_target_pairs={{32,0},{48,16},{64,32},{80,48},{96,64},{112,80},{128,96},{144,112}... | collective-permute-start | bytes 294920 | tf_op jit(solution)/shard_map/ppermute | solution.py:136
  23.4 19.0 %collective-permute-start = (bf16[64,1536]{1,0:T(8,128)(2,1)}, bf16[64,1536]{1,0:T(8,128)(2,1)S(1)}, u32[]{:S(2)}, u32[]{:S(2)}) collective-permute-start(bf16[64,1536]{1,0:T(8,128)(2,1)} %get-tuple-element.15.packed_ref), channel_id=1, source_target_pairs={{0,2},{2,0},{4,6},{6,4},{1,3},{3,1},{5,7},{7,5},{8,10},{10,8},{12,... | collective-permute-start | bytes 589832 | tf_op jit(solution)/shard_map/ppermute | solution.py:154
  27.6 2.6 %copy-start = (bf16[56,192,192]{2,1,0:T(8,128)(2,1)S(1)}, bf16[56,192,192]{2,1,0:T(8,128)(2,1)}, u32[]{:S(2)}) copy-start(bf16[56,192,192]{2,1,0:T(8,128)(2,1)} %blocks_ref.1) | copy-start | bytes 12386308
  30.2 0.9 %copy-start.1 = (bf16[64,1536]{1,0:T(8,128)(2,1)S(1)}, bf16[64,1536]{1,0:T(8,128)(2,1)}, u32[]{:S(2)}) copy-start(bf16[64,1536]{1,0:T(8,128)(2,1)} %get-tuple-element.15.packed_ref) | copy-start | bytes 589828
  34.3 16.2 %collective-permute-start.7 = (bf16[64,1536]{1,0:T(8,128)(2,1)S(1)}, bf16[64,1536]{1,0:T(8,128)(2,1)S(1)}, u32[]{:S(2)}, u32[]{:S(2)}) collective-permute-start(bf16[64,1536]{1,0:T(8,128)(2,1)S(1)} %blocks.1.products_ref.rest_0_), channel_id=1, source_target_pairs={{0,8},{8,0},{1,9},{9,1},{2,10},{10,2},{3,11},{11,3},{4,12},{12,4},... | collective-permute-start | bytes 589832 | tf_op jit(solution)/shard_map/ppermute | solution.py:176
  42.5 12.6 %collective-permute-start.5 = (bf16[128,1536]{1,0:T(8,128)(2,1)S(1)}, bf16[128,1536]{1,0:T(8,128)(2,1)S(1)}, u32[]{:S(2)}, u32[]{:S(2)}) collective-permute-start(bf16[128,1536]{1,0:T(8,128)(2,1)S(1)} %join.1.pair_ref), channel_id=1, source_target_pairs={{0,6},{2,4},{4,2},{6,0},{1,7},{3,5},{5,3},{7,1},{8,14},{10,12},{12... | collective-permute-start | bytes 1179656 | tf_op jit(solution)/shard_map/ppermute | solution.py:178
  45.7 6.7 %collective-permute-start.6 = (bf16[64,1536]{1,0:T(8,128)(2,1)S(1)}, bf16[64,1536]{1,0:T(8,128)(2,1)S(1)}, u32[]{:S(2)}, u32[]{:S(2)}) collective-permute-start(bf16[64,1536]{1,0:T(8,128)(2,1)S(1)} %blocks.1.products_ref.rest_0_), channel_id=1, source_target_pairs={{0,1},{1,0},{2,3},{3,2},{4,5},{5,4},{6,7},{7,6},{8,9},{9,8},{10,11... | collective-permute-start | bytes 589832 | tf_op jit(solution)/shard_map/ppermute | solution.py:177
  50.5 3.3 %collective-permute-start.8 = (bf16[64,1536]{1,0:T(8,128)(2,1)S(1)}, bf16[64,1536]{1,0:T(8,128)(2,1)S(1)}, u32[]{:S(2)}, u32[]{:S(2)}) collective-permute-start(bf16[64,1536]{1,0:T(8,128)(2,1)S(1)} %collective-permute-done.7.rest_2_), channel_id=1, source_target_pairs={{0,1},{1,0},{2,3},{3,2},{4,5},{5,4},{6,7},{7,6},{8,9},{9,8},{10,11... | collective-permute-start | bytes 589832 | tf_op jit(solution)/shard_map/ppermute | solution.py:191
  74.3 9.5 %collective-permute-start.9 = (f32[32,64]{1,0:T(8,128)S(1)}, f32[32,64]{1,0:T(8,128)S(1)}, u32[]{:S(2)}, u32[]{:S(2)}) collective-permute-start(f32[32,64]{1,0:T(8,128)S(1)} %sum.1), channel_id=1, source_target_pairs={{0,0},{1,1},{2,64},{3,65},{4,128},{5,129},{6,192},{7,193},{8,8},{9... | collective-permute-start | bytes 24584 | tf_op jit(solution)/shard_map/ppermute | solution.py:216

commit v12 on v11

--- a/solution.py
+++ b/solution.py
@@ -41,9 +41,8 @@
         pack_pair(basis_ref[2 * pair], basis_ref[2 * pair + 1], packed_ref, 384 * pair)
 
 
-def stage_kernel(blocks_ref, packed_ref, blocks_out_ref, packed_out_ref):
+def stage_kernel(blocks_ref, blocks_out_ref):
     blocks_out_ref[...] = blocks_ref[...]
-    packed_out_ref[...] = packed_ref[...]
 
 
 def join_kernel(own_ref, other_ref, pair_ref):
@@ -128,6 +127,7 @@
         + [shape((WIDTH, GMAX * DOFS), jnp.bfloat16)] * NEIGH,
         in_specs=[SMEM, VMEM],
         out_specs=[VMEM] * (1 + NEIGH),
+        compiler_params=pltpu.CompilerParams(vmem_limit_bytes=16 << 20),
         name="select",
     )(send_list, basis_vectors)
     arriving = []
@@ -135,18 +135,15 @@
         route = [((i - offset) % parts, i) for i in range(parts)]
         arriving.append(lax.ppermute(block, mesh_axes, route))
     swap = [(0, 1), (1, 0)]
-    blocks, own = pl.pallas_call(
+    blocks = pl.pallas_call(
         stage_kernel,
-        out_shape=[
-            shape(stiffness_blocks.shape, jnp.bfloat16),
-            shape((WIDTH, PACKED), jnp.bfloat16),
-        ],
-        in_specs=[VMEM] * 2,
-        out_specs=[VMEM] * 2,
+        out_shape=shape(stiffness_blocks.shape, jnp.bfloat16),
+        in_specs=[VMEM],
+        out_specs=VMEM,
         compiler_params=pltpu.CompilerParams(vmem_limit_bytes=24 << 20),
         cost_estimate=pl.CostEstimate(flops=0, bytes_accessed=12 << 20, transcendentals=0),
         name="stage",
-    )(stiffness_blocks, packed)
+    )(stiffness_blocks)
     line = lax.broadcasted_iota(jnp.int32, (8, CAP), 0)
     listed = jnp.where(line == 0, block_rows[None], block_columns[None])
     listed = jnp.where(line == 2, block_counts[0], listed).astype(jnp.float32)
@@ -163,7 +160,7 @@
         ],
         compiler_params=pltpu.CompilerParams(vmem_limit_bytes=24 << 20),
         name="blocks",
-    )(table, own, blocks, *arriving)
+    )(table, packed, blocks, *arriving)
     other_packed, _ = lax.optimization_barrier((other_packed, products))
     pair = pl.pallas_call(
         join_kernel,
@@ -172,7 +169,7 @@
         out_specs=VMEM,
         compiler_params=pltpu.CompilerParams(vmem_limit_bytes=8 << 20),
         name="join",
-    )(own, other_packed)
+    )(packed, other_packed)
     over_z = lax.ppermute(products, "z_hi", swap)
     over_core = lax.ppermute(products, "core", swap)
     other_pair = lax.ppermute(pair, "x", [(i, i ^ FAR) for i in range(4)])

time: 84.9 us -> 84.5 us (level)
  Pallas kernels: 7.06 us -> 5.92 us
    pallas_call x1, Pallas kernels: 1.85 us -> 0.68 us  [local(): pl.pallas_call(select_kernel, out_shape=[shape((WIDTH, PACKED), jnp.bfloa...]
    unnamed x5 -> x7, local copies, waits for them, and re-layouts: 4.09 us -> 4.77 us
where the time goes in v12:
time: 84.5 us; the launch traced here: 84 us
  starting transfers between devices  42.6 us (50%)
  blocking collectives  18 us (21%)
  waiting for transfers between devices  11 us (13%)
  Pallas kernels  5.92 us (7%)
  local copies, waits for them, and re-layouts  4.77 us (6%)
  other arithmetic  0.85 us (1%)
    ppermute x4, starting transfers between devices, local(): arriving.append(lax.ppermute(block, mesh_axes, route))  21.6 us
    all_to_all x1, blocking collectives, local(): shares = lax.all_to_all(chunks, mesh_axes, 0, 0, tiled=True)  18 us
    ppermute x1, starting transfers between devices, local(): over_z = lax.ppermute(products, 'z_hi', swap)  8.22 us
    ppermute x1, waiting for transfers between devices, local(): return lax.ppermute(block, whole, route).T  6.28 us
    unnamed x7, local copies, waits for them, and re-layouts  4.77 us
    ppermute x1, starting transfers between devices, local(): return lax.ppermute(block, whole, route).T  3.25 us
    ppermute x1, starting transfers between devices, local(): other_pair = lax.ppermute(pair, 'x', [(i, i ^ FAR) for i in range(4)])  3.05 us
    pallas_call x1, Pallas kernels, local(): pl.pallas_call(block_kernel, out_shape=shape((WIDTH, PACKED), jnp.bfloat1...  2.75 us
  transfers between devices with their start and end apart: 10, of which 4 were waited for; matrix products, arithmetic and copies ran while one was open for 1% of the time, Pallas kernels for 5%

profile of v12, /device:TPU:6, one launch (start us, length us, event | category | flops | bytes accessed | tf_op | source)
XLA Modules:
  0.0 84.0 jit_solution(3090285318419170204)
XLA Ops:
  0.0 0.9 %copy-done.1 = bf16[8,64,192]{2,1,0:T(8,128)(2,1)S(1)} copy-done((bf16[8,64,192]{2,1,0:T(8,128)(2,1)S(1)}, bf16[8,64,192]{2,1,0:T(8,128)(2,1)}, u32[]{:S(2)}) %copy-start.1) | copy-done | bytes 196632
  1.0 0.7 copy-done.2
  1.6 0.7 select.1
  2.3 4.3 %collective-permute-start.1 = (bf16[64,768]{1,0:T(8,128)(2,1)S(1)}, bf16[64,768]{1,0:T(8,128)(2,1)S(1)}, u32[]{:S(2)}, u32[]{:S(2)}) collective-permute-start(bf16[64,768]{1,0:T(8,128)(2,1)S(1)} %get-tuple-element.14), channel_id=1, source_target_pairs={{496,0},{0,16},{16,32},{32,48},{48,64},{64,80},{80,96},{96,112},{1... | collective-permute-start | bytes 294920 | tf_op jit(solution)/shard_map/ppermute | solution.py:136
  6.6 8.4 %collective-permute-start.2 = (bf16[64,768]{1,0:T(8,128)(2,1)S(1)}, bf16[64,768]{1,0:T(8,128)(2,1)S(1)}, u32[]{:S(2)}, u32[]{:S(2)}) collective-permute-start(bf16[64,768]{1,0:T(8,128)(2,1)S(1)} %get-tuple-element.15), channel_id=1, source_target_pairs={{16,0},{32,16},{48,32},{64,48},{80,64},{96,80},{112,96},{128,112},... | collective-permute-start | bytes 294920 | tf_op jit(solution)/shard_map/ppermute | solution.py:136
  15.0 1.9 %collective-permute-start.3 = (bf16[64,768]{1,0:T(8,128)(2,1)S(1)}, bf16[64,768]{1,0:T(8,128)(2,1)S(1)}, u32[]{:S(2)}, u32[]{:S(2)}) collective-permute-start(bf16[64,768]{1,0:T(8,128)(2,1)S(1)} %get-tuple-element.16), channel_id=1, source_target_pairs={{480,0},{496,16},{0,32},{16,48},{32,64},{48,80},{64,96},{80,112},{... | collective-permute-start | bytes 294920 | tf_op jit(solution)/shard_map/ppermute | solution.py:136
  17.0 6.9 %collective-permute-start.4 = (bf16[64,768]{1,0:T(8,128)(2,1)S(1)}, bf16[64,768]{1,0:T(8,128)(2,1)S(1)}, u32[]{:S(2)}, u32[]{:S(2)}) collective-permute-start(bf16[64,768]{1,0:T(8,128)(2,1)S(1)} %get-tuple-element.17), channel_id=1, source_target_pairs={{32,0},{48,16},{64,32},{80,48},{96,64},{112,80},{128,96},{144,112}... | collective-permute-start | bytes 294920 | tf_op jit(solution)/shard_map/ppermute | solution.py:136
  23.9 2.7 %collective-permute-start = (bf16[64,1536]{1,0:T(8,128)(2,1)S(1)}, bf16[64,1536]{1,0:T(8,128)(2,1)S(1)}, u32[]{:S(2)}, u32[]{:S(2)}) collective-permute-start(bf16[64,1536]{1,0:T(8,128)(2,1)S(1)} %get-tuple-element.13.own_ref), channel_id=1, source_target_pairs={{0,2},{2,0},{4,6},{6,4},{1,3},{3,1},{5,7},{7,5},{8,10},{10,8},{12,... | collective-permute-start | bytes 589832 | tf_op jit(solution)/shard_map/ppermute | solution.py:151
  27.3 0.8 convert_select_fusion.table_ref
  28.1 2.6 %copy-done = bf16[56,192,192]{2,1,0:T(8,128)(2,1)S(1)} copy-done((bf16[56,192,192]{2,1,0:T(8,128)(2,1)S(1)}, bf16[56,192,192]{2,1,0:T(8,128)(2,1)}, u32[]{:S(2)}) %copy-start) | copy-done | bytes 4128792
  31.0 2.8 %blocks.1.products_ref.rest_0_ = bf16[64,1536]{1,0:T(8,128)(2,1)S(1)} custom-call(f32[8,56]{1,0:T(8,128)S(1)} %convert_select_fusion.table_ref, bf16[64,1536]{1,0:T(8,128)(2,1)S(1)} %get-tuple-element.13.own_ref, bf16[56,192,192]{2,1,0:T(8,128)(2,1)S(1)} %stage.1.blocks_ref, bf16[64,768]{1,0:T(8,128)(2,1)S(1)} %collective-permute-done.1.rest_0_, ...), custom_call_target="tpu_custom_call" | custom-call | tf_op jit(solution)/shard_map/blocks/pallas_call | solution.py:152
  33.8 8.2 %collective-permute-start.7 = (bf16[64,1536]{1,0:T(8,128)(2,1)S(1)}, bf16[64,1536]{1,0:T(8,128)(2,1)S(1)}, u32[]{:S(2)}, u32[]{:S(2)}) collective-permute-start(bf16[64,1536]{1,0:T(8,128)(2,1)S(1)} %blocks.1.products_ref.rest_0_), channel_id=1, source_target_pairs={{0,8},{8,0},{1,9},{9,1},{2,10},{10,2},{3,11},{11,3},{4,12},{12,4},... | collective-permute-start | bytes 589832 | tf_op jit(solution)/shard_map/ppermute | solution.py:173
  42.1 3.0 %collective-permute-start.5 = (bf16[128,1536]{1,0:T(8,128)(2,1)S(1)}, bf16[128,1536]{1,0:T(8,128)(2,1)S(1)}, u32[]{:S(2)}, u32[]{:S(2)}) collective-permute-start(bf16[128,1536]{1,0:T(8,128)(2,1)S(1)} %join.1.pair_ref), channel_id=1, source_target_pairs={{0,6},{2,4},{4,2},{6,0},{1,7},{3,5},{5,3},{7,1},{8,14},{10,12},{12... | collective-permute-start | bytes 1179656 | tf_op jit(solution)/shard_map/ppermute | solution.py:175
  45.2 1.9 %collective-permute-start.6 = (bf16[64,1536]{1,0:T(8,128)(2,1)S(1)}, bf16[64,1536]{1,0:T(8,128)(2,1)S(1)}, u32[]{:S(2)}, u32[]{:S(2)}) collective-permute-start(bf16[64,1536]{1,0:T(8,128)(2,1)S(1)} %blocks.1.products_ref.rest_0_), channel_id=1, source_target_pairs={{0,1},{1,0},{2,3},{3,2},{4,5},{5,4},{6,7},{7,6},{8,9},{9,8},{10,11... | collective-permute-start | bytes 589832 | tf_op jit(solution)/shard_map/ppermute | solution.py:174
  47.1 0.9 %own_tile.1.rest_4_ = bf16[32,16,128]{2,1,0:T(8,128)(2,1)S(1)} custom-call(s32[3]{0:T(128)S(1)} %pad_add_fusion.place_ref, bf16[128,1536]{1,0:T(8,128)(2,1)S(1)} %join.1.pair_ref, bf16[64,1536]{1,0:T(8,128)(2,1)S(1)} %blocks.1.products_ref.rest_0_), custom_call_target="tpu_custom_call" | custom-call | flops 16777216 | bytes 1048576 | tf_op jit(solution)/shard_map/own_tile/pallas_call | solution.py:178
  48.0 2.0 %collective-permute-done.7.rest_2_ = bf16[64,1536]{1,0:T(8,128)(2,1)S(1)} collective-permute-done((bf16[64,1536]{1,0:T(8,128)(2,1)S(1)}, bf16[64,1536]{1,0:T(8,128)(2,1)S(1)}, u32[]{:S(2)}, u32[]{:S(2)}) %collective-permute-start.7) | collective-permute-done | bytes 196640 | tf_op jit(solution)/shard_map/ppermute | solution.py:173
  50.0 1.9 %collective-permute-start.8 = (bf16[64,1536]{1,0:T(8,128)(2,1)S(1)}, bf16[64,1536]{1,0:T(8,128)(2,1)S(1)}, u32[]{:S(2)}, u32[]{:S(2)}) collective-permute-start(bf16[64,1536]{1,0:T(8,128)(2,1)S(1)} %collective-permute-done.7.rest_2_), channel_id=1, source_target_pairs={{0,1},{1,0},{2,3},{3,2},{4,5},{5,4},{6,7},{7,6},{8,9},{9,8},{10,11... | collective-permute-start | bytes 589832 | tf_op jit(solution)/shard_map/ppermute | solution.py:188
  51.9 1.4 %collective-permute-done.8.rest_3_ = bf16[64,1536]{1,0:T(8,128)(2,1)S(1)} collective-permute-done((bf16[64,1536]{1,0:T(8,128)(2,1)S(1)}, bf16[64,1536]{1,0:T(8,128)(2,1)S(1)}, u32[]{:S(2)}, u32[]{:S(2)}) %collective-permute-start.8) | collective-permute-done | bytes 196640 | tf_op jit(solution)/shard_map/ppermute | solution.py:188
  53.3 1.3 %collective-permute-done.5.other_pair_ref = bf16[128,1536]{1,0:T(8,128)(2,1)S(1)} collective-permute-done((bf16[128,1536]{1,0:T(8,128)(2,1)S(1)}, bf16[128,1536]{1,0:T(8,128)(2,1)S(1)}, u32[]{:S(2)}, u32[]{:S(2)}) %collective-permute-start.5) | collective-permute-done | bytes 393248 | tf_op jit(solution)/shard_map/ppermute | solution.py:175
  54.6 1.1 %tile.1 = bf16[32,16,128]{2,1,0:T(8,128)(2,1)S(1)} custom-call(s32[3]{0:T(128)S(1)} %pad_add_fusion.place_ref, bf16[128,1536]{1,0:T(8,128)(2,1)S(1)} %join.1.pair_ref, bf16[128,1536]{1,0:T(8,128)(2,1)S(1)} %collective-permute-done.5.other_pair_ref, bf16[64,1536]{1,0:T(8,128)(2,1)S(1)} %blocks.1.products_ref.rest_0_, ...), custom_call_target="tpu_custom_call", output_to_operand_aliasing={{}: (7, {})} | custom-call | tf_op jit(solution)/shard_map/tile/pallas_call | solution.py:189
  55.8 18.0 %all_to_all.5.parts_ref = bf16[32,16,128]{2,1,0:T(8,128)(2,1)S(1)} all-to-all(bf16[32,16,128]{2,1,0:T(8,128)(2,1)S(1)} %tile.1), channel_id=1, replica_groups=mesh['y'=8,'z_lo'=4,'z_hi'=2,'x'=4,'core'=2] {'y','z_lo'}, dimensions={0} | all-to-all | bytes 262144 | tf_op jit(solution)/shard_map/all_to_all | solution.py:198
  73.8 3.2 %collective-permute-start.9 = (f32[32,64]{1,0:T(8,128)S(1)}, f32[32,64]{1,0:T(8,128)S(1)}, u32[]{:S(2)}, u32[]{:S(2)}) collective-permute-start(f32[32,64]{1,0:T(8,128)S(1)} %sum.1), channel_id=1, source_target_pairs={{0,0},{1,1},{2,64},{3,65},{4,128},{5,129},{6,192},{7,193},{8,8},{9... | collective-permute-start | bytes 24584 | tf_op jit(solution)/shard_map/ppermute | solution.py:213
  77.1 6.3 %collective-permute-done.9 = f32[32,64]{1,0:T(8,128)S(1)} collective-permute-done((f32[32,64]{1,0:T(8,128)S(1)}, f32[32,64]{1,0:T(8,128)S(1)}, u32[]{:S(2)}, u32[]{:S(2)}) %collective-permute-start.9) | collective-permute-done | bytes 8224 | tf_op jit(solution)/shard_map/ppermute | solution.py:213
  83.4 0.6 copy.12
  (15 shorter events, 0.6 us)
Async XLA Ops:
  0.0 0.9 %copy-start.1 = (bf16[8,64,192]{2,1,0:T(8,128)(2,1)S(1)}, bf16[8,64,192]{2,1,0:T(8,128)(2,1)}, u32[]{:S(2)}) copy-start(bf16[8,64,192]{2,1,0:T(8,128)(2,1)} %basis_ref.1) | copy-start | bytes 589828
  1.0 0.7 copy-start.2
  2.3 28.7 %collective-permute-start.1 = (bf16[64,768]{1,0:T(8,128)(2,1)S(1)}, bf16[64,768]{1,0:T(8,128)(2,1)S(1)}, u32[]{:S(2)}, u32[]{:S(2)}) collective-permute-start(bf16[64,768]{1,0:T(8,128)(2,1)S(1)} %get-tuple-element.14), channel_id=1, source_target_pairs={{496,0},{0,16},{16,32},{32,48},{48,64},{64,80},{80,96},{96,112},{1... | collective-permute-start | bytes 294920 | tf_op jit(solution)/shard_map/ppermute | solution.py:136
  6.6 24.4 %collective-permute-start.2 = (bf16[64,768]{1,0:T(8,128)(2,1)S(1)}, bf16[64,768]{1,0:T(8,128)(2,1)S(1)}, u32[]{:S(2)}, u32[]{:S(2)}) collective-permute-start(bf16[64,768]{1,0:T(8,128)(2,1)S(1)} %get-tuple-element.15), channel_id=1, source_target_pairs={{16,0},{32,16},{48,32},{64,48},{80,64},{96,80},{112,96},{128,112},... | collective-permute-start | bytes 294920 | tf_op jit(solution)/shard_map/ppermute | solution.py:136
  15.0 16.0 %collective-permute-start.3 = (bf16[64,768]{1,0:T(8,128)(2,1)S(1)}, bf16[64,768]{1,0:T(8,128)(2,1)S(1)}, u32[]{:S(2)}, u32[]{:S(2)}) collective-permute-start(bf16[64,768]{1,0:T(8,128)(2,1)S(1)} %get-tuple-element.16), channel_id=1, source_target_pairs={{480,0},{496,16},{0,32},{16,48},{32,64},{48,80},{64,96},{80,112},{... | collective-permute-start | bytes 294920 | tf_op jit(solution)/shard_map/ppermute | solution.py:136
  17.0 14.1 %collective-permute-start.4 = (bf16[64,768]{1,0:T(8,128)(2,1)S(1)}, bf16[64,768]{1,0:T(8,128)(2,1)S(1)}, u32[]{:S(2)}, u32[]{:S(2)}) collective-permute-start(bf16[64,768]{1,0:T(8,128)(2,1)S(1)} %get-tuple-element.17), channel_id=1, source_target_pairs={{32,0},{48,16},{64,32},{80,48},{96,64},{112,80},{128,96},{144,112}... | collective-permute-start | bytes 294920 | tf_op jit(solution)/shard_map/ppermute | solution.py:136
  23.9 18.1 %collective-permute-start = (bf16[64,1536]{1,0:T(8,128)(2,1)S(1)}, bf16[64,1536]{1,0:T(8,128)(2,1)S(1)}, u32[]{:S(2)}, u32[]{:S(2)}) collective-permute-start(bf16[64,1536]{1,0:T(8,128)(2,1)S(1)} %get-tuple-element.13.own_ref), channel_id=1, source_target_pairs={{0,2},{2,0},{4,6},{6,4},{1,3},{3,1},{5,7},{7,5},{8,10},{10,8},{12,... | collective-permute-start | bytes 589832 | tf_op jit(solution)/shard_map/ppermute | solution.py:151
  28.1 2.6 %copy-start = (bf16[56,192,192]{2,1,0:T(8,128)(2,1)S(1)}, bf16[56,192,192]{2,1,0:T(8,128)(2,1)}, u32[]{:S(2)}) copy-start(bf16[56,192,192]{2,1,0:T(8,128)(2,1)} %blocks_ref.1) | copy-start | bytes 12386308
  33.8 16.2 %collective-permute-start.7 = (bf16[64,1536]{1,0:T(8,128)(2,1)S(1)}, bf16[64,1536]{1,0:T(8,128)(2,1)S(1)}, u32[]{:S(2)}, u32[]{:S(2)}) collective-permute-start(bf16[64,1536]{1,0:T(8,128)(2,1)S(1)} %blocks.1.products_ref.rest_0_), channel_id=1, source_target_pairs={{0,8},{8,0},{1,9},{9,1},{2,10},{10,2},{3,11},{11,3},{4,12},{12,4},... | collective-permute-start | bytes 589832 | tf_op jit(solution)/shard_map/ppermute | solution.py:173
  42.1 12.6 %collective-permute-start.5 = (bf16[128,1536]{1,0:T(8,128)(2,1)S(1)}, bf16[128,1536]{1,0:T(8,128)(2,1)S(1)}, u32[]{:S(2)}, u32[]{:S(2)}) collective-permute-start(bf16[128,1536]{1,0:T(8,128)(2,1)S(1)} %join.1.pair_ref), channel_id=1, source_target_pairs={{0,6},{2,4},{4,2},{6,0},{1,7},{3,5},{5,3},{7,1},{8,14},{10,12},{12... | collective-permute-start | bytes 1179656 | tf_op jit(solution)/shard_map/ppermute | solution.py:175
  45.2 6.7 %collective-permute-start.6 = (bf16[64,1536]{1,0:T(8,128)(2,1)S(1)}, bf16[64,1536]{1,0:T(8,128)(2,1)S(1)}, u32[]{:S(2)}, u32[]{:S(2)}) collective-permute-start(bf16[64,1536]{1,0:T(8,128)(2,1)S(1)} %blocks.1.products_ref.rest_0_), channel_id=1, source_target_pairs={{0,1},{1,0},{2,3},{3,2},{4,5},{5,4},{6,7},{7,6},{8,9},{9,8},{10,11... | collective-permute-start | bytes 589832 | tf_op jit(solution)/shard_map/ppermute | solution.py:174
  50.0 3.3 %collective-permute-start.8 = (bf16[64,1536]{1,0:T(8,128)(2,1)S(1)}, bf16[64,1536]{1,0:T(8,128)(2,1)S(1)}, u32[]{:S(2)}, u32[]{:S(2)}) collective-permute-start(bf16[64,1536]{1,0:T(8,128)(2,1)S(1)} %collective-permute-done.7.rest_2_), channel_id=1, source_target_pairs={{0,1},{1,0},{2,3},{3,2},{4,5},{5,4},{6,7},{7,6},{8,9},{9,8},{10,11... | collective-permute-start | bytes 589832 | tf_op jit(solution)/shard_map/ppermute | solution.py:188
  73.8 9.5 %collective-permute-start.9 = (f32[32,64]{1,0:T(8,128)S(1)}, f32[32,64]{1,0:T(8,128)S(1)}, u32[]{:S(2)}, u32[]{:S(2)}) collective-permute-start(f32[32,64]{1,0:T(8,128)S(1)} %sum.1), channel_id=1, source_target_pairs={{0,0},{1,1},{2,64},{3,65},{4,128},{5,129},{6,192},{7,193},{8,8},{9... | collective-permute-start | bytes 24584 | tf_op jit(solution)/shard_map/ppermute | solution.py:213

commit v13 on v12

--- a/solution.py
+++ b/solution.py
@@ -16,6 +16,7 @@
 PACKED = OWN * DOFS
 
 neighbour_offsets = (1, -1, 2, -2)
+ghost_order = (2, 3, 0, 1)
 NEAR, FAR = 1, 3
 VMEM = pl.BlockSpec(memory_space=pltpu.VMEM)
 SMEM = pl.BlockSpec(memory_space=pltpu.SMEM)
@@ -52,8 +53,8 @@
 
 def block_kernel(table_ref, own_ref, blocks_ref, *rest):
     *ghost_refs, out_ref, pool, total = rest
-    slot = 0
-    for slabs_ref in (own_ref, *ghost_refs):
+    slots = [OWN + GMAX * neighbour for neighbour in ghost_order]
+    for slot, slabs_ref in zip((0, *slots), (own_ref, *ghost_refs)):
         for at in range(0, slabs_ref.shape[1], 384):
             pool[slot, :, :128] = slabs_ref[:, at : at + 128]
             pool[slot + 1, :, :128] = slabs_ref[:, at + 128 : at + 256]
@@ -101,12 +102,18 @@
     put_tile(place_ref, products_ref[...], pair_ref[...], out_ref, ((0, 0),), 0)
 
 
-def tile_kernel(place_ref, pair_ref, other_pair_ref, *rest):
+def most_tile_kernel(place_ref, pair_ref, other_pair_ref, *rest):
     *product_refs, begun_ref, out_ref = rest
-    steps = ((0, 0), (0, 1), (1, 0), (1, 1))
+    steps = ((0, 0), (0, 1), (1, 0))
     products = jnp.concatenate([ref[...] for ref in product_refs], axis=0)
     put_tile(place_ref, products, other_pair_ref[...], out_ref, steps, FAR)
     put_tile(place_ref, products[WIDTH:], pair_ref[...], out_ref, steps[1:], 0)
+
+
+def last_tile_kernel(place_ref, pair_ref, other_pair_ref, products_ref, begun_ref, out_ref):
+    products = products_ref[...]
+    put_tile(place_ref, products, pair_ref[...], out_ref, ((1, 1),), 0)
+    put_tile(place_ref, products, other_pair_ref[...], out_ref, ((1, 1),), FAR)
 
 
 def sum_kernel(parts_ref, out_ref):
@@ -130,10 +137,11 @@
         compiler_params=pltpu.CompilerParams(vmem_limit_bytes=16 << 20),
         name="select",
     )(send_list, basis_vectors)
-    arriving = []
-    for block, offset in zip(picked, neighbour_offsets):
+    arriving = [None] * NEIGH
+    for neighbour in ghost_order:
+        offset = neighbour_offsets[neighbour]
         route = [((i - offset) % parts, i) for i in range(parts)]
-        arriving.append(lax.ppermute(block, mesh_axes, route))
+        arriving[neighbour] = lax.ppermute(picked[neighbour], mesh_axes, route)
     swap = [(0, 1), (1, 0)]
     blocks = pl.pallas_call(
         stage_kernel,
@@ -160,7 +168,7 @@
         ],
         compiler_params=pltpu.CompilerParams(vmem_limit_bytes=24 << 20),
         name="blocks",
-    )(table, packed, blocks, *arriving)
+    )(table, packed, blocks, *(arriving[neighbour] for neighbour in ghost_order))
     other_packed, _ = lax.optimization_barrier((other_packed, products))
     pair = pl.pallas_call(
         join_kernel,
@@ -186,15 +194,24 @@
     )(place, pair, products)
     behind, begun = lax.optimization_barrier((over_z, begun))
     over_both = lax.ppermute(behind, "core", swap)
+    begun = pl.pallas_call(
+        most_tile_kernel,
+        out_shape=chunks_shape,
+        in_specs=[SMEM] + [VMEM] * 6,
+        out_specs=VMEM,
+        input_output_aliases={6: 0},
+        compiler_params=pltpu.CompilerParams(vmem_limit_bytes=16 << 20),
+        name="most_tile",
+    )(place, pair, other_pair, products, over_core, over_z, begun)
     chunks = pl.pallas_call(
-        tile_kernel,
+        last_tile_kernel,
         out_shape=chunks_shape,
-        in_specs=[SMEM] + [VMEM] * 7,
-        out_specs=VMEM,
-        input_output_aliases={7: 0},
+        in_specs=[SMEM] + [VMEM] * 4,
+        out_specs=VMEM,
+        input_output_aliases={4: 0},
         compiler_params=pltpu.CompilerParams(vmem_limit_bytes=16 << 20),
         name="tile",
-    )(place, pair, other_pair, products, over_core, over_z, over_both, begun)
+    )(place, pair, other_pair, over_both, begun)
     shares = lax.all_to_all(chunks, mesh_axes, 0, 0, tiled=True)
     block = pl.pallas_call(
         sum_kernel,

time: 84.5 us -> 85.2 us (level)
  Pallas kernels: 5.92 us -> 6.8 us
    ppermute x1, waiting for transfers between devices: 1.3 us -> 2.7 us  [local(): other_pair = lax.ppermute(pair, 'x', [(i, i ^ FAR) for i in range(4)])]
    ppermute x1, waiting for transfers between devices: 1.4 us -> 0.01 us  [local(): over_both = lax.ppermute(behind, 'core', swap)]
    ppermute x4, starting transfers between devices: 21.6 us -> 20.7 us  [local(): arriving[neighbour] = lax.ppermute(picked[neighbour], mesh_axes, route)]
    ppermute x1, starting transfers between devices: 8.22 us -> 9.12 us  [local(): over_z = lax.ppermute(products, 'z_hi', swap)]
    pallas_call x1 -> x2, Pallas kernels: 1.14 us -> 2.02 us  [the longest x1 1.03 us: local(): pl.pallas_call(most_tile_kernel, out_shape=chunks_shape, in_specs=[SMEM]...]
  transfers between devices with their start and end apart: 10 -> 10, of which waited for: 4 -> 3; matrix products, arithmetic and copies ran while one was open for 1% -> 1% of each run, Pallas kernels for 5% -> 6%
where the time goes in v13:
time: 85.2 us; the launch traced here: 84.8 us
  starting transfers between devices  42.8 us (50%)
  blocking collectives  17.8 us (21%)
  waiting for transfers between devices  10.9 us (13%)
  Pallas kernels  6.8 us (8%)
  local copies, waits for them, and re-layouts  4.77 us (6%)
    ppermute x4, starting transfers between devices, local(): arriving[neighbour] = lax.ppermute(picked[neighbour], mesh_axes, route)  20.7 us
    all_to_all x1, blocking collectives, local(): shares = lax.all_to_all(chunks, mesh_axes, 0, 0, tiled=True)  17.8 us
    ppermute x1, starting transfers between devices, local(): over_z = lax.ppermute(products, 'z_hi', swap)  9.12 us
    ppermute x1, waiting for transfers between devices, local(): return lax.ppermute(block, whole, route).T  6.14 us
    unnamed x7, local copies, waits for them, and re-layouts  4.77 us
    ppermute x1, starting transfers between devices, local(): return lax.ppermute(block, whole, route).T  3.39 us
    ppermute x1, starting transfers between devices, local(): other_pair = lax.ppermute(pair, 'x', [(i, i ^ FAR) for i in range(4)])  3.05 us
    pallas_call x1, Pallas kernels, local(): pl.pallas_call(block_kernel, out_shape=shape((WIDTH, PACKED), jnp.bfloat1...  2.75 us
  transfers between devices with their start and end apart: 10, of which 3 were waited for; matrix products, arithmetic and copies ran while one was open for 1% of the time, Pallas kernels for 6%

profile of v13, /device:TPU:6, one launch (start us, length us, event | category | flops | bytes accessed | tf_op | source)
XLA Modules:
  0.0 84.8 jit_solution(16958319350653341152)
XLA Ops:
  0.0 0.9 %copy-done.1 = bf16[8,64,192]{2,1,0:T(8,128)(2,1)S(1)} copy-done((bf16[8,64,192]{2,1,0:T(8,128)(2,1)S(1)}, bf16[8,64,192]{2,1,0:T(8,128)(2,1)}, u32[]{:S(2)}) %copy-start.1) | copy-done | bytes 196632
  1.0 0.7 copy-done.2
  1.6 0.7 select.1
  2.3 6.1 %collective-permute-start.1 = (bf16[64,768]{1,0:T(8,128)(2,1)S(1)}, bf16[64,768]{1,0:T(8,128)(2,1)S(1)}, u32[]{:S(2)}, u32[]{:S(2)}) collective-permute-start(bf16[64,768]{1,0:T(8,128)(2,1)S(1)} %get-tuple-element.14), channel_id=1, source_target_pairs={{480,0},{496,16},{0,32},{16,48},{32,64},{48,80},{64,96},{80,112},{... | collective-permute-start | bytes 294920 | tf_op jit(solution)/shard_map/ppermute | solution.py:144
  8.4 4.8 %collective-permute-start.2 = (bf16[64,768]{1,0:T(8,128)(2,1)S(1)}, bf16[64,768]{1,0:T(8,128)(2,1)S(1)}, u32[]{:S(2)}, u32[]{:S(2)}) collective-permute-start(bf16[64,768]{1,0:T(8,128)(2,1)S(1)} %get-tuple-element.15), channel_id=1, source_target_pairs={{32,0},{48,16},{64,32},{80,48},{96,64},{112,80},{128,96},{144,112}... | collective-permute-start | bytes 294920 | tf_op jit(solution)/shard_map/ppermute | solution.py:144
  13.2 4.3 %collective-permute-start.3 = (bf16[64,768]{1,0:T(8,128)(2,1)S(1)}, bf16[64,768]{1,0:T(8,128)(2,1)S(1)}, u32[]{:S(2)}, u32[]{:S(2)}) collective-permute-start(bf16[64,768]{1,0:T(8,128)(2,1)S(1)} %get-tuple-element.16), channel_id=1, source_target_pairs={{496,0},{0,16},{16,32},{32,48},{48,64},{64,80},{80,96},{96,112},{1... | collective-permute-start | bytes 294920 | tf_op jit(solution)/shard_map/ppermute | solution.py:144
  17.5 5.5 %collective-permute-start.4 = (bf16[64,768]{1,0:T(8,128)(2,1)S(1)}, bf16[64,768]{1,0:T(8,128)(2,1)S(1)}, u32[]{:S(2)}, u32[]{:S(2)}) collective-permute-start(bf16[64,768]{1,0:T(8,128)(2,1)S(1)} %get-tuple-element.17), channel_id=1, source_target_pairs={{16,0},{32,16},{48,32},{64,48},{80,64},{96,80},{112,96},{128,112},... | collective-permute-start | bytes 294920 | tf_op jit(solution)/shard_map/ppermute | solution.py:144
  23.0 2.7 %collective-permute-start = (bf16[64,1536]{1,0:T(8,128)(2,1)S(1)}, bf16[64,1536]{1,0:T(8,128)(2,1)S(1)}, u32[]{:S(2)}, u32[]{:S(2)}) collective-permute-start(bf16[64,1536]{1,0:T(8,128)(2,1)S(1)} %get-tuple-element.13.own_ref), channel_id=1, source_target_pairs={{0,2},{2,0},{4,6},{6,4},{1,3},{3,1},{5,7},{7,5},{8,10},{10,8},{12,... | collective-permute-start | bytes 589832 | tf_op jit(solution)/shard_map/ppermute | solution.py:159
  26.4 0.8 convert_select_fusion.table_ref
  27.2 2.6 %copy-done = bf16[56,192,192]{2,1,0:T(8,128)(2,1)S(1)} copy-done((bf16[56,192,192]{2,1,0:T(8,128)(2,1)S(1)}, bf16[56,192,192]{2,1,0:T(8,128)(2,1)}, u32[]{:S(2)}) %copy-start) | copy-done | bytes 4128792
  30.1 2.8 %blocks.1.products_ref.rest_0_ = bf16[64,1536]{1,0:T(8,128)(2,1)S(1)} custom-call(f32[8,56]{1,0:T(8,128)S(1)} %convert_select_fusion.table_ref, bf16[64,1536]{1,0:T(8,128)(2,1)S(1)} %get-tuple-element.13.own_ref, bf16[56,192,192]{2,1,0:T(8,128)(2,1)S(1)} %stage.1.blocks_ref, bf16[64,768]{1,0:T(8,128)(2,1)S(1)} %collective-permute-done.1.rest_0_, ...), custom_call_target="tpu_custom_call" | custom-call | tf_op jit(solution)/shard_map/blocks/pallas_call | solution.py:160
  32.9 9.1 %collective-permute-start.6 = (bf16[64,1536]{1,0:T(8,128)(2,1)S(1)}, bf16[64,1536]{1,0:T(8,128)(2,1)S(1)}, u32[]{:S(2)}, u32[]{:S(2)}) collective-permute-start(bf16[64,1536]{1,0:T(8,128)(2,1)S(1)} %blocks.1.products_ref.rest_0_), channel_id=1, source_target_pairs={{0,8},{8,0},{1,9},{9,1},{2,10},{10,2},{3,11},{11,3},{4,12},{12,4},... | collective-permute-start | bytes 589832 | tf_op jit(solution)/shard_map/ppermute | solution.py:181
  42.1 3.0 %collective-permute-start.5 = (bf16[128,1536]{1,0:T(8,128)(2,1)S(1)}, bf16[128,1536]{1,0:T(8,128)(2,1)S(1)}, u32[]{:S(2)}, u32[]{:S(2)}) collective-permute-start(bf16[128,1536]{1,0:T(8,128)(2,1)S(1)} %join.1.pair_ref), channel_id=1, source_target_pairs={{0,6},{2,4},{4,2},{6,0},{1,7},{3,5},{5,3},{7,1},{8,14},{10,12},{12... | collective-permute-start | bytes 1179656 | tf_op jit(solution)/shard_map/ppermute | solution.py:183
  45.2 1.9 %collective-permute-start.8 = (bf16[64,1536]{1,0:T(8,128)(2,1)S(1)}, bf16[64,1536]{1,0:T(8,128)(2,1)S(1)}, u32[]{:S(2)}, u32[]{:S(2)}) collective-permute-start(bf16[64,1536]{1,0:T(8,128)(2,1)S(1)} %blocks.1.products_ref.rest_0_), channel_id=1, source_target_pairs={{0,1},{1,0},{2,3},{3,2},{4,5},{5,4},{6,7},{7,6},{8,9},{9,8},{10,11... | collective-permute-start | bytes 589832 | tf_op jit(solution)/shard_map/ppermute | solution.py:182
  47.1 0.9 %own_tile.1.rest_3_ = bf16[32,16,128]{2,1,0:T(8,128)(2,1)S(1)} custom-call(s32[3]{0:T(128)S(1)} %pad_add_fusion.place_ref, bf16[128,1536]{1,0:T(8,128)(2,1)S(1)} %join.1.pair_ref, bf16[64,1536]{1,0:T(8,128)(2,1)S(1)} %blocks.1.products_ref.rest_0_), custom_call_target="tpu_custom_call" | custom-call | flops 16777216 | bytes 1048576 | tf_op jit(solution)/shard_map/own_tile/pallas_call | solution.py:186
  48.0 2.0 %collective-permute-done.6.rest_2_ = bf16[64,1536]{1,0:T(8,128)(2,1)S(1)} collective-permute-done((bf16[64,1536]{1,0:T(8,128)(2,1)S(1)}, bf16[64,1536]{1,0:T(8,128)(2,1)S(1)}, u32[]{:S(2)}, u32[]{:S(2)}) %collective-permute-start.6) | collective-permute-done | bytes 196640 | tf_op jit(solution)/shard_map/ppermute | solution.py:181
  50.0 1.9 %collective-permute-start.7 = (bf16[64,1536]{1,0:T(8,128)(2,1)S(1)}, bf16[64,1536]{1,0:T(8,128)(2,1)S(1)}, u32[]{:S(2)}, u32[]{:S(2)}) collective-permute-start(bf16[64,1536]{1,0:T(8,128)(2,1)S(1)} %collective-permute-done.6.rest_2_), channel_id=1, source_target_pairs={{0,1},{1,0},{2,3},{3,2},{4,5},{5,4},{6,7},{7,6},{8,9},{9,8},{10,11... | collective-permute-start | bytes 589832 | tf_op jit(solution)/shard_map/ppermute | solution.py:196
  51.9 2.7 %collective-permute-done.5.other_pair_ref = bf16[128,1536]{1,0:T(8,128)(2,1)S(1)} collective-permute-done((bf16[128,1536]{1,0:T(8,128)(2,1)S(1)}, bf16[128,1536]{1,0:T(8,128)(2,1)S(1)}, u32[]{:S(2)}, u32[]{:S(2)}) %collective-permute-start.5) | collective-permute-done | bytes 393248 | tf_op jit(solution)/shard_map/ppermute | solution.py:183
  54.6 1.0 %most_tile.1.begun_ref = bf16[32,16,128]{2,1,0:T(8,128)(2,1)S(1)} custom-call(s32[3]{0:T(128)S(1)} %pad_add_fusion.place_ref, bf16[128,1536]{1,0:T(8,128)(2,1)S(1)} %join.1.pair_ref, bf16[128,1536]{1,0:T(8,128)(2,1)S(1)} %collective-permute-done.5.other_pair_ref, bf16[64,1536]{1,0:T(8,128)(2,1)S(1)} %blocks.1.products_ref.rest_0_, ...), custom_call_target="tpu_custom_call", output_to_operand_aliasing={{}: (6, {})} | custom-call | tf_op jit(solution)/shard_map/most_tile/pallas_call | solution.py:197
  55.7 1.0 %tile.1 = bf16[32,16,128]{2,1,0:T(8,128)(2,1)S(1)} custom-call(s32[3]{0:T(128)S(1)} %pad_add_fusion.place_ref, bf16[128,1536]{1,0:T(8,128)(2,1)S(1)} %join.1.pair_ref, bf16[128,1536]{1,0:T(8,128)(2,1)S(1)} %collective-permute-done.5.other_pair_ref, bf16[64,1536]{1,0:T(8,128)(2,1)S(1)} %collective-permute-done.7.products_ref, ...), custom_call_target="tpu_custom_call", output_to_operand_aliasing={{}: (4, {})} | custom-call | tf_op jit(solution)/shard_map/tile/pallas_call | solution.py:206
  56.7 17.8 %all_to_all.5.parts_ref = bf16[32,16,128]{2,1,0:T(8,128)(2,1)S(1)} all-to-all(bf16[32,16,128]{2,1,0:T(8,128)(2,1)S(1)} %tile.1), channel_id=1, replica_groups=mesh['y'=8,'z_lo'=4,'z_hi'=2,'x'=4,'core'=2] {'y','z_lo'}, dimensions={0} | all-to-all | bytes 262144 | tf_op jit(solution)/shard_map/all_to_all | solution.py:215
  74.6 3.4 %collective-permute-start.9 = (f32[32,64]{1,0:T(8,128)S(1)}, f32[32,64]{1,0:T(8,128)S(1)}, u32[]{:S(2)}, u32[]{:S(2)}) collective-permute-start(f32[32,64]{1,0:T(8,128)S(1)} %sum.1), channel_id=1, source_target_pairs={{0,0},{1,1},{2,64},{3,65},{4,128},{5,129},{6,192},{7,193},{8,8},{9... | collective-permute-start | bytes 24584 | tf_op jit(solution)/shard_map/ppermute | solution.py:230
  78.0 6.1 %collective-permute-done.9 = f32[32,64]{1,0:T(8,128)S(1)} collective-permute-done((f32[32,64]{1,0:T(8,128)S(1)}, f32[32,64]{1,0:T(8,128)S(1)}, u32[]{:S(2)}, u32[]{:S(2)}) %collective-permute-start.9) | collective-permute-done | bytes 8224 | tf_op jit(solution)/shard_map/ppermute | solution.py:230
  84.1 0.6 copy.14
  (16 shorter events, 0.6 us)
Async XLA Ops:
  0.0 0.9 %copy-start.1 = (bf16[8,64,192]{2,1,0:T(8,128)(2,1)S(1)}, bf16[8,64,192]{2,1,0:T(8,128)(2,1)}, u32[]{:S(2)}) copy-start(bf16[8,64,192]{2,1,0:T(8,128)(2,1)} %basis_ref.1) | copy-start | bytes 589828
  1.0 0.7 copy-start.2
  2.3 27.8 %collective-permute-start.1 = (bf16[64,768]{1,0:T(8,128)(2,1)S(1)}, bf16[64,768]{1,0:T(8,128)(2,1)S(1)}, u32[]{:S(2)}, u32[]{:S(2)}) collective-permute-start(bf16[64,768]{1,0:T(8,128)(2,1)S(1)} %get-tuple-element.14), channel_id=1, source_target_pairs={{480,0},{496,16},{0,32},{16,48},{32,64},{48,80},{64,96},{80,112},{... | collective-permute-start | bytes 294920 | tf_op jit(solution)/shard_map/ppermute | solution.py:144
  8.4 21.7 %collective-permute-start.2 = (bf16[64,768]{1,0:T(8,128)(2,1)S(1)}, bf16[64,768]{1,0:T(8,128)(2,1)S(1)}, u32[]{:S(2)}, u32[]{:S(2)}) collective-permute-start(bf16[64,768]{1,0:T(8,128)(2,1)S(1)} %get-tuple-element.15), channel_id=1, source_target_pairs={{32,0},{48,16},{64,32},{80,48},{96,64},{112,80},{128,96},{144,112}... | collective-permute-start | bytes 294920 | tf_op jit(solution)/shard_map/ppermute | solution.py:144
  13.2 16.9 %collective-permute-start.3 = (bf16[64,768]{1,0:T(8,128)(2,1)S(1)}, bf16[64,768]{1,0:T(8,128)(2,1)S(1)}, u32[]{:S(2)}, u32[]{:S(2)}) collective-permute-start(bf16[64,768]{1,0:T(8,128)(2,1)S(1)} %get-tuple-element.16), channel_id=1, source_target_pairs={{496,0},{0,16},{16,32},{32,48},{48,64},{64,80},{80,96},{96,112},{1... | collective-permute-start | bytes 294920 | tf_op jit(solution)/shard_map/ppermute | solution.py:144
  17.5 12.6 %collective-permute-start.4 = (bf16[64,768]{1,0:T(8,128)(2,1)S(1)}, bf16[64,768]{1,0:T(8,128)(2,1)S(1)}, u32[]{:S(2)}, u32[]{:S(2)}) collective-permute-start(bf16[64,768]{1,0:T(8,128)(2,1)S(1)} %get-tuple-element.17), channel_id=1, source_target_pairs={{16,0},{32,16},{48,32},{64,48},{80,64},{96,80},{112,96},{128,112},... | collective-permute-start | bytes 294920 | tf_op jit(solution)/shard_map/ppermute | solution.py:144
  23.0 19.0 %collective-permute-start = (bf16[64,1536]{1,0:T(8,128)(2,1)S(1)}, bf16[64,1536]{1,0:T(8,128)(2,1)S(1)}, u32[]{:S(2)}, u32[]{:S(2)}) collective-permute-start(bf16[64,1536]{1,0:T(8,128)(2,1)S(1)} %get-tuple-element.13.own_ref), channel_id=1, source_target_pairs={{0,2},{2,0},{4,6},{6,4},{1,3},{3,1},{5,7},{7,5},{8,10},{10,8},{12,... | collective-permute-start | bytes 589832 | tf_op jit(solution)/shard_map/ppermute | solution.py:159
  27.2 2.6 %copy-start = (bf16[56,192,192]{2,1,0:T(8,128)(2,1)S(1)}, bf16[56,192,192]{2,1,0:T(8,128)(2,1)}, u32[]{:S(2)}) copy-start(bf16[56,192,192]{2,1,0:T(8,128)(2,1)} %blocks_ref.1) | copy-start | bytes 12386308
  32.9 17.1 %collective-permute-start.6 = (bf16[64,1536]{1,0:T(8,128)(2,1)S(1)}, bf16[64,1536]{1,0:T(8,128)(2,1)S(1)}, u32[]{:S(2)}, u32[]{:S(2)}) collective-permute-start(bf16[64,1536]{1,0:T(8,128)(2,1)S(1)} %blocks.1.products_ref.rest_0_), channel_id=1, source_target_pairs={{0,8},{8,0},{1,9},{9,1},{2,10},{10,2},{3,11},{11,3},{4,12},{12,4},... | collective-permute-start | bytes 589832 | tf_op jit(solution)/shard_map/ppermute | solution.py:181
  42.1 12.6 %collective-permute-start.5 = (bf16[128,1536]{1,0:T(8,128)(2,1)S(1)}, bf16[128,1536]{1,0:T(8,128)(2,1)S(1)}, u32[]{:S(2)}, u32[]{:S(2)}) collective-permute-start(bf16[128,1536]{1,0:T(8,128)(2,1)S(1)} %join.1.pair_ref), channel_id=1, source_target_pairs={{0,6},{2,4},{4,2},{6,0},{1,7},{3,5},{5,3},{7,1},{8,14},{10,12},{12... | collective-permute-start | bytes 1179656 | tf_op jit(solution)/shard_map/ppermute | solution.py:183
  45.2 6.7 %collective-permute-start.8 = (bf16[64,1536]{1,0:T(8,128)(2,1)S(1)}, bf16[64,1536]{1,0:T(8,128)(2,1)S(1)}, u32[]{:S(2)}, u32[]{:S(2)}) collective-permute-start(bf16[64,1536]{1,0:T(8,128)(2,1)S(1)} %blocks.1.products_ref.rest_0_), channel_id=1, source_target_pairs={{0,1},{1,0},{2,3},{3,2},{4,5},{5,4},{6,7},{7,6},{8,9},{9,8},{10,11... | collective-permute-start | bytes 589832 | tf_op jit(solution)/shard_map/ppermute | solution.py:182
  50.0 5.7 %collective-permute-start.7 = (bf16[64,1536]{1,0:T(8,128)(2,1)S(1)}, bf16[64,1536]{1,0:T(8,128)(2,1)S(1)}, u32[]{:S(2)}, u32[]{:S(2)}) collective-permute-start(bf16[64,1536]{1,0:T(8,128)(2,1)S(1)} %collective-permute-done.6.rest_2_), channel_id=1, source_target_pairs={{0,1},{1,0},{2,3},{3,2},{4,5},{5,4},{6,7},{7,6},{8,9},{9,8},{10,11... | collective-permute-start | bytes 589832 | tf_op jit(solution)/shard_map/ppermute | solution.py:196
  74.6 9.5 %collective-permute-start.9 = (f32[32,64]{1,0:T(8,128)S(1)}, f32[32,64]{1,0:T(8,128)S(1)}, u32[]{:S(2)}, u32[]{:S(2)}) collective-permute-start(f32[32,64]{1,0:T(8,128)S(1)} %sum.1), channel_id=1, source_target_pairs={{0,0},{1,1},{2,64},{3,65},{4,128},{5,129},{6,192},{7,193},{8,8},{9... | collective-permute-start | bytes 24584 | tf_op jit(solution)/shard_map/ppermute | solution.py:230

commit v14 on v12

--- a/solution.py
+++ b/solution.py
@@ -16,6 +16,7 @@
 PACKED = OWN * DOFS
 
 neighbour_offsets = (1, -1, 2, -2)
+ghost_order = (2, 3, 0, 1)
 NEAR, FAR = 1, 3
 VMEM = pl.BlockSpec(memory_space=pltpu.VMEM)
 SMEM = pl.BlockSpec(memory_space=pltpu.SMEM)
@@ -52,8 +53,8 @@
 
 def block_kernel(table_ref, own_ref, blocks_ref, *rest):
     *ghost_refs, out_ref, pool, total = rest
-    slot = 0
-    for slabs_ref in (own_ref, *ghost_refs):
+    slots = [OWN + GMAX * neighbour for neighbour in ghost_order]
+    for slot, slabs_ref in zip((0, *slots), (own_ref, *ghost_refs)):
         for at in range(0, slabs_ref.shape[1], 384):
             pool[slot, :, :128] = slabs_ref[:, at : at + 128]
             pool[slot + 1, :, :128] = slabs_ref[:, at + 128 : at + 256]
@@ -131,9 +132,10 @@
         name="select",
     )(send_list, basis_vectors)
     arriving = []
-    for block, offset in zip(picked, neighbour_offsets):
+    for neighbour in ghost_order:
+        offset = neighbour_offsets[neighbour]
         route = [((i - offset) % parts, i) for i in range(parts)]
-        arriving.append(lax.ppermute(block, mesh_axes, route))
+        arriving.append(lax.ppermute(picked[neighbour], mesh_axes, route))
     swap = [(0, 1), (1, 0)]
     blocks = pl.pallas_call(
         stage_kernel,

time: 84.5 us -> 84.5 us (level)
    ppermute x4, starting transfers between devices: 21.6 us -> 20.7 us  [local(): arriving.append(lax.ppermute(picked[neighbour], mesh_axes, route))]
    ppermute x1, starting transfers between devices: 8.22 us -> 9.12 us  [local(): over_z = lax.ppermute(products, 'z_hi', swap)]
where the time goes in v14:
time: 84.5 us; the launch traced here: 84 us
  starting transfers between devices  42.6 us (50%)
  blocking collectives  18 us (21%)
  waiting for transfers between devices  11 us (13%)
  Pallas kernels  5.92 us (7%)
  local copies, waits for them, and re-layouts  4.77 us (6%)
  other arithmetic  0.85 us (1%)
    ppermute x4, starting transfers between devices, local(): arriving.append(lax.ppermute(picked[neighbour], mesh_axes, route))  20.7 us
    all_to_all x1, blocking collectives, local(): shares = lax.all_to_all(chunks, mesh_axes, 0, 0, tiled=True)  18 us
    ppermute x1, starting transfers between devices, local(): over_z = lax.ppermute(products, 'z_hi', swap)  9.12 us
    ppermute x1, waiting for transfers between devices, local(): return lax.ppermute(block, whole, route).T  6.27 us
    unnamed x7, local copies, waits for them, and re-layouts  4.77 us
    ppermute x1, starting transfers between devices, local(): return lax.ppermute(block, whole, route).T  3.26 us
    ppermute x1, starting transfers between devices, local(): other_pair = lax.ppermute(pair, 'x', [(i, i ^ FAR) for i in range(4)])  3.05 us
    pallas_call x1, Pallas kernels, local(): pl.pallas_call(block_kernel, out_shape=shape((WIDTH, PACKED), jnp.bfloat1...  2.75 us
  transfers between devices with their start and end apart: 10, of which 4 were waited for; matrix products, arithmetic and copies ran while one was open for 1% of the time, Pallas kernels for 5%

profile of v14, /device:TPU:6, one launch (start us, length us, event | category | flops | bytes accessed | tf_op | source)
XLA Modules:
  0.0 84.0 jit_solution(5425131582112038092)
XLA Ops:
  0.0 0.9 %copy-done.1 = bf16[8,64,192]{2,1,0:T(8,128)(2,1)S(1)} copy-done((bf16[8,64,192]{2,1,0:T(8,128)(2,1)S(1)}, bf16[8,64,192]{2,1,0:T(8,128)(2,1)}, u32[]{:S(2)}) %copy-start.1) | copy-done | bytes 196632
  1.0 0.7 copy-done.2
  1.6 0.7 select.1
  2.3 6.1 %collective-permute-start.1 = (bf16[64,768]{1,0:T(8,128)(2,1)S(1)}, bf16[64,768]{1,0:T(8,128)(2,1)S(1)}, u32[]{:S(2)}, u32[]{:S(2)}) collective-permute-start(bf16[64,768]{1,0:T(8,128)(2,1)S(1)} %get-tuple-element.14), channel_id=1, source_target_pairs={{480,0},{496,16},{0,32},{16,48},{32,64},{48,80},{64,96},{80,112},{... | collective-permute-start | bytes 294920 | tf_op jit(solution)/shard_map/ppermute | solution.py:138
  8.4 4.8 %collective-permute-start.2 = (bf16[64,768]{1,0:T(8,128)(2,1)S(1)}, bf16[64,768]{1,0:T(8,128)(2,1)S(1)}, u32[]{:S(2)}, u32[]{:S(2)}) collective-permute-start(bf16[64,768]{1,0:T(8,128)(2,1)S(1)} %get-tuple-element.15), channel_id=1, source_target_pairs={{32,0},{48,16},{64,32},{80,48},{96,64},{112,80},{128,96},{144,112}... | collective-permute-start | bytes 294920 | tf_op jit(solution)/shard_map/ppermute | solution.py:138
  13.2 4.3 %collective-permute-start.3 = (bf16[64,768]{1,0:T(8,128)(2,1)S(1)}, bf16[64,768]{1,0:T(8,128)(2,1)S(1)}, u32[]{:S(2)}, u32[]{:S(2)}) collective-permute-start(bf16[64,768]{1,0:T(8,128)(2,1)S(1)} %get-tuple-element.16), channel_id=1, source_target_pairs={{496,0},{0,16},{16,32},{32,48},{48,64},{64,80},{80,96},{96,112},{1... | collective-permute-start | bytes 294920 | tf_op jit(solution)/shard_map/ppermute | solution.py:138
  17.5 5.5 %collective-permute-start.4 = (bf16[64,768]{1,0:T(8,128)(2,1)S(1)}, bf16[64,768]{1,0:T(8,128)(2,1)S(1)}, u32[]{:S(2)}, u32[]{:S(2)}) collective-permute-start(bf16[64,768]{1,0:T(8,128)(2,1)S(1)} %get-tuple-element.17), channel_id=1, source_target_pairs={{16,0},{32,16},{48,32},{64,48},{80,64},{96,80},{112,96},{128,112},... | collective-permute-start | bytes 294920 | tf_op jit(solution)/shard_map/ppermute | solution.py:138
  23.0 2.7 %collective-permute-start = (bf16[64,1536]{1,0:T(8,128)(2,1)S(1)}, bf16[64,1536]{1,0:T(8,128)(2,1)S(1)}, u32[]{:S(2)}, u32[]{:S(2)}) collective-permute-start(bf16[64,1536]{1,0:T(8,128)(2,1)S(1)} %get-tuple-element.13.own_ref), channel_id=1, source_target_pairs={{0,2},{2,0},{4,6},{6,4},{1,3},{3,1},{5,7},{7,5},{8,10},{10,8},{12,... | collective-permute-start | bytes 589832 | tf_op jit(solution)/shard_map/ppermute | solution.py:153
  26.4 0.8 convert_select_fusion.table_ref
  27.2 2.6 %copy-done = bf16[56,192,192]{2,1,0:T(8,128)(2,1)S(1)} copy-done((bf16[56,192,192]{2,1,0:T(8,128)(2,1)S(1)}, bf16[56,192,192]{2,1,0:T(8,128)(2,1)}, u32[]{:S(2)}) %copy-start) | copy-done | bytes 4128792
  30.1 2.8 %blocks.1.products_ref.rest_0_ = bf16[64,1536]{1,0:T(8,128)(2,1)S(1)} custom-call(f32[8,56]{1,0:T(8,128)S(1)} %convert_select_fusion.table_ref, bf16[64,1536]{1,0:T(8,128)(2,1)S(1)} %get-tuple-element.13.own_ref, bf16[56,192,192]{2,1,0:T(8,128)(2,1)S(1)} %stage.1.blocks_ref, bf16[64,768]{1,0:T(8,128)(2,1)S(1)} %collective-permute-done.1.rest_0_, ...), custom_call_target="tpu_custom_call" | custom-call | tf_op jit(solution)/shard_map/blocks/pallas_call | solution.py:154
  32.9 9.1 %collective-permute-start.7 = (bf16[64,1536]{1,0:T(8,128)(2,1)S(1)}, bf16[64,1536]{1,0:T(8,128)(2,1)S(1)}, u32[]{:S(2)}, u32[]{:S(2)}) collective-permute-start(bf16[64,1536]{1,0:T(8,128)(2,1)S(1)} %blocks.1.products_ref.rest_0_), channel_id=1, source_target_pairs={{0,8},{8,0},{1,9},{9,1},{2,10},{10,2},{3,11},{11,3},{4,12},{12,4},... | collective-permute-start | bytes 589832 | tf_op jit(solution)/shard_map/ppermute | solution.py:175
  42.1 3.0 %collective-permute-start.5 = (bf16[128,1536]{1,0:T(8,128)(2,1)S(1)}, bf16[128,1536]{1,0:T(8,128)(2,1)S(1)}, u32[]{:S(2)}, u32[]{:S(2)}) collective-permute-start(bf16[128,1536]{1,0:T(8,128)(2,1)S(1)} %join.1.pair_ref), channel_id=1, source_target_pairs={{0,6},{2,4},{4,2},{6,0},{1,7},{3,5},{5,3},{7,1},{8,14},{10,12},{12... | collective-permute-start | bytes 1179656 | tf_op jit(solution)/shard_map/ppermute | solution.py:177
  45.2 1.9 %collective-permute-start.6 = (bf16[64,1536]{1,0:T(8,128)(2,1)S(1)}, bf16[64,1536]{1,0:T(8,128)(2,1)S(1)}, u32[]{:S(2)}, u32[]{:S(2)}) collective-permute-start(bf16[64,1536]{1,0:T(8,128)(2,1)S(1)} %blocks.1.products_ref.rest_0_), channel_id=1, source_target_pairs={{0,1},{1,0},{2,3},{3,2},{4,5},{5,4},{6,7},{7,6},{8,9},{9,8},{10,11... | collective-permute-start | bytes 589832 | tf_op jit(solution)/shard_map/ppermute | solution.py:176
  47.1 0.9 %own_tile.1.rest_4_ = bf16[32,16,128]{2,1,0:T(8,128)(2,1)S(1)} custom-call(s32[3]{0:T(128)S(1)} %pad_add_fusion.place_ref, bf16[128,1536]{1,0:T(8,128)(2,1)S(1)} %join.1.pair_ref, bf16[64,1536]{1,0:T(8,128)(2,1)S(1)} %blocks.1.products_ref.rest_0_), custom_call_target="tpu_custom_call" | custom-call | flops 16777216 | bytes 1048576 | tf_op jit(solution)/shard_map/own_tile/pallas_call | solution.py:180
  48.0 2.0 %collective-permute-done.7.rest_2_ = bf16[64,1536]{1,0:T(8,128)(2,1)S(1)} collective-permute-done((bf16[64,1536]{1,0:T(8,128)(2,1)S(1)}, bf16[64,1536]{1,0:T(8,128)(2,1)S(1)}, u32[]{:S(2)}, u32[]{:S(2)}) %collective-permute-start.7) | collective-permute-done | bytes 196640 | tf_op jit(solution)/shard_map/ppermute | solution.py:175
  50.0 1.9 %collective-permute-start.8 = (bf16[64,1536]{1,0:T(8,128)(2,1)S(1)}, bf16[64,1536]{1,0:T(8,128)(2,1)S(1)}, u32[]{:S(2)}, u32[]{:S(2)}) collective-permute-start(bf16[64,1536]{1,0:T(8,128)(2,1)S(1)} %collective-permute-done.7.rest_2_), channel_id=1, source_target_pairs={{0,1},{1,0},{2,3},{3,2},{4,5},{5,4},{6,7},{7,6},{8,9},{9,8},{10,11... | collective-permute-start | bytes 589832 | tf_op jit(solution)/shard_map/ppermute | solution.py:190
  51.9 1.4 %collective-permute-done.8.rest_3_ = bf16[64,1536]{1,0:T(8,128)(2,1)S(1)} collective-permute-done((bf16[64,1536]{1,0:T(8,128)(2,1)S(1)}, bf16[64,1536]{1,0:T(8,128)(2,1)S(1)}, u32[]{:S(2)}, u32[]{:S(2)}) %collective-permute-start.8) | collective-permute-done | bytes 196640 | tf_op jit(solution)/shard_map/ppermute | solution.py:190
  53.3 1.3 %collective-permute-done.5.other_pair_ref = bf16[128,1536]{1,0:T(8,128)(2,1)S(1)} collective-permute-done((bf16[128,1536]{1,0:T(8,128)(2,1)S(1)}, bf16[128,1536]{1,0:T(8,128)(2,1)S(1)}, u32[]{:S(2)}, u32[]{:S(2)}) %collective-permute-start.5) | collective-permute-done | bytes 393248 | tf_op jit(solution)/shard_map/ppermute | solution.py:177
  54.6 1.1 %tile.1 = bf16[32,16,128]{2,1,0:T(8,128)(2,1)S(1)} custom-call(s32[3]{0:T(128)S(1)} %pad_add_fusion.place_ref, bf16[128,1536]{1,0:T(8,128)(2,1)S(1)} %join.1.pair_ref, bf16[128,1536]{1,0:T(8,128)(2,1)S(1)} %collective-permute-done.5.other_pair_ref, bf16[64,1536]{1,0:T(8,128)(2,1)S(1)} %blocks.1.products_ref.rest_0_, ...), custom_call_target="tpu_custom_call", output_to_operand_aliasing={{}: (7, {})} | custom-call | tf_op jit(solution)/shard_map/tile/pallas_call | solution.py:191
  55.8 18.0 %all_to_all.5.parts_ref = bf16[32,16,128]{2,1,0:T(8,128)(2,1)S(1)} all-to-all(bf16[32,16,128]{2,1,0:T(8,128)(2,1)S(1)} %tile.1), channel_id=1, replica_groups=mesh['y'=8,'z_lo'=4,'z_hi'=2,'x'=4,'core'=2] {'y','z_lo'}, dimensions={0} | all-to-all | bytes 262144 | tf_op jit(solution)/shard_map/all_to_all | solution.py:200
  73.8 3.3 %collective-permute-start.9 = (f32[32,64]{1,0:T(8,128)S(1)}, f32[32,64]{1,0:T(8,128)S(1)}, u32[]{:S(2)}, u32[]{:S(2)}) collective-permute-start(f32[32,64]{1,0:T(8,128)S(1)} %sum.1), channel_id=1, source_target_pairs={{0,0},{1,1},{2,64},{3,65},{4,128},{5,129},{6,192},{7,193},{8,8},{9... | collective-permute-start | bytes 24584 | tf_op jit(solution)/shard_map/ppermute | solution.py:215
  77.1 6.3 %collective-permute-done.9 = f32[32,64]{1,0:T(8,128)S(1)} collective-permute-done((f32[32,64]{1,0:T(8,128)S(1)}, f32[32,64]{1,0:T(8,128)S(1)}, u32[]{:S(2)}, u32[]{:S(2)}) %collective-permute-start.9) | collective-permute-done | bytes 8224 | tf_op jit(solution)/shard_map/ppermute | solution.py:215
  83.4 0.6 copy.12
  (15 shorter events, 0.6 us)
Async XLA Ops:
  0.0 0.9 %copy-start.1 = (bf16[8,64,192]{2,1,0:T(8,128)(2,1)S(1)}, bf16[8,64,192]{2,1,0:T(8,128)(2,1)}, u32[]{:S(2)}) copy-start(bf16[8,64,192]{2,1,0:T(8,128)(2,1)} %basis_ref.1) | copy-start | bytes 589828
  1.0 0.7 copy-start.2
  2.3 27.8 %collective-permute-start.1 = (bf16[64,768]{1,0:T(8,128)(2,1)S(1)}, bf16[64,768]{1,0:T(8,128)(2,1)S(1)}, u32[]{:S(2)}, u32[]{:S(2)}) collective-permute-start(bf16[64,768]{1,0:T(8,128)(2,1)S(1)} %get-tuple-element.14), channel_id=1, source_target_pairs={{480,0},{496,16},{0,32},{16,48},{32,64},{48,80},{64,96},{80,112},{... | collective-permute-start | bytes 294920 | tf_op jit(solution)/shard_map/ppermute | solution.py:138
  8.4 21.7 %collective-permute-start.2 = (bf16[64,768]{1,0:T(8,128)(2,1)S(1)}, bf16[64,768]{1,0:T(8,128)(2,1)S(1)}, u32[]{:S(2)}, u32[]{:S(2)}) collective-permute-start(bf16[64,768]{1,0:T(8,128)(2,1)S(1)} %get-tuple-element.15), channel_id=1, source_target_pairs={{32,0},{48,16},{64,32},{80,48},{96,64},{112,80},{128,96},{144,112}... | collective-permute-start | bytes 294920 | tf_op jit(solution)/shard_map/ppermute | solution.py:138
  13.2 16.9 %collective-permute-start.3 = (bf16[64,768]{1,0:T(8,128)(2,1)S(1)}, bf16[64,768]{1,0:T(8,128)(2,1)S(1)}, u32[]{:S(2)}, u32[]{:S(2)}) collective-permute-start(bf16[64,768]{1,0:T(8,128)(2,1)S(1)} %get-tuple-element.16), channel_id=1, source_target_pairs={{496,0},{0,16},{16,32},{32,48},{48,64},{64,80},{80,96},{96,112},{1... | collective-permute-start | bytes 294920 | tf_op jit(solution)/shard_map/ppermute | solution.py:138
  17.5 12.6 %collective-permute-start.4 = (bf16[64,768]{1,0:T(8,128)(2,1)S(1)}, bf16[64,768]{1,0:T(8,128)(2,1)S(1)}, u32[]{:S(2)}, u32[]{:S(2)}) collective-permute-start(bf16[64,768]{1,0:T(8,128)(2,1)S(1)} %get-tuple-element.17), channel_id=1, source_target_pairs={{16,0},{32,16},{48,32},{64,48},{80,64},{96,80},{112,96},{128,112},... | collective-permute-start | bytes 294920 | tf_op jit(solution)/shard_map/ppermute | solution.py:138
  23.0 19.0 %collective-permute-start = (bf16[64,1536]{1,0:T(8,128)(2,1)S(1)}, bf16[64,1536]{1,0:T(8,128)(2,1)S(1)}, u32[]{:S(2)}, u32[]{:S(2)}) collective-permute-start(bf16[64,1536]{1,0:T(8,128)(2,1)S(1)} %get-tuple-element.13.own_ref), channel_id=1, source_target_pairs={{0,2},{2,0},{4,6},{6,4},{1,3},{3,1},{5,7},{7,5},{8,10},{10,8},{12,... | collective-permute-start | bytes 589832 | tf_op jit(solution)/shard_map/ppermute | solution.py:153
  27.2 2.6 %copy-start = (bf16[56,192,192]{2,1,0:T(8,128)(2,1)S(1)}, bf16[56,192,192]{2,1,0:T(8,128)(2,1)}, u32[]{:S(2)}) copy-start(bf16[56,192,192]{2,1,0:T(8,128)(2,1)} %blocks_ref.1) | copy-start | bytes 12386308
  32.9 17.1 %collective-permute-start.7 = (bf16[64,1536]{1,0:T(8,128)(2,1)S(1)}, bf16[64,1536]{1,0:T(8,128)(2,1)S(1)}, u32[]{:S(2)}, u32[]{:S(2)}) collective-permute-start(bf16[64,1536]{1,0:T(8,128)(2,1)S(1)} %blocks.1.products_ref.rest_0_), channel_id=1, source_target_pairs={{0,8},{8,0},{1,9},{9,1},{2,10},{10,2},{3,11},{11,3},{4,12},{12,4},... | collective-permute-start | bytes 589832 | tf_op jit(solution)/shard_map/ppermute | solution.py:175
  42.1 12.6 %collective-permute-start.5 = (bf16[128,1536]{1,0:T(8,128)(2,1)S(1)}, bf16[128,1536]{1,0:T(8,128)(2,1)S(1)}, u32[]{:S(2)}, u32[]{:S(2)}) collective-permute-start(bf16[128,1536]{1,0:T(8,128)(2,1)S(1)} %join.1.pair_ref), channel_id=1, source_target_pairs={{0,6},{2,4},{4,2},{6,0},{1,7},{3,5},{5,3},{7,1},{8,14},{10,12},{12... | collective-permute-start | bytes 1179656 | tf_op jit(solution)/shard_map/ppermute | solution.py:177
  45.2 6.7 %collective-permute-start.6 = (bf16[64,1536]{1,0:T(8,128)(2,1)S(1)}, bf16[64,1536]{1,0:T(8,128)(2,1)S(1)}, u32[]{:S(2)}, u32[]{:S(2)}) collective-permute-start(bf16[64,1536]{1,0:T(8,128)(2,1)S(1)} %blocks.1.products_ref.rest_0_), channel_id=1, source_target_pairs={{0,1},{1,0},{2,3},{3,2},{4,5},{5,4},{6,7},{7,6},{8,9},{9,8},{10,11... | collective-permute-start | bytes 589832 | tf_op jit(solution)/shard_map/ppermute | solution.py:176
  50.0 3.3 %collective-permute-start.8 = (bf16[64,1536]{1,0:T(8,128)(2,1)S(1)}, bf16[64,1536]{1,0:T(8,128)(2,1)S(1)}, u32[]{:S(2)}, u32[]{:S(2)}) collective-permute-start(bf16[64,1536]{1,0:T(8,128)(2,1)S(1)} %collective-permute-done.7.rest_2_), channel_id=1, source_target_pairs={{0,1},{1,0},{2,3},{3,2},{4,5},{5,4},{6,7},{7,6},{8,9},{9,8},{10,11... | collective-permute-start | bytes 589832 | tf_op jit(solution)/shard_map/ppermute | solution.py:190
  73.8 9.5 %collective-permute-start.9 = (f32[32,64]{1,0:T(8,128)S(1)}, f32[32,64]{1,0:T(8,128)S(1)}, u32[]{:S(2)}, u32[]{:S(2)}) collective-permute-start(f32[32,64]{1,0:T(8,128)S(1)} %sum.1), channel_id=1, source_target_pairs={{0,0},{1,1},{2,64},{3,65},{4,128},{5,129},{6,192},{7,193},{8,8},{9... | collective-permute-start | bytes 24584 | tf_op jit(solution)/shard_map/ppermute | solution.py:215

commit v15 on v12

--- a/solution.py
+++ b/solution.py
@@ -175,6 +175,8 @@
     other_pair = lax.ppermute(pair, "x", [(i, i ^ FAR) for i in range(4)])
     place = jnp.stack([lax.axis_index(name) for name in ("z_hi", "x", "core")]).astype(jnp.int32)
     chunks_shape = shape((parts, 16, 128), jnp.bfloat16)
+    over_both = lax.ppermute(over_z, "core", swap)
+    behind, over_z = lax.optimization_barrier((products, over_z))
     begun = pl.pallas_call(
         own_tile_kernel,
         out_shape=chunks_shape,
@@ -183,9 +185,7 @@
         compiler_params=pltpu.CompilerParams(vmem_limit_bytes=16 << 20),
         cost_estimate=pl.CostEstimate(flops=2 << 23, bytes_accessed=1 << 20, transcendentals=0),
         name="own_tile",
-    )(place, pair, products)
-    behind, begun = lax.optimization_barrier((over_z, begun))
-    over_both = lax.ppermute(behind, "core", swap)
+    )(place, pair, behind)
     chunks = pl.pallas_call(
         tile_kernel,
         out_shape=chunks_shape,

time: 84.5 us -> 84.5 us (level)
    ppermute x1, waiting for transfers between devices: 1.4 us -> 0.45 us  [local(): over_both = lax.ppermute(over_z, 'core', swap)]
    ppermute x1, waiting for transfers between devices: 2.01 us -> 2.95 us  [local(): over_z = lax.ppermute(products, 'z_hi', swap)]
where the time goes in v15:
time: 84.5 us; the launch traced here: 84 us
  starting transfers between devices  42.7 us (51%)
  blocking collectives  18 us (21%)
  waiting for transfers between devices  11 us (13%)
  Pallas kernels  5.92 us (7%)
  local copies, waits for them, and re-layouts  4.77 us (6%)
  other arithmetic  0.85 us (1%)
    ppermute x4, starting transfers between devices, local(): arriving.append(lax.ppermute(block, mesh_axes, route))  21.6 us
    all_to_all x1, blocking collectives, local(): shares = lax.all_to_all(chunks, mesh_axes, 0, 0, tiled=True)  18 us
    ppermute x1, starting transfers between devices, local(): over_z = lax.ppermute(products, 'z_hi', swap)  8.22 us
    ppermute x1, waiting for transfers between devices, local(): return lax.ppermute(block, whole, route).T  6.27 us
    unnamed x7, local copies, waits for them, and re-layouts  4.77 us
    ppermute x1, starting transfers between devices, local(): return lax.ppermute(block, whole, route).T  3.25 us
    ppermute x1, starting transfers between devices, local(): other_pair = lax.ppermute(pair, 'x', [(i, i ^ FAR) for i in range(4)])  3.05 us
    ppermute x1, waiting for transfers between devices, local(): over_z = lax.ppermute(products, 'z_hi', swap)  2.95 us
  transfers between devices with their start and end apart: 10, of which 4 were waited for; matrix products, arithmetic and copies ran while one was open for 1% of the time, Pallas kernels for 5%

profile of v15, /device:TPU:6, one launch (start us, length us, event | category | flops | bytes accessed | tf_op | source)
XLA Modules:
  0.0 84.0 jit_solution(1651044604012910453)
XLA Ops:
  0.0 0.9 %copy-done.1 = bf16[8,64,192]{2,1,0:T(8,128)(2,1)S(1)} copy-done((bf16[8,64,192]{2,1,0:T(8,128)(2,1)S(1)}, bf16[8,64,192]{2,1,0:T(8,128)(2,1)}, u32[]{:S(2)}) %copy-start.1) | copy-done | bytes 196632
  1.0 0.7 copy-done.2
  1.6 0.7 select.1
  2.3 4.3 %collective-permute-start.1 = (bf16[64,768]{1,0:T(8,128)(2,1)S(1)}, bf16[64,768]{1,0:T(8,128)(2,1)S(1)}, u32[]{:S(2)}, u32[]{:S(2)}) collective-permute-start(bf16[64,768]{1,0:T(8,128)(2,1)S(1)} %get-tuple-element.14), channel_id=1, source_target_pairs={{496,0},{0,16},{16,32},{32,48},{48,64},{64,80},{80,96},{96,112},{1... | collective-permute-start | bytes 294920 | tf_op jit(solution)/shard_map/ppermute | solution.py:136
  6.6 8.4 %collective-permute-start.2 = (bf16[64,768]{1,0:T(8,128)(2,1)S(1)}, bf16[64,768]{1,0:T(8,128)(2,1)S(1)}, u32[]{:S(2)}, u32[]{:S(2)}) collective-permute-start(bf16[64,768]{1,0:T(8,128)(2,1)S(1)} %get-tuple-element.15), channel_id=1, source_target_pairs={{16,0},{32,16},{48,32},{64,48},{80,64},{96,80},{112,96},{128,112},... | collective-permute-start | bytes 294920 | tf_op jit(solution)/shard_map/ppermute | solution.py:136
  15.0 1.9 %collective-permute-start.3 = (bf16[64,768]{1,0:T(8,128)(2,1)S(1)}, bf16[64,768]{1,0:T(8,128)(2,1)S(1)}, u32[]{:S(2)}, u32[]{:S(2)}) collective-permute-start(bf16[64,768]{1,0:T(8,128)(2,1)S(1)} %get-tuple-element.16), channel_id=1, source_target_pairs={{480,0},{496,16},{0,32},{16,48},{32,64},{48,80},{64,96},{80,112},{... | collective-permute-start | bytes 294920 | tf_op jit(solution)/shard_map/ppermute | solution.py:136
  17.0 6.9 %collective-permute-start.4 = (bf16[64,768]{1,0:T(8,128)(2,1)S(1)}, bf16[64,768]{1,0:T(8,128)(2,1)S(1)}, u32[]{:S(2)}, u32[]{:S(2)}) collective-permute-start(bf16[64,768]{1,0:T(8,128)(2,1)S(1)} %get-tuple-element.17), channel_id=1, source_target_pairs={{32,0},{48,16},{64,32},{80,48},{96,64},{112,80},{128,96},{144,112}... | collective-permute-start | bytes 294920 | tf_op jit(solution)/shard_map/ppermute | solution.py:136
  23.9 2.7 %collective-permute-start = (bf16[64,1536]{1,0:T(8,128)(2,1)S(1)}, bf16[64,1536]{1,0:T(8,128)(2,1)S(1)}, u32[]{:S(2)}, u32[]{:S(2)}) collective-permute-start(bf16[64,1536]{1,0:T(8,128)(2,1)S(1)} %get-tuple-element.13.own_ref), channel_id=1, source_target_pairs={{0,2},{2,0},{4,6},{6,4},{1,3},{3,1},{5,7},{7,5},{8,10},{10,8},{12,... | collective-permute-start | bytes 589832 | tf_op jit(solution)/shard_map/ppermute | solution.py:151
  27.3 0.8 convert_select_fusion.table_ref
  28.1 2.6 %copy-done = bf16[56,192,192]{2,1,0:T(8,128)(2,1)S(1)} copy-done((bf16[56,192,192]{2,1,0:T(8,128)(2,1)S(1)}, bf16[56,192,192]{2,1,0:T(8,128)(2,1)}, u32[]{:S(2)}) %copy-start) | copy-done | bytes 4128792
  31.0 2.8 %blocks.1.products_ref.rest_0_ = bf16[64,1536]{1,0:T(8,128)(2,1)S(1)} custom-call(f32[8,56]{1,0:T(8,128)S(1)} %convert_select_fusion.table_ref, bf16[64,1536]{1,0:T(8,128)(2,1)S(1)} %get-tuple-element.13.own_ref, bf16[56,192,192]{2,1,0:T(8,128)(2,1)S(1)} %stage.1.blocks_ref, bf16[64,768]{1,0:T(8,128)(2,1)S(1)} %collective-permute-done.1.rest_0_, ...), custom_call_target="tpu_custom_call" | custom-call | tf_op jit(solution)/shard_map/blocks/pallas_call | solution.py:152
  33.8 8.2 %collective-permute-start.7 = (bf16[64,1536]{1,0:T(8,128)(2,1)S(1)}, bf16[64,1536]{1,0:T(8,128)(2,1)S(1)}, u32[]{:S(2)}, u32[]{:S(2)}) collective-permute-start(bf16[64,1536]{1,0:T(8,128)(2,1)S(1)} %blocks.1.products_ref.rest_0_), channel_id=1, source_target_pairs={{0,8},{8,0},{1,9},{9,1},{2,10},{10,2},{3,11},{11,3},{4,12},{12,4},... | collective-permute-start | bytes 589832 | tf_op jit(solution)/shard_map/ppermute | solution.py:173
  42.1 3.0 %collective-permute-start.5 = (bf16[128,1536]{1,0:T(8,128)(2,1)S(1)}, bf16[128,1536]{1,0:T(8,128)(2,1)S(1)}, u32[]{:S(2)}, u32[]{:S(2)}) collective-permute-start(bf16[128,1536]{1,0:T(8,128)(2,1)S(1)} %join.1.pair_ref), channel_id=1, source_target_pairs={{0,6},{2,4},{4,2},{6,0},{1,7},{3,5},{5,3},{7,1},{8,14},{10,12},{12... | collective-permute-start | bytes 1179656 | tf_op jit(solution)/shard_map/ppermute | solution.py:175
  45.1 1.9 %collective-permute-start.6 = (bf16[64,1536]{1,0:T(8,128)(2,1)S(1)}, bf16[64,1536]{1,0:T(8,128)(2,1)S(1)}, u32[]{:S(2)}, u32[]{:S(2)}) collective-permute-start(bf16[64,1536]{1,0:T(8,128)(2,1)S(1)} %blocks.1.products_ref.rest_0_), channel_id=1, source_target_pairs={{0,1},{1,0},{2,3},{3,2},{4,5},{5,4},{6,7},{7,6},{8,9},{9,8},{10,11... | collective-permute-start | bytes 589832 | tf_op jit(solution)/shard_map/ppermute | solution.py:174
  47.1 2.9 %collective-permute-done.7.rest_2_ = bf16[64,1536]{1,0:T(8,128)(2,1)S(1)} collective-permute-done((bf16[64,1536]{1,0:T(8,128)(2,1)S(1)}, bf16[64,1536]{1,0:T(8,128)(2,1)S(1)}, u32[]{:S(2)}, u32[]{:S(2)}) %collective-permute-start.7) | collective-permute-done | bytes 196640 | tf_op jit(solution)/shard_map/ppermute | solution.py:173
  50.0 1.9 %collective-permute-start.8 = (bf16[64,1536]{1,0:T(8,128)(2,1)S(1)}, bf16[64,1536]{1,0:T(8,128)(2,1)S(1)}, u32[]{:S(2)}, u32[]{:S(2)}) collective-permute-start(bf16[64,1536]{1,0:T(8,128)(2,1)S(1)} %collective-permute-done.7.rest_2_), channel_id=1, source_target_pairs={{0,1},{1,0},{2,3},{3,2},{4,5},{5,4},{6,7},{7,6},{8,9},{9,8},{10,11... | collective-permute-start | bytes 589832 | tf_op jit(solution)/shard_map/ppermute | solution.py:178
  52.0 0.9 %own_tile.1.rest_4_ = bf16[32,16,128]{2,1,0:T(8,128)(2,1)S(1)} custom-call(s32[3]{0:T(128)S(1)} %pad_add_fusion.place_ref, bf16[128,1536]{1,0:T(8,128)(2,1)S(1)} %join.1.pair_ref, bf16[64,1536]{1,0:T(8,128)(2,1)S(1)} %blocks.1.products_ref.rest_0_), custom_call_target="tpu_custom_call" | custom-call | flops 16777216 | bytes 1048576 | tf_op jit(solution)/shard_map/own_tile/pallas_call | solution.py:180
  52.9 0.4 collective-permute-done.8.rest_3_
  53.3 1.3 %collective-permute-done.5.other_pair_ref = bf16[128,1536]{1,0:T(8,128)(2,1)S(1)} collective-permute-done((bf16[128,1536]{1,0:T(8,128)(2,1)S(1)}, bf16[128,1536]{1,0:T(8,128)(2,1)S(1)}, u32[]{:S(2)}, u32[]{:S(2)}) %collective-permute-start.5) | collective-permute-done | bytes 393248 | tf_op jit(solution)/shard_map/ppermute | solution.py:175
  54.6 1.1 %tile.1 = bf16[32,16,128]{2,1,0:T(8,128)(2,1)S(1)} custom-call(s32[3]{0:T(128)S(1)} %pad_add_fusion.place_ref, bf16[128,1536]{1,0:T(8,128)(2,1)S(1)} %join.1.pair_ref, bf16[128,1536]{1,0:T(8,128)(2,1)S(1)} %collective-permute-done.5.other_pair_ref, bf16[64,1536]{1,0:T(8,128)(2,1)S(1)} %blocks.1.products_ref.rest_0_, ...), custom_call_target="tpu_custom_call", output_to_operand_aliasing={{}: (7, {})} | custom-call | tf_op jit(solution)/shard_map/tile/pallas_call | solution.py:189
  55.8 18.0 %all_to_all.5.parts_ref = bf16[32,16,128]{2,1,0:T(8,128)(2,1)S(1)} all-to-all(bf16[32,16,128]{2,1,0:T(8,128)(2,1)S(1)} %tile.1), channel_id=1, replica_groups=mesh['y'=8,'z_lo'=4,'z_hi'=2,'x'=4,'core'=2] {'y','z_lo'}, dimensions={0} | all-to-all | bytes 262144 | tf_op jit(solution)/shard_map/all_to_all | solution.py:198
  73.8 3.3 %collective-permute-start.9 = (f32[32,64]{1,0:T(8,128)S(1)}, f32[32,64]{1,0:T(8,128)S(1)}, u32[]{:S(2)}, u32[]{:S(2)}) collective-permute-start(f32[32,64]{1,0:T(8,128)S(1)} %sum.1), channel_id=1, source_target_pairs={{0,0},{1,1},{2,64},{3,65},{4,128},{5,129},{6,192},{7,193},{8,8},{9... | collective-permute-start | bytes 24584 | tf_op jit(solution)/shard_map/ppermute | solution.py:213
  77.1 6.3 %collective-permute-done.9 = f32[32,64]{1,0:T(8,128)S(1)} collective-permute-done((f32[32,64]{1,0:T(8,128)S(1)}, f32[32,64]{1,0:T(8,128)S(1)}, u32[]{:S(2)}, u32[]{:S(2)}) %collective-permute-start.9) | collective-permute-done | bytes 8224 | tf_op jit(solution)/shard_map/ppermute | solution.py:213
  83.4 0.6 copy.12
  (15 shorter events, 0.6 us)
Async XLA Ops:
  0.0 0.9 %copy-start.1 = (bf16[8,64,192]{2,1,0:T(8,128)(2,1)S(1)}, bf16[8,64,192]{2,1,0:T(8,128)(2,1)}, u32[]{:S(2)}) copy-start(bf16[8,64,192]{2,1,0:T(8,128)(2,1)} %basis_ref.1) | copy-start | bytes 589828
  1.0 0.7 copy-start.2
  2.3 28.7 %collective-permute-start.1 = (bf16[64,768]{1,0:T(8,128)(2,1)S(1)}, bf16[64,768]{1,0:T(8,128)(2,1)S(1)}, u32[]{:S(2)}, u32[]{:S(2)}) collective-permute-start(bf16[64,768]{1,0:T(8,128)(2,1)S(1)} %get-tuple-element.14), channel_id=1, source_target_pairs={{496,0},{0,16},{16,32},{32,48},{48,64},{64,80},{80,96},{96,112},{1... | collective-permute-start | bytes 294920 | tf_op jit(solution)/shard_map/ppermute | solution.py:136
  6.6 24.4 %collective-permute-start.2 = (bf16[64,768]{1,0:T(8,128)(2,1)S(1)}, bf16[64,768]{1,0:T(8,128)(2,1)S(1)}, u32[]{:S(2)}, u32[]{:S(2)}) collective-permute-start(bf16[64,768]{1,0:T(8,128)(2,1)S(1)} %get-tuple-element.15), channel_id=1, source_target_pairs={{16,0},{32,16},{48,32},{64,48},{80,64},{96,80},{112,96},{128,112},... | collective-permute-start | bytes 294920 | tf_op jit(solution)/shard_map/ppermute | solution.py:136
  15.0 16.0 %collective-permute-start.3 = (bf16[64,768]{1,0:T(8,128)(2,1)S(1)}, bf16[64,768]{1,0:T(8,128)(2,1)S(1)}, u32[]{:S(2)}, u32[]{:S(2)}) collective-permute-start(bf16[64,768]{1,0:T(8,128)(2,1)S(1)} %get-tuple-element.16), channel_id=1, source_target_pairs={{480,0},{496,16},{0,32},{16,48},{32,64},{48,80},{64,96},{80,112},{... | collective-permute-start | bytes 294920 | tf_op jit(solution)/shard_map/ppermute | solution.py:136
  17.0 14.1 %collective-permute-start.4 = (bf16[64,768]{1,0:T(8,128)(2,1)S(1)}, bf16[64,768]{1,0:T(8,128)(2,1)S(1)}, u32[]{:S(2)}, u32[]{:S(2)}) collective-permute-start(bf16[64,768]{1,0:T(8,128)(2,1)S(1)} %get-tuple-element.17), channel_id=1, source_target_pairs={{32,0},{48,16},{64,32},{80,48},{96,64},{112,80},{128,96},{144,112}... | collective-permute-start | bytes 294920 | tf_op jit(solution)/shard_map/ppermute | solution.py:136
  23.9 18.1 %collective-permute-start = (bf16[64,1536]{1,0:T(8,128)(2,1)S(1)}, bf16[64,1536]{1,0:T(8,128)(2,1)S(1)}, u32[]{:S(2)}, u32[]{:S(2)}) collective-permute-start(bf16[64,1536]{1,0:T(8,128)(2,1)S(1)} %get-tuple-element.13.own_ref), channel_id=1, source_target_pairs={{0,2},{2,0},{4,6},{6,4},{1,3},{3,1},{5,7},{7,5},{8,10},{10,8},{12,... | collective-permute-start | bytes 589832 | tf_op jit(solution)/shard_map/ppermute | solution.py:151
  28.1 2.6 %copy-start = (bf16[56,192,192]{2,1,0:T(8,128)(2,1)S(1)}, bf16[56,192,192]{2,1,0:T(8,128)(2,1)}, u32[]{:S(2)}) copy-start(bf16[56,192,192]{2,1,0:T(8,128)(2,1)} %blocks_ref.1) | copy-start | bytes 12386308
  33.8 16.2 %collective-permute-start.7 = (bf16[64,1536]{1,0:T(8,128)(2,1)S(1)}, bf16[64,1536]{1,0:T(8,128)(2,1)S(1)}, u32[]{:S(2)}, u32[]{:S(2)}) collective-permute-start(bf16[64,1536]{1,0:T(8,128)(2,1)S(1)} %blocks.1.products_ref.rest_0_), channel_id=1, source_target_pairs={{0,8},{8,0},{1,9},{9,1},{2,10},{10,2},{3,11},{11,3},{4,12},{12,4},... | collective-permute-start | bytes 589832 | tf_op jit(solution)/shard_map/ppermute | solution.py:173
  42.1 12.6 %collective-permute-start.5 = (bf16[128,1536]{1,0:T(8,128)(2,1)S(1)}, bf16[128,1536]{1,0:T(8,128)(2,1)S(1)}, u32[]{:S(2)}, u32[]{:S(2)}) collective-permute-start(bf16[128,1536]{1,0:T(8,128)(2,1)S(1)} %join.1.pair_ref), channel_id=1, source_target_pairs={{0,6},{2,4},{4,2},{6,0},{1,7},{3,5},{5,3},{7,1},{8,14},{10,12},{12... | collective-permute-start | bytes 1179656 | tf_op jit(solution)/shard_map/ppermute | solution.py:175
  45.1 7.7 %collective-permute-start.6 = (bf16[64,1536]{1,0:T(8,128)(2,1)S(1)}, bf16[64,1536]{1,0:T(8,128)(2,1)S(1)}, u32[]{:S(2)}, u32[]{:S(2)}) collective-permute-start(bf16[64,1536]{1,0:T(8,128)(2,1)S(1)} %blocks.1.products_ref.rest_0_), channel_id=1, source_target_pairs={{0,1},{1,0},{2,3},{3,2},{4,5},{5,4},{6,7},{7,6},{8,9},{9,8},{10,11... | collective-permute-start | bytes 589832 | tf_op jit(solution)/shard_map/ppermute | solution.py:174
  50.0 3.3 %collective-permute-start.8 = (bf16[64,1536]{1,0:T(8,128)(2,1)S(1)}, bf16[64,1536]{1,0:T(8,128)(2,1)S(1)}, u32[]{:S(2)}, u32[]{:S(2)}) collective-permute-start(bf16[64,1536]{1,0:T(8,128)(2,1)S(1)} %collective-permute-done.7.rest_2_), channel_id=1, source_target_pairs={{0,1},{1,0},{2,3},{3,2},{4,5},{5,4},{6,7},{7,6},{8,9},{9,8},{10,11... | collective-permute-start | bytes 589832 | tf_op jit(solution)/shard_map/ppermute | solution.py:178
  73.8 9.5 %collective-permute-start.9 = (f32[32,64]{1,0:T(8,128)S(1)}, f32[32,64]{1,0:T(8,128)S(1)}, u32[]{:S(2)}, u32[]{:S(2)}) collective-permute-start(f32[32,64]{1,0:T(8,128)S(1)} %sum.1), channel_id=1, source_target_pairs={{0,0},{1,1},{2,64},{3,65},{4,128},{5,129},{6,192},{7,193},{8,8},{9... | collective-permute-start | bytes 24584 | tf_op jit(solution)/shard_map/ppermute | solution.py:213

commit v16 on v14

--- a/solution.py
+++ b/solution.py
@@ -177,6 +177,8 @@
     other_pair = lax.ppermute(pair, "x", [(i, i ^ FAR) for i in range(4)])
     place = jnp.stack([lax.axis_index(name) for name in ("z_hi", "x", "core")]).astype(jnp.int32)
     chunks_shape = shape((parts, 16, 128), jnp.bfloat16)
+    over_both = lax.ppermute(over_z, "core", swap)
+    behind, over_z = lax.optimization_barrier((products, over_z))
     begun = pl.pallas_call(
         own_tile_kernel,
         out_shape=chunks_shape,
@@ -185,9 +187,7 @@
         compiler_params=pltpu.CompilerParams(vmem_limit_bytes=16 << 20),
         cost_estimate=pl.CostEstimate(flops=2 << 23, bytes_accessed=1 << 20, transcendentals=0),
         name="own_tile",
-    )(place, pair, products)
-    behind, begun = lax.optimization_barrier((over_z, begun))
-    over_both = lax.ppermute(behind, "core", swap)
+    )(place, pair, behind)
     chunks = pl.pallas_call(
         tile_kernel,
         out_shape=chunks_shape,

time: 84.5 us -> 84.4 us (level)
    ppermute x1, waiting for transfers between devices: 1.4 us -> 0.45 us  [local(): over_both = lax.ppermute(over_z, 'core', swap)]
    ppermute x1, waiting for transfers between devices: 2.01 us -> 2.95 us  [local(): over_z = lax.ppermute(products, 'z_hi', swap)]
where the time goes in v16:
time: 84.4 us; the launch traced here: 84 us
  starting transfers between devices  42.7 us (51%)
  blocking collectives  18 us (21%)
  waiting for transfers between devices  11 us (13%)
  Pallas kernels  5.92 us (7%)
  local copies, waits for them, and re-layouts  4.77 us (6%)
  other arithmetic  0.85 us (1%)
    ppermute x4, starting transfers between devices, local(): arriving.append(lax.ppermute(picked[neighbour], mesh_axes, route))  20.7 us
    all_to_all x1, blocking collectives, local(): shares = lax.all_to_all(chunks, mesh_axes, 0, 0, tiled=True)  18 us
    ppermute x1, starting transfers between devices, local(): over_z = lax.ppermute(products, 'z_hi', swap)  9.12 us
    ppermute x1, waiting for transfers between devices, local(): return lax.ppermute(block, whole, route).T  6.26 us
    unnamed x7, local copies, waits for them, and re-layouts  4.77 us
    ppermute x1, starting transfers between devices, local(): return lax.ppermute(block, whole, route).T  3.26 us
    ppermute x1, starting transfers between devices, local(): other_pair = lax.ppermute(pair, 'x', [(i, i ^ FAR) for i in range(4)])  3.05 us
    ppermute x1, waiting for transfers between devices, local(): over_z = lax.ppermute(products, 'z_hi', swap)  2.95 us
  transfers between devices with their start and end apart: 10, of which 4 were waited for; matrix products, arithmetic and copies ran while one was open for 1% of the time, Pallas kernels for 5%

profile of v16, /device:TPU:6, one launch (start us, length us, event | category | flops | bytes accessed | tf_op | source)
XLA Modules:
  0.0 84.0 jit_solution(4537827263370657584)
XLA Ops:
  0.0 0.9 %copy-done.1 = bf16[8,64,192]{2,1,0:T(8,128)(2,1)S(1)} copy-done((bf16[8,64,192]{2,1,0:T(8,128)(2,1)S(1)}, bf16[8,64,192]{2,1,0:T(8,128)(2,1)}, u32[]{:S(2)}) %copy-start.1) | copy-done | bytes 196632
  1.0 0.7 copy-done.2
  1.6 0.7 select.1
  2.3 6.1 %collective-permute-start.1 = (bf16[64,768]{1,0:T(8,128)(2,1)S(1)}, bf16[64,768]{1,0:T(8,128)(2,1)S(1)}, u32[]{:S(2)}, u32[]{:S(2)}) collective-permute-start(bf16[64,768]{1,0:T(8,128)(2,1)S(1)} %get-tuple-element.14), channel_id=1, source_target_pairs={{480,0},{496,16},{0,32},{16,48},{32,64},{48,80},{64,96},{80,112},{... | collective-permute-start | bytes 294920 | tf_op jit(solution)/shard_map/ppermute | solution.py:138
  8.4 4.8 %collective-permute-start.2 = (bf16[64,768]{1,0:T(8,128)(2,1)S(1)}, bf16[64,768]{1,0:T(8,128)(2,1)S(1)}, u32[]{:S(2)}, u32[]{:S(2)}) collective-permute-start(bf16[64,768]{1,0:T(8,128)(2,1)S(1)} %get-tuple-element.15), channel_id=1, source_target_pairs={{32,0},{48,16},{64,32},{80,48},{96,64},{112,80},{128,96},{144,112}... | collective-permute-start | bytes 294920 | tf_op jit(solution)/shard_map/ppermute | solution.py:138
  13.2 4.3 %collective-permute-start.3 = (bf16[64,768]{1,0:T(8,128)(2,1)S(1)}, bf16[64,768]{1,0:T(8,128)(2,1)S(1)}, u32[]{:S(2)}, u32[]{:S(2)}) collective-permute-start(bf16[64,768]{1,0:T(8,128)(2,1)S(1)} %get-tuple-element.16), channel_id=1, source_target_pairs={{496,0},{0,16},{16,32},{32,48},{48,64},{64,80},{80,96},{96,112},{1... | collective-permute-start | bytes 294920 | tf_op jit(solution)/shard_map/ppermute | solution.py:138
  17.5 5.5 %collective-permute-start.4 = (bf16[64,768]{1,0:T(8,128)(2,1)S(1)}, bf16[64,768]{1,0:T(8,128)(2,1)S(1)}, u32[]{:S(2)}, u32[]{:S(2)}) collective-permute-start(bf16[64,768]{1,0:T(8,128)(2,1)S(1)} %get-tuple-element.17), channel_id=1, source_target_pairs={{16,0},{32,16},{48,32},{64,48},{80,64},{96,80},{112,96},{128,112},... | collective-permute-start | bytes 294920 | tf_op jit(solution)/shard_map/ppermute | solution.py:138
  23.0 2.7 %collective-permute-start = (bf16[64,1536]{1,0:T(8,128)(2,1)S(1)}, bf16[64,1536]{1,0:T(8,128)(2,1)S(1)}, u32[]{:S(2)}, u32[]{:S(2)}) collective-permute-start(bf16[64,1536]{1,0:T(8,128)(2,1)S(1)} %get-tuple-element.13.own_ref), channel_id=1, source_target_pairs={{0,2},{2,0},{4,6},{6,4},{1,3},{3,1},{5,7},{7,5},{8,10},{10,8},{12,... | collective-permute-start | bytes 589832 | tf_op jit(solution)/shard_map/ppermute | solution.py:153
  26.4 0.8 convert_select_fusion.table_ref
  27.2 2.6 %copy-done = bf16[56,192,192]{2,1,0:T(8,128)(2,1)S(1)} copy-done((bf16[56,192,192]{2,1,0:T(8,128)(2,1)S(1)}, bf16[56,192,192]{2,1,0:T(8,128)(2,1)}, u32[]{:S(2)}) %copy-start) | copy-done | bytes 4128792
  30.1 2.8 %blocks.1.products_ref.rest_0_ = bf16[64,1536]{1,0:T(8,128)(2,1)S(1)} custom-call(f32[8,56]{1,0:T(8,128)S(1)} %convert_select_fusion.table_ref, bf16[64,1536]{1,0:T(8,128)(2,1)S(1)} %get-tuple-element.13.own_ref, bf16[56,192,192]{2,1,0:T(8,128)(2,1)S(1)} %stage.1.blocks_ref, bf16[64,768]{1,0:T(8,128)(2,1)S(1)} %collective-permute-done.1.rest_0_, ...), custom_call_target="tpu_custom_call" | custom-call | tf_op jit(solution)/shard_map/blocks/pallas_call | solution.py:154
  32.9 9.1 %collective-permute-start.7 = (bf16[64,1536]{1,0:T(8,128)(2,1)S(1)}, bf16[64,1536]{1,0:T(8,128)(2,1)S(1)}, u32[]{:S(2)}, u32[]{:S(2)}) collective-permute-start(bf16[64,1536]{1,0:T(8,128)(2,1)S(1)} %blocks.1.products_ref.rest_0_), channel_id=1, source_target_pairs={{0,8},{8,0},{1,9},{9,1},{2,10},{10,2},{3,11},{11,3},{4,12},{12,4},... | collective-permute-start | bytes 589832 | tf_op jit(solution)/shard_map/ppermute | solution.py:175
  42.1 3.0 %collective-permute-start.5 = (bf16[128,1536]{1,0:T(8,128)(2,1)S(1)}, bf16[128,1536]{1,0:T(8,128)(2,1)S(1)}, u32[]{:S(2)}, u32[]{:S(2)}) collective-permute-start(bf16[128,1536]{1,0:T(8,128)(2,1)S(1)} %join.1.pair_ref), channel_id=1, source_target_pairs={{0,6},{2,4},{4,2},{6,0},{1,7},{3,5},{5,3},{7,1},{8,14},{10,12},{12... | collective-permute-start | bytes 1179656 | tf_op jit(solution)/shard_map/ppermute | solution.py:177
  45.1 1.9 %collective-permute-start.6 = (bf16[64,1536]{1,0:T(8,128)(2,1)S(1)}, bf16[64,1536]{1,0:T(8,128)(2,1)S(1)}, u32[]{:S(2)}, u32[]{:S(2)}) collective-permute-start(bf16[64,1536]{1,0:T(8,128)(2,1)S(1)} %blocks.1.products_ref.rest_0_), channel_id=1, source_target_pairs={{0,1},{1,0},{2,3},{3,2},{4,5},{5,4},{6,7},{7,6},{8,9},{9,8},{10,11... | collective-permute-start | bytes 589832 | tf_op jit(solution)/shard_map/ppermute | solution.py:176
  47.1 2.9 %collective-permute-done.7.rest_2_ = bf16[64,1536]{1,0:T(8,128)(2,1)S(1)} collective-permute-done((bf16[64,1536]{1,0:T(8,128)(2,1)S(1)}, bf16[64,1536]{1,0:T(8,128)(2,1)S(1)}, u32[]{:S(2)}, u32[]{:S(2)}) %collective-permute-start.7) | collective-permute-done | bytes 196640 | tf_op jit(solution)/shard_map/ppermute | solution.py:175
  50.0 1.9 %collective-permute-start.8 = (bf16[64,1536]{1,0:T(8,128)(2,1)S(1)}, bf16[64,1536]{1,0:T(8,128)(2,1)S(1)}, u32[]{:S(2)}, u32[]{:S(2)}) collective-permute-start(bf16[64,1536]{1,0:T(8,128)(2,1)S(1)} %collective-permute-done.7.rest_2_), channel_id=1, source_target_pairs={{0,1},{1,0},{2,3},{3,2},{4,5},{5,4},{6,7},{7,6},{8,9},{9,8},{10,11... | collective-permute-start | bytes 589832 | tf_op jit(solution)/shard_map/ppermute | solution.py:180
  52.0 0.9 %own_tile.1.rest_4_ = bf16[32,16,128]{2,1,0:T(8,128)(2,1)S(1)} custom-call(s32[3]{0:T(128)S(1)} %pad_add_fusion.place_ref, bf16[128,1536]{1,0:T(8,128)(2,1)S(1)} %join.1.pair_ref, bf16[64,1536]{1,0:T(8,128)(2,1)S(1)} %blocks.1.products_ref.rest_0_), custom_call_target="tpu_custom_call" | custom-call | flops 16777216 | bytes 1048576 | tf_op jit(solution)/shard_map/own_tile/pallas_call | solution.py:182
  52.9 0.5 collective-permute-done.8.rest_3_
  53.3 1.3 %collective-permute-done.5.other_pair_ref = bf16[128,1536]{1,0:T(8,128)(2,1)S(1)} collective-permute-done((bf16[128,1536]{1,0:T(8,128)(2,1)S(1)}, bf16[128,1536]{1,0:T(8,128)(2,1)S(1)}, u32[]{:S(2)}, u32[]{:S(2)}) %collective-permute-start.5) | collective-permute-done | bytes 393248 | tf_op jit(solution)/shard_map/ppermute | solution.py:177
  54.6 1.1 %tile.1 = bf16[32,16,128]{2,1,0:T(8,128)(2,1)S(1)} custom-call(s32[3]{0:T(128)S(1)} %pad_add_fusion.place_ref, bf16[128,1536]{1,0:T(8,128)(2,1)S(1)} %join.1.pair_ref, bf16[128,1536]{1,0:T(8,128)(2,1)S(1)} %collective-permute-done.5.other_pair_ref, bf16[64,1536]{1,0:T(8,128)(2,1)S(1)} %blocks.1.products_ref.rest_0_, ...), custom_call_target="tpu_custom_call", output_to_operand_aliasing={{}: (7, {})} | custom-call | tf_op jit(solution)/shard_map/tile/pallas_call | solution.py:191
  55.8 18.0 %all_to_all.5.parts_ref = bf16[32,16,128]{2,1,0:T(8,128)(2,1)S(1)} all-to-all(bf16[32,16,128]{2,1,0:T(8,128)(2,1)S(1)} %tile.1), channel_id=1, replica_groups=mesh['y'=8,'z_lo'=4,'z_hi'=2,'x'=4,'core'=2] {'y','z_lo'}, dimensions={0} | all-to-all | bytes 262144 | tf_op jit(solution)/shard_map/all_to_all | solution.py:200
  73.8 3.3 %collective-permute-start.9 = (f32[32,64]{1,0:T(8,128)S(1)}, f32[32,64]{1,0:T(8,128)S(1)}, u32[]{:S(2)}, u32[]{:S(2)}) collective-permute-start(f32[32,64]{1,0:T(8,128)S(1)} %sum.1), channel_id=1, source_target_pairs={{0,0},{1,1},{2,64},{3,65},{4,128},{5,129},{6,192},{7,193},{8,8},{9... | collective-permute-start | bytes 24584 | tf_op jit(solution)/shard_map/ppermute | solution.py:215
  77.1 6.3 %collective-permute-done.9 = f32[32,64]{1,0:T(8,128)S(1)} collective-permute-done((f32[32,64]{1,0:T(8,128)S(1)}, f32[32,64]{1,0:T(8,128)S(1)}, u32[]{:S(2)}, u32[]{:S(2)}) %collective-permute-start.9) | collective-permute-done | bytes 8224 | tf_op jit(solution)/shard_map/ppermute | solution.py:215
  83.4 0.6 copy.12
  (15 shorter events, 0.6 us)
Async XLA Ops:
  0.0 0.9 %copy-start.1 = (bf16[8,64,192]{2,1,0:T(8,128)(2,1)S(1)}, bf16[8,64,192]{2,1,0:T(8,128)(2,1)}, u32[]{:S(2)}) copy-start(bf16[8,64,192]{2,1,0:T(8,128)(2,1)} %basis_ref.1) | copy-start | bytes 589828
  1.0 0.7 copy-start.2
  2.3 27.8 %collective-permute-start.1 = (bf16[64,768]{1,0:T(8,128)(2,1)S(1)}, bf16[64,768]{1,0:T(8,128)(2,1)S(1)}, u32[]{:S(2)}, u32[]{:S(2)}) collective-permute-start(bf16[64,768]{1,0:T(8,128)(2,1)S(1)} %get-tuple-element.14), channel_id=1, source_target_pairs={{480,0},{496,16},{0,32},{16,48},{32,64},{48,80},{64,96},{80,112},{... | collective-permute-start | bytes 294920 | tf_op jit(solution)/shard_map/ppermute | solution.py:138
  8.4 21.7 %collective-permute-start.2 = (bf16[64,768]{1,0:T(8,128)(2,1)S(1)}, bf16[64,768]{1,0:T(8,128)(2,1)S(1)}, u32[]{:S(2)}, u32[]{:S(2)}) collective-permute-start(bf16[64,768]{1,0:T(8,128)(2,1)S(1)} %get-tuple-element.15), channel_id=1, source_target_pairs={{32,0},{48,16},{64,32},{80,48},{96,64},{112,80},{128,96},{144,112}... | collective-permute-start | bytes 294920 | tf_op jit(solution)/shard_map/ppermute | solution.py:138
  13.2 16.9 %collective-permute-start.3 = (bf16[64,768]{1,0:T(8,128)(2,1)S(1)}, bf16[64,768]{1,0:T(8,128)(2,1)S(1)}, u32[]{:S(2)}, u32[]{:S(2)}) collective-permute-start(bf16[64,768]{1,0:T(8,128)(2,1)S(1)} %get-tuple-element.16), channel_id=1, source_target_pairs={{496,0},{0,16},{16,32},{32,48},{48,64},{64,80},{80,96},{96,112},{1... | collective-permute-start | bytes 294920 | tf_op jit(solution)/shard_map/ppermute | solution.py:138
  17.5 12.6 %collective-permute-start.4 = (bf16[64,768]{1,0:T(8,128)(2,1)S(1)}, bf16[64,768]{1,0:T(8,128)(2,1)S(1)}, u32[]{:S(2)}, u32[]{:S(2)}) collective-permute-start(bf16[64,768]{1,0:T(8,128)(2,1)S(1)} %get-tuple-element.17), channel_id=1, source_target_pairs={{16,0},{32,16},{48,32},{64,48},{80,64},{96,80},{112,96},{128,112},... | collective-permute-start | bytes 294920 | tf_op jit(solution)/shard_map/ppermute | solution.py:138
  23.0 19.0 %collective-permute-start = (bf16[64,1536]{1,0:T(8,128)(2,1)S(1)}, bf16[64,1536]{1,0:T(8,128)(2,1)S(1)}, u32[]{:S(2)}, u32[]{:S(2)}) collective-permute-start(bf16[64,1536]{1,0:T(8,128)(2,1)S(1)} %get-tuple-element.13.own_ref), channel_id=1, source_target_pairs={{0,2},{2,0},{4,6},{6,4},{1,3},{3,1},{5,7},{7,5},{8,10},{10,8},{12,... | collective-permute-start | bytes 589832 | tf_op jit(solution)/shard_map/ppermute | solution.py:153
  27.2 2.6 %copy-start = (bf16[56,192,192]{2,1,0:T(8,128)(2,1)S(1)}, bf16[56,192,192]{2,1,0:T(8,128)(2,1)}, u32[]{:S(2)}) copy-start(bf16[56,192,192]{2,1,0:T(8,128)(2,1)} %blocks_ref.1) | copy-start | bytes 12386308
  32.9 17.1 %collective-permute-start.7 = (bf16[64,1536]{1,0:T(8,128)(2,1)S(1)}, bf16[64,1536]{1,0:T(8,128)(2,1)S(1)}, u32[]{:S(2)}, u32[]{:S(2)}) collective-permute-start(bf16[64,1536]{1,0:T(8,128)(2,1)S(1)} %blocks.1.products_ref.rest_0_), channel_id=1, source_target_pairs={{0,8},{8,0},{1,9},{9,1},{2,10},{10,2},{3,11},{11,3},{4,12},{12,4},... | collective-permute-start | bytes 589832 | tf_op jit(solution)/shard_map/ppermute | solution.py:175
  42.1 12.6 %collective-permute-start.5 = (bf16[128,1536]{1,0:T(8,128)(2,1)S(1)}, bf16[128,1536]{1,0:T(8,128)(2,1)S(1)}, u32[]{:S(2)}, u32[]{:S(2)}) collective-permute-start(bf16[128,1536]{1,0:T(8,128)(2,1)S(1)} %join.1.pair_ref), channel_id=1, source_target_pairs={{0,6},{2,4},{4,2},{6,0},{1,7},{3,5},{5,3},{7,1},{8,14},{10,12},{12... | collective-permute-start | bytes 1179656 | tf_op jit(solution)/shard_map/ppermute | solution.py:177
  45.1 7.7 %collective-permute-start.6 = (bf16[64,1536]{1,0:T(8,128)(2,1)S(1)}, bf16[64,1536]{1,0:T(8,128)(2,1)S(1)}, u32[]{:S(2)}, u32[]{:S(2)}) collective-permute-start(bf16[64,1536]{1,0:T(8,128)(2,1)S(1)} %blocks.1.products_ref.rest_0_), channel_id=1, source_target_pairs={{0,1},{1,0},{2,3},{3,2},{4,5},{5,4},{6,7},{7,6},{8,9},{9,8},{10,11... | collective-permute-start | bytes 589832 | tf_op jit(solution)/shard_map/ppermute | solution.py:176
  50.0 3.3 %collective-permute-start.8 = (bf16[64,1536]{1,0:T(8,128)(2,1)S(1)}, bf16[64,1536]{1,0:T(8,128)(2,1)S(1)}, u32[]{:S(2)}, u32[]{:S(2)}) collective-permute-start(bf16[64,1536]{1,0:T(8,128)(2,1)S(1)} %collective-permute-done.7.rest_2_), channel_id=1, source_target_pairs={{0,1},{1,0},{2,3},{3,2},{4,5},{5,4},{6,7},{7,6},{8,9},{9,8},{10,11... | collective-permute-start | bytes 589832 | tf_op jit(solution)/shard_map/ppermute | solution.py:180
  73.8 9.5 %collective-permute-start.9 = (f32[32,64]{1,0:T(8,128)S(1)}, f32[32,64]{1,0:T(8,128)S(1)}, u32[]{:S(2)}, u32[]{:S(2)}) collective-permute-start(f32[32,64]{1,0:T(8,128)S(1)} %sum.1), channel_id=1, source_target_pairs={{0,0},{1,1},{2,64},{3,65},{4,128},{5,129},{6,192},{7,193},{8,8},{9... | collective-permute-start | bytes 24584 | tf_op jit(solution)/shard_map/ppermute | solution.py:215
